TPU v7x, 32 devices: a whole 2x2x4 slice. The times are simulated.
32 devices in a mesh: grp: 2 (over y), seq: 4 (over z), dp: 2 (over x), pipe: 2 (over core).
Axes of the slice: x: 2, y: 2, z: 4, core: 2. Of those that a mesh axis runs over, the one named last changes fastest.
Arguments:
- embeddings: bfloat16 [4, 512, 1664], P(('grp', 'dp'), 'seq'), parts along dimension 0, may hold values from -650 to 650
- upstream: bfloat16 [4, 512, 1664], P(('grp', 'dp'), 'seq'), parts along dimension 0, may hold values from -6 to 6
- attn_weights: bfloat16 [4, 1664, 832], P(None, ('seq', 'dp'), 'pipe'), may hold values from -1.2747549 to 1.2747549
Outputs:
- input_grads: bfloat16 [4, 512, 1664], P(('grp', 'dp'), 'seq'), parts along dimension 0
- weight_grads: float32 [8, 1664, 832], P('grp', ('seq', 'dp'), 'pipe'), parts along dimension 0
There are 2 independent parts, one for each index of `grp`. A program takes and returns all parts, laid end to end along the dimension named above; an argument that names none is the same for every part. Nothing has to cross between parts.
All inputs are finite; a program needn't handle non-finite values.
Results may differ from a plain program's by a relative error of at most 0.014.
The roundings to bfloat16 on the way count: a program that leaves them out, or rounds other values in their place, can miss the bound.
Values may be sent and summed in bfloat16 or wider, within the bound.
No kernel may reach another device: no remote copies, remote signals or barrier semaphores. Data moves between devices by JAX's collectives and lax.ppermute only.
A program may use at most 128 MiB of HBM per device.

v0:
```python
import math

import jax
import jax.numpy as jnp
from jax import lax
from jax.sharding import PartitionSpec as P

HD = 104


EPSILON = 1e-06


def local(embeddings, upstream, attn_weights):
    tokens = embeddings[0]
    row_gradients = upstream[0]
    row_count = tokens.shape[0]
    weights = lax.all_gather(attn_weights, ("seq", "dp"), axis=1, tiled=True)
    local_width = weights.shape[2]
    head_count = local_width // HD
    score_scale = HD ** (-0.5)
    features = tokens.astype(jnp.float32)
    row_mean = jnp.mean(features, axis=1, keepdims=True)
    mean_removed = features - row_mean
    variance = jnp.mean(mean_removed * mean_removed, axis=1, keepdims=True)
    inverse_deviation = lax.rsqrt(variance + EPSILON)
    standardized_input = mean_removed * inverse_deviation
    normalized_rows = standardized_input.astype(jnp.bfloat16)
    proj = jnp.einsum(
        "td,cdh->cth", normalized_rows, weights[:3], preferred_element_type=jnp.float32
    ).astype(jnp.bfloat16)
    gathered = lax.all_gather(proj[1:], "seq", axis=1, tiled=True)
    key_count = gathered.shape[1]
    query_heads = proj[0].reshape(row_count, head_count, HD).transpose(1, 0, 2)
    key_heads = gathered[0].reshape(key_count, head_count, HD).transpose(1, 0, 2)
    value_heads = gathered[1].reshape(key_count, head_count, HD).transpose(1, 0, 2)
    grad_att = jnp.dot(row_gradients, weights[3], preferred_element_type=jnp.float32).astype(
        jnp.bfloat16
    )
    grad_heads = grad_att.reshape(row_count, head_count, HD).transpose(1, 0, 2)

    def one_head(items):
        query_rows, key_rows, value_rows, grad_out = items
        scores = jnp.dot(query_rows, key_rows.T, preferred_element_type=jnp.float32) * score_scale
        row_max = jnp.max(scores, axis=1, keepdims=True)
        log_total = row_max + jnp.log(jnp.sum(jnp.exp(scores - row_max), axis=1, keepdims=True))
        probs = jnp.exp(scores - log_total).astype(jnp.bfloat16)
        attended = jnp.dot(probs, value_rows, preferred_element_type=jnp.float32).astype(
            jnp.bfloat16
        )
        row_delta = jnp.sum(
            grad_out.astype(jnp.float32) * attended.astype(jnp.float32), axis=1, keepdims=True
        )
        dprobs = jnp.dot(grad_out, value_rows.T, preferred_element_type=jnp.float32)
        dscores = (probs.astype(jnp.float32) * (dprobs - row_delta) * score_scale).astype(
            jnp.bfloat16
        )
        grad_q = jnp.dot(dscores, key_rows, preferred_element_type=jnp.float32).astype(jnp.bfloat16)
        key_term = jnp.dot(dscores.T, query_rows, preferred_element_type=jnp.float32)
        value_term = jnp.dot(probs.T, grad_out, preferred_element_type=jnp.float32)
        return (attended, grad_q, key_term, value_term)

    attended_h, grad_q_h, key_h, value_h = lax.map(
        one_head, (query_heads, key_heads, value_heads, grad_heads)
    )
    attended_flat = attended_h.transpose(1, 0, 2).reshape(row_count, local_width)
    grad_q = grad_q_h.transpose(1, 0, 2).reshape(1, row_count, local_width)
    key_terms = key_h.transpose(1, 0, 2).reshape(key_count, local_width)
    value_terms = value_h.transpose(1, 0, 2).reshape(key_count, local_width)
    both_terms = jnp.stack([key_terms, value_terms])
    owned = lax.psum_scatter(
        both_terms.astype(jnp.bfloat16), "seq", scatter_dimension=1, tiled=True
    )
    grad_qkv = jnp.concatenate([grad_q, owned], axis=0)
    token_count = row_count * lax.axis_size("seq") * lax.axis_size("dp")
    grad_factor = 1.0 / math.sqrt(token_count)
    terms_qkv = jnp.einsum(
        "td,cth->cdh", normalized_rows, grad_qkv, preferred_element_type=jnp.float32
    )
    term_out = jnp.einsum(
        "td,th->dh", row_gradients, attended_flat, preferred_element_type=jnp.float32
    )
    terms = jnp.concatenate([terms_qkv, term_out[None]], axis=0) * grad_factor
    seq_summed = lax.psum_scatter(
        terms.astype(jnp.bfloat16), "seq", scatter_dimension=1, tiled=True
    )
    weight_grads = lax.psum_scatter(seq_summed, "dp", scatter_dimension=1, tiled=True).astype(
        jnp.float32
    )
    input_part = jnp.einsum(
        "cth,cdh->td", grad_qkv, weights[:3], preferred_element_type=jnp.float32
    )
    reduced_total = lax.psum(input_part.astype(jnp.bfloat16), "pipe").astype(jnp.float32)
    leading_term = jnp.mean(reduced_total, axis=1, keepdims=True)
    trailing_term = jnp.mean(reduced_total * standardized_input, axis=1, keepdims=True)
    input_gradient = (
        row_gradients.astype(jnp.float32)
        + inverse_deviation * (reduced_total - leading_term - standardized_input * trailing_term)
    ).astype(jnp.bfloat16)
    return (input_gradient[None], weight_grads)


def solution(mesh):
    in_specs = (
        P(("grp", "dp"), "seq", None),
        P(("grp", "dp"), "seq", None),
        P(None, ("seq", "dp"), "pipe"),
    )
    out_specs = (P(("grp", "dp"), "seq", None), P("grp", ("seq", "dp"), "pipe"))
    return jax.shard_map(local, mesh=mesh, in_specs=in_specs, out_specs=out_specs, check_vma=False)
```

profile of v0, /device:TPU:8, one launch (start us, length us, event | category | flops | bytes accessed | tf_op | source)
XLA Modules:
  0.0 408.2 jit_solution(12918442514962170128)
XLA Ops:
  7.2 2.7 copy.16
  10.0 1.1 convert_reduce_fusion.1
  11.2 1.3 fusion.46
  12.5 103.4 %all-gather.2.cloned.1.call-done = bf16[4,1664,416]{2,0,1:T(4,128)(2,1)} async-done(((bf16[4,208,416]{2,0,1:T(4,128)(2,1)}), bf16[4,1664,416]{2,0,1:T(4,128)(2,1)}) %all-gather.2.cloned.1.call-update) | async-done | bytes 5537808 | tf_op jit(solution)/shard_map/all_gather | solution.py:18
  115.9 11.3 %copy.29 = bf16[3,1664,416]{1,2,0:T(8,128)(2,1)} copy(bf16[3,1664,416]{2,0,1:T(4,128)(2,1)} %bitcast.176) | data formatting | bytes 8306688
  127.2 3.5 fusion.33
  131.4 8.4 %slice.30 = bf16[1,1664,416]{2,0,1:T(2,128)(2,1)} slice(bf16[4,1664,416]{2,0,1:T(4,128)(2,1)} %all-gather.2.cloned.1.call-done), slice={[3:4], [0:1664], [0:416]} | slice | bytes 2768896 | tf_op jit(solution)/shard_map/slice | solution.py:37
  139.8 8.5 %copy.30 = bf16[1,1664,416]{1,2,0:T(8,128)(2,1)S(1)} copy(bf16[1,1664,416]{2,0,1:T(2,128)(2,1)} %slice.30) | data formatting | bytes 2768896
  148.4 19.5 %all_gather.7 = bf16[2,512,416]{1,2,0:T(8,128)(2,1)S(1)} all-gather(bf16[2,128,416]{1,2,0:T(8,128)(2,1)} %slice.27), channel_id=1, replica_groups=mesh['grp'=2,'seq'=4,'dp'=2,'pipe'=2] {'seq'}, dimensions={1}, use_global_device_ids=true | all-gather | bytes 1064960 | tf_op jit(solution)/shard_map/all_gather | solution.py:32
  167.9 1.0 fusion.57
  168.9 1.3 copy.19
  170.2 1.3 copy.20
  172.0 16.9 %while.16 = (s32[]{:T(128)}, bf16[4,128,104]{1,2,0:T(8,128)(2,1)}, bf16[4,128,104]{1,2,0:T(8,128)(2,1)}, bf16[4,512,104]{1,2,0:T(8,128)(2,1)}, bf16[4,512,104]{1...) while((s32[]{:T(128)}, bf16[4,128,104]{1,2,0:T(8,128)(2,1)}, ...), condition=%wide.region_6.7_spmd, body=%wide.region_2.6_spmd.sunk | while | flops 82589440 | bytes 2916977 | solution.py:63
  172.6 0.8 bitcast_dynamic-update-slice_fusion.2
  173.7 0.9 fusion.90
  174.6 0.9 fusion.91
  175.4 0.8 fusion.92
  176.9 0.8 bitcast_dynamic-update-slice_fusion.2
  178.0 0.8 fusion.90
  178.8 0.9 fusion.91
  179.7 0.8 fusion.92
  181.1 0.8 bitcast_dynamic-update-slice_fusion.2
  182.2 0.8 fusion.90
  183.0 0.9 fusion.91
  185.3 0.8 bitcast_dynamic-update-slice_fusion.2
  186.4 0.8 fusion.90
  187.3 0.9 fusion.91
  188.1 0.8 fusion.92
  188.9 1.2 pad_maximum_fusion
  190.2 1.0 copy.23
  191.2 1.7 reshape.49
  193.0 1.5 convolution_bitcast_fusion.3
  194.5 20.4 %reduce-scatter.10.cloned.1.call-done = bf16[128,832]{1,0:T(8,128)(2,1)} async-done(((bf16[512,832]{1,0:T(8,128)(2,1)}), bf16[128,832]{1,0:T(8,128)(2,1)}) %reduce-scatter.10.cloned.1.call-update) | async-done | bytes 213008
  214.9 1.9 reshape.50
  216.8 1.1 copy.24
  217.9 1.3 convolution_bitcast_fusion.2
  219.3 3.3 fusion.29
  222.5 11.9 %copy.25 = bf16[4,1664,416]{2,0,1:T(4,128)(2,1)} copy(bf16[4,1664,416]{1,2,0:T(8,128)(2,1)} %fusion.29) | data formatting | bytes 11075584
  234.5 12.9 %reshape.51 = bf16[1664,1664]{1,0:T(8,128)(2,1)} reshape(bf16[1664,4,416]{2,1,0:T(4,128)(2,1)} %bitcast.175) | data formatting | bytes 11075584
  247.4 3.8 fusion.30
  251.5 95.6 %reduce-scatter.12.cloned.1.call-done = bf16[416,1664]{1,0:T(8,128)(2,1)} async-done(((bf16[1664,1664]{1,0:T(8,128)(2,1)}), bf16[416,1664]{1,0:T(8,128)(2,1)}) %reduce-scatter.12.cloned.1.call-update) | async-done | bytes 1384464
  347.1 22.1 %all-reduce.2.cloned.1.call-done = bf16[128,1664]{1,0:T(8,128)(2,1)} async-done(((bf16[128,1664]{1,0:T(8,128)(2,1)}), bf16[128,1664]{1,0:T(8,128)(2,1)}) %all-reduce.2.cloned.1.call-update) | async-done | bytes 426000 | tf_op jit(solution)/shard_map/psum | solution.py:93
  369.2 1.3 convert_reduce_fusion
  370.6 2.2 fusion.48
  372.7 23.5 %reduce-scatter.14.cloned.1.call-done = bf16[208,1664]{1,0:T(8,128)(2,1)} async-done(((bf16[416,1664]{1,0:T(8,128)(2,1)}), bf16[208,1664]{1,0:T(8,128)(2,1)}) %reduce-scatter.14.cloned.1.call-update) | async-done | bytes 692240
  396.3 3.1 reshape.54
  399.4 0.8 copy.28
  400.2 1.5 copy.22
  (56 shorter events, 6.1 us)
Async XLA Ops:
  7.2 108.7 %all-gather.2.cloned.1.call-start = ((), (), s32[]{:S(2)}) async-start(), calls=%async_computation.3 | async-start | bytes 7667712 | tf_op jit(solution)/shard_map/all_gather | solution.py:18
  10.0 204.9 %reduce-scatter.10.cloned.1.call-start = ((), (), s32[]{:S(2)}) async-start(), calls=%async_computation.5 | async-start | bytes 1146880
  115.9 11.3 %copy-start = (bf16[1,128,1664]{2,1,0:T(8,128)(2,1)S(1)}, bf16[1,128,1664]{2,1,0:T(8,128)(2,1)}, u32[]{:S(2)}) copy-start(bf16[1,128,1664]{2,1,0:T(8,128)(2,1)} %param.5) | copy-start | bytes 1277956
  139.8 31.7 %copy-start.1 = (bf16[1,128,1664]{2,1,0:T(8,128)(2,1)S(1)}, bf16[1,128,1664]{2,1,0:T(8,128)(2,1)}, u32[]{:S(2)}) copy-start(bf16[1,128,1664]{2,1,0:T(8,128)(2,1)} %param.6) | copy-start | bytes 1277956
  188.9 4.0 copy-start.4
  190.2 27.7 %copy-start.3 = (bf16[4,128,104]{1,2,0:T(8,128)(2,1)S(1)}, bf16[4,128,104]{1,2,0:T(8,128)(2,1)}, u32[]{:S(2)}) copy-start(bf16[4,128,104]{1,2,0:T(8,128)(2,1)} %get-tuple-element.52) | copy-start | bytes 319492
  192.9 154.1 %reduce-scatter.12.cloned.1.call-start = ((), (), s32[]{:S(2)}) async-start(), calls=%async_computation.6 | async-start | bytes 6922240
  247.4 123.2 %copy-start.2 = (bf16[1,128,1664]{2,1,0:T(8,128)(2,1)S(1)}, bf16[1,128,1664]{2,1,0:T(8,128)(2,1)}, u32[]{:S(2)}) copy-start(bf16[1,128,1664]{2,1,0:T(8,128)(2,1)} %param.6) | copy-start | bytes 1277956
  247.4 121.8 %all-reduce.2.cloned.1.call-start = ((), (), s32[]{:S(2)}) async-start(), calls=%async_computation.4 | async-start | bytes 851968 | tf_op jit(solution)/shard_map/psum | solution.py:93
  251.2 145.0 %reduce-scatter.14.cloned.1.call-start = ((), (), s32[]{:S(2)}) async-start(), calls=%async_computation.7 | async-start | bytes 2076672
Sparse Core Ops, SparseCore 0:
  10.8 105.0 all-gather.1
  193.0 21.7 reduce-scatter.9
  247.5 99.5 reduce-scatter.11
  349.8 19.3 all-reduce.1
  371.3 24.9 reduce-scatter.13
where the time goes:
time: 411 us; the launch traced here: 408 us
  waiting for transfers between devices  265 us (64%)
  local copies, waits for them, and re-layouts  71.1 us (17%)
  matrix products  26 us (6%)
  blocking collectives  19.5 us (5%)
  between operations  13.9 us (3%)
  other arithmetic  11.9 us (3%)
    unnamed x8, waiting for transfers between devices  140 us
    all_gather x1, waiting for transfers between devices, local(): weights = lax.all_gather(attn_weights, ('seq', 'dp'), axis=1, tiled=True)  103 us
    unnamed x22, local copies, waits for them, and re-layouts  58.4 us
    psum x1, waiting for transfers between devices, local(): lax.psum(input_part.astype(jnp.bfloat16), 'pipe').astype(jnp.float32)  22.1 us
    all_gather x1, blocking collectives, local(): gathered = lax.all_gather(proj[1:], 'seq', axis=1, tiled=True)  19.5 us
    slice x1, local copies, waits for them, and re-layouts, local(): weights[3]  8.39 us
  transfers between devices with their start and end apart: 5, of which 5 were waited for; matrix products, arithmetic and copies ran while one was open for 3% of the time, Pallas kernels for 0%

commit v1 on v0

v1 whole, which is shorter than its diff:
```python
import functools
import math

import jax
import jax.numpy as jnp
from jax import lax
from jax.experimental import pallas as pl
from jax.experimental.pallas import tpu as pltpu
from jax.sharding import PartitionSpec as P

HD = 104
SLOT = 128

EPSILON = 1e-06
BF = jnp.bfloat16
F32 = jnp.float32
PARAMS = pltpu.CompilerParams(vmem_limit_bytes=56 * 1024 * 1024)
VMEM_SPEC = pl.BlockSpec(memory_space=pltpu.VMEM)
ANY_SPEC = pl.BlockSpec(memory_space=pl.ANY)


def standardize(features):
    row_mean = jnp.mean(features, axis=1, keepdims=True)
    mean_removed = features - row_mean
    variance = jnp.mean(mean_removed * mean_removed, axis=1, keepdims=True)
    inverse_deviation = lax.rsqrt(variance + EPSILON)
    return mean_removed * inverse_deviation, inverse_deviation


def nt(a, b):
    return lax.dot_general(a, b, (((1,), (1,)), ((), ())), preferred_element_type=F32)


def tn(a, b):
    return lax.dot_general(a, b, (((0,), (0,)), ((), ())), preferred_element_type=F32)


def nn(a, b):
    return jnp.dot(a, b, preferred_element_type=F32)


def pack_kernel(n, w_ref, *refs):
    outs, staged = refs[:n], refs[n]
    me = lax.axis_index("seq")
    rows = w_ref.shape[1]
    fill = jnp.zeros((rows, SLOT - HD), BF)
    for head in range(n):
        for mat in range(4):
            block = w_ref[mat, :, head * HD : (head + 1) * HD]
            staged[head, :, mat * SLOT : (mat + 1) * SLOT] = jnp.concatenate([block, fill], axis=1)
    for k in range(n):
        outs[k][...] = staged[me ^ k]


def norm_kernel(x_ref, up_ref, normed_ref, send_ref):
    core = lax.axis_index("pipe")
    normed = standardize(x_ref[...].astype(F32))[0].astype(BF)
    normed_ref[...] = normed

    @pl.when(core == 0)
    def _():
        send_ref[...] = normed

    @pl.when(core != 0)
    def _():
        send_ref[...] = up_ref[...]


def head_kernel(n, *refs):
    normed_ref, up_ref = refs[:2]
    got = refs[2 : 1 + n]
    swapped = refs[1 + n : 2 * n]
    w_own = refs[2 * n : 3 * n]
    w_other = refs[3 * n : 4 * n]
    keep_ref, give_ref, grads_ref, x_full, up_full = refs[4 * n : 4 * n + 5]
    w_full, term_k, term_v, sems, wsems = refs[4 * n + 5 :]
    me = lax.axis_index("seq")
    image = lax.axis_index("dp")
    core = lax.axis_index("pipe")
    rows = normed_ref.shape[0]
    share = w_own[0].shape[0]
    local = [(normed_ref, x_full), (up_ref, up_full)]

    weight_copies = []
    for k in range(n):
        for which, (source, at) in enumerate(((w_own[k], image), (w_other[k], 1 - image))):
            first = pl.multiple_of(((me ^ k) * 2 + at) * share, 16)
            copy = pltpu.make_async_copy(
                source, w_full.at[pl.ds(first, share), :], wsems.at[k, which]
            )
            copy.start()
            weight_copies.append(copy)
    copies = []
    for which, (source, target) in enumerate(local):
        copy = pltpu.make_async_copy(source, target.at[pl.ds(0, rows), :], sems.at[which, 0])
        copy.start()
        copies.append(copy)

    def blocks(first, second):
        made = []
        for k in range(1, n):
            for which, source in ((0, first[k - 1]), (1, second[k - 1])):
                made.append(
                    pltpu.make_async_copy(
                        source,
                        local[which][1].at[pl.ds(k * rows, rows), :],
                        sems.at[which, k],
                    )
                )
        return made

    @pl.when(core == 0)
    def _():
        for copy in blocks(got, swapped):
            copy.start()

    @pl.when(core != 0)
    def _():
        for copy in blocks(swapped, got):
            copy.start()

    for copy in weight_copies + copies + blocks(got, swapped):
        copy.wait()

    scale = HD ** (-0.5)
    qkv = nn(x_full[...], w_full[:, : 3 * SLOT]).astype(BF)
    grad_att = nn(up_full[...], w_full[:, 3 * SLOT :]).astype(BF)
    key_rows = qkv[:, SLOT : 2 * SLOT]
    value_rows = qkv[:, 2 * SLOT :]
    for b in range(n):
        span = slice(b * rows, (b + 1) * rows)
        query = qkv[span, :SLOT]
        grad_out = grad_att[span]
        scores = nt(query, key_rows) * scale
        weight = jnp.exp(scores - jnp.max(scores, axis=1, keepdims=True))
        probs = (weight / jnp.sum(weight, axis=1, keepdims=True)).astype(BF)
        attended = nn(probs, value_rows).astype(BF)
        delta = jnp.sum(grad_out.astype(F32) * attended.astype(F32), axis=1, keepdims=True)
        dprobs = nt(grad_out, value_rows)
        dscores = (probs.astype(F32) * (dprobs - delta) * scale).astype(BF)
        grads_ref[span, :SLOT] = nn(dscores, key_rows).astype(BF)
        grads_ref[span, 3 * SLOT :] = attended
        key_term = tn(dscores, query).astype(BF).astype(F32)
        value_term = tn(probs, grad_out).astype(BF).astype(F32)
        if b == 0:
            term_k[...] = key_term
            term_v[...] = value_term
        else:
            term_k[...] += key_term
            term_v[...] += value_term
    grads_ref[:, SLOT : 2 * SLOT] = term_k[...].astype(BF)
    grads_ref[:, 2 * SLOT : 3 * SLOT] = term_v[...].astype(BF)
    half = rows // 2
    for b in range(n):
        span = slice(b * rows, (b + 1) * rows)
        part = nt(grads_ref[span, : 3 * SLOT], w_full[:, : 3 * SLOT]).astype(BF)

        @pl.when(core == 0)
        def _():
            keep_ref[b] = part[:half]
            give_ref[b] = part[half:]

        @pl.when(core != 0)
        def _():
            keep_ref[b] = part[half:]
            give_ref[b] = part[:half]


def weight_kernel(n, factor, x_ref, up_ref, grads_ref, keep_ref, give_ref, staged):
    me = lax.axis_index("seq")
    image = lax.axis_index("dp")
    share = keep_ref.shape[1]
    staged[:, : 3 * SLOT] = (tn(x_ref[...], grads_ref[:, : 3 * SLOT]) * factor).astype(BF)
    staged[:, 3 * SLOT :] = (tn(up_ref[...], grads_ref[:, 3 * SLOT :]) * factor).astype(BF)
    for k in range(n):
        for target, at in ((keep_ref, image), (give_ref, 1 - image)):
            first = pl.multiple_of(((me ^ k) * 2 + at) * share, 16)
            target[k] = staged[pl.ds(first, share), :]


def sum_kernel(n, mine_ref, theirs_ref, *outs):
    for k in range(n):
        outs[k][...] = (mine_ref[k].astype(F32) + theirs_ref[k].astype(F32)).astype(BF)


def final_kernel(n, x_ref, up_ref, *refs):
    parts, out_ref = refs[:n], refs[n]
    half = out_ref.shape[0]
    core = lax.axis_index("pipe")
    span = pl.ds(pl.multiple_of(core * half, half), half)
    total = parts[0][...].astype(F32)
    for part in parts[1:]:
        total += part[...].astype(F32)
    xhat, inverse_deviation = standardize(x_ref[span, :].astype(F32))
    leading = jnp.mean(total, axis=1, keepdims=True)
    trailing = jnp.mean(total * xhat, axis=1, keepdims=True)
    out_ref[...] = (
        up_ref[span, :].astype(F32) + inverse_deviation * (total - leading - xhat * trailing)
    ).astype(BF)


def join_kernel(mine_ref, theirs_ref, out_ref):
    core = lax.axis_index("pipe")
    half = mine_ref.shape[0]
    out_ref[pl.ds(pl.multiple_of(core * half, half), half), :] = mine_ref[...]
    out_ref[pl.ds(pl.multiple_of((1 - core) * half, half), half), :] = theirs_ref[...]


def unpack_kernel(n, *refs):
    parts, out_ref, staged = refs[:n], refs[n], refs[n + 1]
    me = lax.axis_index("seq")
    for k in range(n):
        staged[me ^ k] = parts[k][...]
    for head in range(n):
        for mat in range(4):
            out_ref[mat, :, head * HD : (head + 1) * HD] = staged[
                head, :, mat * SLOT : mat * SLOT + HD
            ].astype(F32)


def call(kernel, out_shape, args, scratch=(), specs=None):
    single = not isinstance(out_shape, list)
    shapes = [out_shape] if single else out_shape
    out = pl.pallas_call(
        kernel,
        out_shape=[jax.ShapeDtypeStruct(*s) for s in shapes],
        in_specs=[VMEM_SPEC] * len(args) if specs is None else specs,
        out_specs=[VMEM_SPEC] * len(shapes),
        scratch_shapes=list(scratch),
        compiler_params=PARAMS,
    )(*args)
    return out[0] if single else out


def local_heads(embeddings, upstream, attn_weights):
    n = lax.axis_size("seq")
    x, up = embeddings[0], upstream[0]
    rows, width = x.shape
    share = attn_weights.shape[1]
    patches = n * rows
    half = rows // 2

    def across(value, k):
        return lax.ppermute(value, "seq", [(i, i ^ k) for i in range(n)])

    def swap(value, axis):
        return lax.ppermute(value, axis, [(0, 1), (1, 0)])

    chunks = call(
        functools.partial(pack_kernel, n),
        [((share, 4 * SLOT), BF)] * n,
        (attn_weights,),
        [pltpu.VMEM((n, share, 4 * SLOT), BF)],
    )
    w_own = [chunks[0]] + [across(chunks[k], k) for k in range(1, n)]
    w_other = [swap(w, "dp") for w in w_own]
    normed, send = call(norm_kernel, [((rows, width), BF)] * 2, (x, up))
    got = [across(send, k) for k in range(1, n)]
    swapped = [swap(g, "pipe") for g in got]
    args = (normed, up, *got, *swapped, *w_own, *w_other)
    keep, give, grads, x_full, up_full = call(
        functools.partial(head_kernel, n),
        [
            ((n, half, width), BF),
            ((n, half, width), BF),
            ((patches, 4 * SLOT), BF),
            ((patches, width), BF),
            ((patches, width), BF),
        ],
        args,
        [
            pltpu.VMEM((width, 4 * SLOT), BF),
            pltpu.VMEM((patches, SLOT), F32),
            pltpu.VMEM((patches, SLOT), F32),
            pltpu.SemaphoreType.DMA((2, n)),
            pltpu.SemaphoreType.DMA((n, 2)),
        ],
        [ANY_SPEC] * len(args),
    )
    taken = swap(give, "pipe")
    sums = call(functools.partial(sum_kernel, n), [((half, width), BF)] * n, (keep, taken))
    parts = [sums[0]] + [across(sums[k], k) for k in range(1, n)]
    factor = 1.0 / math.sqrt(patches * lax.axis_size("dp"))
    w_keep, w_give = call(
        functools.partial(weight_kernel, n, factor),
        [((n, share, 4 * SLOT), BF)] * 2,
        (x_full, up_full, grads),
        [pltpu.VMEM((width, 4 * SLOT), BF)],
    )
    w_taken = swap(w_give, "dp")
    w_sums = call(
        functools.partial(sum_kernel, n), [((share, 4 * SLOT), BF)] * n, (w_keep, w_taken)
    )
    w_parts = [w_sums[0]] + [across(w_sums[k], k) for k in range(1, n)]
    mine = call(functools.partial(final_kernel, n), ((half, width), BF), (x, up, *parts))
    input_gradient = call(join_kernel, ((rows, width), BF), (mine, swap(mine, "pipe")))
    weight_grads = call(
        functools.partial(unpack_kernel, n),
        ((4, share, n * HD), F32),
        tuple(w_parts),
        [pltpu.VMEM((n, share, 4 * SLOT), BF)],
    )
    return (input_gradient[None], weight_grads)


def local_gathered(embeddings, upstream, attn_weights):
    tokens = embeddings[0]
    row_gradients = upstream[0]
    row_count = tokens.shape[0]
    weights = lax.all_gather(attn_weights, ("seq", "dp"), axis=1, tiled=True)
    local_width = weights.shape[2]
    head_count = local_width // HD
    score_scale = HD ** (-0.5)
    standardized_input, inverse_deviation = standardize(tokens.astype(F32))
    normalized_rows = standardized_input.astype(BF)
    proj = jnp.einsum(
        "td,cdh->cth", normalized_rows, weights[:3], preferred_element_type=F32
    ).astype(BF)
    gathered = lax.all_gather(proj[1:], "seq", axis=1, tiled=True)
    key_count = gathered.shape[1]
    query_heads = proj[0].reshape(row_count, head_count, HD).transpose(1, 0, 2)
    key_heads = gathered[0].reshape(key_count, head_count, HD).transpose(1, 0, 2)
    value_heads = gathered[1].reshape(key_count, head_count, HD).transpose(1, 0, 2)
    grad_att = jnp.dot(row_gradients, weights[3], preferred_element_type=F32).astype(BF)
    grad_heads = grad_att.reshape(row_count, head_count, HD).transpose(1, 0, 2)

    def one_head(items):
        query_rows, key_rows, value_rows, grad_out = items
        scores = nn(query_rows, key_rows.T) * score_scale
        row_max = jnp.max(scores, axis=1, keepdims=True)
        log_total = row_max + jnp.log(jnp.sum(jnp.exp(scores - row_max), axis=1, keepdims=True))
        probs = jnp.exp(scores - log_total).astype(BF)
        attended = nn(probs, value_rows).astype(BF)
        row_delta = jnp.sum(
            grad_out.astype(F32) * attended.astype(F32), axis=1, keepdims=True
        )
        dprobs = nn(grad_out, value_rows.T)
        dscores = (probs.astype(F32) * (dprobs - row_delta) * score_scale).astype(BF)
        grad_q = nn(dscores, key_rows).astype(BF)
        return (attended, grad_q, nn(dscores.T, query_rows), nn(probs.T, grad_out))

    attended_h, grad_q_h, key_h, value_h = lax.map(
        one_head, (query_heads, key_heads, value_heads, grad_heads)
    )
    attended_flat = attended_h.transpose(1, 0, 2).reshape(row_count, local_width)
    grad_q = grad_q_h.transpose(1, 0, 2).reshape(1, row_count, local_width)
    key_terms = key_h.transpose(1, 0, 2).reshape(key_count, local_width)
    value_terms = value_h.transpose(1, 0, 2).reshape(key_count, local_width)
    both_terms = jnp.stack([key_terms, value_terms])
    owned = lax.psum_scatter(both_terms.astype(BF), "seq", scatter_dimension=1, tiled=True)
    grad_qkv = jnp.concatenate([grad_q, owned], axis=0)
    token_count = row_count * lax.axis_size("seq") * lax.axis_size("dp")
    grad_factor = 1.0 / math.sqrt(token_count)
    terms_qkv = jnp.einsum("td,cth->cdh", normalized_rows, grad_qkv, preferred_element_type=F32)
    term_out = jnp.einsum("td,th->dh", row_gradients, attended_flat, preferred_element_type=F32)
    terms = jnp.concatenate([terms_qkv, term_out[None]], axis=0) * grad_factor
    seq_summed = lax.psum_scatter(terms.astype(BF), "seq", scatter_dimension=1, tiled=True)
    weight_grads = lax.psum_scatter(seq_summed, "dp", scatter_dimension=1, tiled=True).astype(F32)
    input_part = jnp.einsum("cth,cdh->td", grad_qkv, weights[:3], preferred_element_type=F32)
    reduced_total = lax.psum(input_part.astype(BF), "pipe").astype(F32)
    leading_term = jnp.mean(reduced_total, axis=1, keepdims=True)
    trailing_term = jnp.mean(reduced_total * standardized_input, axis=1, keepdims=True)
    input_gradient = (
        row_gradients.astype(F32)
        + inverse_deviation * (reduced_total - leading_term - standardized_input * trailing_term)
    ).astype(BF)
    return (input_gradient[None], weight_grads)


def local(embeddings, upstream, attn_weights):
    n = lax.axis_size("seq")
    heads = attn_weights.shape[2] // HD
    one_head_each = (
        heads == n
        and n & (n - 1) == 0
        and lax.axis_size("dp") == 2
        and lax.axis_size("pipe") == 2
        and attn_weights.shape[1] % 16 == 0
        and embeddings.shape[0] == 1
        and embeddings.shape[1] % 32 == 0
    )
    return (local_heads if one_head_each else local_gathered)(embeddings, upstream, attn_weights)


def solution(mesh):
    in_specs = (
        P(("grp", "dp"), "seq", None),
        P(("grp", "dp"), "seq", None),
        P(None, ("seq", "dp"), "pipe"),
    )
    out_specs = (P(("grp", "dp"), "seq", None), P("grp", ("seq", "dp"), "pipe"))
    return jax.shard_map(local, mesh=mesh, in_specs=in_specs, out_specs=out_specs, check_vma=False)
```

time: 411 us -> 151 us (0.37)
  waiting for transfers between devices: 265 us -> 87.8 us
  local copies, waits for them, and re-layouts: 71.1 us -> 5.02 us
  Pallas kernels: 0 us -> 33.1 us
  matrix products: 26 us -> 0 us
  starting transfers between devices: 0.39 us -> 23.4 us
  blocking collectives: 19.5 us -> 0 us
  between operations: 13.9 us -> 0.81 us
  other arithmetic: 11.9 us -> 0 us
    unnamed x8 -> x0, waiting for transfers between devices: 140 us -> none
    all_gather x1 -> x0, waiting for transfers between devices: 103 us -> none  [local(): weights = lax.all_gather(attn_weights, ('seq', 'dp'), axis=1, tiled=True)]
    ppermute x0 -> x22, waiting for transfers between devices: none -> 87.8 us  [the longest x12 64.6 us: across(): return lax.ppermute(value, 'seq', [(i, i ^ k) for i in range(n)])]
    unnamed x22 -> x44, local copies, waits for them, and re-layouts: 58.4 us -> 5.02 us
    pallas_call x0 -> x9, Pallas kernels: none -> 33.1 us  [call(): pl.pallas_call(kernel, out_shape=[jax.ShapeDtypeStruct(*s) for s in shape...]
    dot_general x29 -> x0, matrix products: 26 us -> none  [the longest x1 3.78 us: local(): jnp.einsum('cth,cdh->td', grad_qkv, weights[:3], preferred_element_type=j...]
    ppermute x0 -> x22, starting transfers between devices: none -> 23.4 us  [the longest x12 14.9 us: across(): return lax.ppermute(value, 'seq', [(i, i ^ k) for i in range(n)])]
    psum x1 -> x0, waiting for transfers between devices: 22.1 us -> none  [local(): lax.psum(input_part.astype(jnp.bfloat16), 'pipe').astype(jnp.float32)]
  transfers between devices with their start and end apart: 5 -> 22, of which waited for: 5 -> 9; matrix products, arithmetic and copies ran while one was open for 3% -> 0% of each run, Pallas kernels for 0% -> 12%
where the time goes in v1:
time: 151 us; the launch traced here: 150 us
  waiting for transfers between devices  87.8 us (58%)
  Pallas kernels  33.1 us (22%)
  starting transfers between devices  23.4 us (15%)
  local copies, waits for them, and re-layouts  5.02 us (3%)
    ppermute x12, waiting for transfers between devices, across(): return lax.ppermute(value, 'seq', [(i, i ^ k) for i in range(n)])  64.6 us
    pallas_call x9, Pallas kernels, call(): pl.pallas_call(kernel, out_shape=[jax.ShapeDtypeStruct(*s) for s in shape...  33.1 us
    ppermute x10, waiting for transfers between devices, swap(): return lax.ppermute(value, axis, [(0, 1), (1, 0)])  23.2 us
    ppermute x12, starting transfers between devices, across(): return lax.ppermute(value, 'seq', [(i, i ^ k) for i in range(n)])  14.9 us
    ppermute x10, starting transfers between devices, swap(): return lax.ppermute(value, axis, [(0, 1), (1, 0)])  8.58 us
    unnamed x44, local copies, waits for them, and re-layouts  5.02 us
  transfers between devices with their start and end apart: 22, of which 9 were waited for; matrix products, arithmetic and copies ran while one was open for 0% of the time, Pallas kernels for 12%

profile of v1, /device:TPU:8, one launch (start us, length us, event | category | flops | bytes accessed | tf_op | source)
XLA Modules:
  0.0 150.2 jit_solution(12980867114484613695)
XLA Ops:
  0.6 2.5 %shard_map.51 = (bf16[208,512]{1,0:T(8,128)(2,1)}, bf16[208,512]{1,0:T(8,128)(2,1)}, bf16[208,512]{1,0:T(8,128)(2,1)}, bf16[208,512]{1,0:T(8,128)(2,1)}) custom-call(bf16[4,208,416]{2,1,0:T(8,128)(2,1)} %w_ref.1), custom_call_target="tpu_custom_call" | custom-call | tf_op jit(solution)/shard_map/pallas_call | solution.py:224
  3.2 2.4 %shard_map.50 = (bf16[128,1664]{1,0:T(8,128)(2,1)}, bf16[128,1664]{1,0:T(8,128)(2,1)}) custom-call(bf16[128,1664]{1,0:T(8,128)(2,1)} %bitcast.6, bf16[128,1664]{1,0:T(8,128)(2,1)} %bitcast.3), custom_call_target="tpu_custom_call" | custom-call | tf_op jit(solution)/shard_map/pallas_call | solution.py:224
  5.5 3.2 %collective-permute-start.2 = (bf16[128,1664]{1,0:T(8,128)(2,1)}, bf16[128,1664]{1,0:T(8,128)(2,1)S(1)}, u32[]{:S(2)}, u32[]{:S(2)}) collective-permute-start(bf16[128,1664]{1,0:T(8,128)(2,1)} %get-tuple-element.24), channel_id=1, source_target_pairs={{0,12},{4,8},{8,4},{12,0},{1,13},{5,9},{9,5},{13,1},{2,14},{6,10},... | collective-permute-start | bytes 1277960 | tf_op jit(solution)/shard_map/ppermute | solution.py:244
  8.7 1.2 collective-permute-start.1
  9.9 0.2 collective-permute-start
  10.2 2.8 %collective-permute-start.7 = (bf16[208,512]{1,0:T(8,128)(2,1)}, bf16[208,512]{1,0:T(8,128)(2,1)S(1)}, u32[]{:S(2)}, u32[]{:S(2)}) collective-permute-start(bf16[208,512]{1,0:T(8,128)(2,1)} %get-tuple-element.27), channel_id=1, source_target_pairs={{0,8},{4,12},{8,0},{12,4},{1,9},{5,13},{9,1},{13,5},{2,10},{6,14},... | collective-permute-start | bytes 638984 | tf_op jit(solution)/shard_map/ppermute | solution.py:244
  13.0 0.5 collective-permute-start.8
  13.4 46.4 %collective-permute-done.7.refs_10_ = bf16[208,512]{1,0:T(8,128)(2,1)S(1)} collective-permute-done((bf16[208,512]{1,0:T(8,128)(2,1)}, bf16[208,512]{1,0:T(8,128)(2,1)S(1)}, u32[]{:S(2)}, u32[]{:S(2)}) %collective-permute-start.7) | collective-permute-done | bytes 213024 | tf_op jit(solution)/shard_map/ppermute | solution.py:244
  59.8 1.5 collective-permute-start.9
  61.3 2.8 %collective-permute-done.8.refs_11_ = bf16[208,512]{1,0:T(8,128)(2,1)S(1)} collective-permute-done((bf16[208,512]{1,0:T(8,128)(2,1)}, bf16[208,512]{1,0:T(8,128)(2,1)S(1)}, u32[]{:S(2)}, u32[]{:S(2)}) %collective-permute-start.8) | collective-permute-done | bytes 213024 | tf_op jit(solution)/shard_map/ppermute | solution.py:244
  64.1 1.5 collective-permute-start.10
  65.6 0.5 collective-permute-start.4
  66.1 0.1 collective-permute-start.3
  66.2 1.3 collective-permute-start.11
  67.5 4.1 %collective-permute-done.10.refs_13_ = bf16[208,512]{1,0:T(8,128)(2,1)S(1)} collective-permute-done((bf16[208,512]{1,0:T(8,128)(2,1)S(1)}, bf16[208,512]{1,0:T(8,128)(2,1)S(1)}, u32[]{:S(2)}, u32[]{:S(2)}) %collective-permute-start.10) | collective-permute-done | bytes 213024 | tf_op jit(solution)/shard_map/ppermute | solution.py:247
  71.6 2.2 %collective-permute-start.12 = (bf16[208,512]{1,0:T(8,128)(2,1)S(1)}, bf16[208,512]{1,0:T(8,128)(2,1)S(1)}, u32[]{:S(2)}, u32[]{:S(2)}) collective-permute-start(bf16[208,512]{1,0:T(8,128)(2,1)S(1)} %collective-permute-done.8.refs_11_), channel_id=1, source_target_pairs={{0,2},{2,0},{1,3},{3,1},{4,6},{6,4},{5,7},{7,5},{8,10},{10,8},{9,1... | collective-permute-start | bytes 638984 | tf_op jit(solution)/shard_map/ppermute | solution.py:247
  73.8 2.4 %collective-permute-done.11.refs_14_ = bf16[208,512]{1,0:T(8,128)(2,1)S(1)} collective-permute-done((bf16[208,512]{1,0:T(8,128)(2,1)S(1)}, bf16[208,512]{1,0:T(8,128)(2,1)S(1)}, u32[]{:S(2)}, u32[]{:S(2)}) %collective-permute-start.11) | collective-permute-done | bytes 213024 | tf_op jit(solution)/shard_map/ppermute | solution.py:247
  76.2 3.4 %collective-permute-done.12.refs_15_ = bf16[208,512]{1,0:T(8,128)(2,1)S(1)} collective-permute-done((bf16[208,512]{1,0:T(8,128)(2,1)S(1)}, bf16[208,512]{1,0:T(8,128)(2,1)S(1)}, u32[]{:S(2)}, u32[]{:S(2)}) %collective-permute-start.12) | collective-permute-done | bytes 213024 | tf_op jit(solution)/shard_map/ppermute | solution.py:247
  79.7 0.6 copy-done.21
  80.3 0.2 copy-done.5
  80.4 0.2 copy-done.6
  80.6 0.2 copy-done.7
  80.7 11.5 %shard_map.52 = (bf16[4,64,1664]{2,1,0:T(8,128)(2,1)}, bf16[4,64,1664]{2,1,0:T(8,128)(2,1)}, bf16[512,512]{1,0:T(8,128)(2,1)}, bf16[512,1664]{1,0:T(8,128)(2,1)}, bf16[512,1664]{1,0:T(8,128)(2,1)}) custom-call(bf16[128,1664]{1,0:T(8,128)(2,1)} %get-tuple-element.23.refs_0_, bf16[128,1664]{1,0:T(8,128)(2,1)} %bitcast.4, bf16[128,1664]{1,0:T(8,128)(2,1)} %copy-done.4, ...), custom_call_target="tpu_custom_call" | custom-call | tf_op jit(solution)/shard_map/pallas_call | solution.py:224
  92.2 0.1 collective-permute-start.13
  92.3 4.9 %shard_map.56 = (bf16[4,208,512]{2,1,0:T(8,128)(2,1)}, bf16[4,208,512]{2,1,0:T(8,128)(2,1)}) custom-call(bf16[512,1664]{1,0:T(8,128)(2,1)} %get-tuple-element.35.x_ref, bf16[512,1664]{1,0:T(8,128)(2,1)} %get-tuple-element.36.up_ref, bf16[512,512]{1,0:T(8,128)(2,1)} %get-tuple-element.37.grads_ref), custom_call_target="tpu_custom_call" | custom-call | tf_op jit(solution)/shard_map/pallas_call | solution.py:224
  97.2 1.5 collective-permute-start.18
  98.7 0.9 copy-done.1
  99.6 2.4 %shard_map.53 = (bf16[64,1664]{1,0:T(8,128)(2,1)}, bf16[64,1664]{1,0:T(8,128)(2,1)}, bf16[64,1664]{1,0:T(8,128)(2,1)}, bf16[64,1664]{1,0:T(8,128)(2,1)}) custom-call(bf16[4,64,1664]{2,1,0:T(8,128)(2,1)} %get-tuple-element.29.mine_ref, bf16[4,64,1664]{2,1,0:T(8,128)(2,1)} %copy-done.1), custom_call_target="tpu_custom_call" | custom-call | tf_op jit(solution)/shard_map/pallas_call | solution.py:224
  101.9 1.5 %collective-permute-start.14 = (bf16[64,1664]{1,0:T(8,128)(2,1)}, bf16[64,1664]{1,0:T(8,128)(2,1)S(1)}, u32[]{:S(2)}, u32[]{:S(2)}) collective-permute-start(bf16[64,1664]{1,0:T(8,128)(2,1)} %get-tuple-element.32), channel_id=1, source_target_pairs={{0,4},{4,0},{8,12},{12,8},{1,5},{5,1},{9,13},{13,9},{2,6},{6,2},{1... | collective-permute-start | bytes 638984 | tf_op jit(solution)/shard_map/ppermute | solution.py:244
  103.5 1.7 %collective-permute-start.15 = (bf16[64,1664]{1,0:T(8,128)(2,1)}, bf16[64,1664]{1,0:T(8,128)(2,1)S(1)}, u32[]{:S(2)}, u32[]{:S(2)}) collective-permute-start(bf16[64,1664]{1,0:T(8,128)(2,1)} %get-tuple-element.33), channel_id=1, source_target_pairs={{0,8},{4,12},{8,0},{12,4},{1,9},{5,13},{9,1},{13,5},{2,10},{6,14},... | collective-permute-start | bytes 638984 | tf_op jit(solution)/shard_map/ppermute | solution.py:244
  105.1 0.3 collective-permute-start.16
  105.4 13.3 %collective-permute-done.18.theirs_ref = bf16[4,208,512]{2,1,0:T(8,128)(2,1)S(1)} collective-permute-done((bf16[4,208,512]{2,1,0:T(8,128)(2,1)}, bf16[4,208,512]{2,1,0:T(8,128)(2,1)S(1)}, u32[]{:S(2)}, u32[]{:S(2)}) %collective-permute-start.18) | collective-permute-done | bytes 852000 | tf_op jit(solution)/shard_map/ppermute | solution.py:247
  118.7 0.9 copy-done
  119.6 2.4 %shard_map.57 = (bf16[208,512]{1,0:T(8,128)(2,1)}, bf16[208,512]{1,0:T(8,128)(2,1)}, bf16[208,512]{1,0:T(8,128)(2,1)}, bf16[208,512]{1,0:T(8,128)(2,1)}) custom-call(bf16[4,208,512]{2,1,0:T(8,128)(2,1)} %get-tuple-element.38.mine_ref, bf16[4,208,512]{2,1,0:T(8,128)(2,1)} %copy-done), custom_call_target="tpu_custom_call" | custom-call | tf_op jit(solution)/shard_map/pallas_call | solution.py:224
  122.0 1.5 collective-permute-start.19
  123.5 1.7 %collective-permute-start.20 = (bf16[208,512]{1,0:T(8,128)(2,1)}, bf16[208,512]{1,0:T(8,128)(2,1)S(1)}, u32[]{:S(2)}, u32[]{:S(2)}) collective-permute-start(bf16[208,512]{1,0:T(8,128)(2,1)} %get-tuple-element.42), channel_id=1, source_target_pairs={{0,8},{4,12},{8,0},{12,4},{1,9},{5,13},{9,1},{13,5},{2,10},{6,14},... | collective-permute-start | bytes 638984 | tf_op jit(solution)/shard_map/ppermute | solution.py:244
  125.2 0.3 collective-permute-start.21
  125.5 0.4 copy-done.17
  125.9 0.3 copy-done.18
  126.2 0.1 copy-done.20
  126.3 2.5 %shard_map.54.mine_ref = bf16[64,1664]{1,0:T(8,128)(2,1)} custom-call(bf16[128,1664]{1,0:T(8,128)(2,1)} %bitcast.7, bf16[128,1664]{1,0:T(8,128)(2,1)} %bitcast.5, bf16[64,1664]{1,0:T(8,128)(2,1)} %get-tuple-element.31.refs_0_, bf16[64,1664]{1,0:T(8,128)(2,1)} %copy-done.17, bf16[64,1664]{1,0:T(8,128)(2,1)} %copy-done.18, bf16[64,1664]{1,0:T(8,128)(2,1)} %copy-done.20), custom_call_target="tpu_custom_call" | custom-call | tf_op jit(solution)/shard_map/pallas_call | solution.py:224
  128.8 3.2 %collective-permute-done.19.refs_1_ = bf16[208,512]{1,0:T(8,128)(2,1)S(1)} collective-permute-done((bf16[208,512]{1,0:T(8,128)(2,1)}, bf16[208,512]{1,0:T(8,128)(2,1)S(1)}, u32[]{:S(2)}, u32[]{:S(2)}) %collective-permute-start.19) | collective-permute-done | bytes 213024 | tf_op jit(solution)/shard_map/ppermute | solution.py:244
  132.1 8.3 %collective-permute-done.20.refs_2_ = bf16[208,512]{1,0:T(8,128)(2,1)S(1)} collective-permute-done((bf16[208,512]{1,0:T(8,128)(2,1)}, bf16[208,512]{1,0:T(8,128)(2,1)S(1)}, u32[]{:S(2)}, u32[]{:S(2)}) %collective-permute-start.20) | collective-permute-done | bytes 213024 | tf_op jit(solution)/shard_map/ppermute | solution.py:244
  140.4 3.9 %collective-permute-done.21.refs_3_ = bf16[208,512]{1,0:T(8,128)(2,1)S(1)} collective-permute-done((bf16[208,512]{1,0:T(8,128)(2,1)}, bf16[208,512]{1,0:T(8,128)(2,1)S(1)}, u32[]{:S(2)}, u32[]{:S(2)}) %collective-permute-start.21) | collective-permute-done | bytes 213024 | tf_op jit(solution)/shard_map/ppermute | solution.py:244
  144.2 0.7 copy-done.10
  144.9 2.8 %shard_map.58 = f32[4,208,416]{2,1,0:T(8,128)} custom-call(bf16[208,512]{1,0:T(8,128)(2,1)} %get-tuple-element.40.refs_0_, bf16[208,512]{1,0:T(8,128)(2,1)} %copy-done.8, bf16[208,512]{1,0:T(8,128)(2,1)} %copy-done.9, bf16[208,512]{1,0:T(8,128)(2,1)} %copy-done.10), custom_call_target="tpu_custom_call" | custom-call | tf_op jit(solution)/shard_map/pallas_call | solution.py:224
  147.7 0.7 copy-done.11
  148.4 1.8 %shard_map.55 = bf16[128,1664]{1,0:T(8,128)(2,1)} custom-call(bf16[64,1664]{1,0:T(8,128)(2,1)} %shard_map.54.mine_ref, bf16[64,1664]{1,0:T(8,128)(2,1)} %copy-done.11), custom_call_target="tpu_custom_call" | custom-call | tf_op jit(solution)/shard_map/pallas_call | solution.py:224
  (49 shorter events, 0.1 us)
Async XLA Ops:
  3.2 9.8 %collective-permute-start.6 = (bf16[208,512]{1,0:T(8,128)(2,1)}, bf16[208,512]{1,0:T(8,128)(2,1)S(1)}, u32[]{:S(2)}, u32[]{:S(2)}) collective-permute-start(bf16[208,512]{1,0:T(8,128)(2,1)} %get-tuple-element.26), channel_id=1, source_target_pairs={{0,4},{4,0},{8,12},{12,8},{1,5},{5,1},{9,13},{13,9},{2,6},{6,2},{1... | collective-permute-start | bytes 638984 | tf_op jit(solution)/shard_map/ppermute | solution.py:244
  5.5 60.0 %collective-permute-start.2 = (bf16[128,1664]{1,0:T(8,128)(2,1)}, bf16[128,1664]{1,0:T(8,128)(2,1)S(1)}, u32[]{:S(2)}, u32[]{:S(2)}) collective-permute-start(bf16[128,1664]{1,0:T(8,128)(2,1)} %get-tuple-element.24), channel_id=1, source_target_pairs={{0,12},{4,8},{8,4},{12,0},{1,13},{5,9},{9,5},{13,1},{2,14},{6,10},... | collective-permute-start | bytes 1277960 | tf_op jit(solution)/shard_map/ppermute | solution.py:244
  8.7 56.9 %collective-permute-start.1 = (bf16[128,1664]{1,0:T(8,128)(2,1)}, bf16[128,1664]{1,0:T(8,128)(2,1)S(1)}, u32[]{:S(2)}, u32[]{:S(2)}) collective-permute-start(bf16[128,1664]{1,0:T(8,128)(2,1)} %get-tuple-element.24), channel_id=1, source_target_pairs={{0,8},{4,12},{8,0},{12,4},{1,9},{5,13},{9,1},{13,5},{2,10},{6,14},... | collective-permute-start | bytes 1277960 | tf_op jit(solution)/shard_map/ppermute | solution.py:244
  9.9 56.2 %collective-permute-start = (bf16[128,1664]{1,0:T(8,128)(2,1)}, bf16[128,1664]{1,0:T(8,128)(2,1)S(1)}, u32[]{:S(2)}, u32[]{:S(2)}) collective-permute-start(bf16[128,1664]{1,0:T(8,128)(2,1)} %get-tuple-element.24), channel_id=1, source_target_pairs={{0,4},{4,0},{8,12},{12,8},{1,5},{5,1},{9,13},{13,9},{2,6},{6,2},{1... | collective-permute-start | bytes 1277960 | tf_op jit(solution)/shard_map/ppermute | solution.py:244
  10.2 49.7 %collective-permute-start.7 = (bf16[208,512]{1,0:T(8,128)(2,1)}, bf16[208,512]{1,0:T(8,128)(2,1)S(1)}, u32[]{:S(2)}, u32[]{:S(2)}) collective-permute-start(bf16[208,512]{1,0:T(8,128)(2,1)} %get-tuple-element.27), channel_id=1, source_target_pairs={{0,8},{4,12},{8,0},{12,4},{1,9},{5,13},{9,1},{13,5},{2,10},{6,14},... | collective-permute-start | bytes 638984 | tf_op jit(solution)/shard_map/ppermute | solution.py:244
  13.0 66.7 %copy-start.12 = (bf16[208,512]{1,0:T(8,128)(2,1)}, bf16[208,512]{1,0:T(8,128)(2,1)S(1)}, u32[]{:S(2)}) copy-start(bf16[208,512]{1,0:T(8,128)(2,1)S(1)} %collective-permute-done.6.refs_9_) | copy-start | bytes 638980
  13.0 51.1 %collective-permute-start.8 = (bf16[208,512]{1,0:T(8,128)(2,1)}, bf16[208,512]{1,0:T(8,128)(2,1)S(1)}, u32[]{:S(2)}, u32[]{:S(2)}) collective-permute-start(bf16[208,512]{1,0:T(8,128)(2,1)} %get-tuple-element.28), channel_id=1, source_target_pairs={{0,12},{4,8},{8,4},{12,0},{1,13},{5,9},{9,5},{13,1},{2,14},{6,10},... | collective-permute-start | bytes 638984 | tf_op jit(solution)/shard_map/ppermute | solution.py:244
  59.8 19.8 %copy-start.13 = (bf16[208,512]{1,0:T(8,128)(2,1)}, bf16[208,512]{1,0:T(8,128)(2,1)S(1)}, u32[]{:S(2)}) copy-start(bf16[208,512]{1,0:T(8,128)(2,1)S(1)} %collective-permute-done.7.refs_10_) | copy-start | bytes 638980
  59.8 6.4 %collective-permute-start.9 = (bf16[208,512]{1,0:T(8,128)(2,1)}, bf16[208,512]{1,0:T(8,128)(2,1)S(1)}, u32[]{:S(2)}, u32[]{:S(2)}) collective-permute-start(bf16[208,512]{1,0:T(8,128)(2,1)} %get-tuple-element.25.refs_8_), channel_id=1, source_target_pairs={{0,2},{2,0},{1,3},{3,1},{4,6},{6,4},{5,7},{7,5},{8,10},{10,8},{9,1... | collective-permute-start | bytes 638984 | tf_op jit(solution)/shard_map/ppermute | solution.py:247
  64.1 15.5 %copy-start.14 = (bf16[208,512]{1,0:T(8,128)(2,1)}, bf16[208,512]{1,0:T(8,128)(2,1)S(1)}, u32[]{:S(2)}) copy-start(bf16[208,512]{1,0:T(8,128)(2,1)S(1)} %collective-permute-done.8.refs_11_) | copy-start | bytes 638980
  64.1 7.5 %collective-permute-start.10 = (bf16[208,512]{1,0:T(8,128)(2,1)S(1)}, bf16[208,512]{1,0:T(8,128)(2,1)S(1)}, u32[]{:S(2)}, u32[]{:S(2)}) collective-permute-start(bf16[208,512]{1,0:T(8,128)(2,1)S(1)} %collective-permute-done.6.refs_9_), channel_id=1, source_target_pairs={{0,2},{2,0},{1,3},{3,1},{4,6},{6,4},{5,7},{7,5},{8,10},{10,8},{9,1... | collective-permute-start | bytes 638984 | tf_op jit(solution)/shard_map/ppermute | solution.py:247
  65.6 14.1 %copy-start.2 = (bf16[128,1664]{1,0:T(8,128)(2,1)}, bf16[128,1664]{1,0:T(8,128)(2,1)S(1)}, u32[]{:S(2)}) copy-start(bf16[128,1664]{1,0:T(8,128)(2,1)S(1)} %collective-permute-done.2.refs_4_) | copy-start | bytes 1277956
  65.6 14.0 %collective-permute-start.5 = (bf16[128,1664]{1,0:T(8,128)(2,1)S(1)}, bf16[128,1664]{1,0:T(8,128)(2,1)S(1)}, u32[]{:S(2)}, u32[]{:S(2)}) collective-permute-start(bf16[128,1664]{1,0:T(8,128)(2,1)S(1)} %collective-permute-done.2.refs_4_), channel_id=1, source_target_pairs={{0,1},{1,0},{2,3},{3,2},{4,5},{5,4},{6,7},{7,6},{8,9},{9,8},{10,11... | collective-permute-start | bytes 1277960 | tf_op jit(solution)/shard_map/ppermute | solution.py:247
  65.6 14.1 %copy-start.3 = (bf16[128,1664]{1,0:T(8,128)(2,1)}, bf16[128,1664]{1,0:T(8,128)(2,1)S(1)}, u32[]{:S(2)}) copy-start(bf16[128,1664]{1,0:T(8,128)(2,1)S(1)} %collective-permute-done.1.refs_3_) | copy-start | bytes 1277956
  65.6 14.0 %collective-permute-start.4 = (bf16[128,1664]{1,0:T(8,128)(2,1)S(1)}, bf16[128,1664]{1,0:T(8,128)(2,1)S(1)}, u32[]{:S(2)}, u32[]{:S(2)}) collective-permute-start(bf16[128,1664]{1,0:T(8,128)(2,1)S(1)} %collective-permute-done.1.refs_3_), channel_id=1, source_target_pairs={{0,1},{1,0},{2,3},{3,2},{4,5},{5,4},{6,7},{7,6},{8,9},{9,8},{10,11... | collective-permute-start | bytes 1277960 | tf_op jit(solution)/shard_map/ppermute | solution.py:247
  66.1 13.6 %copy-start.4 = (bf16[128,1664]{1,0:T(8,128)(2,1)}, bf16[128,1664]{1,0:T(8,128)(2,1)S(1)}, u32[]{:S(2)}) copy-start(bf16[128,1664]{1,0:T(8,128)(2,1)S(1)} %collective-permute-done.refs_2_) | copy-start | bytes 1277956
  66.1 13.5 %collective-permute-start.3 = (bf16[128,1664]{1,0:T(8,128)(2,1)S(1)}, bf16[128,1664]{1,0:T(8,128)(2,1)S(1)}, u32[]{:S(2)}, u32[]{:S(2)}) collective-permute-start(bf16[128,1664]{1,0:T(8,128)(2,1)S(1)} %collective-permute-done.refs_2_), channel_id=1, source_target_pairs={{0,1},{1,0},{2,3},{3,2},{4,5},{5,4},{6,7},{7,6},{8,9},{9,8},{10,11... | collective-permute-start | bytes 1277960 | tf_op jit(solution)/shard_map/ppermute | solution.py:247
  66.2 13.5 %copy-start.15 = (bf16[208,512]{1,0:T(8,128)(2,1)}, bf16[208,512]{1,0:T(8,128)(2,1)S(1)}, u32[]{:S(2)}) copy-start(bf16[208,512]{1,0:T(8,128)(2,1)S(1)} %collective-permute-done.9.refs_12_) | copy-start | bytes 638980
  66.2 9.9 %collective-permute-start.11 = (bf16[208,512]{1,0:T(8,128)(2,1)S(1)}, bf16[208,512]{1,0:T(8,128)(2,1)S(1)}, u32[]{:S(2)}, u32[]{:S(2)}) collective-permute-start(bf16[208,512]{1,0:T(8,128)(2,1)S(1)} %collective-permute-done.7.refs_10_), channel_id=1, source_target_pairs={{0,2},{2,0},{1,3},{3,1},{4,6},{6,4},{5,7},{7,5},{8,10},{10,8},{9,1... | collective-permute-start | bytes 638984 | tf_op jit(solution)/shard_map/ppermute | solution.py:247
  71.6 8.1 %copy-start.16 = (bf16[208,512]{1,0:T(8,128)(2,1)}, bf16[208,512]{1,0:T(8,128)(2,1)S(1)}, u32[]{:S(2)}) copy-start(bf16[208,512]{1,0:T(8,128)(2,1)S(1)} %collective-permute-done.10.refs_13_) | copy-start | bytes 638980
  71.6 8.0 %collective-permute-start.12 = (bf16[208,512]{1,0:T(8,128)(2,1)S(1)}, bf16[208,512]{1,0:T(8,128)(2,1)S(1)}, u32[]{:S(2)}, u32[]{:S(2)}) collective-permute-start(bf16[208,512]{1,0:T(8,128)(2,1)S(1)} %collective-permute-done.8.refs_11_), channel_id=1, source_target_pairs={{0,2},{2,0},{1,3},{3,1},{4,6},{6,4},{5,7},{7,5},{8,10},{10,8},{9,1... | collective-permute-start | bytes 638984 | tf_op jit(solution)/shard_map/ppermute | solution.py:247
  76.1 3.5 %copy-start.19 = (bf16[208,512]{1,0:T(8,128)(2,1)}, bf16[208,512]{1,0:T(8,128)(2,1)S(1)}, u32[]{:S(2)}) copy-start(bf16[208,512]{1,0:T(8,128)(2,1)S(1)} %collective-permute-done.11.refs_14_) | copy-start | bytes 638980
  79.6 0.7 copy-start.21
  79.6 0.8 copy-start.5
  79.6 1.0 copy-start.6
  79.6 1.1 copy-start.7
  92.2 6.5 %collective-permute-start.13 = (bf16[4,64,1664]{2,1,0:T(8,128)(2,1)}, bf16[4,64,1664]{2,1,0:T(8,128)(2,1)S(1)}, u32[]{:S(2)}, u32[]{:S(2)}) collective-permute-start(bf16[4,64,1664]{2,1,0:T(8,128)(2,1)} %get-tuple-element.30), channel_id=1, source_target_pairs={{0,1},{1,0},{2,3},{3,2},{4,5},{5,4},{6,7},{7,6},{8,9},{9,8},{10,11... | collective-permute-start | bytes 2555912 | tf_op jit(solution)/shard_map/ppermute | solution.py:247
  97.2 21.6 %collective-permute-start.18 = (bf16[4,208,512]{2,1,0:T(8,128)(2,1)}, bf16[4,208,512]{2,1,0:T(8,128)(2,1)S(1)}, u32[]{:S(2)}, u32[]{:S(2)}) collective-permute-start(bf16[4,208,512]{2,1,0:T(8,128)(2,1)} %get-tuple-element.39), channel_id=1, source_target_pairs={{0,2},{2,0},{1,3},{3,1},{4,6},{6,4},{5,7},{7,5},{8,10},{10,8},{9,1... | collective-permute-start | bytes 2555912 | tf_op jit(solution)/shard_map/ppermute | solution.py:247
  98.7 0.9 copy-start.1
  101.9 23.3 %collective-permute-start.14 = (bf16[64,1664]{1,0:T(8,128)(2,1)}, bf16[64,1664]{1,0:T(8,128)(2,1)S(1)}, u32[]{:S(2)}, u32[]{:S(2)}) collective-permute-start(bf16[64,1664]{1,0:T(8,128)(2,1)} %get-tuple-element.32), channel_id=1, source_target_pairs={{0,4},{4,0},{8,12},{12,8},{1,5},{5,1},{9,13},{13,9},{2,6},{6,2},{1... | collective-permute-start | bytes 638984 | tf_op jit(solution)/shard_map/ppermute | solution.py:244
  103.5 22.1 %collective-permute-start.15 = (bf16[64,1664]{1,0:T(8,128)(2,1)}, bf16[64,1664]{1,0:T(8,128)(2,1)S(1)}, u32[]{:S(2)}, u32[]{:S(2)}) collective-permute-start(bf16[64,1664]{1,0:T(8,128)(2,1)} %get-tuple-element.33), channel_id=1, source_target_pairs={{0,8},{4,12},{8,0},{12,4},{1,9},{5,13},{9,1},{13,5},{2,10},{6,14},... | collective-permute-start | bytes 638984 | tf_op jit(solution)/shard_map/ppermute | solution.py:244
  105.1 20.4 %collective-permute-start.16 = (bf16[64,1664]{1,0:T(8,128)(2,1)}, bf16[64,1664]{1,0:T(8,128)(2,1)S(1)}, u32[]{:S(2)}, u32[]{:S(2)}) collective-permute-start(bf16[64,1664]{1,0:T(8,128)(2,1)} %get-tuple-element.34), channel_id=1, source_target_pairs={{0,12},{4,8},{8,4},{12,0},{1,13},{5,9},{9,5},{13,1},{2,14},{6,10},... | collective-permute-start | bytes 638984 | tf_op jit(solution)/shard_map/ppermute | solution.py:244
  118.7 0.9 copy-start
  122.0 10.0 %collective-permute-start.19 = (bf16[208,512]{1,0:T(8,128)(2,1)}, bf16[208,512]{1,0:T(8,128)(2,1)S(1)}, u32[]{:S(2)}, u32[]{:S(2)}) collective-permute-start(bf16[208,512]{1,0:T(8,128)(2,1)} %get-tuple-element.41), channel_id=1, source_target_pairs={{0,4},{4,0},{8,12},{12,8},{1,5},{5,1},{9,13},{13,9},{2,6},{6,2},{1... | collective-permute-start | bytes 638984 | tf_op jit(solution)/shard_map/ppermute | solution.py:244
  123.5 16.8 %collective-permute-start.20 = (bf16[208,512]{1,0:T(8,128)(2,1)}, bf16[208,512]{1,0:T(8,128)(2,1)S(1)}, u32[]{:S(2)}, u32[]{:S(2)}) collective-permute-start(bf16[208,512]{1,0:T(8,128)(2,1)} %get-tuple-element.42), channel_id=1, source_target_pairs={{0,8},{4,12},{8,0},{12,4},{1,9},{5,13},{9,1},{13,5},{2,10},{6,14},... | collective-permute-start | bytes 638984 | tf_op jit(solution)/shard_map/ppermute | solution.py:244
  125.2 0.7 copy-start.17
  125.2 19.0 %collective-permute-start.21 = (bf16[208,512]{1,0:T(8,128)(2,1)}, bf16[208,512]{1,0:T(8,128)(2,1)S(1)}, u32[]{:S(2)}, u32[]{:S(2)}) collective-permute-start(bf16[208,512]{1,0:T(8,128)(2,1)} %get-tuple-element.43), channel_id=1, source_target_pairs={{0,12},{4,8},{8,4},{12,0},{1,13},{5,9},{9,5},{13,1},{2,14},{6,10},... | collective-permute-start | bytes 638984 | tf_op jit(solution)/shard_map/ppermute | solution.py:244
  125.5 0.7 copy-start.18
  125.5 0.8 copy-start.20
  128.8 18.8 %collective-permute-start.17 = (bf16[64,1664]{1,0:T(8,128)(2,1)}, bf16[64,1664]{1,0:T(8,128)(2,1)S(1)}, u32[]{:S(2)}, u32[]{:S(2)}) collective-permute-start(bf16[64,1664]{1,0:T(8,128)(2,1)} %shard_map.54.mine_ref), channel_id=1, source_target_pairs={{0,1},{1,0},{2,3},{3,2},{4,5},{5,4},{6,7},{7,6},{8,9},{9,8},{10,11... | collective-permute-start | bytes 638984 | tf_op jit(solution)/shard_map/ppermute | solution.py:247
  132.1 12.2 %copy-start.8 = (bf16[208,512]{1,0:T(8,128)(2,1)}, bf16[208,512]{1,0:T(8,128)(2,1)S(1)}, u32[]{:S(2)}) copy-start(bf16[208,512]{1,0:T(8,128)(2,1)S(1)} %collective-permute-done.19.refs_1_) | copy-start | bytes 638980
  140.4 3.9 %copy-start.9 = (bf16[208,512]{1,0:T(8,128)(2,1)}, bf16[208,512]{1,0:T(8,128)(2,1)S(1)}, u32[]{:S(2)}) copy-start(bf16[208,512]{1,0:T(8,128)(2,1)S(1)} %collective-permute-done.20.refs_2_) | copy-start | bytes 638980
  144.2 0.7 copy-start.10
  147.7 0.7 copy-start.11

commit v2 on v1

--- a/solution.py
+++ b/solution.py
@@ -42,84 +42,75 @@
 def pack_kernel(n, w_ref, *refs):
     outs, staged = refs[:n], refs[n]
     me = lax.axis_index("seq")
+    group = lax.axis_index("grp")
     rows = w_ref.shape[1]
     fill = jnp.zeros((rows, SLOT - HD), BF)
     for head in range(n):
         for mat in range(4):
             block = w_ref[mat, :, head * HD : (head + 1) * HD]
-            staged[head, :, mat * SLOT : (mat + 1) * SLOT] = jnp.concatenate([block, fill], axis=1)
-    for k in range(n):
-        outs[k][...] = staged[me ^ k]
-
-
-def norm_kernel(x_ref, up_ref, normed_ref, send_ref):
+            first = (mat % 2) * SLOT
+            staged[mat // 2, head, :, first : first + SLOT] = jnp.concatenate(
+                [block, fill], axis=1
+            )
+    for k in range(n):
+        outs[k][...] = staged[group, me ^ k]
+
+
+def norm_kernel(x_ref, up_ref, send_ref, rest_ref, staged):
     core = lax.axis_index("pipe")
-    normed = standardize(x_ref[...].astype(F32))[0].astype(BF)
-    normed_ref[...] = normed
-
-    @pl.when(core == 0)
-    def _():
-        send_ref[...] = normed
-
-    @pl.when(core != 0)
-    def _():
-        send_ref[...] = up_ref[...]
+    half = x_ref.shape[0] // 2
+    staged[...] = standardize(x_ref[...].astype(F32))[0].astype(BF)
+    for target, at in ((send_ref, core), (rest_ref, 1 - core)):
+        span = pl.ds(pl.multiple_of(at * half, half), half)
+        target[:half] = staged[span, :]
+        target[half:] = up_ref[span, :]
+
+
+def merge_kernel(*refs):
+    share = refs[0].shape[0]
+    for k, ref in enumerate(refs[:-1]):
+        refs[-1][k * share : (k + 1) * share] = ref[...]
 
 
 def head_kernel(n, *refs):
-    normed_ref, up_ref = refs[:2]
-    got = refs[2 : 1 + n]
-    swapped = refs[1 + n : 2 * n]
-    w_own = refs[2 * n : 3 * n]
-    w_other = refs[3 * n : 4 * n]
-    keep_ref, give_ref, grads_ref, x_full, up_full = refs[4 * n : 4 * n + 5]
-    w_full, term_k, term_v, sems, wsems = refs[4 * n + 5 :]
+    got, swapped = refs[:n], refs[n : 2 * n]
+    pieces = refs[2 * n : 2 * n + 4]
+    keep_ref, give_ref, grads_ref, x_full, up_full = refs[2 * n + 4 : 2 * n + 9]
+    w_full, term_k, term_v, sems, wsems = refs[2 * n + 9 :]
     me = lax.axis_index("seq")
     image = lax.axis_index("dp")
-    core = lax.axis_index("pipe")
-    rows = normed_ref.shape[0]
-    share = w_own[0].shape[0]
-    local = [(normed_ref, x_full), (up_ref, up_full)]
-
-    weight_copies = []
-    for k in range(n):
-        for which, (source, at) in enumerate(((w_own[k], image), (w_other[k], 1 - image))):
+    group = lax.axis_index("grp")
+    rows = got[0].shape[0]
+    half = rows // 2
+    share = pieces[0].shape[0] // n
+
+    copies = []
+    for which, source in enumerate(pieces):
+        at = 1 - image if which % 2 else image
+        mats = 1 - group if which // 2 else group
+        for k in range(n):
             first = pl.multiple_of(((me ^ k) * 2 + at) * share, 16)
-            copy = pltpu.make_async_copy(
-                source, w_full.at[pl.ds(first, share), :], wsems.at[k, which]
+            lanes = pl.multiple_of(mats * 2 * SLOT, 2 * SLOT)
+            copies.append(
+                pltpu.make_async_copy(
+                    source.at[pl.ds(k * share, share), :],
+                    w_full.at[pl.ds(first, share), pl.ds(lanes, 2 * SLOT)],
+                    wsems.at[which, k],
+                )
             )
-            copy.start()
-            weight_copies.append(copy)
-    copies = []
-    for which, (source, target) in enumerate(local):
-        copy = pltpu.make_async_copy(source, target.at[pl.ds(0, rows), :], sems.at[which, 0])
-        copy.start()
-        copies.append(copy)
-
-    def blocks(first, second):
-        made = []
-        for k in range(1, n):
-            for which, source in ((0, first[k - 1]), (1, second[k - 1])):
-                made.append(
+    for k in range(n):
+        for side, source in enumerate((got[k], swapped[k])):
+            for which, target in enumerate((x_full, up_full)):
+                copies.append(
                     pltpu.make_async_copy(
-                        source,
-                        local[which][1].at[pl.ds(k * rows, rows), :],
-                        sems.at[which, k],
+                        source.at[pl.ds(which * half, half), :],
+                        target.at[pl.ds(k * rows + side * half, half), :],
+                        sems.at[k, side, which],
                     )
                 )
-        return made
-
-    @pl.when(core == 0)
-    def _():
-        for copy in blocks(got, swapped):
-            copy.start()
-
-    @pl.when(core != 0)
-    def _():
-        for copy in blocks(swapped, got):
-            copy.start()
-
-    for copy in weight_copies + copies + blocks(got, swapped):
+    for copy in copies:
+        copy.start()
+    for copy in copies:
         copy.wait()
 
     scale = HD ** (-0.5)
@@ -150,20 +141,11 @@
             term_v[...] += value_term
     grads_ref[:, SLOT : 2 * SLOT] = term_k[...].astype(BF)
     grads_ref[:, 2 * SLOT : 3 * SLOT] = term_v[...].astype(BF)
-    half = rows // 2
     for b in range(n):
         span = slice(b * rows, (b + 1) * rows)
         part = nt(grads_ref[span, : 3 * SLOT], w_full[:, : 3 * SLOT]).astype(BF)
-
-        @pl.when(core == 0)
-        def _():
-            keep_ref[b] = part[:half]
-            give_ref[b] = part[half:]
-
-        @pl.when(core != 0)
-        def _():
-            keep_ref[b] = part[half:]
-            give_ref[b] = part[:half]
+        keep_ref[b] = part[:half]
+        give_ref[b] = part[half:]
 
 
 def weight_kernel(n, factor, x_ref, up_ref, grads_ref, keep_ref, give_ref, staged):
@@ -239,6 +221,7 @@
     share = attn_weights.shape[1]
     patches = n * rows
     half = rows // 2
+    me = lax.axis_index("seq")
 
     def across(value, k):
         return lax.ppermute(value, "seq", [(i, i ^ k) for i in range(n)])
@@ -246,18 +229,34 @@
     def swap(value, axis):
         return lax.ppermute(value, axis, [(0, 1), (1, 0)])
 
+    def near(values):
+        return [pltpu.with_memory_space_constraint(v, pltpu.VMEM) for v in values]
+
     chunks = call(
         functools.partial(pack_kernel, n),
-        [((share, 4 * SLOT), BF)] * n,
+        [((share, 2 * SLOT), BF)] * n,
         (attn_weights,),
-        [pltpu.VMEM((n, share, 4 * SLOT), BF)],
-    )
-    w_own = [chunks[0]] + [across(chunks[k], k) for k in range(1, n)]
-    w_other = [swap(w, "dp") for w in w_own]
-    normed, send = call(norm_kernel, [((rows, width), BF)] * 2, (x, up))
-    got = [across(send, k) for k in range(1, n)]
-    swapped = [swap(g, "pipe") for g in got]
-    args = (normed, up, *got, *swapped, *w_own, *w_other)
+        [pltpu.VMEM((2, n, share, 2 * SLOT), BF)],
+    )
+    arrived = [across(chunks[k], k) for k in range(1, n)]
+    send, rest = call(
+        norm_kernel, [((rows, width), BF)] * 2, (x, up), [pltpu.VMEM((rows, width), BF)]
+    )
+    send, *arrived = lax.optimization_barrier((send, *arrived))
+    merged = call(merge_kernel, ((n * share, 2 * SLOT), BF), (chunks[0], *near(arrived)))
+    beside = swap(merged, "dp")
+    above = swap(merged, "grp")
+    corner = swap(above, "dp")
+
+    second = across(send, 2)
+    first = across(send, 1)
+    later, second = lax.optimization_barrier((send, second))
+    middle = lax.ppermute(later, "seq", [(1, 2), (2, 1)])
+    passed = lax.ppermute(second, "seq", [(2, 3), (1, 0)])
+    third = jnp.where((me == 0) | (me == n - 1), passed, middle)
+    got = [send, first, second, third]
+    swapped = [rest] + [swap(g, "pipe") for g in got[1:]]
+    args = (*got[:1], *near(got[1:]), rest, *near(swapped[1:]), merged, *near((beside, above, corner)))
     keep, give, grads, x_full, up_full = call(
         functools.partial(head_kernel, n),
         [
@@ -272,13 +271,13 @@
             pltpu.VMEM((width, 4 * SLOT), BF),
             pltpu.VMEM((patches, SLOT), F32),
             pltpu.VMEM((patches, SLOT), F32),
-            pltpu.SemaphoreType.DMA((2, n)),
-            pltpu.SemaphoreType.DMA((n, 2)),
+            pltpu.SemaphoreType.DMA((n, 2, 2)),
+            pltpu.SemaphoreType.DMA((4, n)),
         ],
         [ANY_SPEC] * len(args),
     )
     taken = swap(give, "pipe")
-    sums = call(functools.partial(sum_kernel, n), [((half, width), BF)] * n, (keep, taken))
+    sums = call(functools.partial(sum_kernel, n), [((half, width), BF)] * n, (keep, *near([taken])))
     parts = [sums[0]] + [across(sums[k], k) for k in range(1, n)]
     factor = 1.0 / math.sqrt(patches * lax.axis_size("dp"))
     w_keep, w_give = call(
@@ -289,15 +288,15 @@
     )
     w_taken = swap(w_give, "dp")
     w_sums = call(
-        functools.partial(sum_kernel, n), [((share, 4 * SLOT), BF)] * n, (w_keep, w_taken)
+        functools.partial(sum_kernel, n), [((share, 4 * SLOT), BF)] * n, (w_keep, *near([w_taken]))
     )
     w_parts = [w_sums[0]] + [across(w_sums[k], k) for k in range(1, n)]
-    mine = call(functools.partial(final_kernel, n), ((half, width), BF), (x, up, *parts))
-    input_gradient = call(join_kernel, ((rows, width), BF), (mine, swap(mine, "pipe")))
+    mine = call(functools.partial(final_kernel, n), ((half, width), BF), (x, up, parts[0], *near(parts[1:])))
+    input_gradient = call(join_kernel, ((rows, width), BF), (mine, *near([swap(mine, "pipe")])))
     weight_grads = call(
         functools.partial(unpack_kernel, n),
         ((4, share, n * HD), F32),
-        tuple(w_parts),
+        (w_parts[0], *near(w_parts[1:])),
         [pltpu.VMEM((n, share, 4 * SLOT), BF)],
     )
     return (input_gradient[None], weight_grads)
@@ -372,7 +371,8 @@
     heads = attn_weights.shape[2] // HD
     one_head_each = (
         heads == n
-        and n & (n - 1) == 0
+        and n == 4
+        and lax.axis_size("grp") == 2
         and lax.axis_size("dp") == 2
         and lax.axis_size("pipe") == 2
         and attn_weights.shape[1] % 16 == 0

time: 151 us -> 126 us (0.83)
  waiting for transfers between devices: 87.8 us -> 66.8 us
  local copies, waits for them, and re-layouts: 5.02 us -> 0 us
    ppermute x12 -> x11, waiting for transfers between devices: 64.6 us -> 34.8 us  [across(): return lax.ppermute(value, 'seq', [(i, i ^ k) for i in range(n)])]
    ppermute x0 -> x2, starting transfers between devices: none -> 5.98 us  [the longest x1 3.4 us: local_heads(): middle = lax.ppermute(later, 'seq', [(1, 2), (2, 1)])]
    ppermute x0 -> x2, waiting for transfers between devices: none -> 5.94 us  [the longest x1 4.4 us: local_heads(): middle = lax.ppermute(later, 'seq', [(1, 2), (2, 1)])]
    unnamed x44 -> x0, local copies, waits for them, and re-layouts: 5.02 us -> none
    ppermute x10 -> x9, starting transfers between devices: 8.58 us -> 5.29 us  [swap(): return lax.ppermute(value, axis, [(0, 1), (1, 0)])]
    ppermute x10 -> x9, waiting for transfers between devices: 23.2 us -> 26 us  [swap(): return lax.ppermute(value, axis, [(0, 1), (1, 0)])]
    ppermute x12 -> x11, starting transfers between devices: 14.9 us -> 13.5 us  [across(): return lax.ppermute(value, 'seq', [(i, i ^ k) for i in range(n)])]
    pallas_call x9 -> x10, Pallas kernels: 33.1 us -> 33.7 us  [call(): pl.pallas_call(kernel, out_shape=[jax.ShapeDtypeStruct(*s) for s in shape...]
  transfers between devices with their start and end apart: 22 -> 22, of which waited for: 9 -> 11; matrix products, arithmetic and copies ran while one was open for 0% -> 0% of each run, Pallas kernels for 12% -> 14%
where the time goes in v2:
time: 126 us
  waiting for transfers between devices  66.8 us (53%)
  Pallas kernels  33.7 us (27%)
  starting transfers between devices  24.8 us (20%)
    ppermute x11, waiting for transfers between devices, across(): return lax.ppermute(value, 'seq', [(i, i ^ k) for i in range(n)])  34.8 us
    pallas_call x10, Pallas kernels, call(): pl.pallas_call(kernel, out_shape=[jax.ShapeDtypeStruct(*s) for s in shape...  33.7 us
    ppermute x9, waiting for transfers between devices, swap(): return lax.ppermute(value, axis, [(0, 1), (1, 0)])  26 us
    ppermute x11, starting transfers between devices, across(): return lax.ppermute(value, 'seq', [(i, i ^ k) for i in range(n)])  13.5 us
    ppermute x9, starting transfers between devices, swap(): return lax.ppermute(value, axis, [(0, 1), (1, 0)])  5.29 us
    ppermute x1, waiting for transfers between devices, local_heads(): middle = lax.ppermute(later, 'seq', [(1, 2), (2, 1)])  4.4 us
    ppermute x1, starting transfers between devices, local_heads(): middle = lax.ppermute(later, 'seq', [(1, 2), (2, 1)])  3.4 us
    ppermute x1, starting transfers between devices, local_heads(): passed = lax.ppermute(second, 'seq', [(2, 3), (1, 0)])  2.58 us
  transfers between devices with their start and end apart: 22, of which 11 were waited for; matrix products, arithmetic and copies ran while one was open for 0% of the time, Pallas kernels for 14%

profile of v2, /device:TPU:8, one launch (start us, length us, event | category | flops | bytes accessed | tf_op | source)
XLA Modules:
  0.0 126.0 jit_solution(4242977581721808123)
XLA Ops:
  0.6 2.3 %shard_map.51 = (bf16[208,256]{1,0:T(8,128)(2,1)}, bf16[208,256]{1,0:T(8,128)(2,1)}, bf16[208,256]{1,0:T(8,128)(2,1)}, bf16[208,256]{1,0:T(8,128)(2,1)}) custom-call(bf16[4,208,416]{2,1,0:T(8,128)(2,1)} %w_ref.1), custom_call_target="tpu_custom_call" | custom-call | tf_op jit(solution)/shard_map/pallas_call | solution.py:206
  2.9 0.0 collective-permute-start
  2.9 3.0 %collective-permute-start.1 = (bf16[208,256]{1,0:T(8,128)(2,1)}, bf16[208,256]{1,0:T(8,128)(2,1)S(1)}, u32[]{:S(2)}, u32[]{:S(2)}) collective-permute-start(bf16[208,256]{1,0:T(8,128)(2,1)} %get-tuple-element.31), channel_id=1, source_target_pairs={{0,8},{4,12},{8,0},{12,4},{1,9},{5,13},{9,1},{13,5},{2,10},{6,14},... | collective-permute-start | bytes 319496 | tf_op jit(solution)/shard_map/ppermute | solution.py:227
  6.0 0.5 collective-permute-start.2
  6.4 2.4 %shard_map.50 = (bf16[128,1664]{1,0:T(8,128)(2,1)}, bf16[128,1664]{1,0:T(8,128)(2,1)}) custom-call(bf16[128,1664]{1,0:T(8,128)(2,1)} %bitcast.3, bf16[128,1664]{1,0:T(8,128)(2,1)} %bitcast.5), custom_call_target="tpu_custom_call" | custom-call | tf_op jit(solution)/shard_map/pallas_call | solution.py:206
  8.8 5.2 %collective-permute-done.1.refs_2_ = bf16[208,256]{1,0:T(8,128)(2,1)S(1)} collective-permute-done((bf16[208,256]{1,0:T(8,128)(2,1)}, bf16[208,256]{1,0:T(8,128)(2,1)S(1)}, u32[]{:S(2)}, u32[]{:S(2)}) %collective-permute-start.1) | collective-permute-done | bytes 106528 | tf_op jit(solution)/shard_map/ppermute | solution.py:227
  14.0 1.9 %collective-permute-done.2.refs_3_ = bf16[208,256]{1,0:T(8,128)(2,1)S(1)} collective-permute-done((bf16[208,256]{1,0:T(8,128)(2,1)}, bf16[208,256]{1,0:T(8,128)(2,1)S(1)}, u32[]{:S(2)}, u32[]{:S(2)}) %collective-permute-start.2) | collective-permute-done | bytes 106528 | tf_op jit(solution)/shard_map/ppermute | solution.py:227
  15.9 1.4 %collective-permute-start.4 = (bf16[128,1664]{1,0:T(8,128)(2,1)}, bf16[128,1664]{1,0:T(8,128)(2,1)S(1)}, u32[]{:S(2)}, u32[]{:S(2)}) collective-permute-start(bf16[128,1664]{1,0:T(8,128)(2,1)} %get-tuple-element.35.refs_0_), channel_id=1, source_target_pairs={{0,8},{4,12},{8,0},{12,4},{1,9},{5,13},{9,1},{13,5},{2,10},{6,14},... | collective-permute-start | bytes 1277960 | tf_op jit(solution)/shard_map/ppermute | solution.py:227
  17.2 1.7 %collective-permute-start.3 = (bf16[128,1664]{1,0:T(8,128)(2,1)}, bf16[128,1664]{1,0:T(8,128)(2,1)S(1)}, u32[]{:S(2)}, u32[]{:S(2)}) collective-permute-start(bf16[128,1664]{1,0:T(8,128)(2,1)} %get-tuple-element.35.refs_0_), channel_id=1, source_target_pairs={{0,4},{4,0},{8,12},{12,8},{1,5},{5,1},{9,13},{13,9},{2,6},{6,2},{1... | collective-permute-start | bytes 1277960 | tf_op jit(solution)/shard_map/ppermute | solution.py:227
  18.9 1.7 %shard_map.52.refs_8_ = bf16[832,256]{1,0:T(8,128)(2,1)} custom-call(bf16[208,256]{1,0:T(8,128)(2,1)} %get-tuple-element.37.refs_0_, bf16[208,256]{1,0:T(8,128)(2,1)S(1)} %collective-permute-done.refs_1_, bf16[208,256]{1,0:T(8,128)(2,1)S(1)} %collective-permute-done.1.refs_2_, bf16[208,256]{1,0:T(8,128)(2,1)S(1)} %collective-permute-done.2.refs_3_), custom_call_target="tpu_custom_call" | custom-call | tf_op jit(solution)/shard_map/pallas_call | solution.py:206
  20.6 1.5 %collective-permute-start.11 = (bf16[832,256]{1,0:T(8,128)(2,1)}, bf16[832,256]{1,0:T(8,128)(2,1)S(1)}, u32[]{:S(2)}, u32[]{:S(2)}) collective-permute-start(bf16[832,256]{1,0:T(8,128)(2,1)} %shard_map.52.refs_8_), channel_id=1, source_target_pairs={{0,16},{16,0},{1,17},{17,1},{2,18},{18,2},{3,19},{19,3},{4,20},{20... | collective-permute-start | bytes 1277960 | tf_op jit(solution)/shard_map/ppermute | solution.py:230
  22.1 11.5 %collective-permute-done.4.refs_2_ = bf16[128,1664]{1,0:T(8,128)(2,1)S(1)} collective-permute-done((bf16[128,1664]{1,0:T(8,128)(2,1)}, bf16[128,1664]{1,0:T(8,128)(2,1)S(1)}, u32[]{:S(2)}, u32[]{:S(2)}) %collective-permute-start.4) | collective-permute-done | bytes 426016 | tf_op jit(solution)/shard_map/ppermute | solution.py:227
  33.7 3.4 %collective-permute-start.6 = (bf16[128,1664]{1,0:T(8,128)(2,1)}, bf16[128,1664]{1,0:T(8,128)(2,1)S(1)}, u32[]{:S(2)}, u32[]{:S(2)}) collective-permute-start(bf16[128,1664]{1,0:T(8,128)(2,1)} %get-tuple-element.35.refs_0_), channel_id=1, source_target_pairs={{4,8},{8,4},{5,9},{9,5},{6,10},{10,6},{7,11},{11,7},{20,24},{24,20... | collective-permute-start | bytes 1277960 | tf_op jit(solution)/shard_map/ppermute | solution.py:254
  37.1 2.6 %collective-permute-start.5 = (bf16[128,1664]{1,0:T(8,128)(2,1)S(1)}, bf16[128,1664]{1,0:T(8,128)(2,1)S(1)}, u32[]{:S(2)}, u32[]{:S(2)}) collective-permute-start(bf16[128,1664]{1,0:T(8,128)(2,1)S(1)} %collective-permute-done.4.refs_2_), channel_id=1, source_target_pairs={{8,12},{4,0},{9,13},{5,1},{10,14},{6,2},{11,15},{7,3},{24,28},{20,... | collective-permute-start | bytes 1277960 | tf_op jit(solution)/shard_map/ppermute | solution.py:255
  39.7 1.6 %collective-permute-start.10 = (bf16[832,256]{1,0:T(8,128)(2,1)}, bf16[832,256]{1,0:T(8,128)(2,1)S(1)}, u32[]{:S(2)}, u32[]{:S(2)}) collective-permute-start(bf16[832,256]{1,0:T(8,128)(2,1)} %shard_map.52.refs_8_), channel_id=1, source_target_pairs={{0,2},{2,0},{1,3},{3,1},{4,6},{6,4},{5,7},{7,5},{8,10},{10,8},{9,1... | collective-permute-start | bytes 1277960 | tf_op jit(solution)/shard_map/ppermute | solution.py:230
  41.2 0.0 collective-permute-start.8
  41.2 0.0 collective-permute-done.3.refs_1_
  41.2 0.6 collective-permute-start.12
  41.8 4.4 %collective-permute-done.6 = bf16[128,1664]{1,0:T(8,128)(2,1)S(1)} collective-permute-done((bf16[128,1664]{1,0:T(8,128)(2,1)}, bf16[128,1664]{1,0:T(8,128)(2,1)S(1)}, u32[]{:S(2)}, u32[]{:S(2)}) %collective-permute-start.6) | collective-permute-done | bytes 426016 | tf_op jit(solution)/shard_map/ppermute | solution.py:254
  46.2 1.5 %collective-permute-done.5 = bf16[128,1664]{1,0:T(8,128)(2,1)S(1)} collective-permute-done((bf16[128,1664]{1,0:T(8,128)(2,1)S(1)}, bf16[128,1664]{1,0:T(8,128)(2,1)S(1)}, u32[]{:S(2)}, u32[]{:S(2)}) %collective-permute-start.5) | collective-permute-done | bytes 426016 | tf_op jit(solution)/shard_map/ppermute | solution.py:255
  47.8 0.1 collective-permute-start.9
  47.9 4.8 %collective-permute-done.10.refs_9_ = bf16[832,256]{1,0:T(8,128)(2,1)S(1)} collective-permute-done((bf16[832,256]{1,0:T(8,128)(2,1)}, bf16[832,256]{1,0:T(8,128)(2,1)S(1)}, u32[]{:S(2)}, u32[]{:S(2)}) %collective-permute-start.10) | collective-permute-done | bytes 426016 | tf_op jit(solution)/shard_map/ppermute | solution.py:230
  52.7 6.7 %collective-permute-done.12.refs_11_ = bf16[832,256]{1,0:T(8,128)(2,1)S(1)} collective-permute-done((bf16[832,256]{1,0:T(8,128)(2,1)S(1)}, bf16[832,256]{1,0:T(8,128)(2,1)S(1)}, u32[]{:S(2)}, u32[]{:S(2)}) %collective-permute-start.12) | collective-permute-done | bytes 426016 | tf_op jit(solution)/shard_map/ppermute | solution.py:230
  59.5 0.0 collective-permute-done.7.refs_5_
  59.5 0.0 collective-permute-done.9.refs_7_
  59.5 11.8 %shard_map.53 = (bf16[4,64,1664]{2,1,0:T(8,128)(2,1)}, bf16[4,64,1664]{2,1,0:T(8,128)(2,1)}, bf16[512,512]{1,0:T(8,128)(2,1)}, bf16[512,1664]{1,0:T(8,128)(2,1)}, bf16[512,1664]{1,0:T(8,128)(2,1)}) custom-call(bf16[128,1664]{1,0:T(8,128)(2,1)} %get-tuple-element.35.refs_0_, bf16[128,1664]{1,0:T(8,128)(2,1)S(1)} %collective-permute-done.3.refs_1_, ...), custom_call_target="tpu_custom_call" | custom-call | tf_op jit(solution)/shard_map/pallas_call | solution.py:206
  71.2 0.1 collective-permute-start.13
  71.3 4.9 %shard_map.57 = (bf16[4,208,512]{2,1,0:T(8,128)(2,1)}, bf16[4,208,512]{2,1,0:T(8,128)(2,1)}) custom-call(bf16[512,1664]{1,0:T(8,128)(2,1)} %get-tuple-element.47.x_ref, bf16[512,1664]{1,0:T(8,128)(2,1)} %get-tuple-element.48.up_ref, bf16[512,512]{1,0:T(8,128)(2,1)} %get-tuple-element.49.grads_ref), custom_call_target="tpu_custom_call" | custom-call | tf_op jit(solution)/shard_map/pallas_call | solution.py:206
  76.2 1.5 %collective-permute-start.18 = (bf16[4,208,512]{2,1,0:T(8,128)(2,1)}, bf16[4,208,512]{2,1,0:T(8,128)(2,1)S(1)}, u32[]{:S(2)}, u32[]{:S(2)}) collective-permute-start(bf16[4,208,512]{2,1,0:T(8,128)(2,1)} %get-tuple-element.51), channel_id=1, source_target_pairs={{0,2},{2,0},{1,3},{3,1},{4,6},{6,4},{5,7},{7,5},{8,10},{10,8},{9,1... | collective-permute-start | bytes 2555912 | tf_op jit(solution)/shard_map/ppermute | solution.py:230
  77.7 0.0 collective-permute-done.13.theirs_ref
  77.7 2.1 %shard_map.54 = (bf16[64,1664]{1,0:T(8,128)(2,1)}, bf16[64,1664]{1,0:T(8,128)(2,1)}, bf16[64,1664]{1,0:T(8,128)(2,1)}, bf16[64,1664]{1,0:T(8,128)(2,1)}) custom-call(bf16[4,64,1664]{2,1,0:T(8,128)(2,1)} %get-tuple-element.41.mine_ref, bf16[4,64,1664]{2,1,0:T(8,128)(2,1)S(1)} %collective-permute-done.13.theirs_ref), custom_call_target="tpu_custom_call" | custom-call | tf_op jit(solution)/shard_map/pallas_call | solution.py:206
  79.8 0.0 collective-permute-start.14
  79.8 0.9 collective-permute-start.15
  80.7 2.6 %collective-permute-start.16 = (bf16[64,1664]{1,0:T(8,128)(2,1)}, bf16[64,1664]{1,0:T(8,128)(2,1)S(1)}, u32[]{:S(2)}, u32[]{:S(2)}) collective-permute-start(bf16[64,1664]{1,0:T(8,128)(2,1)} %get-tuple-element.46), channel_id=1, source_target_pairs={{0,12},{4,8},{8,4},{12,0},{1,13},{5,9},{9,5},{13,1},{2,14},{6,10},... | collective-permute-start | bytes 638984 | tf_op jit(solution)/shard_map/ppermute | solution.py:227
  83.2 14.5 %collective-permute-done.18.theirs_ref = bf16[4,208,512]{2,1,0:T(8,128)(2,1)S(1)} collective-permute-done((bf16[4,208,512]{2,1,0:T(8,128)(2,1)}, bf16[4,208,512]{2,1,0:T(8,128)(2,1)S(1)}, u32[]{:S(2)}, u32[]{:S(2)}) %collective-permute-start.18) | collective-permute-done | bytes 852000 | tf_op jit(solution)/shard_map/ppermute | solution.py:230
  97.8 2.2 %shard_map.58 = (bf16[208,512]{1,0:T(8,128)(2,1)}, bf16[208,512]{1,0:T(8,128)(2,1)}, bf16[208,512]{1,0:T(8,128)(2,1)}, bf16[208,512]{1,0:T(8,128)(2,1)}) custom-call(bf16[4,208,512]{2,1,0:T(8,128)(2,1)} %get-tuple-element.50.mine_ref, bf16[4,208,512]{2,1,0:T(8,128)(2,1)S(1)} %collective-permute-done.18.theirs_ref), custom_call_target="tpu_custom_call" | custom-call | tf_op jit(solution)/shard_map/pallas_call | solution.py:206
  99.9 0.0 collective-permute-start.19
  99.9 0.9 collective-permute-start.20
  100.8 0.0 collective-permute-done.14.refs_1_
  100.8 2.6 %collective-permute-start.21 = (bf16[208,512]{1,0:T(8,128)(2,1)}, bf16[208,512]{1,0:T(8,128)(2,1)S(1)}, u32[]{:S(2)}, u32[]{:S(2)}) collective-permute-start(bf16[208,512]{1,0:T(8,128)(2,1)} %get-tuple-element.55), channel_id=1, source_target_pairs={{0,12},{4,8},{8,4},{12,0},{1,13},{5,9},{9,5},{13,1},{2,14},{6,10},... | collective-permute-start | bytes 638984 | tf_op jit(solution)/shard_map/ppermute | solution.py:227
  103.4 0.0 collective-permute-done.15.refs_2_
  103.4 0.0 collective-permute-done.16.refs_3_
  103.4 2.3 %shard_map.55.mine_ref = bf16[64,1664]{1,0:T(8,128)(2,1)} custom-call(bf16[128,1664]{1,0:T(8,128)(2,1)} %bitcast.4, bf16[128,1664]{1,0:T(8,128)(2,1)} %bitcast.6, bf16[64,1664]{1,0:T(8,128)(2,1)} %get-tuple-element.43.refs_0_, bf16[64,1664]{1,0:T(8,128)(2,1)S(1)} %collective-permute-done.14.refs_1_, bf16[64,1664]{1,0:T(8,128)(2,1)S(1)} %collective-permute-done.15.refs_2_, ...), custom_call_target="tpu_custom_call" | custom-call | tf_op jit(solution)/shard_map/pallas_call | solution.py:206
  105.7 2.5 %collective-permute-done.19.refs_1_ = bf16[208,512]{1,0:T(8,128)(2,1)S(1)} collective-permute-done((bf16[208,512]{1,0:T(8,128)(2,1)}, bf16[208,512]{1,0:T(8,128)(2,1)S(1)}, u32[]{:S(2)}, u32[]{:S(2)}) %collective-permute-start.19) | collective-permute-done | bytes 213024 | tf_op jit(solution)/shard_map/ppermute | solution.py:227
  108.3 7.5 %collective-permute-done.20.refs_2_ = bf16[208,512]{1,0:T(8,128)(2,1)S(1)} collective-permute-done((bf16[208,512]{1,0:T(8,128)(2,1)}, bf16[208,512]{1,0:T(8,128)(2,1)S(1)}, u32[]{:S(2)}, u32[]{:S(2)}) %collective-permute-start.20) | collective-permute-done | bytes 213024 | tf_op jit(solution)/shard_map/ppermute | solution.py:227
  115.8 6.1 %collective-permute-done.21.refs_3_ = bf16[208,512]{1,0:T(8,128)(2,1)S(1)} collective-permute-done((bf16[208,512]{1,0:T(8,128)(2,1)}, bf16[208,512]{1,0:T(8,128)(2,1)S(1)}, u32[]{:S(2)}, u32[]{:S(2)}) %collective-permute-start.21) | collective-permute-done | bytes 213024 | tf_op jit(solution)/shard_map/ppermute | solution.py:227
  121.9 2.4 %shard_map.59 = f32[4,208,416]{2,1,0:T(8,128)} custom-call(bf16[208,512]{1,0:T(8,128)(2,1)} %get-tuple-element.52.refs_0_, bf16[208,512]{1,0:T(8,128)(2,1)S(1)} %collective-permute-done.19.refs_1_, bf16[208,512]{1,0:T(8,128)(2,1)S(1)} %collective-permute-done.20.refs_2_, bf16[208,512]{1,0:T(8,128)(2,1)S(1)} %collective-permute-done.21.refs_3_), custom_call_target="tpu_custom_call" | custom-call | tf_op jit(solution)/shard_map/pallas_call | solution.py:206
  124.3 1.7 %shard_map.56 = bf16[128,1664]{1,0:T(8,128)(2,1)} custom-call(bf16[64,1664]{1,0:T(8,128)(2,1)} %shard_map.55.mine_ref, bf16[64,1664]{1,0:T(8,128)(2,1)S(1)} %collective-permute-done.17.theirs_ref), custom_call_target="tpu_custom_call" | custom-call | tf_op jit(solution)/shard_map/pallas_call | solution.py:206
  (7 shorter events, 0.1 us)
Async XLA Ops:
  2.9 5.9 %collective-permute-start = (bf16[208,256]{1,0:T(8,128)(2,1)}, bf16[208,256]{1,0:T(8,128)(2,1)S(1)}, u32[]{:S(2)}, u32[]{:S(2)}) collective-permute-start(bf16[208,256]{1,0:T(8,128)(2,1)} %get-tuple-element.30), channel_id=1, source_target_pairs={{0,4},{4,0},{8,12},{12,8},{1,5},{5,1},{9,13},{13,9},{2,6},{6,2},{1... | collective-permute-start | bytes 319496 | tf_op jit(solution)/shard_map/ppermute | solution.py:227
  2.9 11.0 %collective-permute-start.1 = (bf16[208,256]{1,0:T(8,128)(2,1)}, bf16[208,256]{1,0:T(8,128)(2,1)S(1)}, u32[]{:S(2)}, u32[]{:S(2)}) collective-permute-start(bf16[208,256]{1,0:T(8,128)(2,1)} %get-tuple-element.31), channel_id=1, source_target_pairs={{0,8},{4,12},{8,0},{12,4},{1,9},{5,13},{9,1},{13,5},{2,10},{6,14},... | collective-permute-start | bytes 319496 | tf_op jit(solution)/shard_map/ppermute | solution.py:227
  6.0 9.9 %collective-permute-start.2 = (bf16[208,256]{1,0:T(8,128)(2,1)}, bf16[208,256]{1,0:T(8,128)(2,1)S(1)}, u32[]{:S(2)}, u32[]{:S(2)}) collective-permute-start(bf16[208,256]{1,0:T(8,128)(2,1)} %get-tuple-element.32), channel_id=1, source_target_pairs={{0,12},{4,8},{8,4},{12,0},{1,13},{5,9},{9,5},{13,1},{2,14},{6,10},... | collective-permute-start | bytes 319496 | tf_op jit(solution)/shard_map/ppermute | solution.py:227
  15.9 17.8 %collective-permute-start.4 = (bf16[128,1664]{1,0:T(8,128)(2,1)}, bf16[128,1664]{1,0:T(8,128)(2,1)S(1)}, u32[]{:S(2)}, u32[]{:S(2)}) collective-permute-start(bf16[128,1664]{1,0:T(8,128)(2,1)} %get-tuple-element.35.refs_0_), channel_id=1, source_target_pairs={{0,8},{4,12},{8,0},{12,4},{1,9},{5,13},{9,1},{13,5},{2,10},{6,14},... | collective-permute-start | bytes 1277960 | tf_op jit(solution)/shard_map/ppermute | solution.py:227
  17.2 24.0 %collective-permute-start.3 = (bf16[128,1664]{1,0:T(8,128)(2,1)}, bf16[128,1664]{1,0:T(8,128)(2,1)S(1)}, u32[]{:S(2)}, u32[]{:S(2)}) collective-permute-start(bf16[128,1664]{1,0:T(8,128)(2,1)} %get-tuple-element.35.refs_0_), channel_id=1, source_target_pairs={{0,4},{4,0},{8,12},{12,8},{1,5},{5,1},{9,13},{13,9},{2,6},{6,2},{1... | collective-permute-start | bytes 1277960 | tf_op jit(solution)/shard_map/ppermute | solution.py:227
  20.6 20.6 %collective-permute-start.11 = (bf16[832,256]{1,0:T(8,128)(2,1)}, bf16[832,256]{1,0:T(8,128)(2,1)S(1)}, u32[]{:S(2)}, u32[]{:S(2)}) collective-permute-start(bf16[832,256]{1,0:T(8,128)(2,1)} %shard_map.52.refs_8_), channel_id=1, source_target_pairs={{0,16},{16,0},{1,17},{17,1},{2,18},{18,2},{3,19},{19,3},{4,20},{20... | collective-permute-start | bytes 1277960 | tf_op jit(solution)/shard_map/ppermute | solution.py:230
  33.7 12.6 %collective-permute-start.6 = (bf16[128,1664]{1,0:T(8,128)(2,1)}, bf16[128,1664]{1,0:T(8,128)(2,1)S(1)}, u32[]{:S(2)}, u32[]{:S(2)}) collective-permute-start(bf16[128,1664]{1,0:T(8,128)(2,1)} %get-tuple-element.35.refs_0_), channel_id=1, source_target_pairs={{4,8},{8,4},{5,9},{9,5},{6,10},{10,6},{7,11},{11,7},{20,24},{24,20... | collective-permute-start | bytes 1277960 | tf_op jit(solution)/shard_map/ppermute | solution.py:254
  37.1 10.7 %collective-permute-start.5 = (bf16[128,1664]{1,0:T(8,128)(2,1)S(1)}, bf16[128,1664]{1,0:T(8,128)(2,1)S(1)}, u32[]{:S(2)}, u32[]{:S(2)}) collective-permute-start(bf16[128,1664]{1,0:T(8,128)(2,1)S(1)} %collective-permute-done.4.refs_2_), channel_id=1, source_target_pairs={{8,12},{4,0},{9,13},{5,1},{10,14},{6,2},{11,15},{7,3},{24,28},{20,... | collective-permute-start | bytes 1277960 | tf_op jit(solution)/shard_map/ppermute | solution.py:255
  39.7 13.0 %collective-permute-start.10 = (bf16[832,256]{1,0:T(8,128)(2,1)}, bf16[832,256]{1,0:T(8,128)(2,1)S(1)}, u32[]{:S(2)}, u32[]{:S(2)}) collective-permute-start(bf16[832,256]{1,0:T(8,128)(2,1)} %shard_map.52.refs_8_), channel_id=1, source_target_pairs={{0,2},{2,0},{1,3},{3,1},{4,6},{6,4},{5,7},{7,5},{8,10},{10,8},{9,1... | collective-permute-start | bytes 1277960 | tf_op jit(solution)/shard_map/ppermute | solution.py:230
  41.2 18.2 %collective-permute-start.8 = (bf16[128,1664]{1,0:T(8,128)(2,1)S(1)}, bf16[128,1664]{1,0:T(8,128)(2,1)S(1)}, u32[]{:S(2)}, u32[]{:S(2)}) collective-permute-start(bf16[128,1664]{1,0:T(8,128)(2,1)S(1)} %collective-permute-done.4.refs_2_), channel_id=1, source_target_pairs={{0,1},{1,0},{2,3},{3,2},{4,5},{5,4},{6,7},{7,6},{8,9},{9,8},{10,11... | collective-permute-start | bytes 1277960 | tf_op jit(solution)/shard_map/ppermute | solution.py:230
  41.2 18.2 %collective-permute-start.12 = (bf16[832,256]{1,0:T(8,128)(2,1)S(1)}, bf16[832,256]{1,0:T(8,128)(2,1)S(1)}, u32[]{:S(2)}, u32[]{:S(2)}) collective-permute-start(bf16[832,256]{1,0:T(8,128)(2,1)S(1)} %collective-permute-done.11.refs_10_), channel_id=1, source_target_pairs={{0,2},{2,0},{1,3},{3,1},{4,6},{6,4},{5,7},{7,5},{8,10},{10,8},{9,1... | collective-permute-start | bytes 1277960 | tf_op jit(solution)/shard_map/ppermute | solution.py:230
  46.2 13.2 %collective-permute-start.7 = (bf16[128,1664]{1,0:T(8,128)(2,1)S(1)}, bf16[128,1664]{1,0:T(8,128)(2,1)S(1)}, u32[]{:S(2)}, u32[]{:S(2)}) collective-permute-start(bf16[128,1664]{1,0:T(8,128)(2,1)S(1)} %collective-permute-done.3.refs_1_), channel_id=1, source_target_pairs={{0,1},{1,0},{2,3},{3,2},{4,5},{5,4},{6,7},{7,6},{8,9},{9,8},{10,11... | collective-permute-start | bytes 1277960 | tf_op jit(solution)/shard_map/ppermute | solution.py:230
  47.8 11.6 %collective-permute-start.9 = (bf16[128,1664]{1,0:T(8,128)(2,1)S(1)}, bf16[128,1664]{1,0:T(8,128)(2,1)S(1)}, u32[]{:S(2)}, u32[]{:S(2)}) collective-permute-start(bf16[128,1664]{1,0:T(8,128)(2,1)S(1)} %broadcast_select_fusion.refs_3_), channel_id=1, source_target_pairs={{0,1},{1,0},{2,3},{3,2},{4,5},{5,4},{6,7},{7,6},{8,9},{9,8},{10,11... | collective-permute-start | bytes 1277960 | tf_op jit(solution)/shard_map/ppermute | solution.py:230
  71.2 6.4 %collective-permute-start.13 = (bf16[4,64,1664]{2,1,0:T(8,128)(2,1)}, bf16[4,64,1664]{2,1,0:T(8,128)(2,1)S(1)}, u32[]{:S(2)}, u32[]{:S(2)}) collective-permute-start(bf16[4,64,1664]{2,1,0:T(8,128)(2,1)} %get-tuple-element.42), channel_id=1, source_target_pairs={{0,1},{1,0},{2,3},{3,2},{4,5},{5,4},{6,7},{7,6},{8,9},{9,8},{10,11... | collective-permute-start | bytes 2555912 | tf_op jit(solution)/shard_map/ppermute | solution.py:230
  76.2 21.6 %collective-permute-start.18 = (bf16[4,208,512]{2,1,0:T(8,128)(2,1)}, bf16[4,208,512]{2,1,0:T(8,128)(2,1)S(1)}, u32[]{:S(2)}, u32[]{:S(2)}) collective-permute-start(bf16[4,208,512]{2,1,0:T(8,128)(2,1)} %get-tuple-element.51), channel_id=1, source_target_pairs={{0,2},{2,0},{1,3},{3,1},{4,6},{6,4},{5,7},{7,5},{8,10},{10,8},{9,1... | collective-permute-start | bytes 2555912 | tf_op jit(solution)/shard_map/ppermute | solution.py:230
  79.8 21.0 %collective-permute-start.14 = (bf16[64,1664]{1,0:T(8,128)(2,1)}, bf16[64,1664]{1,0:T(8,128)(2,1)S(1)}, u32[]{:S(2)}, u32[]{:S(2)}) collective-permute-start(bf16[64,1664]{1,0:T(8,128)(2,1)} %get-tuple-element.44), channel_id=1, source_target_pairs={{0,4},{4,0},{8,12},{12,8},{1,5},{5,1},{9,13},{13,9},{2,6},{6,2},{1... | collective-permute-start | bytes 638984 | tf_op jit(solution)/shard_map/ppermute | solution.py:227
  79.8 23.6 %collective-permute-start.15 = (bf16[64,1664]{1,0:T(8,128)(2,1)}, bf16[64,1664]{1,0:T(8,128)(2,1)S(1)}, u32[]{:S(2)}, u32[]{:S(2)}) collective-permute-start(bf16[64,1664]{1,0:T(8,128)(2,1)} %get-tuple-element.45), channel_id=1, source_target_pairs={{0,8},{4,12},{8,0},{12,4},{1,9},{5,13},{9,1},{13,5},{2,10},{6,14},... | collective-permute-start | bytes 638984 | tf_op jit(solution)/shard_map/ppermute | solution.py:227
  80.7 22.8 %collective-permute-start.16 = (bf16[64,1664]{1,0:T(8,128)(2,1)}, bf16[64,1664]{1,0:T(8,128)(2,1)S(1)}, u32[]{:S(2)}, u32[]{:S(2)}) collective-permute-start(bf16[64,1664]{1,0:T(8,128)(2,1)} %get-tuple-element.46), channel_id=1, source_target_pairs={{0,12},{4,8},{8,4},{12,0},{1,13},{5,9},{9,5},{13,1},{2,14},{6,10},... | collective-permute-start | bytes 638984 | tf_op jit(solution)/shard_map/ppermute | solution.py:227
  99.9 8.4 %collective-permute-start.19 = (bf16[208,512]{1,0:T(8,128)(2,1)}, bf16[208,512]{1,0:T(8,128)(2,1)S(1)}, u32[]{:S(2)}, u32[]{:S(2)}) collective-permute-start(bf16[208,512]{1,0:T(8,128)(2,1)} %get-tuple-element.53), channel_id=1, source_target_pairs={{0,4},{4,0},{8,12},{12,8},{1,5},{5,1},{9,13},{13,9},{2,6},{6,2},{1... | collective-permute-start | bytes 638984 | tf_op jit(solution)/shard_map/ppermute | solution.py:227
  99.9 15.9 %collective-permute-start.20 = (bf16[208,512]{1,0:T(8,128)(2,1)}, bf16[208,512]{1,0:T(8,128)(2,1)S(1)}, u32[]{:S(2)}, u32[]{:S(2)}) collective-permute-start(bf16[208,512]{1,0:T(8,128)(2,1)} %get-tuple-element.54), channel_id=1, source_target_pairs={{0,8},{4,12},{8,0},{12,4},{1,9},{5,13},{9,1},{13,5},{2,10},{6,14},... | collective-permute-start | bytes 638984 | tf_op jit(solution)/shard_map/ppermute | solution.py:227
  100.8 21.1 %collective-permute-start.21 = (bf16[208,512]{1,0:T(8,128)(2,1)}, bf16[208,512]{1,0:T(8,128)(2,1)S(1)}, u32[]{:S(2)}, u32[]{:S(2)}) collective-permute-start(bf16[208,512]{1,0:T(8,128)(2,1)} %get-tuple-element.55), channel_id=1, source_target_pairs={{0,12},{4,8},{8,4},{12,0},{1,13},{5,9},{9,5},{13,1},{2,14},{6,10},... | collective-permute-start | bytes 638984 | tf_op jit(solution)/shard_map/ppermute | solution.py:227
  105.7 18.6 %collective-permute-start.17 = (bf16[64,1664]{1,0:T(8,128)(2,1)}, bf16[64,1664]{1,0:T(8,128)(2,1)S(1)}, u32[]{:S(2)}, u32[]{:S(2)}) collective-permute-start(bf16[64,1664]{1,0:T(8,128)(2,1)} %shard_map.55.mine_ref), channel_id=1, source_target_pairs={{0,1},{1,0},{2,3},{3,2},{4,5},{5,4},{6,7},{7,6},{8,9},{9,8},{10,11... | collective-permute-start | bytes 638984 | tf_op jit(solution)/shard_map/ppermute | solution.py:230

commit v3 on v2

--- a/solution.py
+++ b/solution.py
@@ -14,7 +14,7 @@
 EPSILON = 1e-06
 BF = jnp.bfloat16
 F32 = jnp.float32
-PARAMS = pltpu.CompilerParams(vmem_limit_bytes=56 * 1024 * 1024)
+PARAMS = pltpu.CompilerParams(vmem_limit_bytes=24 * 1024 * 1024)
 VMEM_SPEC = pl.BlockSpec(memory_space=pltpu.VMEM)
 ANY_SPEC = pl.BlockSpec(memory_space=pl.ANY)
 
@@ -72,11 +72,11 @@
         refs[-1][k * share : (k + 1) * share] = ref[...]
 
 
-def head_kernel(n, *refs):
+def head_kernel(n, factor, *refs):
     got, swapped = refs[:n], refs[n : 2 * n]
     pieces = refs[2 * n : 2 * n + 4]
-    keep_ref, give_ref, grads_ref, x_full, up_full = refs[2 * n + 4 : 2 * n + 9]
-    w_full, term_k, term_v, sems, wsems = refs[2 * n + 9 :]
+    keep_ref, give_ref, w_keep_ref, w_give_ref = refs[2 * n + 4 : 2 * n + 8]
+    x_full, up_full, w_full, grads, staged, term_k, term_v, sems, wsems = refs[2 * n + 8 :]
     me = lax.axis_index("seq")
     image = lax.axis_index("dp")
     group = lax.axis_index("grp")
@@ -129,8 +129,8 @@
         delta = jnp.sum(grad_out.astype(F32) * attended.astype(F32), axis=1, keepdims=True)
         dprobs = nt(grad_out, value_rows)
         dscores = (probs.astype(F32) * (dprobs - delta) * scale).astype(BF)
-        grads_ref[span, :SLOT] = nn(dscores, key_rows).astype(BF)
-        grads_ref[span, 3 * SLOT :] = attended
+        grads[span, :SLOT] = nn(dscores, key_rows).astype(BF)
+        grads[span, 3 * SLOT :] = attended
         key_term = tn(dscores, query).astype(BF).astype(F32)
         value_term = tn(probs, grad_out).astype(BF).astype(F32)
         if b == 0:
@@ -139,23 +139,17 @@
         else:
             term_k[...] += key_term
             term_v[...] += value_term
-    grads_ref[:, SLOT : 2 * SLOT] = term_k[...].astype(BF)
-    grads_ref[:, 2 * SLOT : 3 * SLOT] = term_v[...].astype(BF)
+    grads[:, SLOT : 2 * SLOT] = term_k[...].astype(BF)
+    grads[:, 2 * SLOT : 3 * SLOT] = term_v[...].astype(BF)
     for b in range(n):
         span = slice(b * rows, (b + 1) * rows)
-        part = nt(grads_ref[span, : 3 * SLOT], w_full[:, : 3 * SLOT]).astype(BF)
+        part = nt(grads[span, : 3 * SLOT], w_full[:, : 3 * SLOT]).astype(BF)
         keep_ref[b] = part[:half]
         give_ref[b] = part[half:]
-
-
-def weight_kernel(n, factor, x_ref, up_ref, grads_ref, keep_ref, give_ref, staged):
-    me = lax.axis_index("seq")
-    image = lax.axis_index("dp")
-    share = keep_ref.shape[1]
-    staged[:, : 3 * SLOT] = (tn(x_ref[...], grads_ref[:, : 3 * SLOT]) * factor).astype(BF)
-    staged[:, 3 * SLOT :] = (tn(up_ref[...], grads_ref[:, 3 * SLOT :]) * factor).astype(BF)
-    for k in range(n):
-        for target, at in ((keep_ref, image), (give_ref, 1 - image)):
+    staged[:, : 3 * SLOT] = (tn(x_full[...], grads[:, : 3 * SLOT]) * factor).astype(BF)
+    staged[:, 3 * SLOT :] = (tn(up_full[...], grads[:, 3 * SLOT :]) * factor).astype(BF)
+    for k in range(n):
+        for target, at in ((w_keep_ref, image), (w_give_ref, 1 - image)):
             first = pl.multiple_of(((me ^ k) * 2 + at) * share, 16)
             target[k] = staged[pl.ds(first, share), :]
 
@@ -181,16 +175,13 @@
     ).astype(BF)
 
 
-def join_kernel(mine_ref, theirs_ref, out_ref):
+def join_kernel(n, mine_ref, theirs_ref, *refs):
+    parts, (input_ref, out_ref, staged) = refs[:n], refs[n:]
+    me = lax.axis_index("seq")
     core = lax.axis_index("pipe")
     half = mine_ref.shape[0]
-    out_ref[pl.ds(pl.multiple_of(core * half, half), half), :] = mine_ref[...]
-    out_ref[pl.ds(pl.multiple_of((1 - core) * half, half), half), :] = theirs_ref[...]
-
-
-def unpack_kernel(n, *refs):
-    parts, out_ref, staged = refs[:n], refs[n], refs[n + 1]
-    me = lax.axis_index("seq")
+    input_ref[pl.ds(pl.multiple_of(core * half, half), half), :] = mine_ref[...]
+    input_ref[pl.ds(pl.multiple_of((1 - core) * half, half), half), :] = theirs_ref[...]
     for k in range(n):
         staged[me ^ k] = parts[k][...]
     for head in range(n):
@@ -200,18 +191,21 @@
             ].astype(F32)
 
 
-def call(kernel, out_shape, args, scratch=(), specs=None):
+def call(kernel, out_shape, args, scratch=(), plain=0, out_space=pltpu.VMEM):
     single = not isinstance(out_shape, list)
     shapes = [out_shape] if single else out_shape
+    args = list(args[:plain]) + [
+        pltpu.with_memory_space_constraint(a, pltpu.VMEM) for a in args[plain:]
+    ]
     out = pl.pallas_call(
         kernel,
-        out_shape=[jax.ShapeDtypeStruct(*s) for s in shapes],
-        in_specs=[VMEM_SPEC] * len(args) if specs is None else specs,
+        out_shape=[out_space(*s) for s in shapes],
+        in_specs=[VMEM_SPEC] * len(args),
         out_specs=[VMEM_SPEC] * len(shapes),
         scratch_shapes=list(scratch),
         compiler_params=PARAMS,
     )(*args)
-    return out[0] if single else out
+    return out[0] if single else list(out)
 
 
 def local_heads(embeddings, upstream, attn_weights):
@@ -229,75 +223,65 @@
     def swap(value, axis):
         return lax.ppermute(value, axis, [(0, 1), (1, 0)])
 
-    def near(values):
-        return [pltpu.with_memory_space_constraint(v, pltpu.VMEM) for v in values]
 
     chunks = call(
         functools.partial(pack_kernel, n),
         [((share, 2 * SLOT), BF)] * n,
         (attn_weights,),
         [pltpu.VMEM((2, n, share, 2 * SLOT), BF)],
+        plain=1,
     )
     arrived = [across(chunks[k], k) for k in range(1, n)]
     send, rest = call(
-        norm_kernel, [((rows, width), BF)] * 2, (x, up), [pltpu.VMEM((rows, width), BF)]
+        norm_kernel, [((rows, width), BF)] * 2, (x, up), [pltpu.VMEM((rows, width), BF)], plain=2
     )
     send, *arrived = lax.optimization_barrier((send, *arrived))
-    merged = call(merge_kernel, ((n * share, 2 * SLOT), BF), (chunks[0], *near(arrived)))
+    merged = call(merge_kernel, ((n * share, 2 * SLOT), BF), (chunks[0], *arrived))
     beside = swap(merged, "dp")
     above = swap(merged, "grp")
-    corner = swap(above, "dp")
-
     second = across(send, 2)
     first = across(send, 1)
-    later, second = lax.optimization_barrier((send, second))
+    later, second, beside, above = lax.optimization_barrier((send, second, beside, above))
+    corner = swap(above, "dp")
     middle = lax.ppermute(later, "seq", [(1, 2), (2, 1)])
     passed = lax.ppermute(second, "seq", [(2, 3), (1, 0)])
     third = jnp.where((me == 0) | (me == n - 1), passed, middle)
     got = [send, first, second, third]
     swapped = [rest] + [swap(g, "pipe") for g in got[1:]]
-    args = (*got[:1], *near(got[1:]), rest, *near(swapped[1:]), merged, *near((beside, above, corner)))
-    keep, give, grads, x_full, up_full = call(
-        functools.partial(head_kernel, n),
-        [
-            ((n, half, width), BF),
-            ((n, half, width), BF),
-            ((patches, 4 * SLOT), BF),
-            ((patches, width), BF),
-            ((patches, width), BF),
-        ],
+    args = (*got, *swapped, merged, beside, above, corner)
+    factor = 1.0 / math.sqrt(patches * lax.axis_size("dp"))
+    keep, give, w_keep, w_give = call(
+        functools.partial(head_kernel, n, factor),
+        [((n, half, width), BF)] * 2 + [((n, share, 4 * SLOT), BF)] * 2,
         args,
         [
+            pltpu.VMEM((patches, width), BF),
+            pltpu.VMEM((patches, width), BF),
+            pltpu.VMEM((width, 4 * SLOT), BF),
+            pltpu.VMEM((patches, 4 * SLOT), BF),
             pltpu.VMEM((width, 4 * SLOT), BF),
             pltpu.VMEM((patches, SLOT), F32),
             pltpu.VMEM((patches, SLOT), F32),
             pltpu.SemaphoreType.DMA((n, 2, 2)),
             pltpu.SemaphoreType.DMA((4, n)),
         ],
-        [ANY_SPEC] * len(args),
     )
     taken = swap(give, "pipe")
-    sums = call(functools.partial(sum_kernel, n), [((half, width), BF)] * n, (keep, *near([taken])))
-    parts = [sums[0]] + [across(sums[k], k) for k in range(1, n)]
-    factor = 1.0 / math.sqrt(patches * lax.axis_size("dp"))
-    w_keep, w_give = call(
-        functools.partial(weight_kernel, n, factor),
-        [((n, share, 4 * SLOT), BF)] * 2,
-        (x_full, up_full, grads),
-        [pltpu.VMEM((width, 4 * SLOT), BF)],
-    )
     w_taken = swap(w_give, "dp")
+    sums = call(functools.partial(sum_kernel, n), [((half, width), BF)] * n, (keep, taken))
+    parts = [across(sums[k], k) for k in range(1, n)]
+    w_taken, sums[0] = lax.optimization_barrier((w_taken, sums[0]))
     w_sums = call(
-        functools.partial(sum_kernel, n), [((share, 4 * SLOT), BF)] * n, (w_keep, *near([w_taken]))
+        functools.partial(sum_kernel, n), [((share, 4 * SLOT), BF)] * n, (w_keep, w_taken)
     )
     w_parts = [w_sums[0]] + [across(w_sums[k], k) for k in range(1, n)]
-    mine = call(functools.partial(final_kernel, n), ((half, width), BF), (x, up, parts[0], *near(parts[1:])))
-    input_gradient = call(join_kernel, ((rows, width), BF), (mine, *near([swap(mine, "pipe")])))
-    weight_grads = call(
-        functools.partial(unpack_kernel, n),
-        ((4, share, n * HD), F32),
-        (w_parts[0], *near(w_parts[1:])),
+    mine = call(functools.partial(final_kernel, n), ((half, width), BF), (x, up, sums[0], *parts), plain=2)
+    input_gradient, weight_grads = call(
+        functools.partial(join_kernel, n),
+        [((rows, width), BF), ((4, share, n * HD), F32)],
+        (mine, swap(mine, "pipe"), *w_parts),
         [pltpu.VMEM((n, share, 4 * SLOT), BF)],
+        out_space=jax.ShapeDtypeStruct,
     )
     return (input_gradient[None], weight_grads)
 

time: 126 us -> 112 us (0.89)
  Pallas kernels: 33.7 us -> 16.1 us
  local copies, waits for them, and re-layouts: 0 us -> 3.17 us
    pallas_call x10 -> x8, Pallas kernels: 33.7 us -> 16.1 us  [call(): pl.pallas_call(kernel, out_shape=[out_space(*s) for s in shapes], in_spec...]
    unnamed x0 -> x10, local copies, waits for them, and re-layouts: none -> 3.17 us
    ppermute x11, waiting for transfers between devices: 34.8 us -> 32.9 us  [across(): return lax.ppermute(value, 'seq', [(i, i ^ k) for i in range(n)])]
  transfers between devices with their start and end apart: 22 -> 22, of which waited for: 11 -> 13; matrix products, arithmetic and copies ran while one was open for 0% -> 0% of each run, Pallas kernels for 14% -> 1%
where the time goes in v3:
time: 112 us
  waiting for transfers between devices  66.7 us (60%)
  starting transfers between devices  25.2 us (22%)
  Pallas kernels  16.1 us (14%)
  local copies, waits for them, and re-layouts  3.17 us (3%)
    ppermute x11, waiting for transfers between devices, across(): return lax.ppermute(value, 'seq', [(i, i ^ k) for i in range(n)])  32.9 us
    ppermute x9, waiting for transfers between devices, swap(): return lax.ppermute(value, axis, [(0, 1), (1, 0)])  27.2 us
    pallas_call x8, Pallas kernels, call(): pl.pallas_call(kernel, out_shape=[out_space(*s) for s in shapes], in_spec...  16.1 us
    ppermute x11, starting transfers between devices, across(): return lax.ppermute(value, 'seq', [(i, i ^ k) for i in range(n)])  13.7 us
    ppermute x1, waiting for transfers between devices, local_heads(): middle = lax.ppermute(later, 'seq', [(1, 2), (2, 1)])  4.74 us
    ppermute x9, starting transfers between devices, swap(): return lax.ppermute(value, axis, [(0, 1), (1, 0)])  4.68 us
    ppermute x1, starting transfers between devices, local_heads(): passed = lax.ppermute(second, 'seq', [(2, 3), (1, 0)])  3.43 us
    ppermute x1, starting transfers between devices, local_heads(): middle = lax.ppermute(later, 'seq', [(1, 2), (2, 1)])  3.4 us
  transfers between devices with their start and end apart: 22, of which 13 were waited for; matrix products, arithmetic and copies ran while one was open for 0% of the time, Pallas kernels for 1%

profile of v3, /device:TPU:8, one launch (start us, length us, event | category | flops | bytes accessed | tf_op | source)
XLA Modules:
  0.0 112.0 jit_solution(9273011180000109654)
XLA Ops:
  0.6 1.1 %copy-done.4 = bf16[4,208,416]{2,1,0:T(8,128)(2,1)S(1)} copy-done((bf16[4,208,416]{2,1,0:T(8,128)(2,1)S(1)}, bf16[4,208,416]{2,1,0:T(8,128)(2,1)}, u32[]{:S(2)}) %copy-start.4) | copy-done | bytes 692248
  1.8 0.4 shard_map.51
  2.2 0.1 collective-permute-start
  2.3 3.0 %collective-permute-start.1 = (bf16[208,256]{1,0:T(8,128)(2,1)S(1)}, bf16[208,256]{1,0:T(8,128)(2,1)S(1)}, u32[]{:S(2)}, u32[]{:S(2)}) collective-permute-start(bf16[208,256]{1,0:T(8,128)(2,1)S(1)} %get-tuple-element.34), channel_id=1, source_target_pairs={{0,8},{4,12},{8,0},{12,4},{1,9},{5,13},{9,1},{13,5},{2,10},{6,14},... | collective-permute-start | bytes 319496 | tf_op jit(solution)/shard_map/ppermute | solution.py:221
  5.3 0.5 collective-permute-start.2
  5.8 1.0 copy-done
  6.8 1.0 copy-done.2
  7.8 0.3 shard_map.50
  8.2 4.8 %collective-permute-done.1.refs_2_ = bf16[208,256]{1,0:T(8,128)(2,1)S(1)} collective-permute-done((bf16[208,256]{1,0:T(8,128)(2,1)S(1)}, bf16[208,256]{1,0:T(8,128)(2,1)S(1)}, u32[]{:S(2)}, u32[]{:S(2)}) %collective-permute-start.1) | collective-permute-done | bytes 106528 | tf_op jit(solution)/shard_map/ppermute | solution.py:221
  13.0 2.0 %collective-permute-done.2.refs_3_ = bf16[208,256]{1,0:T(8,128)(2,1)S(1)} collective-permute-done((bf16[208,256]{1,0:T(8,128)(2,1)S(1)}, bf16[208,256]{1,0:T(8,128)(2,1)S(1)}, u32[]{:S(2)}, u32[]{:S(2)}) %collective-permute-start.2) | collective-permute-done | bytes 106528 | tf_op jit(solution)/shard_map/ppermute | solution.py:221
  15.1 1.6 %collective-permute-start.6 = (bf16[832,256]{1,0:T(8,128)(2,1)S(1)}, bf16[832,256]{1,0:T(8,128)(2,1)S(1)}, u32[]{:S(2)}, u32[]{:S(2)}) collective-permute-start(bf16[832,256]{1,0:T(8,128)(2,1)S(1)} %shard_map.52.refs_8_), channel_id=1, source_target_pairs={{0,16},{16,0},{1,17},{17,1},{2,18},{18,2},{3,19},{19,3},{4,20},{20... | collective-permute-start | bytes 1277960 | tf_op jit(solution)/shard_map/ppermute | solution.py:224
  16.7 1.5 %collective-permute-start.5 = (bf16[832,256]{1,0:T(8,128)(2,1)S(1)}, bf16[832,256]{1,0:T(8,128)(2,1)S(1)}, u32[]{:S(2)}, u32[]{:S(2)}) collective-permute-start(bf16[832,256]{1,0:T(8,128)(2,1)S(1)} %shard_map.52.refs_8_), channel_id=1, source_target_pairs={{0,2},{2,0},{1,3},{3,1},{4,6},{6,4},{5,7},{7,5},{8,10},{10,8},{9,1... | collective-permute-start | bytes 1277960 | tf_op jit(solution)/shard_map/ppermute | solution.py:224
  18.1 1.3 %collective-permute-start.4 = (bf16[128,1664]{1,0:T(8,128)(2,1)S(1)}, bf16[128,1664]{1,0:T(8,128)(2,1)S(1)}, u32[]{:S(2)}, u32[]{:S(2)}) collective-permute-start(bf16[128,1664]{1,0:T(8,128)(2,1)S(1)} %get-tuple-element.42.refs_0_), channel_id=1, source_target_pairs={{0,8},{4,12},{8,0},{12,4},{1,9},{5,13},{9,1},{13,5},{2,10},{6,14},... | collective-permute-start | bytes 1277960 | tf_op jit(solution)/shard_map/ppermute | solution.py:221
  19.5 1.7 %collective-permute-start.3 = (bf16[128,1664]{1,0:T(8,128)(2,1)S(1)}, bf16[128,1664]{1,0:T(8,128)(2,1)S(1)}, u32[]{:S(2)}, u32[]{:S(2)}) collective-permute-start(bf16[128,1664]{1,0:T(8,128)(2,1)S(1)} %get-tuple-element.42.refs_0_), channel_id=1, source_target_pairs={{0,4},{4,0},{8,12},{12,8},{1,5},{5,1},{9,13},{13,9},{2,6},{6,2},{1... | collective-permute-start | bytes 1277960 | tf_op jit(solution)/shard_map/ppermute | solution.py:221
  21.2 4.2 %collective-permute-done.6.refs_10_ = bf16[832,256]{1,0:T(8,128)(2,1)S(1)} collective-permute-done((bf16[832,256]{1,0:T(8,128)(2,1)S(1)}, bf16[832,256]{1,0:T(8,128)(2,1)S(1)}, u32[]{:S(2)}, u32[]{:S(2)}) %collective-permute-start.6) | collective-permute-done | bytes 426016 | tf_op jit(solution)/shard_map/ppermute | solution.py:224
  25.4 1.3 %collective-permute-done.5.refs_9_ = bf16[832,256]{1,0:T(8,128)(2,1)S(1)} collective-permute-done((bf16[832,256]{1,0:T(8,128)(2,1)S(1)}, bf16[832,256]{1,0:T(8,128)(2,1)S(1)}, u32[]{:S(2)}, u32[]{:S(2)}) %collective-permute-start.5) | collective-permute-done | bytes 426016 | tf_op jit(solution)/shard_map/ppermute | solution.py:224
  26.7 8.3 %collective-permute-done.4.refs_2_ = bf16[128,1664]{1,0:T(8,128)(2,1)S(1)} collective-permute-done((bf16[128,1664]{1,0:T(8,128)(2,1)S(1)}, bf16[128,1664]{1,0:T(8,128)(2,1)S(1)}, u32[]{:S(2)}, u32[]{:S(2)}) %collective-permute-start.4) | collective-permute-done | bytes 426016 | tf_op jit(solution)/shard_map/ppermute | solution.py:221
  35.0 3.4 %collective-permute-start.8 = (bf16[128,1664]{1,0:T(8,128)(2,1)S(1)}, bf16[128,1664]{1,0:T(8,128)(2,1)S(1)}, u32[]{:S(2)}, u32[]{:S(2)}) collective-permute-start(bf16[128,1664]{1,0:T(8,128)(2,1)S(1)} %get-tuple-element.42.refs_0_), channel_id=1, source_target_pairs={{4,8},{8,4},{5,9},{9,5},{6,10},{10,6},{7,11},{11,7},{20,24},{24,20... | collective-permute-start | bytes 1277960 | tf_op jit(solution)/shard_map/ppermute | solution.py:246
  38.4 3.4 %collective-permute-start.7 = (bf16[128,1664]{1,0:T(8,128)(2,1)S(1)}, bf16[128,1664]{1,0:T(8,128)(2,1)}, u32[]{:S(2)}, u32[]{:S(2)}) collective-permute-start(bf16[128,1664]{1,0:T(8,128)(2,1)S(1)} %collective-permute-done.4.refs_2_), channel_id=1, source_target_pairs={{8,12},{4,0},{9,13},{5,1},{10,14},{6,2},{11,15},{7,3},{24,28},{20,... | collective-permute-start | bytes 1277960 | tf_op jit(solution)/shard_map/ppermute | solution.py:247
  41.9 0.5 collective-permute-start.12
  42.4 0.2 collective-permute-start.9
  42.6 4.7 %collective-permute-done.8 = bf16[128,1664]{1,0:T(8,128)(2,1)S(1)} collective-permute-done((bf16[128,1664]{1,0:T(8,128)(2,1)S(1)}, bf16[128,1664]{1,0:T(8,128)(2,1)S(1)}, u32[]{:S(2)}, u32[]{:S(2)}) %collective-permute-start.8) | collective-permute-done | bytes 426016 | tf_op jit(solution)/shard_map/ppermute | solution.py:246
  47.4 1.9 %collective-permute-done.7 = bf16[128,1664]{1,0:T(8,128)(2,1)} collective-permute-done((bf16[128,1664]{1,0:T(8,128)(2,1)S(1)}, bf16[128,1664]{1,0:T(8,128)(2,1)}, u32[]{:S(2)}, u32[]{:S(2)}) %collective-permute-start.7) | collective-permute-done | bytes 426016 | tf_op jit(solution)/shard_map/ppermute | solution.py:247
  49.2 0.1 broadcast_select_fusion.refs_3_
  49.3 0.1 collective-permute-start.11
  49.4 4.7 %collective-permute-done.12.refs_11_ = bf16[832,256]{1,0:T(8,128)(2,1)S(1)} collective-permute-done((bf16[832,256]{1,0:T(8,128)(2,1)S(1)}, bf16[832,256]{1,0:T(8,128)(2,1)S(1)}, u32[]{:S(2)}, u32[]{:S(2)}) %collective-permute-start.12) | collective-permute-done | bytes 426016 | tf_op jit(solution)/shard_map/ppermute | solution.py:224
  54.1 0.0 collective-permute-done.9.refs_5_
  54.1 0.0 collective-permute-done.11.refs_7_
  54.1 12.8 %shard_map.53 = (bf16[4,64,1664]{2,1,0:T(8,128)(2,1)S(1)}, bf16[4,64,1664]{2,1,0:T(8,128)(2,1)S(1)}, bf16[4,208,512]{2,1,0:T(8,128)(2,1)S(1)}, bf16[4,208,512]{2,1,0:T(8,128)(2,1)S(1)}) custom-call(bf16[128,1664]{1,0:T(8,128)(2,1)S(1)} %get-tuple-element.42.refs_0_, bf16[128,1664]{1,0:T(8,128)(2,1)S(1)} %collective-permute-done.3.refs_1_, ...), custom_call_target="tpu_custom_call" | custom-call | tf_op jit(solution)/shard_map/pallas_call | solution.py:200
  66.9 0.1 collective-permute-start.14
  67.0 0.6 collective-permute-start.13
  67.6 1.8 %collective-permute-done.14.theirs_ref = bf16[4,64,1664]{2,1,0:T(8,128)(2,1)S(1)} collective-permute-done((bf16[4,64,1664]{2,1,0:T(8,128)(2,1)S(1)}, bf16[4,64,1664]{2,1,0:T(8,128)(2,1)S(1)}, u32[]{:S(2)}, u32[]{:S(2)}) %collective-permute-start.14) | collective-permute-done | bytes 852000 | tf_op jit(solution)/shard_map/ppermute | solution.py:224
  69.4 0.2 shard_map.54
  69.6 0.6 collective-permute-start.15
  70.2 1.3 %collective-permute-start.16 = (bf16[64,1664]{1,0:T(8,128)(2,1)S(1)}, bf16[64,1664]{1,0:T(8,128)(2,1)S(1)}, u32[]{:S(2)}, u32[]{:S(2)}) collective-permute-start(bf16[64,1664]{1,0:T(8,128)(2,1)S(1)} %get-tuple-element.52), channel_id=1, source_target_pairs={{0,8},{4,12},{8,0},{12,4},{1,9},{5,13},{9,1},{13,5},{2,10},{6,14},... | collective-permute-start | bytes 638984 | tf_op jit(solution)/shard_map/ppermute | solution.py:221
  71.6 1.6 %collective-permute-start.17 = (bf16[64,1664]{1,0:T(8,128)(2,1)S(1)}, bf16[64,1664]{1,0:T(8,128)(2,1)S(1)}, u32[]{:S(2)}, u32[]{:S(2)}) collective-permute-start(bf16[64,1664]{1,0:T(8,128)(2,1)S(1)} %get-tuple-element.53), channel_id=1, source_target_pairs={{0,12},{4,8},{8,4},{12,0},{1,13},{5,9},{9,5},{13,1},{2,14},{6,10},... | collective-permute-start | bytes 638984 | tf_op jit(solution)/shard_map/ppermute | solution.py:221
  73.1 15.2 %collective-permute-done.13.theirs_ref = bf16[4,208,512]{2,1,0:T(8,128)(2,1)S(1)} collective-permute-done((bf16[4,208,512]{2,1,0:T(8,128)(2,1)S(1)}, bf16[4,208,512]{2,1,0:T(8,128)(2,1)S(1)}, u32[]{:S(2)}, u32[]{:S(2)}) %collective-permute-start.13) | collective-permute-done | bytes 852000 | tf_op jit(solution)/shard_map/ppermute | solution.py:224
  88.4 0.2 shard_map.56
  88.6 0.6 collective-permute-start.19
  89.2 1.4 %collective-permute-start.20 = (bf16[208,512]{1,0:T(8,128)(2,1)S(1)}, bf16[208,512]{1,0:T(8,128)(2,1)S(1)}, u32[]{:S(2)}, u32[]{:S(2)}) collective-permute-start(bf16[208,512]{1,0:T(8,128)(2,1)S(1)} %get-tuple-element.58), channel_id=1, source_target_pairs={{0,8},{4,12},{8,0},{12,4},{1,9},{5,13},{9,1},{13,5},{2,10},{6,14},... | collective-permute-start | bytes 638984 | tf_op jit(solution)/shard_map/ppermute | solution.py:221
  90.6 0.0 collective-permute-done.15.refs_1_
  90.6 1.6 %collective-permute-start.21 = (bf16[208,512]{1,0:T(8,128)(2,1)S(1)}, bf16[208,512]{1,0:T(8,128)(2,1)S(1)}, u32[]{:S(2)}, u32[]{:S(2)}) collective-permute-start(bf16[208,512]{1,0:T(8,128)(2,1)S(1)} %get-tuple-element.59), channel_id=1, source_target_pairs={{0,12},{4,8},{8,4},{12,0},{1,13},{5,9},{9,5},{13,1},{2,14},{6,10},... | collective-permute-start | bytes 638984 | tf_op jit(solution)/shard_map/ppermute | solution.py:221
  92.1 0.5 shard_map.55.mine_ref
  92.6 0.1 collective-permute-start.18
  92.7 4.1 %collective-permute-done.19.refs_1_ = bf16[208,512]{1,0:T(8,128)(2,1)S(1)} collective-permute-done((bf16[208,512]{1,0:T(8,128)(2,1)S(1)}, bf16[208,512]{1,0:T(8,128)(2,1)S(1)}, u32[]{:S(2)}, u32[]{:S(2)}) %collective-permute-start.19) | collective-permute-done | bytes 213024 | tf_op jit(solution)/shard_map/ppermute | solution.py:221
  96.8 8.6 %collective-permute-done.20.refs_2_ = bf16[208,512]{1,0:T(8,128)(2,1)S(1)} collective-permute-done((bf16[208,512]{1,0:T(8,128)(2,1)S(1)}, bf16[208,512]{1,0:T(8,128)(2,1)S(1)}, u32[]{:S(2)}, u32[]{:S(2)}) %collective-permute-start.20) | collective-permute-done | bytes 213024 | tf_op jit(solution)/shard_map/ppermute | solution.py:221
  105.4 5.0 %collective-permute-done.21.refs_3_ = bf16[208,512]{1,0:T(8,128)(2,1)S(1)} collective-permute-done((bf16[208,512]{1,0:T(8,128)(2,1)S(1)}, bf16[208,512]{1,0:T(8,128)(2,1)S(1)}, u32[]{:S(2)}, u32[]{:S(2)}) %collective-permute-start.21) | collective-permute-done | bytes 213024 | tf_op jit(solution)/shard_map/ppermute | solution.py:221
  110.4 1.6 %shard_map.57 = (bf16[128,1664]{1,0:T(8,128)(2,1)}, f32[4,208,416]{2,1,0:T(8,128)}) custom-call(bf16[64,1664]{1,0:T(8,128)(2,1)S(1)} %shard_map.55.mine_ref, bf16[64,1664]{1,0:T(8,128)(2,1)S(1)} %collective-permute-done.18.theirs_ref, bf16[208,512]{1,0:T(8,128)(2,1)S(1)} %get-tuple-element.56.refs_0_, bf16[208,512]{1,0:T(8,128)(2,1)S(1)} %collective-permute-done.19.refs_1_, ...), custom_call_target="tpu_custom_call" | custom-call | tf_op jit(solution)/shard_map/pallas_call | solution.py:200
  (15 shorter events, 0.1 us)
Async XLA Ops:
  0.6 1.2 %copy-start.4 = (bf16[4,208,416]{2,1,0:T(8,128)(2,1)S(1)}, bf16[4,208,416]{2,1,0:T(8,128)(2,1)}, u32[]{:S(2)}) copy-start(bf16[4,208,416]{2,1,0:T(8,128)(2,1)} %w_ref.1) | copy-start | bytes 2076676
  2.2 5.9 %collective-permute-start = (bf16[208,256]{1,0:T(8,128)(2,1)S(1)}, bf16[208,256]{1,0:T(8,128)(2,1)S(1)}, u32[]{:S(2)}, u32[]{:S(2)}) collective-permute-start(bf16[208,256]{1,0:T(8,128)(2,1)S(1)} %get-tuple-element.33), channel_id=1, source_target_pairs={{0,4},{4,0},{8,12},{12,8},{1,5},{5,1},{9,13},{13,9},{2,6},{6,2},{1... | collective-permute-start | bytes 319496 | tf_op jit(solution)/shard_map/ppermute | solution.py:221
  2.3 10.7 %collective-permute-start.1 = (bf16[208,256]{1,0:T(8,128)(2,1)S(1)}, bf16[208,256]{1,0:T(8,128)(2,1)S(1)}, u32[]{:S(2)}, u32[]{:S(2)}) collective-permute-start(bf16[208,256]{1,0:T(8,128)(2,1)S(1)} %get-tuple-element.34), channel_id=1, source_target_pairs={{0,8},{4,12},{8,0},{12,4},{1,9},{5,13},{9,1},{13,5},{2,10},{6,14},... | collective-permute-start | bytes 319496 | tf_op jit(solution)/shard_map/ppermute | solution.py:221
  5.3 9.7 %collective-permute-start.2 = (bf16[208,256]{1,0:T(8,128)(2,1)S(1)}, bf16[208,256]{1,0:T(8,128)(2,1)S(1)}, u32[]{:S(2)}, u32[]{:S(2)}) collective-permute-start(bf16[208,256]{1,0:T(8,128)(2,1)S(1)} %get-tuple-element.35), channel_id=1, source_target_pairs={{0,12},{4,8},{8,4},{12,0},{1,13},{5,9},{9,5},{13,1},{2,14},{6,10},... | collective-permute-start | bytes 319496 | tf_op jit(solution)/shard_map/ppermute | solution.py:221
  5.8 1.0 copy-start
  6.8 1.0 copy-start.2
  15.1 10.4 %collective-permute-start.6 = (bf16[832,256]{1,0:T(8,128)(2,1)S(1)}, bf16[832,256]{1,0:T(8,128)(2,1)S(1)}, u32[]{:S(2)}, u32[]{:S(2)}) collective-permute-start(bf16[832,256]{1,0:T(8,128)(2,1)S(1)} %shard_map.52.refs_8_), channel_id=1, source_target_pairs={{0,16},{16,0},{1,17},{17,1},{2,18},{18,2},{3,19},{19,3},{4,20},{20... | collective-permute-start | bytes 1277960 | tf_op jit(solution)/shard_map/ppermute | solution.py:224
  16.7 10.0 %collective-permute-start.5 = (bf16[832,256]{1,0:T(8,128)(2,1)S(1)}, bf16[832,256]{1,0:T(8,128)(2,1)S(1)}, u32[]{:S(2)}, u32[]{:S(2)}) collective-permute-start(bf16[832,256]{1,0:T(8,128)(2,1)S(1)} %shard_map.52.refs_8_), channel_id=1, source_target_pairs={{0,2},{2,0},{1,3},{3,1},{4,6},{6,4},{5,7},{7,5},{8,10},{10,8},{9,1... | collective-permute-start | bytes 1277960 | tf_op jit(solution)/shard_map/ppermute | solution.py:224
  18.1 16.9 %collective-permute-start.4 = (bf16[128,1664]{1,0:T(8,128)(2,1)S(1)}, bf16[128,1664]{1,0:T(8,128)(2,1)S(1)}, u32[]{:S(2)}, u32[]{:S(2)}) collective-permute-start(bf16[128,1664]{1,0:T(8,128)(2,1)S(1)} %get-tuple-element.42.refs_0_), channel_id=1, source_target_pairs={{0,8},{4,12},{8,0},{12,4},{1,9},{5,13},{9,1},{13,5},{2,10},{6,14},... | collective-permute-start | bytes 1277960 | tf_op jit(solution)/shard_map/ppermute | solution.py:221
  19.5 22.9 %collective-permute-start.3 = (bf16[128,1664]{1,0:T(8,128)(2,1)S(1)}, bf16[128,1664]{1,0:T(8,128)(2,1)S(1)}, u32[]{:S(2)}, u32[]{:S(2)}) collective-permute-start(bf16[128,1664]{1,0:T(8,128)(2,1)S(1)} %get-tuple-element.42.refs_0_), channel_id=1, source_target_pairs={{0,4},{4,0},{8,12},{12,8},{1,5},{5,1},{9,13},{13,9},{2,6},{6,2},{1... | collective-permute-start | bytes 1277960 | tf_op jit(solution)/shard_map/ppermute | solution.py:221
  35.0 12.3 %collective-permute-start.8 = (bf16[128,1664]{1,0:T(8,128)(2,1)S(1)}, bf16[128,1664]{1,0:T(8,128)(2,1)S(1)}, u32[]{:S(2)}, u32[]{:S(2)}) collective-permute-start(bf16[128,1664]{1,0:T(8,128)(2,1)S(1)} %get-tuple-element.42.refs_0_), channel_id=1, source_target_pairs={{4,8},{8,4},{5,9},{9,5},{6,10},{10,6},{7,11},{11,7},{20,24},{24,20... | collective-permute-start | bytes 1277960 | tf_op jit(solution)/shard_map/ppermute | solution.py:246
  38.4 10.8 %collective-permute-start.7 = (bf16[128,1664]{1,0:T(8,128)(2,1)S(1)}, bf16[128,1664]{1,0:T(8,128)(2,1)}, u32[]{:S(2)}, u32[]{:S(2)}) collective-permute-start(bf16[128,1664]{1,0:T(8,128)(2,1)S(1)} %collective-permute-done.4.refs_2_), channel_id=1, source_target_pairs={{8,12},{4,0},{9,13},{5,1},{10,14},{6,2},{11,15},{7,3},{24,28},{20,... | collective-permute-start | bytes 1277960 | tf_op jit(solution)/shard_map/ppermute | solution.py:247
  41.9 12.2 %collective-permute-start.10 = (bf16[128,1664]{1,0:T(8,128)(2,1)S(1)}, bf16[128,1664]{1,0:T(8,128)(2,1)S(1)}, u32[]{:S(2)}, u32[]{:S(2)}) collective-permute-start(bf16[128,1664]{1,0:T(8,128)(2,1)S(1)} %collective-permute-done.4.refs_2_), channel_id=1, source_target_pairs={{0,1},{1,0},{2,3},{3,2},{4,5},{5,4},{6,7},{7,6},{8,9},{9,8},{10,11... | collective-permute-start | bytes 1277960 | tf_op jit(solution)/shard_map/ppermute | solution.py:224
  41.9 12.2 %collective-permute-start.12 = (bf16[832,256]{1,0:T(8,128)(2,1)S(1)}, bf16[832,256]{1,0:T(8,128)(2,1)S(1)}, u32[]{:S(2)}, u32[]{:S(2)}) collective-permute-start(bf16[832,256]{1,0:T(8,128)(2,1)S(1)} %collective-permute-done.6.refs_10_), channel_id=1, source_target_pairs={{0,2},{2,0},{1,3},{3,1},{4,6},{6,4},{5,7},{7,5},{8,10},{10,8},{9,1... | collective-permute-start | bytes 1277960 | tf_op jit(solution)/shard_map/ppermute | solution.py:224
  42.4 11.7 %collective-permute-start.9 = (bf16[128,1664]{1,0:T(8,128)(2,1)S(1)}, bf16[128,1664]{1,0:T(8,128)(2,1)S(1)}, u32[]{:S(2)}, u32[]{:S(2)}) collective-permute-start(bf16[128,1664]{1,0:T(8,128)(2,1)S(1)} %collective-permute-done.3.refs_1_), channel_id=1, source_target_pairs={{0,1},{1,0},{2,3},{3,2},{4,5},{5,4},{6,7},{7,6},{8,9},{9,8},{10,11... | collective-permute-start | bytes 1277960 | tf_op jit(solution)/shard_map/ppermute | solution.py:224
  49.3 4.8 %collective-permute-start.11 = (bf16[128,1664]{1,0:T(8,128)(2,1)S(1)}, bf16[128,1664]{1,0:T(8,128)(2,1)S(1)}, u32[]{:S(2)}, u32[]{:S(2)}) collective-permute-start(bf16[128,1664]{1,0:T(8,128)(2,1)S(1)} %broadcast_select_fusion.refs_3_), channel_id=1, source_target_pairs={{0,1},{1,0},{2,3},{3,2},{4,5},{5,4},{6,7},{7,6},{8,9},{9,8},{10,11... | collective-permute-start | bytes 1277960 | tf_op jit(solution)/shard_map/ppermute | solution.py:224
  66.9 2.4 %collective-permute-start.14 = (bf16[4,64,1664]{2,1,0:T(8,128)(2,1)S(1)}, bf16[4,64,1664]{2,1,0:T(8,128)(2,1)S(1)}, u32[]{:S(2)}, u32[]{:S(2)}) collective-permute-start(bf16[4,64,1664]{2,1,0:T(8,128)(2,1)S(1)} %get-tuple-element.48), channel_id=1, source_target_pairs={{0,1},{1,0},{2,3},{3,2},{4,5},{5,4},{6,7},{7,6},{8,9},{9,8},{10,11... | collective-permute-start | bytes 2555912 | tf_op jit(solution)/shard_map/ppermute | solution.py:224
  67.0 21.4 %collective-permute-start.13 = (bf16[4,208,512]{2,1,0:T(8,128)(2,1)S(1)}, bf16[4,208,512]{2,1,0:T(8,128)(2,1)S(1)}, u32[]{:S(2)}, u32[]{:S(2)}) collective-permute-start(bf16[4,208,512]{2,1,0:T(8,128)(2,1)S(1)} %get-tuple-element.46), channel_id=1, source_target_pairs={{0,2},{2,0},{1,3},{3,1},{4,6},{6,4},{5,7},{7,5},{8,10},{10,8},{9,1... | collective-permute-start | bytes 2555912 | tf_op jit(solution)/shard_map/ppermute | solution.py:224
  69.4 22.8 %copy-start.1 = (bf16[1,128,1664]{2,1,0:T(8,128)(2,1)S(1)}, bf16[1,128,1664]{2,1,0:T(8,128)(2,1)}, u32[]{:S(2)}) copy-start(bf16[1,128,1664]{2,1,0:T(8,128)(2,1)} %param.3) | copy-start | bytes 1277956
  69.4 22.8 %copy-start.3 = (bf16[1,128,1664]{2,1,0:T(8,128)(2,1)S(1)}, bf16[1,128,1664]{2,1,0:T(8,128)(2,1)}, u32[]{:S(2)}) copy-start(bf16[1,128,1664]{2,1,0:T(8,128)(2,1)} %param.4) | copy-start | bytes 1277956
  69.6 21.0 %collective-permute-start.15 = (bf16[64,1664]{1,0:T(8,128)(2,1)S(1)}, bf16[64,1664]{1,0:T(8,128)(2,1)S(1)}, u32[]{:S(2)}, u32[]{:S(2)}) collective-permute-start(bf16[64,1664]{1,0:T(8,128)(2,1)S(1)} %get-tuple-element.51), channel_id=1, source_target_pairs={{0,4},{4,0},{8,12},{12,8},{1,5},{5,1},{9,13},{13,9},{2,6},{6,2},{1... | collective-permute-start | bytes 638984 | tf_op jit(solution)/shard_map/ppermute | solution.py:221
  70.2 21.9 %collective-permute-start.16 = (bf16[64,1664]{1,0:T(8,128)(2,1)S(1)}, bf16[64,1664]{1,0:T(8,128)(2,1)S(1)}, u32[]{:S(2)}, u32[]{:S(2)}) collective-permute-start(bf16[64,1664]{1,0:T(8,128)(2,1)S(1)} %get-tuple-element.52), channel_id=1, source_target_pairs={{0,8},{4,12},{8,0},{12,4},{1,9},{5,13},{9,1},{13,5},{2,10},{6,14},... | collective-permute-start | bytes 638984 | tf_op jit(solution)/shard_map/ppermute | solution.py:221
  71.6 20.6 %collective-permute-start.17 = (bf16[64,1664]{1,0:T(8,128)(2,1)S(1)}, bf16[64,1664]{1,0:T(8,128)(2,1)S(1)}, u32[]{:S(2)}, u32[]{:S(2)}) collective-permute-start(bf16[64,1664]{1,0:T(8,128)(2,1)S(1)} %get-tuple-element.53), channel_id=1, source_target_pairs={{0,12},{4,8},{8,4},{12,0},{1,13},{5,9},{9,5},{13,1},{2,14},{6,10},... | collective-permute-start | bytes 638984 | tf_op jit(solution)/shard_map/ppermute | solution.py:221
  88.6 8.2 %collective-permute-start.19 = (bf16[208,512]{1,0:T(8,128)(2,1)S(1)}, bf16[208,512]{1,0:T(8,128)(2,1)S(1)}, u32[]{:S(2)}, u32[]{:S(2)}) collective-permute-start(bf16[208,512]{1,0:T(8,128)(2,1)S(1)} %get-tuple-element.57), channel_id=1, source_target_pairs={{0,4},{4,0},{8,12},{12,8},{1,5},{5,1},{9,13},{13,9},{2,6},{6,2},{1... | collective-permute-start | bytes 638984 | tf_op jit(solution)/shard_map/ppermute | solution.py:221
  89.2 16.2 %collective-permute-start.20 = (bf16[208,512]{1,0:T(8,128)(2,1)S(1)}, bf16[208,512]{1,0:T(8,128)(2,1)S(1)}, u32[]{:S(2)}, u32[]{:S(2)}) collective-permute-start(bf16[208,512]{1,0:T(8,128)(2,1)S(1)} %get-tuple-element.58), channel_id=1, source_target_pairs={{0,8},{4,12},{8,0},{12,4},{1,9},{5,13},{9,1},{13,5},{2,10},{6,14},... | collective-permute-start | bytes 638984 | tf_op jit(solution)/shard_map/ppermute | solution.py:221
  90.6 19.8 %collective-permute-start.21 = (bf16[208,512]{1,0:T(8,128)(2,1)S(1)}, bf16[208,512]{1,0:T(8,128)(2,1)S(1)}, u32[]{:S(2)}, u32[]{:S(2)}) collective-permute-start(bf16[208,512]{1,0:T(8,128)(2,1)S(1)} %get-tuple-element.59), channel_id=1, source_target_pairs={{0,12},{4,8},{8,4},{12,0},{1,13},{5,9},{9,5},{13,1},{2,14},{6,10},... | collective-permute-start | bytes 638984 | tf_op jit(solution)/shard_map/ppermute | solution.py:221
  92.6 17.8 %collective-permute-start.18 = (bf16[64,1664]{1,0:T(8,128)(2,1)S(1)}, bf16[64,1664]{1,0:T(8,128)(2,1)S(1)}, u32[]{:S(2)}, u32[]{:S(2)}) collective-permute-start(bf16[64,1664]{1,0:T(8,128)(2,1)S(1)} %shard_map.55.mine_ref), channel_id=1, source_target_pairs={{0,1},{1,0},{2,3},{3,2},{4,5},{5,4},{6,7},{7,6},{8,9},{9,8},{10,11... | collective-permute-start | bytes 638984 | tf_op jit(solution)/shard_map/ppermute | solution.py:224

commit v4 on v3

--- a/solution.py
+++ b/solution.py
@@ -73,45 +73,43 @@
 
 
 def head_kernel(n, factor, *refs):
-    got, swapped = refs[:n], refs[n : 2 * n]
-    pieces = refs[2 * n : 2 * n + 4]
-    keep_ref, give_ref, w_keep_ref, w_give_ref = refs[2 * n + 4 : 2 * n + 8]
-    x_full, up_full, w_full, grads, staged, term_k, term_v, sems, wsems = refs[2 * n + 8 :]
+    blocks = [(refs[2 * k], refs[2 * k + 1]) for k in range(n + 1)]
+    pieces = refs[2 * n + 2 : 2 * n + 6]
+    keep_ref, give_ref, w_keep_ref, w_give_ref = refs[2 * n + 6 : 2 * n + 10]
+    x_full, up_full, w_full, grads, staged, term_k, term_v = refs[2 * n + 10 :]
     me = lax.axis_index("seq")
     image = lax.axis_index("dp")
     group = lax.axis_index("grp")
-    rows = got[0].shape[0]
+    rows = blocks[0][0].shape[0]
     half = rows // 2
     share = pieces[0].shape[0] // n
 
-    copies = []
     for which, source in enumerate(pieces):
         at = 1 - image if which % 2 else image
         mats = 1 - group if which // 2 else group
         for k in range(n):
             first = pl.multiple_of(((me ^ k) * 2 + at) * share, 16)
             lanes = pl.multiple_of(mats * 2 * SLOT, 2 * SLOT)
-            copies.append(
-                pltpu.make_async_copy(
-                    source.at[pl.ds(k * share, share), :],
-                    w_full.at[pl.ds(first, share), pl.ds(lanes, 2 * SLOT)],
-                    wsems.at[which, k],
-                )
-            )
-    for k in range(n):
-        for side, source in enumerate((got[k], swapped[k])):
-            for which, target in enumerate((x_full, up_full)):
-                copies.append(
-                    pltpu.make_async_copy(
-                        source.at[pl.ds(which * half, half), :],
-                        target.at[pl.ds(k * rows + side * half, half), :],
-                        sems.at[k, side, which],
-                    )
-                )
-    for copy in copies:
-        copy.start()
-    for copy in copies:
-        copy.wait()
+            w_full[pl.ds(first, share), pl.ds(lanes, 2 * SLOT)] = source[
+                k * share : (k + 1) * share, :
+            ]
+
+    def place(k, sides):
+        for side, source in enumerate(sides):
+            span = slice(k * rows + side * half, k * rows + (side + 1) * half)
+            x_full[span, :] = source[:half, :]
+            up_full[span, :] = source[half:, :]
+
+    for k in range(n - 1):
+        place(k, blocks[k])
+
+    @pl.when((me == 0) | (me == n - 1))
+    def _():
+        place(n - 1, blocks[n])
+
+    @pl.when((me != 0) & (me != n - 1))
+    def _():
+        place(n - 1, blocks[n - 1])
 
     scale = HD ** (-0.5)
     qkv = nn(x_full[...], w_full[:, : 3 * SLOT]).astype(BF)
@@ -235,7 +233,6 @@
     send, rest = call(
         norm_kernel, [((rows, width), BF)] * 2, (x, up), [pltpu.VMEM((rows, width), BF)], plain=2
     )
-    send, *arrived = lax.optimization_barrier((send, *arrived))
     merged = call(merge_kernel, ((n * share, 2 * SLOT), BF), (chunks[0], *arrived))
     beside = swap(merged, "dp")
     above = swap(merged, "grp")
@@ -245,10 +242,10 @@
     corner = swap(above, "dp")
     middle = lax.ppermute(later, "seq", [(1, 2), (2, 1)])
     passed = lax.ppermute(second, "seq", [(2, 3), (1, 0)])
-    third = jnp.where((me == 0) | (me == n - 1), passed, middle)
-    got = [send, first, second, third]
-    swapped = [rest] + [swap(g, "pipe") for g in got[1:]]
-    args = (*got, *swapped, merged, beside, above, corner)
+    args = [send, rest]
+    for block in (first, second, middle, passed):
+        args += [block, swap(block, "pipe")]
+    args += [merged, beside, above, corner]
     factor = 1.0 / math.sqrt(patches * lax.axis_size("dp"))
     keep, give, w_keep, w_give = call(
         functools.partial(head_kernel, n, factor),
@@ -262,8 +259,6 @@
             pltpu.VMEM((width, 4 * SLOT), BF),
             pltpu.VMEM((patches, SLOT), F32),
             pltpu.VMEM((patches, SLOT), F32),
-            pltpu.SemaphoreType.DMA((n, 2, 2)),
-            pltpu.SemaphoreType.DMA((4, n)),
         ],
     )
     taken = swap(give, "pipe")

time: 112 us -> 108 us (0.964)
  Pallas kernels: 16.1 us -> 11 us
  starting transfers between devices: 25.2 us -> 27 us
  waiting for transfers between devices: 66.7 us -> 65.5 us
    ppermute x9 -> x10, waiting for transfers between devices: 27.2 us -> 22 us  [swap(): return lax.ppermute(value, axis, [(0, 1), (1, 0)])]
    pallas_call x8, Pallas kernels: 16.1 us -> 11 us  [call(): pl.pallas_call(kernel, out_shape=[out_space(*s) for s in shapes], in_spec...]
    ppermute x11, waiting for transfers between devices: 32.9 us -> 36.4 us  [across(): return lax.ppermute(value, 'seq', [(i, i ^ k) for i in range(n)])]
    ppermute x1, waiting for transfers between devices: 1.87 us -> 4.69 us  [local_heads(): passed = lax.ppermute(second, 'seq', [(2, 3), (1, 0)])]
    ppermute x1, waiting for transfers between devices: 4.74 us -> 2.32 us  [local_heads(): middle = lax.ppermute(later, 'seq', [(1, 2), (2, 1)])]
    ppermute x9 -> x10, starting transfers between devices: 4.68 us -> 6.8 us  [swap(): return lax.ppermute(value, axis, [(0, 1), (1, 0)])]
    ppermute x1, starting transfers between devices: 3.43 us -> 1.32 us  [local_heads(): passed = lax.ppermute(second, 'seq', [(2, 3), (1, 0)])]
    ppermute x11, starting transfers between devices: 13.7 us -> 15.4 us  [across(): return lax.ppermute(value, 'seq', [(i, i ^ k) for i in range(n)])]
  transfers between devices with their start and end apart: 22 -> 23, of which waited for: 13 -> 14; matrix products, arithmetic and copies ran while one was open for 0% -> 0% of each run, Pallas kernels for 1% -> 1%
where the time goes in v4:
time: 108 us; the launch traced here: 107 us
  waiting for transfers between devices  65.5 us (61%)
  starting transfers between devices  27 us (25%)
  Pallas kernels  11 us (10%)
  local copies, waits for them, and re-layouts  3.17 us (3%)
    ppermute x11, waiting for transfers between devices, across(): return lax.ppermute(value, 'seq', [(i, i ^ k) for i in range(n)])  36.4 us
    ppermute x10, waiting for transfers between devices, swap(): return lax.ppermute(value, axis, [(0, 1), (1, 0)])  22 us
    ppermute x11, starting transfers between devices, across(): return lax.ppermute(value, 'seq', [(i, i ^ k) for i in range(n)])  15.4 us
    pallas_call x8, Pallas kernels, call(): pl.pallas_call(kernel, out_shape=[out_space(*s) for s in shapes], in_spec...  11 us
    ppermute x10, starting transfers between devices, swap(): return lax.ppermute(value, axis, [(0, 1), (1, 0)])  6.8 us
    ppermute x1, waiting for transfers between devices, local_heads(): passed = lax.ppermute(second, 'seq', [(2, 3), (1, 0)])  4.69 us
    ppermute x1, starting transfers between devices, local_heads(): middle = lax.ppermute(later, 'seq', [(1, 2), (2, 1)])  3.56 us
    unnamed x10, local copies, waits for them, and re-layouts  3.17 us
  transfers between devices with their start and end apart: 23, of which 14 were waited for; matrix products, arithmetic and copies ran while one was open for 0% of the time, Pallas kernels for 1%

profile of v4, /device:TPU:8, one launch (start us, length us, event | category | flops | bytes accessed | tf_op | source)
XLA Modules:
  0.0 107.4 jit_solution(5969373282808433180)
XLA Ops:
  0.6 1.1 %copy-done.4 = bf16[4,208,416]{2,1,0:T(8,128)(2,1)S(1)} copy-done((bf16[4,208,416]{2,1,0:T(8,128)(2,1)S(1)}, bf16[4,208,416]{2,1,0:T(8,128)(2,1)}, u32[]{:S(2)}) %copy-start.4) | copy-done | bytes 692248
  1.8 0.4 shard_map.51
  2.2 0.1 collective-permute-start.3
  2.3 3.0 %collective-permute-start.4 = (bf16[208,256]{1,0:T(8,128)(2,1)S(1)}, bf16[208,256]{1,0:T(8,128)(2,1)S(1)}, u32[]{:S(2)}, u32[]{:S(2)}) collective-permute-start(bf16[208,256]{1,0:T(8,128)(2,1)S(1)} %get-tuple-element.32), channel_id=1, source_target_pairs={{0,8},{4,12},{8,0},{12,4},{1,9},{5,13},{9,1},{13,5},{2,10},{6,14},... | collective-permute-start | bytes 319496 | tf_op jit(solution)/shard_map/ppermute | solution.py:219
  5.3 0.5 collective-permute-start.5
  5.8 1.0 copy-done
  6.8 1.0 copy-done.2
  7.8 0.3 shard_map.50
  8.1 3.6 %collective-permute-start.2 = (bf16[128,1664]{1,0:T(8,128)(2,1)S(1)}, bf16[128,1664]{1,0:T(8,128)(2,1)S(1)}, u32[]{:S(2)}, u32[]{:S(2)}) collective-permute-start(bf16[128,1664]{1,0:T(8,128)(2,1)S(1)} %get-tuple-element.35.refs_0_), channel_id=1, source_target_pairs={{0,8},{4,12},{8,0},{12,4},{1,9},{5,13},{9,1},{13,5},{2,10},{6,14},... | collective-permute-start | bytes 1277960 | tf_op jit(solution)/shard_map/ppermute | solution.py:219
  11.7 0.0 collective-permute-done.3.refs_1_
  11.7 10.4 %collective-permute-done.4.refs_2_ = bf16[208,256]{1,0:T(8,128)(2,1)S(1)} collective-permute-done((bf16[208,256]{1,0:T(8,128)(2,1)S(1)}, bf16[208,256]{1,0:T(8,128)(2,1)S(1)}, u32[]{:S(2)}, u32[]{:S(2)}) %collective-permute-start.4) | collective-permute-done | bytes 106528 | tf_op jit(solution)/shard_map/ppermute | solution.py:219
  22.1 3.3 %collective-permute-done.5.refs_3_ = bf16[208,256]{1,0:T(8,128)(2,1)S(1)} collective-permute-done((bf16[208,256]{1,0:T(8,128)(2,1)S(1)}, bf16[208,256]{1,0:T(8,128)(2,1)S(1)}, u32[]{:S(2)}, u32[]{:S(2)}) %collective-permute-start.5) | collective-permute-done | bytes 106528 | tf_op jit(solution)/shard_map/ppermute | solution.py:219
  25.4 1.6 %collective-permute-start.7 = (bf16[832,256]{1,0:T(8,128)(2,1)S(1)}, bf16[832,256]{1,0:T(8,128)(2,1)S(1)}, u32[]{:S(2)}, u32[]{:S(2)}) collective-permute-start(bf16[832,256]{1,0:T(8,128)(2,1)S(1)} %shard_map.52.refs_10_), channel_id=1, source_target_pairs={{0,16},{16,0},{1,17},{17,1},{2,18},{18,2},{3,19},{19,3},{4,20},{20... | collective-permute-start | bytes 1277960 | tf_op jit(solution)/shard_map/ppermute | solution.py:222
  27.0 1.5 %collective-permute-start.6 = (bf16[832,256]{1,0:T(8,128)(2,1)S(1)}, bf16[832,256]{1,0:T(8,128)(2,1)S(1)}, u32[]{:S(2)}, u32[]{:S(2)}) collective-permute-start(bf16[832,256]{1,0:T(8,128)(2,1)S(1)} %shard_map.52.refs_10_), channel_id=1, source_target_pairs={{0,2},{2,0},{1,3},{3,1},{4,6},{6,4},{5,7},{7,5},{8,10},{10,8},{9,1... | collective-permute-start | bytes 1277960 | tf_op jit(solution)/shard_map/ppermute | solution.py:222
  28.5 0.0 collective-permute-start
  28.5 3.9 %collective-permute-done.2.refs_4_ = bf16[128,1664]{1,0:T(8,128)(2,1)S(1)} collective-permute-done((bf16[128,1664]{1,0:T(8,128)(2,1)S(1)}, bf16[128,1664]{1,0:T(8,128)(2,1)S(1)}, u32[]{:S(2)}, u32[]{:S(2)}) %collective-permute-start.2) | collective-permute-done | bytes 426016 | tf_op jit(solution)/shard_map/ppermute | solution.py:219
  32.4 2.1 %collective-permute-done.7.refs_12_ = bf16[832,256]{1,0:T(8,128)(2,1)S(1)} collective-permute-done((bf16[832,256]{1,0:T(8,128)(2,1)S(1)}, bf16[832,256]{1,0:T(8,128)(2,1)S(1)}, u32[]{:S(2)}, u32[]{:S(2)}) %collective-permute-start.7) | collective-permute-done | bytes 426016 | tf_op jit(solution)/shard_map/ppermute | solution.py:222
  34.5 1.3 %collective-permute-done.6.refs_11_ = bf16[832,256]{1,0:T(8,128)(2,1)S(1)} collective-permute-done((bf16[832,256]{1,0:T(8,128)(2,1)S(1)}, bf16[832,256]{1,0:T(8,128)(2,1)S(1)}, u32[]{:S(2)}, u32[]{:S(2)}) %collective-permute-start.6) | collective-permute-done | bytes 426016 | tf_op jit(solution)/shard_map/ppermute | solution.py:222
  35.8 3.6 %collective-permute-start.9 = (bf16[128,1664]{1,0:T(8,128)(2,1)S(1)}, bf16[128,1664]{1,0:T(8,128)(2,1)S(1)}, u32[]{:S(2)}, u32[]{:S(2)}) collective-permute-start(bf16[128,1664]{1,0:T(8,128)(2,1)S(1)} %get-tuple-element.35.refs_0_), channel_id=1, source_target_pairs={{4,8},{8,4},{5,9},{9,5},{6,10},{10,6},{7,11},{11,7},{20,24},{24,20... | collective-permute-start | bytes 1277960 | tf_op jit(solution)/shard_map/ppermute | solution.py:243
  39.4 1.3 %collective-permute-start.11 = (bf16[128,1664]{1,0:T(8,128)(2,1)S(1)}, bf16[128,1664]{1,0:T(8,128)(2,1)S(1)}, u32[]{:S(2)}, u32[]{:S(2)}) collective-permute-start(bf16[128,1664]{1,0:T(8,128)(2,1)S(1)} %collective-permute-done.2.refs_4_), channel_id=1, source_target_pairs={{8,12},{4,0},{9,13},{5,1},{10,14},{6,2},{11,15},{7,3},{24,28},{20,... | collective-permute-start | bytes 1277960 | tf_op jit(solution)/shard_map/ppermute | solution.py:244
  40.7 0.8 collective-permute-done.refs_2_
  41.5 0.5 collective-permute-start.8
  42.0 1.5 %collective-permute-start.13 = (bf16[832,256]{1,0:T(8,128)(2,1)S(1)}, bf16[832,256]{1,0:T(8,128)(2,1)S(1)}, u32[]{:S(2)}, u32[]{:S(2)}) collective-permute-start(bf16[832,256]{1,0:T(8,128)(2,1)S(1)} %collective-permute-done.7.refs_12_), channel_id=1, source_target_pairs={{0,2},{2,0},{1,3},{3,1},{4,6},{6,4},{5,7},{7,5},{8,10},{10,8},{9,1... | collective-permute-start | bytes 1277960 | tf_op jit(solution)/shard_map/ppermute | solution.py:222
  43.5 2.3 %collective-permute-done.9.refs_6_ = bf16[128,1664]{1,0:T(8,128)(2,1)S(1)} collective-permute-done((bf16[128,1664]{1,0:T(8,128)(2,1)S(1)}, bf16[128,1664]{1,0:T(8,128)(2,1)S(1)}, u32[]{:S(2)}, u32[]{:S(2)}) %collective-permute-start.9) | collective-permute-done | bytes 426016 | tf_op jit(solution)/shard_map/ppermute | solution.py:243
  45.8 0.0 collective-permute-start.10
  45.8 4.7 %collective-permute-done.11.refs_8_ = bf16[128,1664]{1,0:T(8,128)(2,1)S(1)} collective-permute-done((bf16[128,1664]{1,0:T(8,128)(2,1)S(1)}, bf16[128,1664]{1,0:T(8,128)(2,1)S(1)}, u32[]{:S(2)}, u32[]{:S(2)}) %collective-permute-start.11) | collective-permute-done | bytes 426016 | tf_op jit(solution)/shard_map/ppermute | solution.py:244
  50.5 0.0 collective-permute-start.12
  50.5 3.2 %collective-permute-done.13.refs_13_ = bf16[832,256]{1,0:T(8,128)(2,1)S(1)} collective-permute-done((bf16[832,256]{1,0:T(8,128)(2,1)S(1)}, bf16[832,256]{1,0:T(8,128)(2,1)S(1)}, u32[]{:S(2)}, u32[]{:S(2)}) %collective-permute-start.13) | collective-permute-done | bytes 426016 | tf_op jit(solution)/shard_map/ppermute | solution.py:222
  53.7 7.7 %shard_map.53 = (bf16[4,64,1664]{2,1,0:T(8,128)(2,1)S(1)}, bf16[4,64,1664]{2,1,0:T(8,128)(2,1)S(1)}, bf16[4,208,512]{2,1,0:T(8,128)(2,1)S(1)}, bf16[4,208,512]{2,1,0:T(8,128)(2,1)S(1)}) custom-call(bf16[128,1664]{1,0:T(8,128)(2,1)S(1)} %get-tuple-element.35.refs_0_, bf16[128,1664]{1,0:T(8,128)(2,1)S(1)} %get-tuple-element.29.refs_1_, ...), custom_call_target="tpu_custom_call" | custom-call | tf_op jit(solution)/shard_map/pallas_call | solution.py:198
  61.5 0.1 collective-permute-start.15
  61.6 1.6 %collective-permute-start.14 = (bf16[4,208,512]{2,1,0:T(8,128)(2,1)S(1)}, bf16[4,208,512]{2,1,0:T(8,128)(2,1)S(1)}, u32[]{:S(2)}, u32[]{:S(2)}) collective-permute-start(bf16[4,208,512]{2,1,0:T(8,128)(2,1)S(1)} %get-tuple-element.38), channel_id=1, source_target_pairs={{0,2},{2,0},{1,3},{3,1},{4,6},{6,4},{5,7},{7,5},{8,10},{10,8},{9,1... | collective-permute-start | bytes 2555912 | tf_op jit(solution)/shard_map/ppermute | solution.py:222
  63.1 0.8 collective-permute-done.15.theirs_ref
  63.9 0.2 shard_map.54
  64.1 2.5 %collective-permute-start.16 = (bf16[64,1664]{1,0:T(8,128)(2,1)S(1)}, bf16[64,1664]{1,0:T(8,128)(2,1)S(1)}, u32[]{:S(2)}, u32[]{:S(2)}) collective-permute-start(bf16[64,1664]{1,0:T(8,128)(2,1)S(1)} %get-tuple-element.43), channel_id=1, source_target_pairs={{0,4},{4,0},{8,12},{12,8},{1,5},{5,1},{9,13},{13,9},{2,6},{6,2},{1... | collective-permute-start | bytes 638984 | tf_op jit(solution)/shard_map/ppermute | solution.py:219
  66.7 1.1 %collective-permute-start.17 = (bf16[64,1664]{1,0:T(8,128)(2,1)S(1)}, bf16[64,1664]{1,0:T(8,128)(2,1)S(1)}, u32[]{:S(2)}, u32[]{:S(2)}) collective-permute-start(bf16[64,1664]{1,0:T(8,128)(2,1)S(1)} %get-tuple-element.44), channel_id=1, source_target_pairs={{0,8},{4,12},{8,0},{12,4},{1,9},{5,13},{9,1},{13,5},{2,10},{6,14},... | collective-permute-start | bytes 638984 | tf_op jit(solution)/shard_map/ppermute | solution.py:219
  67.8 0.5 collective-permute-start.18
  68.3 14.7 %collective-permute-done.14.theirs_ref = bf16[4,208,512]{2,1,0:T(8,128)(2,1)S(1)} collective-permute-done((bf16[4,208,512]{2,1,0:T(8,128)(2,1)S(1)}, bf16[4,208,512]{2,1,0:T(8,128)(2,1)S(1)}, u32[]{:S(2)}, u32[]{:S(2)}) %collective-permute-start.14) | collective-permute-done | bytes 852000 | tf_op jit(solution)/shard_map/ppermute | solution.py:222
  82.9 0.2 shard_map.56
  83.1 2.5 %collective-permute-start.20 = (bf16[208,512]{1,0:T(8,128)(2,1)S(1)}, bf16[208,512]{1,0:T(8,128)(2,1)S(1)}, u32[]{:S(2)}, u32[]{:S(2)}) collective-permute-start(bf16[208,512]{1,0:T(8,128)(2,1)S(1)} %get-tuple-element.49), channel_id=1, source_target_pairs={{0,4},{4,0},{8,12},{12,8},{1,5},{5,1},{9,13},{13,9},{2,6},{6,2},{1... | collective-permute-start | bytes 638984 | tf_op jit(solution)/shard_map/ppermute | solution.py:219
  85.7 1.1 %collective-permute-start.21 = (bf16[208,512]{1,0:T(8,128)(2,1)S(1)}, bf16[208,512]{1,0:T(8,128)(2,1)S(1)}, u32[]{:S(2)}, u32[]{:S(2)}) collective-permute-start(bf16[208,512]{1,0:T(8,128)(2,1)S(1)} %get-tuple-element.50), channel_id=1, source_target_pairs={{0,8},{4,12},{8,0},{12,4},{1,9},{5,13},{9,1},{13,5},{2,10},{6,14},... | collective-permute-start | bytes 638984 | tf_op jit(solution)/shard_map/ppermute | solution.py:219
  86.8 0.5 collective-permute-start.22
  87.3 0.0 collective-permute-done.18.refs_3_
  87.3 0.5 shard_map.55.mine_ref
  87.7 0.1 collective-permute-start.19
  87.8 6.0 %collective-permute-done.20.refs_1_ = bf16[208,512]{1,0:T(8,128)(2,1)S(1)} collective-permute-done((bf16[208,512]{1,0:T(8,128)(2,1)S(1)}, bf16[208,512]{1,0:T(8,128)(2,1)S(1)}, u32[]{:S(2)}, u32[]{:S(2)}) %collective-permute-start.20) | collective-permute-done | bytes 213024 | tf_op jit(solution)/shard_map/ppermute | solution.py:219
  93.8 7.8 %collective-permute-done.21.refs_2_ = bf16[208,512]{1,0:T(8,128)(2,1)S(1)} collective-permute-done((bf16[208,512]{1,0:T(8,128)(2,1)S(1)}, bf16[208,512]{1,0:T(8,128)(2,1)S(1)}, u32[]{:S(2)}, u32[]{:S(2)}) %collective-permute-start.21) | collective-permute-done | bytes 213024 | tf_op jit(solution)/shard_map/ppermute | solution.py:219
  101.6 4.2 %collective-permute-done.22.refs_3_ = bf16[208,512]{1,0:T(8,128)(2,1)S(1)} collective-permute-done((bf16[208,512]{1,0:T(8,128)(2,1)S(1)}, bf16[208,512]{1,0:T(8,128)(2,1)S(1)}, u32[]{:S(2)}, u32[]{:S(2)}) %collective-permute-start.22) | collective-permute-done | bytes 213024 | tf_op jit(solution)/shard_map/ppermute | solution.py:219
  105.8 1.6 %shard_map.57 = (bf16[128,1664]{1,0:T(8,128)(2,1)}, f32[4,208,416]{2,1,0:T(8,128)}) custom-call(bf16[64,1664]{1,0:T(8,128)(2,1)S(1)} %shard_map.55.mine_ref, bf16[64,1664]{1,0:T(8,128)(2,1)S(1)} %collective-permute-done.19.theirs_ref, bf16[208,512]{1,0:T(8,128)(2,1)S(1)} %get-tuple-element.48.refs_0_, bf16[208,512]{1,0:T(8,128)(2,1)S(1)} %collective-permute-done.20.refs_1_, ...), custom_call_target="tpu_custom_call" | custom-call | tf_op jit(solution)/shard_map/pallas_call | solution.py:198
  (16 shorter events, 0.1 us)
Async XLA Ops:
  0.6 1.2 %copy-start.4 = (bf16[4,208,416]{2,1,0:T(8,128)(2,1)S(1)}, bf16[4,208,416]{2,1,0:T(8,128)(2,1)}, u32[]{:S(2)}) copy-start(bf16[4,208,416]{2,1,0:T(8,128)(2,1)} %w_ref.1) | copy-start | bytes 2076676
  2.2 9.5 %collective-permute-start.3 = (bf16[208,256]{1,0:T(8,128)(2,1)S(1)}, bf16[208,256]{1,0:T(8,128)(2,1)S(1)}, u32[]{:S(2)}, u32[]{:S(2)}) collective-permute-start(bf16[208,256]{1,0:T(8,128)(2,1)S(1)} %get-tuple-element.31), channel_id=1, source_target_pairs={{0,4},{4,0},{8,12},{12,8},{1,5},{5,1},{9,13},{13,9},{2,6},{6,2},{1... | collective-permute-start | bytes 319496 | tf_op jit(solution)/shard_map/ppermute | solution.py:219
  2.3 19.8 %collective-permute-start.4 = (bf16[208,256]{1,0:T(8,128)(2,1)S(1)}, bf16[208,256]{1,0:T(8,128)(2,1)S(1)}, u32[]{:S(2)}, u32[]{:S(2)}) collective-permute-start(bf16[208,256]{1,0:T(8,128)(2,1)S(1)} %get-tuple-element.32), channel_id=1, source_target_pairs={{0,8},{4,12},{8,0},{12,4},{1,9},{5,13},{9,1},{13,5},{2,10},{6,14},... | collective-permute-start | bytes 319496 | tf_op jit(solution)/shard_map/ppermute | solution.py:219
  5.3 20.1 %collective-permute-start.5 = (bf16[208,256]{1,0:T(8,128)(2,1)S(1)}, bf16[208,256]{1,0:T(8,128)(2,1)S(1)}, u32[]{:S(2)}, u32[]{:S(2)}) collective-permute-start(bf16[208,256]{1,0:T(8,128)(2,1)S(1)} %get-tuple-element.33), channel_id=1, source_target_pairs={{0,12},{4,8},{8,4},{12,0},{1,13},{5,9},{9,5},{13,1},{2,14},{6,10},... | collective-permute-start | bytes 319496 | tf_op jit(solution)/shard_map/ppermute | solution.py:219
  5.8 1.0 copy-start
  6.8 1.0 copy-start.2
  8.1 24.3 %collective-permute-start.2 = (bf16[128,1664]{1,0:T(8,128)(2,1)S(1)}, bf16[128,1664]{1,0:T(8,128)(2,1)S(1)}, u32[]{:S(2)}, u32[]{:S(2)}) collective-permute-start(bf16[128,1664]{1,0:T(8,128)(2,1)S(1)} %get-tuple-element.35.refs_0_), channel_id=1, source_target_pairs={{0,8},{4,12},{8,0},{12,4},{1,9},{5,13},{9,1},{13,5},{2,10},{6,14},... | collective-permute-start | bytes 1277960 | tf_op jit(solution)/shard_map/ppermute | solution.py:219
  25.4 9.1 %collective-permute-start.7 = (bf16[832,256]{1,0:T(8,128)(2,1)S(1)}, bf16[832,256]{1,0:T(8,128)(2,1)S(1)}, u32[]{:S(2)}, u32[]{:S(2)}) collective-permute-start(bf16[832,256]{1,0:T(8,128)(2,1)S(1)} %shard_map.52.refs_10_), channel_id=1, source_target_pairs={{0,16},{16,0},{1,17},{17,1},{2,18},{18,2},{3,19},{19,3},{4,20},{20... | collective-permute-start | bytes 1277960 | tf_op jit(solution)/shard_map/ppermute | solution.py:222
  27.0 8.8 %collective-permute-start.6 = (bf16[832,256]{1,0:T(8,128)(2,1)S(1)}, bf16[832,256]{1,0:T(8,128)(2,1)S(1)}, u32[]{:S(2)}, u32[]{:S(2)}) collective-permute-start(bf16[832,256]{1,0:T(8,128)(2,1)S(1)} %shard_map.52.refs_10_), channel_id=1, source_target_pairs={{0,2},{2,0},{1,3},{3,1},{4,6},{6,4},{5,7},{7,5},{8,10},{10,8},{9,1... | collective-permute-start | bytes 1277960 | tf_op jit(solution)/shard_map/ppermute | solution.py:222
  28.5 13.0 %collective-permute-start = (bf16[128,1664]{1,0:T(8,128)(2,1)S(1)}, bf16[128,1664]{1,0:T(8,128)(2,1)S(1)}, u32[]{:S(2)}, u32[]{:S(2)}) collective-permute-start(bf16[128,1664]{1,0:T(8,128)(2,1)S(1)} %get-tuple-element.35.refs_0_), channel_id=1, source_target_pairs={{0,4},{4,0},{8,12},{12,8},{1,5},{5,1},{9,13},{13,9},{2,6},{6,2},{1... | collective-permute-start | bytes 1277960 | tf_op jit(solution)/shard_map/ppermute | solution.py:219
  35.8 10.0 %collective-permute-start.9 = (bf16[128,1664]{1,0:T(8,128)(2,1)S(1)}, bf16[128,1664]{1,0:T(8,128)(2,1)S(1)}, u32[]{:S(2)}, u32[]{:S(2)}) collective-permute-start(bf16[128,1664]{1,0:T(8,128)(2,1)S(1)} %get-tuple-element.35.refs_0_), channel_id=1, source_target_pairs={{4,8},{8,4},{5,9},{9,5},{6,10},{10,6},{7,11},{11,7},{20,24},{24,20... | collective-permute-start | bytes 1277960 | tf_op jit(solution)/shard_map/ppermute | solution.py:243
  39.4 11.1 %collective-permute-start.11 = (bf16[128,1664]{1,0:T(8,128)(2,1)S(1)}, bf16[128,1664]{1,0:T(8,128)(2,1)S(1)}, u32[]{:S(2)}, u32[]{:S(2)}) collective-permute-start(bf16[128,1664]{1,0:T(8,128)(2,1)S(1)} %collective-permute-done.2.refs_4_), channel_id=1, source_target_pairs={{8,12},{4,0},{9,13},{5,1},{10,14},{6,2},{11,15},{7,3},{24,28},{20,... | collective-permute-start | bytes 1277960 | tf_op jit(solution)/shard_map/ppermute | solution.py:244
  41.5 9.0 %collective-permute-start.1 = (bf16[128,1664]{1,0:T(8,128)(2,1)S(1)}, bf16[128,1664]{1,0:T(8,128)(2,1)S(1)}, u32[]{:S(2)}, u32[]{:S(2)}) collective-permute-start(bf16[128,1664]{1,0:T(8,128)(2,1)S(1)} %collective-permute-done.refs_2_), channel_id=1, source_target_pairs={{0,1},{1,0},{2,3},{3,2},{4,5},{5,4},{6,7},{7,6},{8,9},{9,8},{10,11... | collective-permute-start | bytes 1277960 | tf_op jit(solution)/shard_map/ppermute | solution.py:222
  41.5 12.2 %collective-permute-start.8 = (bf16[128,1664]{1,0:T(8,128)(2,1)S(1)}, bf16[128,1664]{1,0:T(8,128)(2,1)S(1)}, u32[]{:S(2)}, u32[]{:S(2)}) collective-permute-start(bf16[128,1664]{1,0:T(8,128)(2,1)S(1)} %collective-permute-done.2.refs_4_), channel_id=1, source_target_pairs={{0,1},{1,0},{2,3},{3,2},{4,5},{5,4},{6,7},{7,6},{8,9},{9,8},{10,11... | collective-permute-start | bytes 1277960 | tf_op jit(solution)/shard_map/ppermute | solution.py:222
  42.0 11.7 %collective-permute-start.13 = (bf16[832,256]{1,0:T(8,128)(2,1)S(1)}, bf16[832,256]{1,0:T(8,128)(2,1)S(1)}, u32[]{:S(2)}, u32[]{:S(2)}) collective-permute-start(bf16[832,256]{1,0:T(8,128)(2,1)S(1)} %collective-permute-done.7.refs_12_), channel_id=1, source_target_pairs={{0,2},{2,0},{1,3},{3,1},{4,6},{6,4},{5,7},{7,5},{8,10},{10,8},{9,1... | collective-permute-start | bytes 1277960 | tf_op jit(solution)/shard_map/ppermute | solution.py:222
  45.8 7.9 %collective-permute-start.10 = (bf16[128,1664]{1,0:T(8,128)(2,1)S(1)}, bf16[128,1664]{1,0:T(8,128)(2,1)S(1)}, u32[]{:S(2)}, u32[]{:S(2)}) collective-permute-start(bf16[128,1664]{1,0:T(8,128)(2,1)S(1)} %collective-permute-done.9.refs_6_), channel_id=1, source_target_pairs={{0,1},{1,0},{2,3},{3,2},{4,5},{5,4},{6,7},{7,6},{8,9},{9,8},{10,11... | collective-permute-start | bytes 1277960 | tf_op jit(solution)/shard_map/ppermute | solution.py:222
  50.5 3.2 %collective-permute-start.12 = (bf16[128,1664]{1,0:T(8,128)(2,1)S(1)}, bf16[128,1664]{1,0:T(8,128)(2,1)S(1)}, u32[]{:S(2)}, u32[]{:S(2)}) collective-permute-start(bf16[128,1664]{1,0:T(8,128)(2,1)S(1)} %collective-permute-done.11.refs_8_), channel_id=1, source_target_pairs={{0,1},{1,0},{2,3},{3,2},{4,5},{5,4},{6,7},{7,6},{8,9},{9,8},{10,11... | collective-permute-start | bytes 1277960 | tf_op jit(solution)/shard_map/ppermute | solution.py:222
  61.5 2.4 %collective-permute-start.15 = (bf16[4,64,1664]{2,1,0:T(8,128)(2,1)S(1)}, bf16[4,64,1664]{2,1,0:T(8,128)(2,1)S(1)}, u32[]{:S(2)}, u32[]{:S(2)}) collective-permute-start(bf16[4,64,1664]{2,1,0:T(8,128)(2,1)S(1)} %get-tuple-element.40), channel_id=1, source_target_pairs={{0,1},{1,0},{2,3},{3,2},{4,5},{5,4},{6,7},{7,6},{8,9},{9,8},{10,11... | collective-permute-start | bytes 2555912 | tf_op jit(solution)/shard_map/ppermute | solution.py:222
  61.6 21.4 %collective-permute-start.14 = (bf16[4,208,512]{2,1,0:T(8,128)(2,1)S(1)}, bf16[4,208,512]{2,1,0:T(8,128)(2,1)S(1)}, u32[]{:S(2)}, u32[]{:S(2)}) collective-permute-start(bf16[4,208,512]{2,1,0:T(8,128)(2,1)S(1)} %get-tuple-element.38), channel_id=1, source_target_pairs={{0,2},{2,0},{1,3},{3,1},{4,6},{6,4},{5,7},{7,5},{8,10},{10,8},{9,1... | collective-permute-start | bytes 2555912 | tf_op jit(solution)/shard_map/ppermute | solution.py:222
  63.9 23.3 %copy-start.1 = (bf16[1,128,1664]{2,1,0:T(8,128)(2,1)S(1)}, bf16[1,128,1664]{2,1,0:T(8,128)(2,1)}, u32[]{:S(2)}) copy-start(bf16[1,128,1664]{2,1,0:T(8,128)(2,1)} %param.3) | copy-start | bytes 1277956
  63.9 23.3 %copy-start.3 = (bf16[1,128,1664]{2,1,0:T(8,128)(2,1)S(1)}, bf16[1,128,1664]{2,1,0:T(8,128)(2,1)}, u32[]{:S(2)}) copy-start(bf16[1,128,1664]{2,1,0:T(8,128)(2,1)} %param.4) | copy-start | bytes 1277956
  64.1 22.6 %collective-permute-start.16 = (bf16[64,1664]{1,0:T(8,128)(2,1)S(1)}, bf16[64,1664]{1,0:T(8,128)(2,1)S(1)}, u32[]{:S(2)}, u32[]{:S(2)}) collective-permute-start(bf16[64,1664]{1,0:T(8,128)(2,1)S(1)} %get-tuple-element.43), channel_id=1, source_target_pairs={{0,4},{4,0},{8,12},{12,8},{1,5},{5,1},{9,13},{13,9},{2,6},{6,2},{1... | collective-permute-start | bytes 638984 | tf_op jit(solution)/shard_map/ppermute | solution.py:219
  66.7 20.6 %collective-permute-start.17 = (bf16[64,1664]{1,0:T(8,128)(2,1)S(1)}, bf16[64,1664]{1,0:T(8,128)(2,1)S(1)}, u32[]{:S(2)}, u32[]{:S(2)}) collective-permute-start(bf16[64,1664]{1,0:T(8,128)(2,1)S(1)} %get-tuple-element.44), channel_id=1, source_target_pairs={{0,8},{4,12},{8,0},{12,4},{1,9},{5,13},{9,1},{13,5},{2,10},{6,14},... | collective-permute-start | bytes 638984 | tf_op jit(solution)/shard_map/ppermute | solution.py:219
  67.8 19.5 %collective-permute-start.18 = (bf16[64,1664]{1,0:T(8,128)(2,1)S(1)}, bf16[64,1664]{1,0:T(8,128)(2,1)S(1)}, u32[]{:S(2)}, u32[]{:S(2)}) collective-permute-start(bf16[64,1664]{1,0:T(8,128)(2,1)S(1)} %get-tuple-element.45), channel_id=1, source_target_pairs={{0,12},{4,8},{8,4},{12,0},{1,13},{5,9},{9,5},{13,1},{2,14},{6,10},... | collective-permute-start | bytes 638984 | tf_op jit(solution)/shard_map/ppermute | solution.py:219
  83.1 10.7 %collective-permute-start.20 = (bf16[208,512]{1,0:T(8,128)(2,1)S(1)}, bf16[208,512]{1,0:T(8,128)(2,1)S(1)}, u32[]{:S(2)}, u32[]{:S(2)}) collective-permute-start(bf16[208,512]{1,0:T(8,128)(2,1)S(1)} %get-tuple-element.49), channel_id=1, source_target_pairs={{0,4},{4,0},{8,12},{12,8},{1,5},{5,1},{9,13},{13,9},{2,6},{6,2},{1... | collective-permute-start | bytes 638984 | tf_op jit(solution)/shard_map/ppermute | solution.py:219
  85.7 15.9 %collective-permute-start.21 = (bf16[208,512]{1,0:T(8,128)(2,1)S(1)}, bf16[208,512]{1,0:T(8,128)(2,1)S(1)}, u32[]{:S(2)}, u32[]{:S(2)}) collective-permute-start(bf16[208,512]{1,0:T(8,128)(2,1)S(1)} %get-tuple-element.50), channel_id=1, source_target_pairs={{0,8},{4,12},{8,0},{12,4},{1,9},{5,13},{9,1},{13,5},{2,10},{6,14},... | collective-permute-start | bytes 638984 | tf_op jit(solution)/shard_map/ppermute | solution.py:219
  86.8 19.0 %collective-permute-start.22 = (bf16[208,512]{1,0:T(8,128)(2,1)S(1)}, bf16[208,512]{1,0:T(8,128)(2,1)S(1)}, u32[]{:S(2)}, u32[]{:S(2)}) collective-permute-start(bf16[208,512]{1,0:T(8,128)(2,1)S(1)} %get-tuple-element.51), channel_id=1, source_target_pairs={{0,12},{4,8},{8,4},{12,0},{1,13},{5,9},{9,5},{13,1},{2,14},{6,10},... | collective-permute-start | bytes 638984 | tf_op jit(solution)/shard_map/ppermute | solution.py:219
  87.7 18.1 %collective-permute-start.19 = (bf16[64,1664]{1,0:T(8,128)(2,1)S(1)}, bf16[64,1664]{1,0:T(8,128)(2,1)S(1)}, u32[]{:S(2)}, u32[]{:S(2)}) collective-permute-start(bf16[64,1664]{1,0:T(8,128)(2,1)S(1)} %shard_map.55.mine_ref), channel_id=1, source_target_pairs={{0,1},{1,0},{2,3},{3,2},{4,5},{5,4},{6,7},{7,6},{8,9},{9,8},{10,11... | collective-permute-start | bytes 638984 | tf_op jit(solution)/shard_map/ppermute | solution.py:222

commit v5 on v4

--- a/solution.py
+++ b/solution.py
@@ -39,21 +39,75 @@
     return jnp.dot(a, b, preferred_element_type=F32)
 
 
+SPARE = SLOT - HD
+LEFT = HD - 3 * SPARE
+FOLD = SLOT // LEFT
+
+
+def packed_rows(share):
+    group = -(-share // (16 * FOLD)) * 16
+    return 3 * share + group
+
+
+def half_rows(share):
+    return -(-packed_rows(share) // 32) * 16
+
+
+def packed(mats):
+    last = mats[3]
+    share = last.shape[0]
+    group = packed_rows(share) - 3 * share
+    tiles = [
+        jnp.concatenate([mats[j], last[:, j * SPARE : (j + 1) * SPARE]], axis=1) for j in range(3)
+    ]
+    tail = last[:, 3 * SPARE :]
+    fill = jnp.zeros((FOLD * group - share, LEFT), BF)
+    columns = [tail[j * group : (j + 1) * group] for j in range(FOLD - 1)]
+    columns.append(jnp.concatenate([tail[(FOLD - 1) * group :], fill], axis=0))
+    return tiles + [jnp.concatenate(columns, axis=1)]
+
+
+def unpacked(ref, share):
+    tiles = [ref[j * share : (j + 1) * share, :] for j in range(3)]
+    rest = ref[3 * share :, :]
+    group = rest.shape[0]
+    columns = [rest[:, j * LEFT : (j + 1) * LEFT] for j in range(FOLD)]
+    columns[-1] = columns[-1][: share - (FOLD - 1) * group]
+    last = [tile[:, HD:] for tile in tiles] + [jnp.concatenate(columns, axis=0)]
+    return [tile[:, :HD] for tile in tiles] + [jnp.concatenate(last, axis=1)]
+
+
 def pack_kernel(n, w_ref, *refs):
     outs, staged = refs[:n], refs[n]
     me = lax.axis_index("seq")
     group = lax.axis_index("grp")
-    rows = w_ref.shape[1]
-    fill = jnp.zeros((rows, SLOT - HD), BF)
+    share = w_ref.shape[1]
+    count = outs[0].shape[0]
     for head in range(n):
-        for mat in range(4):
-            block = w_ref[mat, :, head * HD : (head + 1) * HD]
-            first = (mat % 2) * SLOT
-            staged[mat // 2, head, :, first : first + SLOT] = jnp.concatenate(
-                [block, fill], axis=1
-            )
+        mats = [w_ref[mat, :, head * HD : (head + 1) * HD] for mat in range(4)]
+        for j, tile in enumerate(packed(mats)):
+            staged[head, j * share : j * share + tile.shape[0], :] = tile
+    first = pl.multiple_of(group * (staged.shape[1] - count), 16)
     for k in range(n):
-        outs[k][...] = staged[group, me ^ k]
+        outs[k][...] = staged[me ^ k, pl.ds(first, count), :]
+
+
+def weights_kernel(n, share, *refs):
+    pieces, w_ref, staged = refs[:4], refs[4], refs[5]
+    me = lax.axis_index("seq")
+    image = lax.axis_index("dp")
+    group = lax.axis_index("grp")
+    count = pieces[0].shape[0] // n
+    fill = jnp.zeros((share, SPARE), BF)
+    for k in range(n):
+        for other in range(2):
+            for piece, at in ((pieces[other], group), (pieces[2 + other], 1 - group)):
+                first = pl.multiple_of(at * (staged.shape[1] - count), 16)
+                staged[2 * k + other, pl.ds(first, count), :] = piece[k * count : (k + 1) * count]
+            at = 1 - image if other else image
+            span = pl.ds(pl.multiple_of(((me ^ k) * 2 + at) * share, 16), share)
+            for mat, block in enumerate(unpacked(staged.at[2 * k + other], share)):
+                w_ref[span, mat * SLOT : (mat + 1) * SLOT] = jnp.concatenate([block, fill], axis=1)
 
 
 def norm_kernel(x_ref, up_ref, send_ref, rest_ref, staged):
@@ -74,25 +128,13 @@
 
 def head_kernel(n, factor, *refs):
     blocks = [(refs[2 * k], refs[2 * k + 1]) for k in range(n + 1)]
-    pieces = refs[2 * n + 2 : 2 * n + 6]
-    keep_ref, give_ref, w_keep_ref, w_give_ref = refs[2 * n + 6 : 2 * n + 10]
-    x_full, up_full, w_full, grads, staged, term_k, term_v = refs[2 * n + 10 :]
+    w_full, keep_ref, give_ref, w_keep_ref, w_give_ref = refs[2 * n + 2 : 2 * n + 7]
+    x_full, up_full, grads, staged, term_k, term_v = refs[2 * n + 7 :]
     me = lax.axis_index("seq")
     image = lax.axis_index("dp")
-    group = lax.axis_index("grp")
     rows = blocks[0][0].shape[0]
     half = rows // 2
-    share = pieces[0].shape[0] // n
-
-    for which, source in enumerate(pieces):
-        at = 1 - image if which % 2 else image
-        mats = 1 - group if which // 2 else group
-        for k in range(n):
-            first = pl.multiple_of(((me ^ k) * 2 + at) * share, 16)
-            lanes = pl.multiple_of(mats * 2 * SLOT, 2 * SLOT)
-            w_full[pl.ds(first, share), pl.ds(lanes, 2 * SLOT)] = source[
-                k * share : (k + 1) * share, :
-            ]
+    share = w_full.shape[0] // (2 * n)
 
     def place(k, sides):
         for side, source in enumerate(sides):
@@ -149,7 +191,11 @@
     for k in range(n):
         for target, at in ((w_keep_ref, image), (w_give_ref, 1 - image)):
             first = pl.multiple_of(((me ^ k) * 2 + at) * share, 16)
-            target[k] = staged[pl.ds(first, share), :]
+            mats = [
+                staged[pl.ds(first, share), mat * SLOT : mat * SLOT + HD] for mat in range(4)
+            ]
+            for j, tile in enumerate(packed(mats)):
+                target[k, j * share : j * share + tile.shape[0], :] = tile
 
 
 def sum_kernel(n, mine_ref, theirs_ref, *outs):
@@ -158,8 +204,8 @@
 
 
 def final_kernel(n, x_ref, up_ref, *refs):
-    parts, out_ref = refs[:n], refs[n]
-    half = out_ref.shape[0]
+    parts, (out_ref, rest_ref) = refs[:n], refs[n:]
+    half = 2 * out_ref.shape[0]
     core = lax.axis_index("pipe")
     span = pl.ds(pl.multiple_of(core * half, half), half)
     total = parts[0][...].astype(F32)
@@ -168,25 +214,27 @@
     xhat, inverse_deviation = standardize(x_ref[span, :].astype(F32))
     leading = jnp.mean(total, axis=1, keepdims=True)
     trailing = jnp.mean(total * xhat, axis=1, keepdims=True)
-    out_ref[...] = (
+    result = (
         up_ref[span, :].astype(F32) + inverse_deviation * (total - leading - xhat * trailing)
     ).astype(BF)
-
-
-def join_kernel(n, mine_ref, theirs_ref, *refs):
-    parts, (input_ref, out_ref, staged) = refs[:n], refs[n:]
+    out_ref[...] = result[: half // 2]
+    rest_ref[...] = result[half // 2 :]
+
+
+def join_kernel(n, *refs):
+    pairs, parts, (input_ref, out_ref, staged) = refs[:4], refs[4 : 4 + n], refs[4 + n :]
     me = lax.axis_index("seq")
     core = lax.axis_index("pipe")
-    half = mine_ref.shape[0]
-    input_ref[pl.ds(pl.multiple_of(core * half, half), half), :] = mine_ref[...]
-    input_ref[pl.ds(pl.multiple_of((1 - core) * half, half), half), :] = theirs_ref[...]
+    count = pairs[0].shape[0]
+    for i, ref in enumerate(pairs):
+        side = core if i < 2 else 1 - core
+        first = pl.multiple_of((2 * side + i % 2) * count, count)
+        input_ref[pl.ds(first, count), :] = ref[...]
     for k in range(n):
         staged[me ^ k] = parts[k][...]
     for head in range(n):
-        for mat in range(4):
-            out_ref[mat, :, head * HD : (head + 1) * HD] = staged[
-                head, :, mat * SLOT : mat * SLOT + HD
-            ].astype(F32)
+        for mat, block in enumerate(unpacked(staged.at[head], out_ref.shape[1])):
+            out_ref[mat, :, head * HD : (head + 1) * HD] = block.astype(F32)
 
 
 def call(kernel, out_shape, args, scratch=(), plain=0, out_space=pltpu.VMEM):
@@ -222,39 +270,49 @@
         return lax.ppermute(value, axis, [(0, 1), (1, 0)])
 
 
+    full, count = packed_rows(share), half_rows(share)
     chunks = call(
         functools.partial(pack_kernel, n),
-        [((share, 2 * SLOT), BF)] * n,
+        [((count, SLOT), BF)] * n,
         (attn_weights,),
-        [pltpu.VMEM((2, n, share, 2 * SLOT), BF)],
+        [pltpu.VMEM((n, full, SLOT), BF)],
         plain=1,
     )
     arrived = [across(chunks[k], k) for k in range(1, n)]
     send, rest = call(
         norm_kernel, [((rows, width), BF)] * 2, (x, up), [pltpu.VMEM((rows, width), BF)], plain=2
     )
-    merged = call(merge_kernel, ((n * share, 2 * SLOT), BF), (chunks[0], *arrived))
+    send, arrived[0] = lax.optimization_barrier((send, arrived[0]))
+    merged = call(merge_kernel, ((n * count, SLOT), BF), (chunks[0], *arrived))
     beside = swap(merged, "dp")
     above = swap(merged, "grp")
     second = across(send, 2)
     first = across(send, 1)
-    later, second, beside, above = lax.optimization_barrier((send, second, beside, above))
+    later, first, second, beside, above = lax.optimization_barrier(
+        (send, first, second, beside, above)
+    )
     corner = swap(above, "dp")
+    weights = call(
+        functools.partial(weights_kernel, n, share),
+        ((width, 4 * SLOT), BF),
+        (merged, beside, above, corner),
+        [pltpu.VMEM((2 * n, full, SLOT), BF)],
+    )
     middle = lax.ppermute(later, "seq", [(1, 2), (2, 1)])
     passed = lax.ppermute(second, "seq", [(2, 3), (1, 0)])
+    weights, middle, passed = lax.optimization_barrier((weights, middle, passed))
     args = [send, rest]
     for block in (first, second, middle, passed):
         args += [block, swap(block, "pipe")]
-    args += [merged, beside, above, corner]
+    args.append(weights)
     factor = 1.0 / math.sqrt(patches * lax.axis_size("dp"))
     keep, give, w_keep, w_give = call(
         functools.partial(head_kernel, n, factor),
-        [((n, half, width), BF)] * 2 + [((n, share, 4 * SLOT), BF)] * 2,
+        [((n, half, width), BF)] * 2 + [((n, full, SLOT), BF)] * 2,
         args,
         [
             pltpu.VMEM((patches, width), BF),
             pltpu.VMEM((patches, width), BF),
-            pltpu.VMEM((width, 4 * SLOT), BF),
             pltpu.VMEM((patches, 4 * SLOT), BF),
             pltpu.VMEM((width, 4 * SLOT), BF),
             pltpu.VMEM((patches, SLOT), F32),
@@ -267,15 +325,20 @@
     parts = [across(sums[k], k) for k in range(1, n)]
     w_taken, sums[0] = lax.optimization_barrier((w_taken, sums[0]))
     w_sums = call(
-        functools.partial(sum_kernel, n), [((share, 4 * SLOT), BF)] * n, (w_keep, w_taken)
+        functools.partial(sum_kernel, n), [((full, SLOT), BF)] * n, (w_keep, w_taken)
     )
     w_parts = [w_sums[0]] + [across(w_sums[k], k) for k in range(1, n)]
-    mine = call(functools.partial(final_kernel, n), ((half, width), BF), (x, up, sums[0], *parts), plain=2)
+    mine = call(
+        functools.partial(final_kernel, n),
+        [((half // 2, width), BF)] * 2,
+        (x, up, sums[0], *parts),
+        plain=2,
+    )
     input_gradient, weight_grads = call(
         functools.partial(join_kernel, n),
         [((rows, width), BF), ((4, share, n * HD), F32)],
-        (mine, swap(mine, "pipe"), *w_parts),
-        [pltpu.VMEM((n, share, 4 * SLOT), BF)],
+        (*mine, *[swap(m, "pipe") for m in mine], *w_parts),
+        [pltpu.VMEM((n, full, SLOT), BF)],
         out_space=jax.ShapeDtypeStruct,
     )
     return (input_gradient[None], weight_grads)

time: 108 us -> 99 us (0.917)
  waiting for transfers between devices: 65.5 us -> 55.2 us
  Pallas kernels: 11 us -> 12.4 us
    ppermute x11, waiting for transfers between devices: 36.4 us -> 29.1 us  [across(): return lax.ppermute(value, 'seq', [(i, i ^ k) for i in range(n)])]
    ppermute x1, waiting for transfers between devices: 4.69 us -> 0.01 us  [local_heads(): passed = lax.ppermute(second, 'seq', [(2, 3), (1, 0)])]
    ppermute x10 -> x11, waiting for transfers between devices: 22 us -> 26 us  [swap(): return lax.ppermute(value, axis, [(0, 1), (1, 0)])]
    ppermute x1, waiting for transfers between devices: 2.32 us -> 0.01 us  [local_heads(): middle = lax.ppermute(later, 'seq', [(1, 2), (2, 1)])]
    pallas_call x8 -> x9, Pallas kernels: 11 us -> 12.4 us  [call(): pl.pallas_call(kernel, out_shape=[out_space(*s) for s in shapes], in_spec...]
    ppermute x10 -> x11, starting transfers between devices: 6.8 us -> 7.99 us  [swap(): return lax.ppermute(value, axis, [(0, 1), (1, 0)])]
    ppermute x11, starting transfers between devices: 15.4 us -> 14.2 us  [across(): return lax.ppermute(value, 'seq', [(i, i ^ k) for i in range(n)])]
  transfers between devices with their start and end apart: 23 -> 24, of which waited for: 14 -> 12; matrix products, arithmetic and copies ran while one was open for 0% -> 0% of each run, Pallas kernels for 1% -> 2%
where the time goes in v5:
time: 99 us; the launch traced here: 98.7 us
  waiting for transfers between devices  55.2 us (56%)
  starting transfers between devices  27.2 us (27%)
  Pallas kernels  12.4 us (13%)
  local copies, waits for them, and re-layouts  3.18 us (3%)
    ppermute x11, waiting for transfers between devices, across(): return lax.ppermute(value, 'seq', [(i, i ^ k) for i in range(n)])  29.1 us
    ppermute x11, waiting for transfers between devices, swap(): return lax.ppermute(value, axis, [(0, 1), (1, 0)])  26 us
    ppermute x11, starting transfers between devices, across(): return lax.ppermute(value, 'seq', [(i, i ^ k) for i in range(n)])  14.2 us
    pallas_call x9, Pallas kernels, call(): pl.pallas_call(kernel, out_shape=[out_space(*s) for s in shapes], in_spec...  12.4 us
    ppermute x11, starting transfers between devices, swap(): return lax.ppermute(value, axis, [(0, 1), (1, 0)])  7.99 us
    ppermute x1, starting transfers between devices, local_heads(): middle = lax.ppermute(later, 'seq', [(1, 2), (2, 1)])  3.66 us
    unnamed x10, local copies, waits for them, and re-layouts  3.18 us
  transfers between devices with their start and end apart: 24, of which 12 were waited for; matrix products, arithmetic and copies ran while one was open for 0% of the time, Pallas kernels for 2%

profile of v5, /device:TPU:8, one launch (start us, length us, event | category | flops | bytes accessed | tf_op | source)
XLA Modules:
  0.0 98.7 jit_solution(1930608615250176173)
XLA Ops:
  0.6 1.1 %copy-done.4 = bf16[4,208,416]{2,1,0:T(8,128)(2,1)S(1)} copy-done((bf16[4,208,416]{2,1,0:T(8,128)(2,1)S(1)}, bf16[4,208,416]{2,1,0:T(8,128)(2,1)}, u32[]{:S(2)}) %copy-start.4) | copy-done | bytes 692248
  1.8 0.6 shard_map.51
  2.4 0.1 collective-permute-start
  2.4 3.0 %collective-permute-start.3 = (bf16[352,128]{1,0:T(8,128)(2,1)S(1)}, bf16[352,128]{1,0:T(8,128)(2,1)S(1)}, u32[]{:S(2)}, u32[]{:S(2)}) collective-permute-start(bf16[352,128]{1,0:T(8,128)(2,1)S(1)} %get-tuple-element.42), channel_id=1, source_target_pairs={{0,8},{4,12},{8,0},{12,4},{1,9},{5,13},{9,1},{13,5},{2,10},{6,14},... | collective-permute-start | bytes 270344 | tf_op jit(solution)/shard_map/ppermute | solution.py:267
  5.5 0.5 collective-permute-start.4
  5.9 1.0 %copy-done = bf16[1,128,1664]{2,1,0:T(8,128)(2,1)S(1)} copy-done((bf16[1,128,1664]{2,1,0:T(8,128)(2,1)S(1)}, bf16[1,128,1664]{2,1,0:T(8,128)(2,1)}, u32[]{:S(2)}) %copy-start) | copy-done | bytes 426008
  6.9 1.0 %copy-done.2 = bf16[1,128,1664]{2,1,0:T(8,128)(2,1)S(1)} copy-done((bf16[1,128,1664]{2,1,0:T(8,128)(2,1)S(1)}, bf16[1,128,1664]{2,1,0:T(8,128)(2,1)}, u32[]{:S(2)}) %copy-start.2) | copy-done | bytes 426008
  7.9 0.3 shard_map.50
  8.3 0.0 collective-permute-done.refs_1_
  8.3 3.6 %collective-permute-start.2 = (bf16[128,1664]{1,0:T(8,128)(2,1)S(1)}, bf16[128,1664]{1,0:T(8,128)(2,1)S(1)}, u32[]{:S(2)}, u32[]{:S(2)}) collective-permute-start(bf16[128,1664]{1,0:T(8,128)(2,1)S(1)} %get-tuple-element.48.refs_0_), channel_id=1, source_target_pairs={{0,8},{4,12},{8,0},{12,4},{1,9},{5,13},{9,1},{13,5},{2,10},{6,14},... | collective-permute-start | bytes 1277960 | tf_op jit(solution)/shard_map/ppermute | solution.py:267
  11.8 9.0 %collective-permute-done.3.refs_2_ = bf16[352,128]{1,0:T(8,128)(2,1)S(1)} collective-permute-done((bf16[352,128]{1,0:T(8,128)(2,1)S(1)}, bf16[352,128]{1,0:T(8,128)(2,1)S(1)}, u32[]{:S(2)}, u32[]{:S(2)}) %collective-permute-start.3) | collective-permute-done | bytes 90144 | tf_op jit(solution)/shard_map/ppermute | solution.py:267
  20.8 3.1 %collective-permute-done.4.refs_3_ = bf16[352,128]{1,0:T(8,128)(2,1)S(1)} collective-permute-done((bf16[352,128]{1,0:T(8,128)(2,1)S(1)}, bf16[352,128]{1,0:T(8,128)(2,1)S(1)}, u32[]{:S(2)}, u32[]{:S(2)}) %collective-permute-start.4) | collective-permute-done | bytes 90144 | tf_op jit(solution)/shard_map/ppermute | solution.py:267
  24.0 1.6 %collective-permute-start.6 = (bf16[1408,128]{1,0:T(8,128)(2,1)S(1)}, bf16[1408,128]{1,0:T(8,128)(2,1)S(1)}, u32[]{:S(2)}, u32[]{:S(2)}) collective-permute-start(bf16[1408,128]{1,0:T(8,128)(2,1)S(1)} %shard_map.52.refs_0_), channel_id=1, source_target_pairs={{0,16},{16,0},{1,17},{17,1},{2,18},{18,2},{3,19},{19,3},{4,20},{20... | collective-permute-start | bytes 1081352 | tf_op jit(solution)/shard_map/ppermute | solution.py:270
  25.6 1.5 %collective-permute-start.5 = (bf16[1408,128]{1,0:T(8,128)(2,1)S(1)}, bf16[1408,128]{1,0:T(8,128)(2,1)S(1)}, u32[]{:S(2)}, u32[]{:S(2)}) collective-permute-start(bf16[1408,128]{1,0:T(8,128)(2,1)S(1)} %shard_map.52.refs_0_), channel_id=1, source_target_pairs={{0,2},{2,0},{1,3},{3,1},{4,6},{6,4},{5,7},{7,5},{8,10},{10,8},{9,1... | collective-permute-start | bytes 1081352 | tf_op jit(solution)/shard_map/ppermute | solution.py:270
  27.0 4.5 %collective-permute-done.6.refs_2_ = bf16[1408,128]{1,0:T(8,128)(2,1)S(1)} collective-permute-done((bf16[1408,128]{1,0:T(8,128)(2,1)S(1)}, bf16[1408,128]{1,0:T(8,128)(2,1)S(1)}, u32[]{:S(2)}, u32[]{:S(2)}) %collective-permute-start.6) | collective-permute-done | bytes 360480 | tf_op jit(solution)/shard_map/ppermute | solution.py:270
  31.6 1.4 %collective-permute-done.5.refs_1_ = bf16[1408,128]{1,0:T(8,128)(2,1)S(1)} collective-permute-done((bf16[1408,128]{1,0:T(8,128)(2,1)S(1)}, bf16[1408,128]{1,0:T(8,128)(2,1)S(1)}, u32[]{:S(2)}, u32[]{:S(2)}) %collective-permute-start.5) | collective-permute-done | bytes 360480 | tf_op jit(solution)/shard_map/ppermute | solution.py:270
  33.0 3.7 %collective-permute-start.10 = (bf16[128,1664]{1,0:T(8,128)(2,1)S(1)}, bf16[128,1664]{1,0:T(8,128)(2,1)S(1)}, u32[]{:S(2)}, u32[]{:S(2)}) collective-permute-start(bf16[128,1664]{1,0:T(8,128)(2,1)S(1)} %get-tuple-element.48.refs_0_), channel_id=1, source_target_pairs={{4,8},{8,4},{5,9},{9,5},{6,10},{10,6},{7,11},{11,7},{20,24},{24,20... | collective-permute-start | bytes 1277960 | tf_op jit(solution)/shard_map/ppermute | solution.py:301
  36.7 1.3 %collective-permute-start.11 = (bf16[128,1664]{1,0:T(8,128)(2,1)S(1)}, bf16[128,1664]{1,0:T(8,128)(2,1)S(1)}, u32[]{:S(2)}, u32[]{:S(2)}) collective-permute-start(bf16[128,1664]{1,0:T(8,128)(2,1)S(1)} %collective-permute-done.2.refs_4_), channel_id=1, source_target_pairs={{8,12},{4,0},{9,13},{5,1},{10,14},{6,2},{11,15},{7,3},{24,28},{20,... | collective-permute-start | bytes 1277960 | tf_op jit(solution)/shard_map/ppermute | solution.py:302
  38.0 1.6 %collective-permute-start.9 = (bf16[1408,128]{1,0:T(8,128)(2,1)S(1)}, bf16[1408,128]{1,0:T(8,128)(2,1)S(1)}, u32[]{:S(2)}, u32[]{:S(2)}) collective-permute-start(bf16[1408,128]{1,0:T(8,128)(2,1)S(1)} %collective-permute-done.6.refs_2_), channel_id=1, source_target_pairs={{0,2},{2,0},{1,3},{3,1},{4,6},{6,4},{5,7},{7,5},{8,10},{10,8},{9,1... | collective-permute-start | bytes 1081352 | tf_op jit(solution)/shard_map/ppermute | solution.py:270
  39.5 0.5 collective-permute-start.7
  40.1 5.4 %collective-permute-done.9.refs_3_ = bf16[1408,128]{1,0:T(8,128)(2,1)S(1)} collective-permute-done((bf16[1408,128]{1,0:T(8,128)(2,1)S(1)}, bf16[1408,128]{1,0:T(8,128)(2,1)S(1)}, u32[]{:S(2)}, u32[]{:S(2)}) %collective-permute-start.9) | collective-permute-done | bytes 360480 | tf_op jit(solution)/shard_map/ppermute | solution.py:270
  45.5 0.9 shard_map.53.refs_10_
  46.4 0.1 collective-permute-start.12
  46.5 0.5 collective-permute-start.13
  47.0 1.3 %collective-permute-done.12.refs_7_ = bf16[128,1664]{1,0:T(8,128)(2,1)S(1)} collective-permute-done((bf16[128,1664]{1,0:T(8,128)(2,1)S(1)}, bf16[128,1664]{1,0:T(8,128)(2,1)S(1)}, u32[]{:S(2)}, u32[]{:S(2)}) %collective-permute-start.12) | collective-permute-done | bytes 426016 | tf_op jit(solution)/shard_map/ppermute | solution.py:270
  48.3 0.6 collective-permute-done.13.refs_9_
  48.9 7.9 %shard_map.54 = (bf16[4,64,1664]{2,1,0:T(8,128)(2,1)S(1)}, bf16[4,64,1664]{2,1,0:T(8,128)(2,1)S(1)}, bf16[4,688,128]{2,1,0:T(8,128)(2,1)S(1)}, bf16[4,688,128]{2,1,0:T(8,128)(2,1)S(1)}) custom-call(bf16[128,1664]{1,0:T(8,128)(2,1)S(1)} %get-tuple-element.48.refs_0_, bf16[128,1664]{1,0:T(8,128)(2,1)S(1)} %get-tuple-element.39.refs_1_, ...), custom_call_target="tpu_custom_call" | custom-call | tf_op jit(solution)/shard_map/pallas_call | solution.py:246
  56.8 0.0 copy-start.1
  56.8 0.0 copy-start.3
  56.8 0.2 collective-permute-start.15
  57.0 1.5 %collective-permute-start.14 = (bf16[4,688,128]{2,1,0:T(8,128)(2,1)S(1)}, bf16[4,688,128]{2,1,0:T(8,128)(2,1)S(1)}, u32[]{:S(2)}, u32[]{:S(2)}) collective-permute-start(bf16[4,688,128]{2,1,0:T(8,128)(2,1)S(1)} %get-tuple-element.52), channel_id=1, source_target_pairs={{0,2},{2,0},{1,3},{3,1},{4,6},{6,4},{5,7},{7,5},{8,10},{10,8},{9,1... | collective-permute-start | bytes 2113544 | tf_op jit(solution)/shard_map/ppermute | solution.py:270
  58.5 0.7 collective-permute-done.15.theirs_ref
  59.3 0.2 shard_map.55
  59.5 0.4 collective-permute-start.16
  59.9 2.4 %collective-permute-start.17 = (bf16[64,1664]{1,0:T(8,128)(2,1)S(1)}, bf16[64,1664]{1,0:T(8,128)(2,1)S(1)}, u32[]{:S(2)}, u32[]{:S(2)}) collective-permute-start(bf16[64,1664]{1,0:T(8,128)(2,1)S(1)} %get-tuple-element.58), channel_id=1, source_target_pairs={{0,8},{4,12},{8,0},{12,4},{1,9},{5,13},{9,1},{13,5},{2,10},{6,14},... | collective-permute-start | bytes 638984 | tf_op jit(solution)/shard_map/ppermute | solution.py:267
  62.3 0.8 collective-permute-start.18
  63.0 12.1 %collective-permute-done.14.theirs_ref = bf16[4,688,128]{2,1,0:T(8,128)(2,1)S(1)} collective-permute-done((bf16[4,688,128]{2,1,0:T(8,128)(2,1)S(1)}, bf16[4,688,128]{2,1,0:T(8,128)(2,1)S(1)}, u32[]{:S(2)}, u32[]{:S(2)}) %collective-permute-start.14) | collective-permute-done | bytes 704544 | tf_op jit(solution)/shard_map/ppermute | solution.py:270
  75.1 0.2 shard_map.57
  75.3 0.4 collective-permute-start.21
  75.7 2.4 %collective-permute-start.22 = (bf16[688,128]{1,0:T(8,128)(2,1)S(1)}, bf16[688,128]{1,0:T(8,128)(2,1)S(1)}, u32[]{:S(2)}, u32[]{:S(2)}) collective-permute-start(bf16[688,128]{1,0:T(8,128)(2,1)S(1)} %get-tuple-element.66), channel_id=1, source_target_pairs={{0,8},{4,12},{8,0},{12,4},{1,9},{5,13},{9,1},{13,5},{2,10},{6,14},... | collective-permute-start | bytes 528392 | tf_op jit(solution)/shard_map/ppermute | solution.py:267
  78.0 0.8 collective-permute-start.23
  78.8 11.6 %collective-permute-done.18.refs_3_ = bf16[64,1664]{1,0:T(8,128)(2,1)S(1)} collective-permute-done((bf16[64,1664]{1,0:T(8,128)(2,1)S(1)}, bf16[64,1664]{1,0:T(8,128)(2,1)S(1)}, u32[]{:S(2)}, u32[]{:S(2)}) %collective-permute-start.18) | collective-permute-done | bytes 213024 | tf_op jit(solution)/shard_map/ppermute | solution.py:267
  90.4 0.4 shard_map.56
  90.8 0.1 collective-permute-start.19
  90.9 0.5 collective-permute-start.20
  91.4 1.5 %collective-permute-done.22.refs_6_ = bf16[688,128]{1,0:T(8,128)(2,1)S(1)} collective-permute-done((bf16[688,128]{1,0:T(8,128)(2,1)S(1)}, bf16[688,128]{1,0:T(8,128)(2,1)S(1)}, u32[]{:S(2)}, u32[]{:S(2)}) %collective-permute-start.22) | collective-permute-done | bytes 176160 | tf_op jit(solution)/shard_map/ppermute | solution.py:267
  92.9 3.9 %collective-permute-done.23.refs_7_ = bf16[688,128]{1,0:T(8,128)(2,1)S(1)} collective-permute-done((bf16[688,128]{1,0:T(8,128)(2,1)S(1)}, bf16[688,128]{1,0:T(8,128)(2,1)S(1)}, u32[]{:S(2)}, u32[]{:S(2)}) %collective-permute-start.23) | collective-permute-done | bytes 176160 | tf_op jit(solution)/shard_map/ppermute | solution.py:267
  96.9 1.9 %shard_map.58 = (bf16[128,1664]{1,0:T(8,128)(2,1)}, f32[4,208,416]{2,1,0:T(8,128)}) custom-call(bf16[32,1664]{1,0:T(8,128)(2,1)S(1)} %get-tuple-element.60.refs_0_, bf16[32,1664]{1,0:T(8,128)(2,1)S(1)} %get-tuple-element.61.refs_1_, bf16[32,1664]{1,0:T(8,128)(2,1)S(1)} %collective-permute-done.19.refs_2_, ...), custom_call_target="tpu_custom_call" | custom-call | tf_op jit(solution)/shard_map/pallas_call | solution.py:246
  (19 shorter events, 0.1 us)
Async XLA Ops:
  0.6 1.2 %copy-start.4 = (bf16[4,208,416]{2,1,0:T(8,128)(2,1)S(1)}, bf16[4,208,416]{2,1,0:T(8,128)(2,1)}, u32[]{:S(2)}) copy-start(bf16[4,208,416]{2,1,0:T(8,128)(2,1)} %w_ref.1) | copy-start | bytes 2076676
  2.4 5.9 %collective-permute-start = (bf16[352,128]{1,0:T(8,128)(2,1)S(1)}, bf16[352,128]{1,0:T(8,128)(2,1)S(1)}, u32[]{:S(2)}, u32[]{:S(2)}) collective-permute-start(bf16[352,128]{1,0:T(8,128)(2,1)S(1)} %get-tuple-element.37), channel_id=1, source_target_pairs={{0,4},{4,0},{8,12},{12,8},{1,5},{5,1},{9,13},{13,9},{2,6},{6,2},{1... | collective-permute-start | bytes 270344 | tf_op jit(solution)/shard_map/ppermute | solution.py:267
  2.4 18.4 %collective-permute-start.3 = (bf16[352,128]{1,0:T(8,128)(2,1)S(1)}, bf16[352,128]{1,0:T(8,128)(2,1)S(1)}, u32[]{:S(2)}, u32[]{:S(2)}) collective-permute-start(bf16[352,128]{1,0:T(8,128)(2,1)S(1)} %get-tuple-element.42), channel_id=1, source_target_pairs={{0,8},{4,12},{8,0},{12,4},{1,9},{5,13},{9,1},{13,5},{2,10},{6,14},... | collective-permute-start | bytes 270344 | tf_op jit(solution)/shard_map/ppermute | solution.py:267
  5.5 18.5 %collective-permute-start.4 = (bf16[352,128]{1,0:T(8,128)(2,1)S(1)}, bf16[352,128]{1,0:T(8,128)(2,1)S(1)}, u32[]{:S(2)}, u32[]{:S(2)}) collective-permute-start(bf16[352,128]{1,0:T(8,128)(2,1)S(1)} %get-tuple-element.43), channel_id=1, source_target_pairs={{0,12},{4,8},{8,4},{12,0},{1,13},{5,9},{9,5},{13,1},{2,14},{6,10},... | collective-permute-start | bytes 270344 | tf_op jit(solution)/shard_map/ppermute | solution.py:267
  5.9 1.0 %copy-start = (bf16[1,128,1664]{2,1,0:T(8,128)(2,1)S(1)}, bf16[1,128,1664]{2,1,0:T(8,128)(2,1)}, u32[]{:S(2)}) copy-start(bf16[1,128,1664]{2,1,0:T(8,128)(2,1)} %param.3) | copy-start | bytes 1277956
  6.9 1.0 %copy-start.2 = (bf16[1,128,1664]{2,1,0:T(8,128)(2,1)S(1)}, bf16[1,128,1664]{2,1,0:T(8,128)(2,1)}, u32[]{:S(2)}) copy-start(bf16[1,128,1664]{2,1,0:T(8,128)(2,1)} %param.4) | copy-start | bytes 1277956
  8.3 24.7 %collective-permute-start.2 = (bf16[128,1664]{1,0:T(8,128)(2,1)S(1)}, bf16[128,1664]{1,0:T(8,128)(2,1)S(1)}, u32[]{:S(2)}, u32[]{:S(2)}) collective-permute-start(bf16[128,1664]{1,0:T(8,128)(2,1)S(1)} %get-tuple-element.48.refs_0_), channel_id=1, source_target_pairs={{0,8},{4,12},{8,0},{12,4},{1,9},{5,13},{9,1},{13,5},{2,10},{6,14},... | collective-permute-start | bytes 1277960 | tf_op jit(solution)/shard_map/ppermute | solution.py:267
  11.8 21.2 %collective-permute-start.1 = (bf16[128,1664]{1,0:T(8,128)(2,1)S(1)}, bf16[128,1664]{1,0:T(8,128)(2,1)S(1)}, u32[]{:S(2)}, u32[]{:S(2)}) collective-permute-start(bf16[128,1664]{1,0:T(8,128)(2,1)S(1)} %get-tuple-element.48.refs_0_), channel_id=1, source_target_pairs={{0,4},{4,0},{8,12},{12,8},{1,5},{5,1},{9,13},{13,9},{2,6},{6,2},{1... | collective-permute-start | bytes 1277960 | tf_op jit(solution)/shard_map/ppermute | solution.py:267
  24.0 7.6 %collective-permute-start.6 = (bf16[1408,128]{1,0:T(8,128)(2,1)S(1)}, bf16[1408,128]{1,0:T(8,128)(2,1)S(1)}, u32[]{:S(2)}, u32[]{:S(2)}) collective-permute-start(bf16[1408,128]{1,0:T(8,128)(2,1)S(1)} %shard_map.52.refs_0_), channel_id=1, source_target_pairs={{0,16},{16,0},{1,17},{17,1},{2,18},{18,2},{3,19},{19,3},{4,20},{20... | collective-permute-start | bytes 1081352 | tf_op jit(solution)/shard_map/ppermute | solution.py:270
  25.6 7.4 %collective-permute-start.5 = (bf16[1408,128]{1,0:T(8,128)(2,1)S(1)}, bf16[1408,128]{1,0:T(8,128)(2,1)S(1)}, u32[]{:S(2)}, u32[]{:S(2)}) collective-permute-start(bf16[1408,128]{1,0:T(8,128)(2,1)S(1)} %shard_map.52.refs_0_), channel_id=1, source_target_pairs={{0,2},{2,0},{1,3},{3,1},{4,6},{6,4},{5,7},{7,5},{8,10},{10,8},{9,1... | collective-permute-start | bytes 1081352 | tf_op jit(solution)/shard_map/ppermute | solution.py:270
  33.0 13.4 %collective-permute-start.10 = (bf16[128,1664]{1,0:T(8,128)(2,1)S(1)}, bf16[128,1664]{1,0:T(8,128)(2,1)S(1)}, u32[]{:S(2)}, u32[]{:S(2)}) collective-permute-start(bf16[128,1664]{1,0:T(8,128)(2,1)S(1)} %get-tuple-element.48.refs_0_), channel_id=1, source_target_pairs={{4,8},{8,4},{5,9},{9,5},{6,10},{10,6},{7,11},{11,7},{20,24},{24,20... | collective-permute-start | bytes 1277960 | tf_op jit(solution)/shard_map/ppermute | solution.py:301
  36.7 9.8 %collective-permute-start.11 = (bf16[128,1664]{1,0:T(8,128)(2,1)S(1)}, bf16[128,1664]{1,0:T(8,128)(2,1)S(1)}, u32[]{:S(2)}, u32[]{:S(2)}) collective-permute-start(bf16[128,1664]{1,0:T(8,128)(2,1)S(1)} %collective-permute-done.2.refs_4_), channel_id=1, source_target_pairs={{8,12},{4,0},{9,13},{5,1},{10,14},{6,2},{11,15},{7,3},{24,28},{20,... | collective-permute-start | bytes 1277960 | tf_op jit(solution)/shard_map/ppermute | solution.py:302
  38.0 7.5 %collective-permute-start.9 = (bf16[1408,128]{1,0:T(8,128)(2,1)S(1)}, bf16[1408,128]{1,0:T(8,128)(2,1)S(1)}, u32[]{:S(2)}, u32[]{:S(2)}) collective-permute-start(bf16[1408,128]{1,0:T(8,128)(2,1)S(1)} %collective-permute-done.6.refs_2_), channel_id=1, source_target_pairs={{0,2},{2,0},{1,3},{3,1},{4,6},{6,4},{5,7},{7,5},{8,10},{10,8},{9,1... | collective-permute-start | bytes 1081352 | tf_op jit(solution)/shard_map/ppermute | solution.py:270
  39.5 7.5 %collective-permute-start.8 = (bf16[128,1664]{1,0:T(8,128)(2,1)S(1)}, bf16[128,1664]{1,0:T(8,128)(2,1)S(1)}, u32[]{:S(2)}, u32[]{:S(2)}) collective-permute-start(bf16[128,1664]{1,0:T(8,128)(2,1)S(1)} %collective-permute-done.2.refs_4_), channel_id=1, source_target_pairs={{0,1},{1,0},{2,3},{3,2},{4,5},{5,4},{6,7},{7,6},{8,9},{9,8},{10,11... | collective-permute-start | bytes 1277960 | tf_op jit(solution)/shard_map/ppermute | solution.py:270
  39.5 7.5 %collective-permute-start.7 = (bf16[128,1664]{1,0:T(8,128)(2,1)S(1)}, bf16[128,1664]{1,0:T(8,128)(2,1)S(1)}, u32[]{:S(2)}, u32[]{:S(2)}) collective-permute-start(bf16[128,1664]{1,0:T(8,128)(2,1)S(1)} %collective-permute-done.1.refs_2_), channel_id=1, source_target_pairs={{0,1},{1,0},{2,3},{3,2},{4,5},{5,4},{6,7},{7,6},{8,9},{9,8},{10,11... | collective-permute-start | bytes 1277960 | tf_op jit(solution)/shard_map/ppermute | solution.py:270
  46.4 1.8 %collective-permute-start.12 = (bf16[128,1664]{1,0:T(8,128)(2,1)S(1)}, bf16[128,1664]{1,0:T(8,128)(2,1)S(1)}, u32[]{:S(2)}, u32[]{:S(2)}) collective-permute-start(bf16[128,1664]{1,0:T(8,128)(2,1)S(1)} %collective-permute-done.10.refs_6_), channel_id=1, source_target_pairs={{0,1},{1,0},{2,3},{3,2},{4,5},{5,4},{6,7},{7,6},{8,9},{9,8},{10,11... | collective-permute-start | bytes 1277960 | tf_op jit(solution)/shard_map/ppermute | solution.py:270
  46.5 2.4 %collective-permute-start.13 = (bf16[128,1664]{1,0:T(8,128)(2,1)S(1)}, bf16[128,1664]{1,0:T(8,128)(2,1)S(1)}, u32[]{:S(2)}, u32[]{:S(2)}) collective-permute-start(bf16[128,1664]{1,0:T(8,128)(2,1)S(1)} %collective-permute-done.11.refs_8_), channel_id=1, source_target_pairs={{0,1},{1,0},{2,3},{3,2},{4,5},{5,4},{6,7},{7,6},{8,9},{9,8},{10,11... | collective-permute-start | bytes 1277960 | tf_op jit(solution)/shard_map/ppermute | solution.py:270
  56.8 33.6 %copy-start.1 = (bf16[1,128,1664]{2,1,0:T(8,128)(2,1)S(1)}, bf16[1,128,1664]{2,1,0:T(8,128)(2,1)}, u32[]{:S(2)}) copy-start(bf16[1,128,1664]{2,1,0:T(8,128)(2,1)} %param.3) | copy-start | bytes 1277956
  56.8 33.6 %copy-start.3 = (bf16[1,128,1664]{2,1,0:T(8,128)(2,1)S(1)}, bf16[1,128,1664]{2,1,0:T(8,128)(2,1)}, u32[]{:S(2)}) copy-start(bf16[1,128,1664]{2,1,0:T(8,128)(2,1)} %param.4) | copy-start | bytes 1277956
  56.8 2.4 %collective-permute-start.15 = (bf16[4,64,1664]{2,1,0:T(8,128)(2,1)S(1)}, bf16[4,64,1664]{2,1,0:T(8,128)(2,1)S(1)}, u32[]{:S(2)}, u32[]{:S(2)}) collective-permute-start(bf16[4,64,1664]{2,1,0:T(8,128)(2,1)S(1)} %get-tuple-element.54), channel_id=1, source_target_pairs={{0,1},{1,0},{2,3},{3,2},{4,5},{5,4},{6,7},{7,6},{8,9},{9,8},{10,11... | collective-permute-start | bytes 2555912 | tf_op jit(solution)/shard_map/ppermute | solution.py:270
  57.0 18.1 %collective-permute-start.14 = (bf16[4,688,128]{2,1,0:T(8,128)(2,1)S(1)}, bf16[4,688,128]{2,1,0:T(8,128)(2,1)S(1)}, u32[]{:S(2)}, u32[]{:S(2)}) collective-permute-start(bf16[4,688,128]{2,1,0:T(8,128)(2,1)S(1)} %get-tuple-element.52), channel_id=1, source_target_pairs={{0,2},{2,0},{1,3},{3,1},{4,6},{6,4},{5,7},{7,5},{8,10},{10,8},{9,1... | collective-permute-start | bytes 2113544 | tf_op jit(solution)/shard_map/ppermute | solution.py:270
  59.5 18.6 %collective-permute-start.16 = (bf16[64,1664]{1,0:T(8,128)(2,1)S(1)}, bf16[64,1664]{1,0:T(8,128)(2,1)S(1)}, u32[]{:S(2)}, u32[]{:S(2)}) collective-permute-start(bf16[64,1664]{1,0:T(8,128)(2,1)S(1)} %get-tuple-element.57), channel_id=1, source_target_pairs={{0,4},{4,0},{8,12},{12,8},{1,5},{5,1},{9,13},{13,9},{2,6},{6,2},{1... | collective-permute-start | bytes 638984 | tf_op jit(solution)/shard_map/ppermute | solution.py:267
  59.9 19.0 %collective-permute-start.17 = (bf16[64,1664]{1,0:T(8,128)(2,1)S(1)}, bf16[64,1664]{1,0:T(8,128)(2,1)S(1)}, u32[]{:S(2)}, u32[]{:S(2)}) collective-permute-start(bf16[64,1664]{1,0:T(8,128)(2,1)S(1)} %get-tuple-element.58), channel_id=1, source_target_pairs={{0,8},{4,12},{8,0},{12,4},{1,9},{5,13},{9,1},{13,5},{2,10},{6,14},... | collective-permute-start | bytes 638984 | tf_op jit(solution)/shard_map/ppermute | solution.py:267
  62.3 28.1 %collective-permute-start.18 = (bf16[64,1664]{1,0:T(8,128)(2,1)S(1)}, bf16[64,1664]{1,0:T(8,128)(2,1)S(1)}, u32[]{:S(2)}, u32[]{:S(2)}) collective-permute-start(bf16[64,1664]{1,0:T(8,128)(2,1)S(1)} %get-tuple-element.59), channel_id=1, source_target_pairs={{0,12},{4,8},{8,4},{12,0},{1,13},{5,9},{9,5},{13,1},{2,14},{6,10},... | collective-permute-start | bytes 638984 | tf_op jit(solution)/shard_map/ppermute | solution.py:267
  75.3 16.1 %collective-permute-start.21 = (bf16[688,128]{1,0:T(8,128)(2,1)S(1)}, bf16[688,128]{1,0:T(8,128)(2,1)S(1)}, u32[]{:S(2)}, u32[]{:S(2)}) collective-permute-start(bf16[688,128]{1,0:T(8,128)(2,1)S(1)} %get-tuple-element.65), channel_id=1, source_target_pairs={{0,4},{4,0},{8,12},{12,8},{1,5},{5,1},{9,13},{13,9},{2,6},{6,2},{1... | collective-permute-start | bytes 528392 | tf_op jit(solution)/shard_map/ppermute | solution.py:267
  75.7 17.3 %collective-permute-start.22 = (bf16[688,128]{1,0:T(8,128)(2,1)S(1)}, bf16[688,128]{1,0:T(8,128)(2,1)S(1)}, u32[]{:S(2)}, u32[]{:S(2)}) collective-permute-start(bf16[688,128]{1,0:T(8,128)(2,1)S(1)} %get-tuple-element.66), channel_id=1, source_target_pairs={{0,8},{4,12},{8,0},{12,4},{1,9},{5,13},{9,1},{13,5},{2,10},{6,14},... | collective-permute-start | bytes 528392 | tf_op jit(solution)/shard_map/ppermute | solution.py:267
  78.0 18.8 %collective-permute-start.23 = (bf16[688,128]{1,0:T(8,128)(2,1)S(1)}, bf16[688,128]{1,0:T(8,128)(2,1)S(1)}, u32[]{:S(2)}, u32[]{:S(2)}) collective-permute-start(bf16[688,128]{1,0:T(8,128)(2,1)S(1)} %get-tuple-element.67), channel_id=1, source_target_pairs={{0,12},{4,8},{8,4},{12,0},{1,13},{5,9},{9,5},{13,1},{2,14},{6,10},... | collective-permute-start | bytes 528392 | tf_op jit(solution)/shard_map/ppermute | solution.py:267
  90.8 6.0 %collective-permute-start.19 = (bf16[32,1664]{1,0:T(8,128)(2,1)S(1)}, bf16[32,1664]{1,0:T(8,128)(2,1)S(1)}, u32[]{:S(2)}, u32[]{:S(2)}) collective-permute-start(bf16[32,1664]{1,0:T(8,128)(2,1)S(1)} %get-tuple-element.60.refs_0_), channel_id=1, source_target_pairs={{0,1},{1,0},{2,3},{3,2},{4,5},{5,4},{6,7},{7,6},{8,9},{9,8},{10,11... | collective-permute-start | bytes 319496 | tf_op jit(solution)/shard_map/ppermute | solution.py:270
  90.9 6.0 %collective-permute-start.20 = (bf16[32,1664]{1,0:T(8,128)(2,1)S(1)}, bf16[32,1664]{1,0:T(8,128)(2,1)S(1)}, u32[]{:S(2)}, u32[]{:S(2)}) collective-permute-start(bf16[32,1664]{1,0:T(8,128)(2,1)S(1)} %get-tuple-element.61.refs_1_), channel_id=1, source_target_pairs={{0,1},{1,0},{2,3},{3,2},{4,5},{5,4},{6,7},{7,6},{8,9},{9,8},{10,11... | collective-permute-start | bytes 319496 | tf_op jit(solution)/shard_map/ppermute | solution.py:270

commit v6 on v5

--- a/solution.py
+++ b/solution.py
@@ -126,42 +126,55 @@
         refs[-1][k * share : (k + 1) * share] = ref[...]
 
 
-def head_kernel(n, factor, *refs):
-    blocks = [(refs[2 * k], refs[2 * k + 1]) for k in range(n + 1)]
-    w_full, keep_ref, give_ref, w_keep_ref, w_give_ref = refs[2 * n + 2 : 2 * n + 7]
-    x_full, up_full, grads, staged, term_k, term_v = refs[2 * n + 7 :]
-    me = lax.axis_index("seq")
-    image = lax.axis_index("dp")
-    rows = blocks[0][0].shape[0]
+def project(x, up, w_ref):
+    return [
+        nn(x, w_ref[:, : 3 * SLOT]).astype(BF),
+        nn(up, w_ref[:, 3 * SLOT :]).astype(BF),
+    ]
+
+
+def place(row, sides, x_ref, up_ref):
+    half = sides[0].shape[0] // 2
+    for side, source in enumerate(sides):
+        span = slice(row + side * half, row + (side + 1) * half)
+        x_ref[span, :] = source[:half, :]
+        up_ref[span, :] = source[half:, :]
+
+
+def project_kernel(n, *refs):
+    w_ref, x_ref, up_ref, made_ref = refs[2 * n - 2 :]
+    rows = refs[0].shape[0]
+    for k in range(n - 1):
+        place(k * rows, refs[2 * k : 2 * k + 2], x_ref, up_ref)
+    made_ref[:, : 3 * SLOT], made_ref[:, 3 * SLOT :] = project(x_ref[...], up_ref[...], w_ref)
+
+
+def head_kernel(n, *refs):
+    middle, passed = refs[:2], refs[2:4]
+    made_ref, w_ref, keep_ref, give_ref, grads, x_ref, up_ref = refs[4:11]
+    made, term_k, term_v = refs[11:]
+    me = lax.axis_index("seq")
+    rows = x_ref.shape[0]
     half = rows // 2
-    share = w_full.shape[0] // (2 * n)
-
-    def place(k, sides):
-        for side, source in enumerate(sides):
-            span = slice(k * rows + side * half, k * rows + (side + 1) * half)
-            x_full[span, :] = source[:half, :]
-            up_full[span, :] = source[half:, :]
-
-    for k in range(n - 1):
-        place(k, blocks[k])
+    ready = (n - 1) * rows
 
     @pl.when((me == 0) | (me == n - 1))
     def _():
-        place(n - 1, blocks[n])
+        place(0, passed, x_ref, up_ref)
 
     @pl.when((me != 0) & (me != n - 1))
     def _():
-        place(n - 1, blocks[n - 1])
-
+        place(0, middle, x_ref, up_ref)
+
+    made[:ready, :] = made_ref[...]
+    made[ready:, : 3 * SLOT], made[ready:, 3 * SLOT :] = project(x_ref[...], up_ref[...], w_ref)
     scale = HD ** (-0.5)
-    qkv = nn(x_full[...], w_full[:, : 3 * SLOT]).astype(BF)
-    grad_att = nn(up_full[...], w_full[:, 3 * SLOT :]).astype(BF)
-    key_rows = qkv[:, SLOT : 2 * SLOT]
-    value_rows = qkv[:, 2 * SLOT :]
+    key_rows = made[:, SLOT : 2 * SLOT]
+    value_rows = made[:, 2 * SLOT : 3 * SLOT]
     for b in range(n):
         span = slice(b * rows, (b + 1) * rows)
-        query = qkv[span, :SLOT]
-        grad_out = grad_att[span]
+        query = made[span, :SLOT]
+        grad_out = made[span, 3 * SLOT :]
         scores = nt(query, key_rows) * scale
         weight = jnp.exp(scores - jnp.max(scores, axis=1, keepdims=True))
         probs = (weight / jnp.sum(weight, axis=1, keepdims=True)).astype(BF)
@@ -183,13 +196,24 @@
     grads[:, 2 * SLOT : 3 * SLOT] = term_v[...].astype(BF)
     for b in range(n):
         span = slice(b * rows, (b + 1) * rows)
-        part = nt(grads[span, : 3 * SLOT], w_full[:, : 3 * SLOT]).astype(BF)
+        part = nt(grads[span, : 3 * SLOT], w_ref[:, : 3 * SLOT]).astype(BF)
         keep_ref[b] = part[:half]
         give_ref[b] = part[half:]
-    staged[:, : 3 * SLOT] = (tn(x_full[...], grads[:, : 3 * SLOT]) * factor).astype(BF)
-    staged[:, 3 * SLOT :] = (tn(up_full[...], grads[:, 3 * SLOT :]) * factor).astype(BF)
+
+
+def weight_kernel(n, factor, x_ref, x_last, up_ref, up_last, grads, keep_ref, give_ref, staged):
+    me = lax.axis_index("seq")
+    image = lax.axis_index("dp")
+    ready = x_ref.shape[0]
+    share = staged.shape[0] // (2 * n)
+    for lanes, first, last in (
+        (slice(0, 3 * SLOT), x_ref, x_last),
+        (slice(3 * SLOT, 4 * SLOT), up_ref, up_last),
+    ):
+        total = tn(first[...], grads[:ready, lanes]) + tn(last[...], grads[ready:, lanes])
+        staged[:, lanes] = (total * factor).astype(BF)
     for k in range(n):
-        for target, at in ((w_keep_ref, image), (w_give_ref, 1 - image)):
+        for target, at in ((keep_ref, image), (give_ref, 1 - image)):
             first = pl.multiple_of(((me ^ k) * 2 + at) * share, 16)
             mats = [
                 staged[pl.ds(first, share), mat * SLOT : mat * SLOT + HD] for mat in range(4)
@@ -301,23 +325,28 @@
     middle = lax.ppermute(later, "seq", [(1, 2), (2, 1)])
     passed = lax.ppermute(second, "seq", [(2, 3), (1, 0)])
     weights, middle, passed = lax.optimization_barrier((weights, middle, passed))
-    args = [send, rest]
-    for block in (first, second, middle, passed):
-        args += [block, swap(block, "pipe")]
-    args.append(weights)
-    factor = 1.0 / math.sqrt(patches * lax.axis_size("dp"))
-    keep, give, w_keep, w_give = call(
-        functools.partial(head_kernel, n, factor),
-        [((n, half, width), BF)] * 2 + [((n, full, SLOT), BF)] * 2,
-        args,
+    ready = patches - rows
+    x_head, up_head, made = call(
+        functools.partial(project_kernel, n),
+        [((ready, width), BF)] * 2 + [((ready, 4 * SLOT), BF)],
+        (send, rest, first, swap(first, "pipe"), second, swap(second, "pipe"), weights),
+    )
+    keep, give, grads, x_last, up_last = call(
+        functools.partial(head_kernel, n),
+        [((n, half, width), BF)] * 2 + [((patches, 4 * SLOT), BF)] + [((rows, width), BF)] * 2,
+        (middle, swap(middle, "pipe"), passed, swap(passed, "pipe"), made, weights),
         [
-            pltpu.VMEM((patches, width), BF),
-            pltpu.VMEM((patches, width), BF),
             pltpu.VMEM((patches, 4 * SLOT), BF),
-            pltpu.VMEM((width, 4 * SLOT), BF),
             pltpu.VMEM((patches, SLOT), F32),
             pltpu.VMEM((patches, SLOT), F32),
         ],
+    )
+    factor = 1.0 / math.sqrt(patches * lax.axis_size("dp"))
+    w_keep, w_give = call(
+        functools.partial(weight_kernel, n, factor),
+        [((n, full, SLOT), BF)] * 2,
+        (x_head, x_last, up_head, up_last, grads),
+        [pltpu.VMEM((width, 4 * SLOT), BF)],
     )
     taken = swap(give, "pipe")
     w_taken = swap(w_give, "dp")

time: 99 us -> 97.5 us (0.985)
  waiting for transfers between devices: 55.2 us -> 53.2 us
    ppermute x11, waiting for transfers between devices: 26 us -> 24.8 us  [swap(): return lax.ppermute(value, axis, [(0, 1), (1, 0)])]
    pallas_call x9 -> x11, Pallas kernels: 12.4 us -> 12.9 us  [call(): pl.pallas_call(kernel, out_shape=[out_space(*s) for s in shapes], in_spec...]
  transfers between devices with their start and end apart: 24 -> 24, of which waited for: 12 -> 11; matrix products, arithmetic and copies ran while one was open for 0% -> 0% of each run, Pallas kernels for 2% -> 6%
where the time goes in v6:
time: 97.5 us; the launch traced here: 97.2 us
  waiting for transfers between devices  53.2 us (55%)
  starting transfers between devices  27.2 us (28%)
  Pallas kernels  12.9 us (13%)
  local copies, waits for them, and re-layouts  3.18 us (3%)
    ppermute x11, waiting for transfers between devices, across(): return lax.ppermute(value, 'seq', [(i, i ^ k) for i in range(n)])  28.3 us
    ppermute x11, waiting for transfers between devices, swap(): return lax.ppermute(value, axis, [(0, 1), (1, 0)])  24.8 us
    ppermute x11, starting transfers between devices, across(): return lax.ppermute(value, 'seq', [(i, i ^ k) for i in range(n)])  14.2 us
    pallas_call x11, Pallas kernels, call(): pl.pallas_call(kernel, out_shape=[out_space(*s) for s in shapes], in_spec...  12.9 us
    ppermute x11, starting transfers between devices, swap(): return lax.ppermute(value, axis, [(0, 1), (1, 0)])  8.05 us
    ppermute x1, starting transfers between devices, local_heads(): middle = lax.ppermute(later, 'seq', [(1, 2), (2, 1)])  3.66 us
    unnamed x10, local copies, waits for them, and re-layouts  3.18 us
  transfers between devices with their start and end apart: 24, of which 11 were waited for; matrix products, arithmetic and copies ran while one was open for 0% of the time, Pallas kernels for 6%

profile of v6, /device:TPU:8, one launch (start us, length us, event | category | flops | bytes accessed | tf_op | source)
XLA Modules:
  0.0 97.2 jit_solution(5793362089135657612)
XLA Ops:
  0.6 1.1 %copy-done.4 = bf16[4,208,416]{2,1,0:T(8,128)(2,1)S(1)} copy-done((bf16[4,208,416]{2,1,0:T(8,128)(2,1)S(1)}, bf16[4,208,416]{2,1,0:T(8,128)(2,1)}, u32[]{:S(2)}) %copy-start.4) | copy-done | bytes 692248
  1.8 0.6 shard_map.51
  2.4 0.1 collective-permute-start
  2.4 3.0 %collective-permute-start.3 = (bf16[352,128]{1,0:T(8,128)(2,1)S(1)}, bf16[352,128]{1,0:T(8,128)(2,1)S(1)}, u32[]{:S(2)}, u32[]{:S(2)}) collective-permute-start(bf16[352,128]{1,0:T(8,128)(2,1)S(1)} %get-tuple-element.48), channel_id=1, source_target_pairs={{0,8},{4,12},{8,0},{12,4},{1,9},{5,13},{9,1},{13,5},{2,10},{6,14},... | collective-permute-start | bytes 270344 | tf_op jit(solution)/shard_map/ppermute | solution.py:291
  5.5 0.5 collective-permute-start.4
  5.9 1.0 %copy-done = bf16[1,128,1664]{2,1,0:T(8,128)(2,1)S(1)} copy-done((bf16[1,128,1664]{2,1,0:T(8,128)(2,1)S(1)}, bf16[1,128,1664]{2,1,0:T(8,128)(2,1)}, u32[]{:S(2)}) %copy-start) | copy-done | bytes 426008
  6.9 1.0 %copy-done.2 = bf16[1,128,1664]{2,1,0:T(8,128)(2,1)S(1)} copy-done((bf16[1,128,1664]{2,1,0:T(8,128)(2,1)S(1)}, bf16[1,128,1664]{2,1,0:T(8,128)(2,1)}, u32[]{:S(2)}) %copy-start.2) | copy-done | bytes 426008
  7.9 0.3 shard_map.50
  8.3 3.6 %collective-permute-start.2 = (bf16[128,1664]{1,0:T(8,128)(2,1)S(1)}, bf16[128,1664]{1,0:T(8,128)(2,1)S(1)}, u32[]{:S(2)}, u32[]{:S(2)}) collective-permute-start(bf16[128,1664]{1,0:T(8,128)(2,1)S(1)} %get-tuple-element.54.refs_0_), channel_id=1, source_target_pairs={{0,8},{4,12},{8,0},{12,4},{1,9},{5,13},{9,1},{13,5},{2,10},{6,14},... | collective-permute-start | bytes 1277960 | tf_op jit(solution)/shard_map/ppermute | solution.py:291
  11.8 9.0 %collective-permute-done.3.refs_2_ = bf16[352,128]{1,0:T(8,128)(2,1)S(1)} collective-permute-done((bf16[352,128]{1,0:T(8,128)(2,1)S(1)}, bf16[352,128]{1,0:T(8,128)(2,1)S(1)}, u32[]{:S(2)}, u32[]{:S(2)}) %collective-permute-start.3) | collective-permute-done | bytes 90144 | tf_op jit(solution)/shard_map/ppermute | solution.py:291
  20.8 3.1 %collective-permute-done.4.refs_3_ = bf16[352,128]{1,0:T(8,128)(2,1)S(1)} collective-permute-done((bf16[352,128]{1,0:T(8,128)(2,1)S(1)}, bf16[352,128]{1,0:T(8,128)(2,1)S(1)}, u32[]{:S(2)}, u32[]{:S(2)}) %collective-permute-start.4) | collective-permute-done | bytes 90144 | tf_op jit(solution)/shard_map/ppermute | solution.py:291
  24.0 1.6 %collective-permute-start.6 = (bf16[1408,128]{1,0:T(8,128)(2,1)S(1)}, bf16[1408,128]{1,0:T(8,128)(2,1)S(1)}, u32[]{:S(2)}, u32[]{:S(2)}) collective-permute-start(bf16[1408,128]{1,0:T(8,128)(2,1)S(1)} %shard_map.52.refs_0_), channel_id=1, source_target_pairs={{0,16},{16,0},{1,17},{17,1},{2,18},{18,2},{3,19},{19,3},{4,20},{20... | collective-permute-start | bytes 1081352 | tf_op jit(solution)/shard_map/ppermute | solution.py:294
  25.6 1.5 %collective-permute-start.5 = (bf16[1408,128]{1,0:T(8,128)(2,1)S(1)}, bf16[1408,128]{1,0:T(8,128)(2,1)S(1)}, u32[]{:S(2)}, u32[]{:S(2)}) collective-permute-start(bf16[1408,128]{1,0:T(8,128)(2,1)S(1)} %shard_map.52.refs_0_), channel_id=1, source_target_pairs={{0,2},{2,0},{1,3},{3,1},{4,6},{6,4},{5,7},{7,5},{8,10},{10,8},{9,1... | collective-permute-start | bytes 1081352 | tf_op jit(solution)/shard_map/ppermute | solution.py:294
  27.0 4.5 %collective-permute-done.6.refs_2_ = bf16[1408,128]{1,0:T(8,128)(2,1)S(1)} collective-permute-done((bf16[1408,128]{1,0:T(8,128)(2,1)S(1)}, bf16[1408,128]{1,0:T(8,128)(2,1)S(1)}, u32[]{:S(2)}, u32[]{:S(2)}) %collective-permute-start.6) | collective-permute-done | bytes 360480 | tf_op jit(solution)/shard_map/ppermute | solution.py:294
  31.6 1.4 %collective-permute-done.5.refs_1_ = bf16[1408,128]{1,0:T(8,128)(2,1)S(1)} collective-permute-done((bf16[1408,128]{1,0:T(8,128)(2,1)S(1)}, bf16[1408,128]{1,0:T(8,128)(2,1)S(1)}, u32[]{:S(2)}, u32[]{:S(2)}) %collective-permute-start.5) | collective-permute-done | bytes 360480 | tf_op jit(solution)/shard_map/ppermute | solution.py:294
  33.0 3.7 %collective-permute-start.10 = (bf16[128,1664]{1,0:T(8,128)(2,1)S(1)}, bf16[128,1664]{1,0:T(8,128)(2,1)S(1)}, u32[]{:S(2)}, u32[]{:S(2)}) collective-permute-start(bf16[128,1664]{1,0:T(8,128)(2,1)S(1)} %get-tuple-element.54.refs_0_), channel_id=1, source_target_pairs={{4,8},{8,4},{5,9},{9,5},{6,10},{10,6},{7,11},{11,7},{20,24},{24,20... | collective-permute-start | bytes 1277960 | tf_op jit(solution)/shard_map/ppermute | solution.py:325
  36.7 1.3 %collective-permute-start.11 = (bf16[128,1664]{1,0:T(8,128)(2,1)S(1)}, bf16[128,1664]{1,0:T(8,128)(2,1)S(1)}, u32[]{:S(2)}, u32[]{:S(2)}) collective-permute-start(bf16[128,1664]{1,0:T(8,128)(2,1)S(1)} %collective-permute-done.2.refs_4_), channel_id=1, source_target_pairs={{8,12},{4,0},{9,13},{5,1},{10,14},{6,2},{11,15},{7,3},{24,28},{20,... | collective-permute-start | bytes 1277960 | tf_op jit(solution)/shard_map/ppermute | solution.py:326
  38.0 1.6 %collective-permute-start.9 = (bf16[1408,128]{1,0:T(8,128)(2,1)S(1)}, bf16[1408,128]{1,0:T(8,128)(2,1)S(1)}, u32[]{:S(2)}, u32[]{:S(2)}) collective-permute-start(bf16[1408,128]{1,0:T(8,128)(2,1)S(1)} %collective-permute-done.6.refs_2_), channel_id=1, source_target_pairs={{0,2},{2,0},{1,3},{3,1},{4,6},{6,4},{5,7},{7,5},{8,10},{10,8},{9,1... | collective-permute-start | bytes 1081352 | tf_op jit(solution)/shard_map/ppermute | solution.py:294
  39.5 0.5 collective-permute-start.7
  40.1 5.4 %collective-permute-done.9.refs_3_ = bf16[1408,128]{1,0:T(8,128)(2,1)S(1)} collective-permute-done((bf16[1408,128]{1,0:T(8,128)(2,1)S(1)}, bf16[1408,128]{1,0:T(8,128)(2,1)S(1)}, u32[]{:S(2)}, u32[]{:S(2)}) %collective-permute-start.9) | collective-permute-done | bytes 360480 | tf_op jit(solution)/shard_map/ppermute | solution.py:294
  45.5 0.9 shard_map.53.refs_6_.refs_5_
  46.4 0.1 collective-permute-start.12
  46.5 0.5 collective-permute-start.13
  47.0 1.2 %shard_map.54 = (bf16[384,1664]{1,0:T(8,128)(2,1)S(1)}, bf16[384,1664]{1,0:T(8,128)(2,1)S(1)}, bf16[384,512]{1,0:T(8,128)(2,1)S(1)}) custom-call(bf16[128,1664]{1,0:T(8,128)(2,1)S(1)} %get-tuple-element.54.refs_0_, bf16[128,1664]{1,0:T(8,128)(2,1)S(1)} %get-tuple-element.45.refs_1_, bf16[128,1664]{1,0:T(8,128)(2,1)S(1)} %collective-permute-done.1.refs_2_, ...), custom_call_target="tpu_custom_call" | custom-call | tf_op jit(solution)/shard_map/pallas_call | solution.py:270
  48.2 0.1 collective-permute-done.12.refs_1_
  48.3 0.6 collective-permute-done.13.refs_3_
  48.9 4.9 %shard_map.55 = (bf16[4,64,1664]{2,1,0:T(8,128)(2,1)S(1)}, bf16[4,64,1664]{2,1,0:T(8,128)(2,1)S(1)}, bf16[512,512]{1,0:T(8,128)(2,1)S(1)}, bf16[128,1664]{1,0:T(8,128)(2,1)S(1)}, bf16[128,1664]{1,0:T(8,128)(2,1)S(1)}) custom-call(bf16[128,1664]{1,0:T(8,128)(2,1)S(1)} %collective-permute-done.10.refs_0_, ...), custom_call_target="tpu_custom_call" | custom-call | tf_op jit(solution)/shard_map/pallas_call | solution.py:270
  53.8 0.2 collective-permute-start.15
  54.0 2.2 %shard_map.56 = (bf16[4,688,128]{2,1,0:T(8,128)(2,1)S(1)}, bf16[4,688,128]{2,1,0:T(8,128)(2,1)S(1)}) custom-call(bf16[384,1664]{1,0:T(8,128)(2,1)S(1)} %get-tuple-element.56.x_ref, bf16[128,1664]{1,0:T(8,128)(2,1)S(1)} %get-tuple-element.60.x_last, bf16[384,1664]{1,0:T(8,128)(2,1)S(1)} %get-tuple-element.61.up_ref, ...), custom_call_target="tpu_custom_call" | custom-call | tf_op jit(solution)/shard_map/pallas_call | solution.py:270
  56.3 0.0 copy-start.1
  56.3 0.0 copy-start.3
  56.3 1.6 %collective-permute-start.14 = (bf16[4,688,128]{2,1,0:T(8,128)(2,1)S(1)}, bf16[4,688,128]{2,1,0:T(8,128)(2,1)S(1)}, u32[]{:S(2)}, u32[]{:S(2)}) collective-permute-start(bf16[4,688,128]{2,1,0:T(8,128)(2,1)S(1)} %get-tuple-element.64), channel_id=1, source_target_pairs={{0,2},{2,0},{1,3},{3,1},{4,6},{6,4},{5,7},{7,5},{8,10},{10,8},{9,1... | collective-permute-start | bytes 2113544 | tf_op jit(solution)/shard_map/ppermute | solution.py:294
  57.8 0.2 shard_map.57
  58.0 0.4 collective-permute-start.16
  58.5 2.4 %collective-permute-start.17 = (bf16[64,1664]{1,0:T(8,128)(2,1)S(1)}, bf16[64,1664]{1,0:T(8,128)(2,1)S(1)}, u32[]{:S(2)}, u32[]{:S(2)}) collective-permute-start(bf16[64,1664]{1,0:T(8,128)(2,1)S(1)} %get-tuple-element.70), channel_id=1, source_target_pairs={{0,8},{4,12},{8,0},{12,4},{1,9},{5,13},{9,1},{13,5},{2,10},{6,14},... | collective-permute-start | bytes 638984 | tf_op jit(solution)/shard_map/ppermute | solution.py:291
  60.8 0.8 collective-permute-start.18
  61.6 12.8 %collective-permute-done.14.theirs_ref = bf16[4,688,128]{2,1,0:T(8,128)(2,1)S(1)} collective-permute-done((bf16[4,688,128]{2,1,0:T(8,128)(2,1)S(1)}, bf16[4,688,128]{2,1,0:T(8,128)(2,1)S(1)}, u32[]{:S(2)}, u32[]{:S(2)}) %collective-permute-start.14) | collective-permute-done | bytes 704544 | tf_op jit(solution)/shard_map/ppermute | solution.py:294
  74.4 0.2 shard_map.59
  74.6 0.4 collective-permute-start.21
  75.0 2.4 %collective-permute-start.22 = (bf16[688,128]{1,0:T(8,128)(2,1)S(1)}, bf16[688,128]{1,0:T(8,128)(2,1)S(1)}, u32[]{:S(2)}, u32[]{:S(2)}) collective-permute-start(bf16[688,128]{1,0:T(8,128)(2,1)S(1)} %get-tuple-element.78), channel_id=1, source_target_pairs={{0,8},{4,12},{8,0},{12,4},{1,9},{5,13},{9,1},{13,5},{2,10},{6,14},... | collective-permute-start | bytes 528392 | tf_op jit(solution)/shard_map/ppermute | solution.py:291
  77.4 0.8 collective-permute-start.23
  78.1 10.8 %collective-permute-done.18.refs_3_ = bf16[64,1664]{1,0:T(8,128)(2,1)S(1)} collective-permute-done((bf16[64,1664]{1,0:T(8,128)(2,1)S(1)}, bf16[64,1664]{1,0:T(8,128)(2,1)S(1)}, u32[]{:S(2)}, u32[]{:S(2)}) %collective-permute-start.18) | collective-permute-done | bytes 213024 | tf_op jit(solution)/shard_map/ppermute | solution.py:291
  89.0 0.4 shard_map.58
  89.4 0.1 collective-permute-start.19
  89.5 0.5 collective-permute-start.20
  90.0 1.5 %collective-permute-done.22.refs_6_ = bf16[688,128]{1,0:T(8,128)(2,1)S(1)} collective-permute-done((bf16[688,128]{1,0:T(8,128)(2,1)S(1)}, bf16[688,128]{1,0:T(8,128)(2,1)S(1)}, u32[]{:S(2)}, u32[]{:S(2)}) %collective-permute-start.22) | collective-permute-done | bytes 176160 | tf_op jit(solution)/shard_map/ppermute | solution.py:291
  91.5 3.9 %collective-permute-done.23.refs_7_ = bf16[688,128]{1,0:T(8,128)(2,1)S(1)} collective-permute-done((bf16[688,128]{1,0:T(8,128)(2,1)S(1)}, bf16[688,128]{1,0:T(8,128)(2,1)S(1)}, u32[]{:S(2)}, u32[]{:S(2)}) %collective-permute-start.23) | collective-permute-done | bytes 176160 | tf_op jit(solution)/shard_map/ppermute | solution.py:291
  95.4 1.9 %shard_map.60 = (bf16[128,1664]{1,0:T(8,128)(2,1)}, f32[4,208,416]{2,1,0:T(8,128)}) custom-call(bf16[32,1664]{1,0:T(8,128)(2,1)S(1)} %get-tuple-element.72.refs_0_, bf16[32,1664]{1,0:T(8,128)(2,1)S(1)} %get-tuple-element.73.refs_1_, bf16[32,1664]{1,0:T(8,128)(2,1)S(1)} %collective-permute-done.19.refs_2_, ...), custom_call_target="tpu_custom_call" | custom-call | tf_op jit(solution)/shard_map/pallas_call | solution.py:270
  (21 shorter events, 0.1 us)
Async XLA Ops:
  0.6 1.2 %copy-start.4 = (bf16[4,208,416]{2,1,0:T(8,128)(2,1)S(1)}, bf16[4,208,416]{2,1,0:T(8,128)(2,1)}, u32[]{:S(2)}) copy-start(bf16[4,208,416]{2,1,0:T(8,128)(2,1)} %w_ref.1) | copy-start | bytes 2076676
  2.4 5.9 %collective-permute-start = (bf16[352,128]{1,0:T(8,128)(2,1)S(1)}, bf16[352,128]{1,0:T(8,128)(2,1)S(1)}, u32[]{:S(2)}, u32[]{:S(2)}) collective-permute-start(bf16[352,128]{1,0:T(8,128)(2,1)S(1)} %get-tuple-element.43), channel_id=1, source_target_pairs={{0,4},{4,0},{8,12},{12,8},{1,5},{5,1},{9,13},{13,9},{2,6},{6,2},{1... | collective-permute-start | bytes 270344 | tf_op jit(solution)/shard_map/ppermute | solution.py:291
  2.4 18.4 %collective-permute-start.3 = (bf16[352,128]{1,0:T(8,128)(2,1)S(1)}, bf16[352,128]{1,0:T(8,128)(2,1)S(1)}, u32[]{:S(2)}, u32[]{:S(2)}) collective-permute-start(bf16[352,128]{1,0:T(8,128)(2,1)S(1)} %get-tuple-element.48), channel_id=1, source_target_pairs={{0,8},{4,12},{8,0},{12,4},{1,9},{5,13},{9,1},{13,5},{2,10},{6,14},... | collective-permute-start | bytes 270344 | tf_op jit(solution)/shard_map/ppermute | solution.py:291
  5.5 18.5 %collective-permute-start.4 = (bf16[352,128]{1,0:T(8,128)(2,1)S(1)}, bf16[352,128]{1,0:T(8,128)(2,1)S(1)}, u32[]{:S(2)}, u32[]{:S(2)}) collective-permute-start(bf16[352,128]{1,0:T(8,128)(2,1)S(1)} %get-tuple-element.49), channel_id=1, source_target_pairs={{0,12},{4,8},{8,4},{12,0},{1,13},{5,9},{9,5},{13,1},{2,14},{6,10},... | collective-permute-start | bytes 270344 | tf_op jit(solution)/shard_map/ppermute | solution.py:291
  5.9 1.0 %copy-start = (bf16[1,128,1664]{2,1,0:T(8,128)(2,1)S(1)}, bf16[1,128,1664]{2,1,0:T(8,128)(2,1)}, u32[]{:S(2)}) copy-start(bf16[1,128,1664]{2,1,0:T(8,128)(2,1)} %param.3) | copy-start | bytes 1277956
  6.9 1.0 %copy-start.2 = (bf16[1,128,1664]{2,1,0:T(8,128)(2,1)S(1)}, bf16[1,128,1664]{2,1,0:T(8,128)(2,1)}, u32[]{:S(2)}) copy-start(bf16[1,128,1664]{2,1,0:T(8,128)(2,1)} %param.4) | copy-start | bytes 1277956
  8.3 24.7 %collective-permute-start.2 = (bf16[128,1664]{1,0:T(8,128)(2,1)S(1)}, bf16[128,1664]{1,0:T(8,128)(2,1)S(1)}, u32[]{:S(2)}, u32[]{:S(2)}) collective-permute-start(bf16[128,1664]{1,0:T(8,128)(2,1)S(1)} %get-tuple-element.54.refs_0_), channel_id=1, source_target_pairs={{0,8},{4,12},{8,0},{12,4},{1,9},{5,13},{9,1},{13,5},{2,10},{6,14},... | collective-permute-start | bytes 1277960 | tf_op jit(solution)/shard_map/ppermute | solution.py:291
  11.8 21.2 %collective-permute-start.1 = (bf16[128,1664]{1,0:T(8,128)(2,1)S(1)}, bf16[128,1664]{1,0:T(8,128)(2,1)S(1)}, u32[]{:S(2)}, u32[]{:S(2)}) collective-permute-start(bf16[128,1664]{1,0:T(8,128)(2,1)S(1)} %get-tuple-element.54.refs_0_), channel_id=1, source_target_pairs={{0,4},{4,0},{8,12},{12,8},{1,5},{5,1},{9,13},{13,9},{2,6},{6,2},{1... | collective-permute-start | bytes 1277960 | tf_op jit(solution)/shard_map/ppermute | solution.py:291
  24.0 7.6 %collective-permute-start.6 = (bf16[1408,128]{1,0:T(8,128)(2,1)S(1)}, bf16[1408,128]{1,0:T(8,128)(2,1)S(1)}, u32[]{:S(2)}, u32[]{:S(2)}) collective-permute-start(bf16[1408,128]{1,0:T(8,128)(2,1)S(1)} %shard_map.52.refs_0_), channel_id=1, source_target_pairs={{0,16},{16,0},{1,17},{17,1},{2,18},{18,2},{3,19},{19,3},{4,20},{20... | collective-permute-start | bytes 1081352 | tf_op jit(solution)/shard_map/ppermute | solution.py:294
  25.6 7.4 %collective-permute-start.5 = (bf16[1408,128]{1,0:T(8,128)(2,1)S(1)}, bf16[1408,128]{1,0:T(8,128)(2,1)S(1)}, u32[]{:S(2)}, u32[]{:S(2)}) collective-permute-start(bf16[1408,128]{1,0:T(8,128)(2,1)S(1)} %shard_map.52.refs_0_), channel_id=1, source_target_pairs={{0,2},{2,0},{1,3},{3,1},{4,6},{6,4},{5,7},{7,5},{8,10},{10,8},{9,1... | collective-permute-start | bytes 1081352 | tf_op jit(solution)/shard_map/ppermute | solution.py:294
  33.0 13.4 %collective-permute-start.10 = (bf16[128,1664]{1,0:T(8,128)(2,1)S(1)}, bf16[128,1664]{1,0:T(8,128)(2,1)S(1)}, u32[]{:S(2)}, u32[]{:S(2)}) collective-permute-start(bf16[128,1664]{1,0:T(8,128)(2,1)S(1)} %get-tuple-element.54.refs_0_), channel_id=1, source_target_pairs={{4,8},{8,4},{5,9},{9,5},{6,10},{10,6},{7,11},{11,7},{20,24},{24,20... | collective-permute-start | bytes 1277960 | tf_op jit(solution)/shard_map/ppermute | solution.py:325
  36.7 9.8 %collective-permute-start.11 = (bf16[128,1664]{1,0:T(8,128)(2,1)S(1)}, bf16[128,1664]{1,0:T(8,128)(2,1)S(1)}, u32[]{:S(2)}, u32[]{:S(2)}) collective-permute-start(bf16[128,1664]{1,0:T(8,128)(2,1)S(1)} %collective-permute-done.2.refs_4_), channel_id=1, source_target_pairs={{8,12},{4,0},{9,13},{5,1},{10,14},{6,2},{11,15},{7,3},{24,28},{20,... | collective-permute-start | bytes 1277960 | tf_op jit(solution)/shard_map/ppermute | solution.py:326
  38.0 7.5 %collective-permute-start.9 = (bf16[1408,128]{1,0:T(8,128)(2,1)S(1)}, bf16[1408,128]{1,0:T(8,128)(2,1)S(1)}, u32[]{:S(2)}, u32[]{:S(2)}) collective-permute-start(bf16[1408,128]{1,0:T(8,128)(2,1)S(1)} %collective-permute-done.6.refs_2_), channel_id=1, source_target_pairs={{0,2},{2,0},{1,3},{3,1},{4,6},{6,4},{5,7},{7,5},{8,10},{10,8},{9,1... | collective-permute-start | bytes 1081352 | tf_op jit(solution)/shard_map/ppermute | solution.py:294
  39.5 7.5 %collective-permute-start.8 = (bf16[128,1664]{1,0:T(8,128)(2,1)S(1)}, bf16[128,1664]{1,0:T(8,128)(2,1)S(1)}, u32[]{:S(2)}, u32[]{:S(2)}) collective-permute-start(bf16[128,1664]{1,0:T(8,128)(2,1)S(1)} %collective-permute-done.2.refs_4_), channel_id=1, source_target_pairs={{0,1},{1,0},{2,3},{3,2},{4,5},{5,4},{6,7},{7,6},{8,9},{9,8},{10,11... | collective-permute-start | bytes 1277960 | tf_op jit(solution)/shard_map/ppermute | solution.py:294
  39.5 7.5 %collective-permute-start.7 = (bf16[128,1664]{1,0:T(8,128)(2,1)S(1)}, bf16[128,1664]{1,0:T(8,128)(2,1)S(1)}, u32[]{:S(2)}, u32[]{:S(2)}) collective-permute-start(bf16[128,1664]{1,0:T(8,128)(2,1)S(1)} %collective-permute-done.1.refs_2_), channel_id=1, source_target_pairs={{0,1},{1,0},{2,3},{3,2},{4,5},{5,4},{6,7},{7,6},{8,9},{9,8},{10,11... | collective-permute-start | bytes 1277960 | tf_op jit(solution)/shard_map/ppermute | solution.py:294
  46.4 1.8 %collective-permute-start.12 = (bf16[128,1664]{1,0:T(8,128)(2,1)S(1)}, bf16[128,1664]{1,0:T(8,128)(2,1)S(1)}, u32[]{:S(2)}, u32[]{:S(2)}) collective-permute-start(bf16[128,1664]{1,0:T(8,128)(2,1)S(1)} %collective-permute-done.10.refs_0_), channel_id=1, source_target_pairs={{0,1},{1,0},{2,3},{3,2},{4,5},{5,4},{6,7},{7,6},{8,9},{9,8},{10,11... | collective-permute-start | bytes 1277960 | tf_op jit(solution)/shard_map/ppermute | solution.py:294
  46.5 2.4 %collective-permute-start.13 = (bf16[128,1664]{1,0:T(8,128)(2,1)S(1)}, bf16[128,1664]{1,0:T(8,128)(2,1)S(1)}, u32[]{:S(2)}, u32[]{:S(2)}) collective-permute-start(bf16[128,1664]{1,0:T(8,128)(2,1)S(1)} %collective-permute-done.11.refs_2_), channel_id=1, source_target_pairs={{0,1},{1,0},{2,3},{3,2},{4,5},{5,4},{6,7},{7,6},{8,9},{9,8},{10,11... | collective-permute-start | bytes 1277960 | tf_op jit(solution)/shard_map/ppermute | solution.py:294
  53.8 4.0 %collective-permute-start.15 = (bf16[4,64,1664]{2,1,0:T(8,128)(2,1)S(1)}, bf16[4,64,1664]{2,1,0:T(8,128)(2,1)S(1)}, u32[]{:S(2)}, u32[]{:S(2)}) collective-permute-start(bf16[4,64,1664]{2,1,0:T(8,128)(2,1)S(1)} %get-tuple-element.66), channel_id=1, source_target_pairs={{0,1},{1,0},{2,3},{3,2},{4,5},{5,4},{6,7},{7,6},{8,9},{9,8},{10,11... | collective-permute-start | bytes 2555912 | tf_op jit(solution)/shard_map/ppermute | solution.py:294
  56.3 32.7 %copy-start.1 = (bf16[1,128,1664]{2,1,0:T(8,128)(2,1)S(1)}, bf16[1,128,1664]{2,1,0:T(8,128)(2,1)}, u32[]{:S(2)}) copy-start(bf16[1,128,1664]{2,1,0:T(8,128)(2,1)} %param.3) | copy-start | bytes 1277956
  56.3 32.7 %copy-start.3 = (bf16[1,128,1664]{2,1,0:T(8,128)(2,1)S(1)}, bf16[1,128,1664]{2,1,0:T(8,128)(2,1)}, u32[]{:S(2)}) copy-start(bf16[1,128,1664]{2,1,0:T(8,128)(2,1)} %param.4) | copy-start | bytes 1277956
  56.3 18.1 %collective-permute-start.14 = (bf16[4,688,128]{2,1,0:T(8,128)(2,1)S(1)}, bf16[4,688,128]{2,1,0:T(8,128)(2,1)S(1)}, u32[]{:S(2)}, u32[]{:S(2)}) collective-permute-start(bf16[4,688,128]{2,1,0:T(8,128)(2,1)S(1)} %get-tuple-element.64), channel_id=1, source_target_pairs={{0,2},{2,0},{1,3},{3,1},{4,6},{6,4},{5,7},{7,5},{8,10},{10,8},{9,1... | collective-permute-start | bytes 2113544 | tf_op jit(solution)/shard_map/ppermute | solution.py:294
  58.0 19.3 %collective-permute-start.16 = (bf16[64,1664]{1,0:T(8,128)(2,1)S(1)}, bf16[64,1664]{1,0:T(8,128)(2,1)S(1)}, u32[]{:S(2)}, u32[]{:S(2)}) collective-permute-start(bf16[64,1664]{1,0:T(8,128)(2,1)S(1)} %get-tuple-element.69), channel_id=1, source_target_pairs={{0,4},{4,0},{8,12},{12,8},{1,5},{5,1},{9,13},{13,9},{2,6},{6,2},{1... | collective-permute-start | bytes 638984 | tf_op jit(solution)/shard_map/ppermute | solution.py:291
  58.5 19.7 %collective-permute-start.17 = (bf16[64,1664]{1,0:T(8,128)(2,1)S(1)}, bf16[64,1664]{1,0:T(8,128)(2,1)S(1)}, u32[]{:S(2)}, u32[]{:S(2)}) collective-permute-start(bf16[64,1664]{1,0:T(8,128)(2,1)S(1)} %get-tuple-element.70), channel_id=1, source_target_pairs={{0,8},{4,12},{8,0},{12,4},{1,9},{5,13},{9,1},{13,5},{2,10},{6,14},... | collective-permute-start | bytes 638984 | tf_op jit(solution)/shard_map/ppermute | solution.py:291
  60.8 28.1 %collective-permute-start.18 = (bf16[64,1664]{1,0:T(8,128)(2,1)S(1)}, bf16[64,1664]{1,0:T(8,128)(2,1)S(1)}, u32[]{:S(2)}, u32[]{:S(2)}) collective-permute-start(bf16[64,1664]{1,0:T(8,128)(2,1)S(1)} %get-tuple-element.71), channel_id=1, source_target_pairs={{0,12},{4,8},{8,4},{12,0},{1,13},{5,9},{9,5},{13,1},{2,14},{6,10},... | collective-permute-start | bytes 638984 | tf_op jit(solution)/shard_map/ppermute | solution.py:291
  74.6 15.4 %collective-permute-start.21 = (bf16[688,128]{1,0:T(8,128)(2,1)S(1)}, bf16[688,128]{1,0:T(8,128)(2,1)S(1)}, u32[]{:S(2)}, u32[]{:S(2)}) collective-permute-start(bf16[688,128]{1,0:T(8,128)(2,1)S(1)} %get-tuple-element.77), channel_id=1, source_target_pairs={{0,4},{4,0},{8,12},{12,8},{1,5},{5,1},{9,13},{13,9},{2,6},{6,2},{1... | collective-permute-start | bytes 528392 | tf_op jit(solution)/shard_map/ppermute | solution.py:291
  75.0 16.5 %collective-permute-start.22 = (bf16[688,128]{1,0:T(8,128)(2,1)S(1)}, bf16[688,128]{1,0:T(8,128)(2,1)S(1)}, u32[]{:S(2)}, u32[]{:S(2)}) collective-permute-start(bf16[688,128]{1,0:T(8,128)(2,1)S(1)} %get-tuple-element.78), channel_id=1, source_target_pairs={{0,8},{4,12},{8,0},{12,4},{1,9},{5,13},{9,1},{13,5},{2,10},{6,14},... | collective-permute-start | bytes 528392 | tf_op jit(solution)/shard_map/ppermute | solution.py:291
  77.4 18.0 %collective-permute-start.23 = (bf16[688,128]{1,0:T(8,128)(2,1)S(1)}, bf16[688,128]{1,0:T(8,128)(2,1)S(1)}, u32[]{:S(2)}, u32[]{:S(2)}) collective-permute-start(bf16[688,128]{1,0:T(8,128)(2,1)S(1)} %get-tuple-element.79), channel_id=1, source_target_pairs={{0,12},{4,8},{8,4},{12,0},{1,13},{5,9},{9,5},{13,1},{2,14},{6,10},... | collective-permute-start | bytes 528392 | tf_op jit(solution)/shard_map/ppermute | solution.py:291
  89.4 6.0 %collective-permute-start.19 = (bf16[32,1664]{1,0:T(8,128)(2,1)S(1)}, bf16[32,1664]{1,0:T(8,128)(2,1)S(1)}, u32[]{:S(2)}, u32[]{:S(2)}) collective-permute-start(bf16[32,1664]{1,0:T(8,128)(2,1)S(1)} %get-tuple-element.72.refs_0_), channel_id=1, source_target_pairs={{0,1},{1,0},{2,3},{3,2},{4,5},{5,4},{6,7},{7,6},{8,9},{9,8},{10,11... | collective-permute-start | bytes 319496 | tf_op jit(solution)/shard_map/ppermute | solution.py:294
  89.5 5.9 %collective-permute-start.20 = (bf16[32,1664]{1,0:T(8,128)(2,1)S(1)}, bf16[32,1664]{1,0:T(8,128)(2,1)S(1)}, u32[]{:S(2)}, u32[]{:S(2)}) collective-permute-start(bf16[32,1664]{1,0:T(8,128)(2,1)S(1)} %get-tuple-element.73.refs_1_), channel_id=1, source_target_pairs={{0,1},{1,0},{2,3},{3,2},{4,5},{5,4},{6,7},{7,6},{8,9},{9,8},{10,11... | collective-permute-start | bytes 319496 | tf_op jit(solution)/shard_map/ppermute | solution.py:294

commit v7 on v6

--- a/solution.py
+++ b/solution.py
@@ -40,6 +40,7 @@
 
 
 SPARE = SLOT - HD
+ORDER = (0, 2, 3, 1)
 LEFT = HD - 3 * SPARE
 FOLD = SLOT // LEFT
 
@@ -88,8 +89,8 @@
         for j, tile in enumerate(packed(mats)):
             staged[head, j * share : j * share + tile.shape[0], :] = tile
     first = pl.multiple_of(group * (staged.shape[1] - count), 16)
-    for k in range(n):
-        outs[k][...] = staged[me ^ k, pl.ds(first, count), :]
+    for out, k in zip(outs, ORDER):
+        out[...] = staged[me ^ k, pl.ds(first, count), :]
 
 
 def weights_kernel(n, share, *refs):
@@ -122,7 +123,7 @@
 
 def merge_kernel(*refs):
     share = refs[0].shape[0]
-    for k, ref in enumerate(refs[:-1]):
+    for k, ref in zip(ORDER, refs[:-1]):
         refs[-1][k * share : (k + 1) * share] = ref[...]
 
 
@@ -222,9 +223,9 @@
                 target[k, j * share : j * share + tile.shape[0], :] = tile
 
 
-def sum_kernel(n, mine_ref, theirs_ref, *outs):
-    for k in range(n):
-        outs[k][...] = (mine_ref[k].astype(F32) + theirs_ref[k].astype(F32)).astype(BF)
+def sum_kernel(mine_ref, theirs_ref, *outs):
+    for out, k in zip(outs, ORDER):
+        out[...] = (mine_ref[k].astype(F32) + theirs_ref[k].astype(F32)).astype(BF)
 
 
 def final_kernel(n, x_ref, up_ref, *refs):
@@ -254,8 +255,8 @@
         side = core if i < 2 else 1 - core
         first = pl.multiple_of((2 * side + i % 2) * count, count)
         input_ref[pl.ds(first, count), :] = ref[...]
-    for k in range(n):
-        staged[me ^ k] = parts[k][...]
+    for part, k in zip(parts, ORDER):
+        staged[me ^ k] = part[...]
     for head in range(n):
         for mat, block in enumerate(unpacked(staged.at[head], out_ref.shape[1])):
             out_ref[mat, :, head * HD : (head + 1) * HD] = block.astype(F32)
@@ -290,6 +291,9 @@
     def across(value, k):
         return lax.ppermute(value, "seq", [(i, i ^ k) for i in range(n)])
 
+    def exchange(values):
+        return [across(value, k) for value, k in zip(values[1:], ORDER[1:])]
+
     def swap(value, axis):
         return lax.ppermute(value, axis, [(0, 1), (1, 0)])
 
@@ -302,11 +306,10 @@
         [pltpu.VMEM((n, full, SLOT), BF)],
         plain=1,
     )
-    arrived = [across(chunks[k], k) for k in range(1, n)]
+    arrived = exchange(chunks)
     send, rest = call(
         norm_kernel, [((rows, width), BF)] * 2, (x, up), [pltpu.VMEM((rows, width), BF)], plain=2
     )
-    send, arrived[0] = lax.optimization_barrier((send, arrived[0]))
     merged = call(merge_kernel, ((n * count, SLOT), BF), (chunks[0], *arrived))
     beside = swap(merged, "dp")
     above = swap(merged, "grp")
@@ -350,13 +353,13 @@
     )
     taken = swap(give, "pipe")
     w_taken = swap(w_give, "dp")
-    sums = call(functools.partial(sum_kernel, n), [((half, width), BF)] * n, (keep, taken))
-    parts = [across(sums[k], k) for k in range(1, n)]
+    sums = call(sum_kernel, [((half, width), BF)] * n, (keep, taken))
+    parts = exchange(sums)
     w_taken, sums[0] = lax.optimization_barrier((w_taken, sums[0]))
     w_sums = call(
-        functools.partial(sum_kernel, n), [((full, SLOT), BF)] * n, (w_keep, w_taken)
-    )
-    w_parts = [w_sums[0]] + [across(w_sums[k], k) for k in range(1, n)]
+        sum_kernel, [((full, SLOT), BF)] * n, (w_keep, w_taken)
+    )
+    w_parts = [w_sums[0]] + exchange(w_sums)
     mine = call(
         functools.partial(final_kernel, n),
         [((half // 2, width), BF)] * 2,

time: 97.5 us -> 98.1 us (level)
  starting transfers between devices: 27.2 us -> 31.1 us
  waiting for transfers between devices: 53.2 us -> 49.9 us
    ppermute x11, waiting for transfers between devices: 24.8 us -> 20.6 us  [swap(): return lax.ppermute(value, axis, [(0, 1), (1, 0)])]
    ppermute x11, starting transfers between devices: 14.2 us -> 16.5 us  [across(): return lax.ppermute(value, 'seq', [(i, i ^ k) for i in range(n)])]
    ppermute x1, starting transfers between devices: 3.66 us -> 4.87 us  [local_heads(): middle = lax.ppermute(later, 'seq', [(1, 2), (2, 1)])]
where the time goes in v7:
time: 98.1 us; the launch traced here: 97.8 us
  waiting for transfers between devices  49.9 us (51%)
  starting transfers between devices  31.1 us (32%)
  Pallas kernels  12.9 us (13%)
  local copies, waits for them, and re-layouts  3.18 us (3%)
    ppermute x11, waiting for transfers between devices, across(): return lax.ppermute(value, 'seq', [(i, i ^ k) for i in range(n)])  29.2 us
    ppermute x11, waiting for transfers between devices, swap(): return lax.ppermute(value, axis, [(0, 1), (1, 0)])  20.6 us
    ppermute x11, starting transfers between devices, across(): return lax.ppermute(value, 'seq', [(i, i ^ k) for i in range(n)])  16.5 us
    pallas_call x11, Pallas kernels, call(): pl.pallas_call(kernel, out_shape=[out_space(*s) for s in shapes], in_spec...  12.9 us
    ppermute x11, starting transfers between devices, swap(): return lax.ppermute(value, axis, [(0, 1), (1, 0)])  8.43 us
    ppermute x1, starting transfers between devices, local_heads(): middle = lax.ppermute(later, 'seq', [(1, 2), (2, 1)])  4.87 us
    unnamed x10, local copies, waits for them, and re-layouts  3.18 us
  transfers between devices with their start and end apart: 24, of which 11 were waited for; matrix products, arithmetic and copies ran while one was open for 0% of the time, Pallas kernels for 6%

profile of v7, /device:TPU:8, one launch (start us, length us, event | category | flops | bytes accessed | tf_op | source)
XLA Modules:
  0.0 97.8 jit_solution(13920253050921180505)
XLA Ops:
  0.6 1.1 %copy-done.4 = bf16[4,208,416]{2,1,0:T(8,128)(2,1)S(1)} copy-done((bf16[4,208,416]{2,1,0:T(8,128)(2,1)S(1)}, bf16[4,208,416]{2,1,0:T(8,128)(2,1)}, u32[]{:S(2)}) %copy-start.4) | copy-done | bytes 692248
  1.8 0.6 shard_map.51
  2.4 2.7 %collective-permute-start.2 = (bf16[352,128]{1,0:T(8,128)(2,1)S(1)}, bf16[352,128]{1,0:T(8,128)(2,1)S(1)}, u32[]{:S(2)}, u32[]{:S(2)}) collective-permute-start(bf16[352,128]{1,0:T(8,128)(2,1)S(1)} %get-tuple-element.43), channel_id=1, source_target_pairs={{0,8},{4,12},{8,0},{12,4},{1,9},{5,13},{9,1},{13,5},{2,10},{6,14},... | collective-permute-start | bytes 270344 | tf_op jit(solution)/shard_map/ppermute | solution.py:292
  5.0 1.8 %collective-permute-start.4 = (bf16[352,128]{1,0:T(8,128)(2,1)S(1)}, bf16[352,128]{1,0:T(8,128)(2,1)S(1)}, u32[]{:S(2)}, u32[]{:S(2)}) collective-permute-start(bf16[352,128]{1,0:T(8,128)(2,1)S(1)} %get-tuple-element.45), channel_id=1, source_target_pairs={{0,4},{4,0},{8,12},{12,8},{1,5},{5,1},{9,13},{13,9},{2,6},{6,2},{1... | collective-permute-start | bytes 270344 | tf_op jit(solution)/shard_map/ppermute | solution.py:292
  6.8 1.0 %copy-done = bf16[1,128,1664]{2,1,0:T(8,128)(2,1)S(1)} copy-done((bf16[1,128,1664]{2,1,0:T(8,128)(2,1)S(1)}, bf16[1,128,1664]{2,1,0:T(8,128)(2,1)}, u32[]{:S(2)}) %copy-start) | copy-done | bytes 426008
  7.8 1.0 %copy-done.2 = bf16[1,128,1664]{2,1,0:T(8,128)(2,1)S(1)} copy-done((bf16[1,128,1664]{2,1,0:T(8,128)(2,1)S(1)}, bf16[1,128,1664]{2,1,0:T(8,128)(2,1)}, u32[]{:S(2)}) %copy-start.2) | copy-done | bytes 426008
  8.8 0.3 shard_map.50
  9.2 1.8 %collective-permute-start.1 = (bf16[128,1664]{1,0:T(8,128)(2,1)S(1)}, bf16[128,1664]{1,0:T(8,128)(2,1)S(1)}, u32[]{:S(2)}, u32[]{:S(2)}) collective-permute-start(bf16[128,1664]{1,0:T(8,128)(2,1)S(1)} %get-tuple-element.50.refs_0_), channel_id=1, source_target_pairs={{0,8},{4,12},{8,0},{12,4},{1,9},{5,13},{9,1},{13,5},{2,10},{6,14},... | collective-permute-start | bytes 1277960 | tf_op jit(solution)/shard_map/ppermute | solution.py:292
  10.9 1.3 %collective-permute-start = (bf16[128,1664]{1,0:T(8,128)(2,1)S(1)}, bf16[128,1664]{1,0:T(8,128)(2,1)S(1)}, u32[]{:S(2)}, u32[]{:S(2)}) collective-permute-start(bf16[128,1664]{1,0:T(8,128)(2,1)S(1)} %get-tuple-element.50.refs_0_), channel_id=1, source_target_pairs={{0,4},{4,0},{8,12},{12,8},{1,5},{5,1},{9,13},{13,9},{2,6},{6,2},{1... | collective-permute-start | bytes 1277960 | tf_op jit(solution)/shard_map/ppermute | solution.py:292
  12.3 9.4 %collective-permute-done.3.refs_2_ = bf16[352,128]{1,0:T(8,128)(2,1)S(1)} collective-permute-done((bf16[352,128]{1,0:T(8,128)(2,1)S(1)}, bf16[352,128]{1,0:T(8,128)(2,1)S(1)}, u32[]{:S(2)}, u32[]{:S(2)}) %collective-permute-start.3) | collective-permute-done | bytes 90144 | tf_op jit(solution)/shard_map/ppermute | solution.py:292
  21.7 2.0 %collective-permute-start.6 = (bf16[1408,128]{1,0:T(8,128)(2,1)S(1)}, bf16[1408,128]{1,0:T(8,128)(2,1)S(1)}, u32[]{:S(2)}, u32[]{:S(2)}) collective-permute-start(bf16[1408,128]{1,0:T(8,128)(2,1)S(1)} %shard_map.52.refs_0_), channel_id=1, source_target_pairs={{0,16},{16,0},{1,17},{17,1},{2,18},{18,2},{3,19},{19,3},{4,20},{20... | collective-permute-start | bytes 1081352 | tf_op jit(solution)/shard_map/ppermute | solution.py:298
  23.6 1.5 %collective-permute-start.5 = (bf16[1408,128]{1,0:T(8,128)(2,1)S(1)}, bf16[1408,128]{1,0:T(8,128)(2,1)S(1)}, u32[]{:S(2)}, u32[]{:S(2)}) collective-permute-start(bf16[1408,128]{1,0:T(8,128)(2,1)S(1)} %shard_map.52.refs_0_), channel_id=1, source_target_pairs={{0,2},{2,0},{1,3},{3,1},{4,6},{6,4},{5,7},{7,5},{8,10},{10,8},{9,1... | collective-permute-start | bytes 1081352 | tf_op jit(solution)/shard_map/ppermute | solution.py:298
  25.1 5.7 %collective-permute-done.1.refs_4_ = bf16[128,1664]{1,0:T(8,128)(2,1)S(1)} collective-permute-done((bf16[128,1664]{1,0:T(8,128)(2,1)S(1)}, bf16[128,1664]{1,0:T(8,128)(2,1)S(1)}, u32[]{:S(2)}, u32[]{:S(2)}) %collective-permute-start.1) | collective-permute-done | bytes 426016 | tf_op jit(solution)/shard_map/ppermute | solution.py:292
  30.9 0.4 collective-permute-done.6.refs_2_
  31.3 1.2 %collective-permute-done.5.refs_1_ = bf16[1408,128]{1,0:T(8,128)(2,1)S(1)} collective-permute-done((bf16[1408,128]{1,0:T(8,128)(2,1)S(1)}, bf16[1408,128]{1,0:T(8,128)(2,1)S(1)}, u32[]{:S(2)}, u32[]{:S(2)}) %collective-permute-start.5) | collective-permute-done | bytes 360480 | tf_op jit(solution)/shard_map/ppermute | solution.py:298
  32.5 4.9 %collective-permute-start.10 = (bf16[128,1664]{1,0:T(8,128)(2,1)S(1)}, bf16[128,1664]{1,0:T(8,128)(2,1)S(1)}, u32[]{:S(2)}, u32[]{:S(2)}) collective-permute-start(bf16[128,1664]{1,0:T(8,128)(2,1)S(1)} %get-tuple-element.50.refs_0_), channel_id=1, source_target_pairs={{4,8},{8,4},{5,9},{9,5},{6,10},{10,6},{7,11},{11,7},{20,24},{24,20... | collective-permute-start | bytes 1277960 | tf_op jit(solution)/shard_map/ppermute | solution.py:328
  37.4 1.3 %collective-permute-start.11 = (bf16[128,1664]{1,0:T(8,128)(2,1)S(1)}, bf16[128,1664]{1,0:T(8,128)(2,1)S(1)}, u32[]{:S(2)}, u32[]{:S(2)}) collective-permute-start(bf16[128,1664]{1,0:T(8,128)(2,1)S(1)} %collective-permute-done.1.refs_4_), channel_id=1, source_target_pairs={{8,12},{4,0},{9,13},{5,1},{10,14},{6,2},{11,15},{7,3},{24,28},{20,... | collective-permute-start | bytes 1277960 | tf_op jit(solution)/shard_map/ppermute | solution.py:329
  38.7 1.6 %collective-permute-start.9 = (bf16[1408,128]{1,0:T(8,128)(2,1)S(1)}, bf16[1408,128]{1,0:T(8,128)(2,1)S(1)}, u32[]{:S(2)}, u32[]{:S(2)}) collective-permute-start(bf16[1408,128]{1,0:T(8,128)(2,1)S(1)} %collective-permute-done.6.refs_2_), channel_id=1, source_target_pairs={{0,2},{2,0},{1,3},{3,1},{4,6},{6,4},{5,7},{7,5},{8,10},{10,8},{9,1... | collective-permute-start | bytes 1081352 | tf_op jit(solution)/shard_map/ppermute | solution.py:298
  40.3 0.5 collective-permute-start.7
  40.8 6.4 %collective-permute-done.9.refs_3_ = bf16[1408,128]{1,0:T(8,128)(2,1)S(1)} collective-permute-done((bf16[1408,128]{1,0:T(8,128)(2,1)S(1)}, bf16[1408,128]{1,0:T(8,128)(2,1)S(1)}, u32[]{:S(2)}, u32[]{:S(2)}) %collective-permute-start.9) | collective-permute-done | bytes 360480 | tf_op jit(solution)/shard_map/ppermute | solution.py:298
  47.2 0.9 shard_map.53.refs_6_.refs_5_
  48.1 0.1 collective-permute-start.12
  48.2 0.5 collective-permute-start.13
  48.7 1.2 %shard_map.54 = (bf16[384,1664]{1,0:T(8,128)(2,1)S(1)}, bf16[384,1664]{1,0:T(8,128)(2,1)S(1)}, bf16[384,512]{1,0:T(8,128)(2,1)S(1)}) custom-call(bf16[128,1664]{1,0:T(8,128)(2,1)S(1)} %get-tuple-element.50.refs_0_, bf16[128,1664]{1,0:T(8,128)(2,1)S(1)} %get-tuple-element.41.refs_1_, bf16[128,1664]{1,0:T(8,128)(2,1)S(1)} %collective-permute-done.refs_2_, ...), custom_call_target="tpu_custom_call" | custom-call | tf_op jit(solution)/shard_map/pallas_call | solution.py:271
  49.9 0.1 collective-permute-done.12.refs_1_
  50.0 0.6 collective-permute-done.13.refs_3_
  50.6 4.9 %shard_map.55 = (bf16[4,64,1664]{2,1,0:T(8,128)(2,1)S(1)}, bf16[4,64,1664]{2,1,0:T(8,128)(2,1)S(1)}, bf16[512,512]{1,0:T(8,128)(2,1)S(1)}, bf16[128,1664]{1,0:T(8,128)(2,1)S(1)}, bf16[128,1664]{1,0:T(8,128)(2,1)S(1)}) custom-call(bf16[128,1664]{1,0:T(8,128)(2,1)S(1)} %collective-permute-done.10.refs_0_, ...), custom_call_target="tpu_custom_call" | custom-call | tf_op jit(solution)/shard_map/pallas_call | solution.py:271
  55.5 0.2 collective-permute-start.15
  55.7 2.2 %shard_map.56 = (bf16[4,688,128]{2,1,0:T(8,128)(2,1)S(1)}, bf16[4,688,128]{2,1,0:T(8,128)(2,1)S(1)}) custom-call(bf16[384,1664]{1,0:T(8,128)(2,1)S(1)} %get-tuple-element.52.x_ref, bf16[128,1664]{1,0:T(8,128)(2,1)S(1)} %get-tuple-element.56.x_last, bf16[384,1664]{1,0:T(8,128)(2,1)S(1)} %get-tuple-element.57.up_ref, ...), custom_call_target="tpu_custom_call" | custom-call | tf_op jit(solution)/shard_map/pallas_call | solution.py:271
  58.0 0.0 copy-start.1
  58.0 0.0 copy-start.3
  58.0 1.6 %collective-permute-start.14 = (bf16[4,688,128]{2,1,0:T(8,128)(2,1)S(1)}, bf16[4,688,128]{2,1,0:T(8,128)(2,1)S(1)}, u32[]{:S(2)}, u32[]{:S(2)}) collective-permute-start(bf16[4,688,128]{2,1,0:T(8,128)(2,1)S(1)} %get-tuple-element.60), channel_id=1, source_target_pairs={{0,2},{2,0},{1,3},{3,1},{4,6},{6,4},{5,7},{7,5},{8,10},{10,8},{9,1... | collective-permute-start | bytes 2113544 | tf_op jit(solution)/shard_map/ppermute | solution.py:298
  59.6 0.2 shard_map.57
  59.8 0.4 collective-permute-start.16
  60.2 1.7 %collective-permute-start.17 = (bf16[64,1664]{1,0:T(8,128)(2,1)S(1)}, bf16[64,1664]{1,0:T(8,128)(2,1)S(1)}, u32[]{:S(2)}, u32[]{:S(2)}) collective-permute-start(bf16[64,1664]{1,0:T(8,128)(2,1)S(1)} %get-tuple-element.66), channel_id=1, source_target_pairs={{0,12},{4,8},{8,4},{12,0},{1,13},{5,9},{9,5},{13,1},{2,14},{6,10},... | collective-permute-start | bytes 638984 | tf_op jit(solution)/shard_map/ppermute | solution.py:292
  61.9 2.4 %collective-permute-start.18 = (bf16[64,1664]{1,0:T(8,128)(2,1)S(1)}, bf16[64,1664]{1,0:T(8,128)(2,1)S(1)}, u32[]{:S(2)}, u32[]{:S(2)}) collective-permute-start(bf16[64,1664]{1,0:T(8,128)(2,1)S(1)} %get-tuple-element.67), channel_id=1, source_target_pairs={{0,4},{4,0},{8,12},{12,8},{1,5},{5,1},{9,13},{13,9},{2,6},{6,2},{1... | collective-permute-start | bytes 638984 | tf_op jit(solution)/shard_map/ppermute | solution.py:292
  64.2 11.9 %collective-permute-done.14.theirs_ref = bf16[4,688,128]{2,1,0:T(8,128)(2,1)S(1)} collective-permute-done((bf16[4,688,128]{2,1,0:T(8,128)(2,1)S(1)}, bf16[4,688,128]{2,1,0:T(8,128)(2,1)S(1)}, u32[]{:S(2)}, u32[]{:S(2)}) %collective-permute-start.14) | collective-permute-done | bytes 704544 | tf_op jit(solution)/shard_map/ppermute | solution.py:298
  76.1 0.2 shard_map.59
  76.3 0.4 collective-permute-start.21
  76.7 1.7 %collective-permute-start.22 = (bf16[688,128]{1,0:T(8,128)(2,1)S(1)}, bf16[688,128]{1,0:T(8,128)(2,1)S(1)}, u32[]{:S(2)}, u32[]{:S(2)}) collective-permute-start(bf16[688,128]{1,0:T(8,128)(2,1)S(1)} %get-tuple-element.74), channel_id=1, source_target_pairs={{0,12},{4,8},{8,4},{12,0},{1,13},{5,9},{9,5},{13,1},{2,14},{6,10},... | collective-permute-start | bytes 528392 | tf_op jit(solution)/shard_map/ppermute | solution.py:292
  78.4 2.4 %collective-permute-start.23 = (bf16[688,128]{1,0:T(8,128)(2,1)S(1)}, bf16[688,128]{1,0:T(8,128)(2,1)S(1)}, u32[]{:S(2)}, u32[]{:S(2)}) collective-permute-start(bf16[688,128]{1,0:T(8,128)(2,1)S(1)} %get-tuple-element.75), channel_id=1, source_target_pairs={{0,4},{4,0},{8,12},{12,8},{1,5},{5,1},{9,13},{13,9},{2,6},{6,2},{1... | collective-permute-start | bytes 528392 | tf_op jit(solution)/shard_map/ppermute | solution.py:292
  80.7 8.5 %collective-permute-done.17.refs_2_ = bf16[64,1664]{1,0:T(8,128)(2,1)S(1)} collective-permute-done((bf16[64,1664]{1,0:T(8,128)(2,1)S(1)}, bf16[64,1664]{1,0:T(8,128)(2,1)S(1)}, u32[]{:S(2)}, u32[]{:S(2)}) %collective-permute-start.17) | collective-permute-done | bytes 213024 | tf_op jit(solution)/shard_map/ppermute | solution.py:292
  89.3 0.5 shard_map.58
  89.7 0.1 collective-permute-start.19
  89.8 0.5 collective-permute-start.20
  90.3 0.6 collective-permute-done.21.refs_5_
  90.9 5.0 %collective-permute-done.22.refs_6_ = bf16[688,128]{1,0:T(8,128)(2,1)S(1)} collective-permute-done((bf16[688,128]{1,0:T(8,128)(2,1)S(1)}, bf16[688,128]{1,0:T(8,128)(2,1)S(1)}, u32[]{:S(2)}, u32[]{:S(2)}) %collective-permute-start.22) | collective-permute-done | bytes 176160 | tf_op jit(solution)/shard_map/ppermute | solution.py:292
  95.9 1.9 %shard_map.60 = (bf16[128,1664]{1,0:T(8,128)(2,1)}, f32[4,208,416]{2,1,0:T(8,128)}) custom-call(bf16[32,1664]{1,0:T(8,128)(2,1)S(1)} %get-tuple-element.68.refs_0_, bf16[32,1664]{1,0:T(8,128)(2,1)S(1)} %get-tuple-element.69.refs_1_, bf16[32,1664]{1,0:T(8,128)(2,1)S(1)} %collective-permute-done.19.refs_2_, ...), custom_call_target="tpu_custom_call" | custom-call | tf_op jit(solution)/shard_map/pallas_call | solution.py:271
  (21 shorter events, 0.1 us)
Async XLA Ops:
  0.6 1.2 %copy-start.4 = (bf16[4,208,416]{2,1,0:T(8,128)(2,1)S(1)}, bf16[4,208,416]{2,1,0:T(8,128)(2,1)}, u32[]{:S(2)}) copy-start(bf16[4,208,416]{2,1,0:T(8,128)(2,1)} %w_ref.1) | copy-start | bytes 2076676
  2.4 9.9 %collective-permute-start.2 = (bf16[352,128]{1,0:T(8,128)(2,1)S(1)}, bf16[352,128]{1,0:T(8,128)(2,1)S(1)}, u32[]{:S(2)}, u32[]{:S(2)}) collective-permute-start(bf16[352,128]{1,0:T(8,128)(2,1)S(1)} %get-tuple-element.43), channel_id=1, source_target_pairs={{0,8},{4,12},{8,0},{12,4},{1,9},{5,13},{9,1},{13,5},{2,10},{6,14},... | collective-permute-start | bytes 270344 | tf_op jit(solution)/shard_map/ppermute | solution.py:292
  5.0 16.6 %collective-permute-start.3 = (bf16[352,128]{1,0:T(8,128)(2,1)S(1)}, bf16[352,128]{1,0:T(8,128)(2,1)S(1)}, u32[]{:S(2)}, u32[]{:S(2)}) collective-permute-start(bf16[352,128]{1,0:T(8,128)(2,1)S(1)} %get-tuple-element.44), channel_id=1, source_target_pairs={{0,12},{4,8},{8,4},{12,0},{1,13},{5,9},{9,5},{13,1},{2,14},{6,10},... | collective-permute-start | bytes 270344 | tf_op jit(solution)/shard_map/ppermute | solution.py:292
  5.0 16.6 %collective-permute-start.4 = (bf16[352,128]{1,0:T(8,128)(2,1)S(1)}, bf16[352,128]{1,0:T(8,128)(2,1)S(1)}, u32[]{:S(2)}, u32[]{:S(2)}) collective-permute-start(bf16[352,128]{1,0:T(8,128)(2,1)S(1)} %get-tuple-element.45), channel_id=1, source_target_pairs={{0,4},{4,0},{8,12},{12,8},{1,5},{5,1},{9,13},{13,9},{2,6},{6,2},{1... | collective-permute-start | bytes 270344 | tf_op jit(solution)/shard_map/ppermute | solution.py:292
  6.8 1.0 %copy-start = (bf16[1,128,1664]{2,1,0:T(8,128)(2,1)S(1)}, bf16[1,128,1664]{2,1,0:T(8,128)(2,1)}, u32[]{:S(2)}) copy-start(bf16[1,128,1664]{2,1,0:T(8,128)(2,1)} %param.3) | copy-start | bytes 1277956
  7.8 1.0 %copy-start.2 = (bf16[1,128,1664]{2,1,0:T(8,128)(2,1)S(1)}, bf16[1,128,1664]{2,1,0:T(8,128)(2,1)}, u32[]{:S(2)}) copy-start(bf16[1,128,1664]{2,1,0:T(8,128)(2,1)} %param.4) | copy-start | bytes 1277956
  9.2 21.7 %collective-permute-start.1 = (bf16[128,1664]{1,0:T(8,128)(2,1)S(1)}, bf16[128,1664]{1,0:T(8,128)(2,1)S(1)}, u32[]{:S(2)}, u32[]{:S(2)}) collective-permute-start(bf16[128,1664]{1,0:T(8,128)(2,1)S(1)} %get-tuple-element.50.refs_0_), channel_id=1, source_target_pairs={{0,8},{4,12},{8,0},{12,4},{1,9},{5,13},{9,1},{13,5},{2,10},{6,14},... | collective-permute-start | bytes 1277960 | tf_op jit(solution)/shard_map/ppermute | solution.py:292
  10.9 19.9 %collective-permute-start = (bf16[128,1664]{1,0:T(8,128)(2,1)S(1)}, bf16[128,1664]{1,0:T(8,128)(2,1)S(1)}, u32[]{:S(2)}, u32[]{:S(2)}) collective-permute-start(bf16[128,1664]{1,0:T(8,128)(2,1)S(1)} %get-tuple-element.50.refs_0_), channel_id=1, source_target_pairs={{0,4},{4,0},{8,12},{12,8},{1,5},{5,1},{9,13},{13,9},{2,6},{6,2},{1... | collective-permute-start | bytes 1277960 | tf_op jit(solution)/shard_map/ppermute | solution.py:292
  21.7 9.6 %collective-permute-start.6 = (bf16[1408,128]{1,0:T(8,128)(2,1)S(1)}, bf16[1408,128]{1,0:T(8,128)(2,1)S(1)}, u32[]{:S(2)}, u32[]{:S(2)}) collective-permute-start(bf16[1408,128]{1,0:T(8,128)(2,1)S(1)} %shard_map.52.refs_0_), channel_id=1, source_target_pairs={{0,16},{16,0},{1,17},{17,1},{2,18},{18,2},{3,19},{19,3},{4,20},{20... | collective-permute-start | bytes 1081352 | tf_op jit(solution)/shard_map/ppermute | solution.py:298
  23.6 8.8 %collective-permute-start.5 = (bf16[1408,128]{1,0:T(8,128)(2,1)S(1)}, bf16[1408,128]{1,0:T(8,128)(2,1)S(1)}, u32[]{:S(2)}, u32[]{:S(2)}) collective-permute-start(bf16[1408,128]{1,0:T(8,128)(2,1)S(1)} %shard_map.52.refs_0_), channel_id=1, source_target_pairs={{0,2},{2,0},{1,3},{3,1},{4,6},{6,4},{5,7},{7,5},{8,10},{10,8},{9,1... | collective-permute-start | bytes 1081352 | tf_op jit(solution)/shard_map/ppermute | solution.py:298
  32.5 15.6 %collective-permute-start.10 = (bf16[128,1664]{1,0:T(8,128)(2,1)S(1)}, bf16[128,1664]{1,0:T(8,128)(2,1)S(1)}, u32[]{:S(2)}, u32[]{:S(2)}) collective-permute-start(bf16[128,1664]{1,0:T(8,128)(2,1)S(1)} %get-tuple-element.50.refs_0_), channel_id=1, source_target_pairs={{4,8},{8,4},{5,9},{9,5},{6,10},{10,6},{7,11},{11,7},{20,24},{24,20... | collective-permute-start | bytes 1277960 | tf_op jit(solution)/shard_map/ppermute | solution.py:328
  37.4 10.8 %collective-permute-start.11 = (bf16[128,1664]{1,0:T(8,128)(2,1)S(1)}, bf16[128,1664]{1,0:T(8,128)(2,1)S(1)}, u32[]{:S(2)}, u32[]{:S(2)}) collective-permute-start(bf16[128,1664]{1,0:T(8,128)(2,1)S(1)} %collective-permute-done.1.refs_4_), channel_id=1, source_target_pairs={{8,12},{4,0},{9,13},{5,1},{10,14},{6,2},{11,15},{7,3},{24,28},{20,... | collective-permute-start | bytes 1277960 | tf_op jit(solution)/shard_map/ppermute | solution.py:329
  38.7 8.5 %collective-permute-start.9 = (bf16[1408,128]{1,0:T(8,128)(2,1)S(1)}, bf16[1408,128]{1,0:T(8,128)(2,1)S(1)}, u32[]{:S(2)}, u32[]{:S(2)}) collective-permute-start(bf16[1408,128]{1,0:T(8,128)(2,1)S(1)} %collective-permute-done.6.refs_2_), channel_id=1, source_target_pairs={{0,2},{2,0},{1,3},{3,1},{4,6},{6,4},{5,7},{7,5},{8,10},{10,8},{9,1... | collective-permute-start | bytes 1081352 | tf_op jit(solution)/shard_map/ppermute | solution.py:298
  40.3 8.5 %collective-permute-start.8 = (bf16[128,1664]{1,0:T(8,128)(2,1)S(1)}, bf16[128,1664]{1,0:T(8,128)(2,1)S(1)}, u32[]{:S(2)}, u32[]{:S(2)}) collective-permute-start(bf16[128,1664]{1,0:T(8,128)(2,1)S(1)} %collective-permute-done.1.refs_4_), channel_id=1, source_target_pairs={{0,1},{1,0},{2,3},{3,2},{4,5},{5,4},{6,7},{7,6},{8,9},{9,8},{10,11... | collective-permute-start | bytes 1277960 | tf_op jit(solution)/shard_map/ppermute | solution.py:298
  40.3 8.5 %collective-permute-start.7 = (bf16[128,1664]{1,0:T(8,128)(2,1)S(1)}, bf16[128,1664]{1,0:T(8,128)(2,1)S(1)}, u32[]{:S(2)}, u32[]{:S(2)}) collective-permute-start(bf16[128,1664]{1,0:T(8,128)(2,1)S(1)} %collective-permute-done.refs_2_), channel_id=1, source_target_pairs={{0,1},{1,0},{2,3},{3,2},{4,5},{5,4},{6,7},{7,6},{8,9},{9,8},{10,11... | collective-permute-start | bytes 1277960 | tf_op jit(solution)/shard_map/ppermute | solution.py:298
  48.1 1.8 %collective-permute-start.12 = (bf16[128,1664]{1,0:T(8,128)(2,1)S(1)}, bf16[128,1664]{1,0:T(8,128)(2,1)S(1)}, u32[]{:S(2)}, u32[]{:S(2)}) collective-permute-start(bf16[128,1664]{1,0:T(8,128)(2,1)S(1)} %collective-permute-done.10.refs_0_), channel_id=1, source_target_pairs={{0,1},{1,0},{2,3},{3,2},{4,5},{5,4},{6,7},{7,6},{8,9},{9,8},{10,11... | collective-permute-start | bytes 1277960 | tf_op jit(solution)/shard_map/ppermute | solution.py:298
  48.2 2.4 %collective-permute-start.13 = (bf16[128,1664]{1,0:T(8,128)(2,1)S(1)}, bf16[128,1664]{1,0:T(8,128)(2,1)S(1)}, u32[]{:S(2)}, u32[]{:S(2)}) collective-permute-start(bf16[128,1664]{1,0:T(8,128)(2,1)S(1)} %collective-permute-done.11.refs_2_), channel_id=1, source_target_pairs={{0,1},{1,0},{2,3},{3,2},{4,5},{5,4},{6,7},{7,6},{8,9},{9,8},{10,11... | collective-permute-start | bytes 1277960 | tf_op jit(solution)/shard_map/ppermute | solution.py:298
  55.5 4.0 %collective-permute-start.15 = (bf16[4,64,1664]{2,1,0:T(8,128)(2,1)S(1)}, bf16[4,64,1664]{2,1,0:T(8,128)(2,1)S(1)}, u32[]{:S(2)}, u32[]{:S(2)}) collective-permute-start(bf16[4,64,1664]{2,1,0:T(8,128)(2,1)S(1)} %get-tuple-element.62), channel_id=1, source_target_pairs={{0,1},{1,0},{2,3},{3,2},{4,5},{5,4},{6,7},{7,6},{8,9},{9,8},{10,11... | collective-permute-start | bytes 2555912 | tf_op jit(solution)/shard_map/ppermute | solution.py:298
  58.0 31.3 %copy-start.1 = (bf16[1,128,1664]{2,1,0:T(8,128)(2,1)S(1)}, bf16[1,128,1664]{2,1,0:T(8,128)(2,1)}, u32[]{:S(2)}) copy-start(bf16[1,128,1664]{2,1,0:T(8,128)(2,1)} %param.3) | copy-start | bytes 1277956
  58.0 31.3 %copy-start.3 = (bf16[1,128,1664]{2,1,0:T(8,128)(2,1)S(1)}, bf16[1,128,1664]{2,1,0:T(8,128)(2,1)}, u32[]{:S(2)}) copy-start(bf16[1,128,1664]{2,1,0:T(8,128)(2,1)} %param.4) | copy-start | bytes 1277956
  58.0 18.1 %collective-permute-start.14 = (bf16[4,688,128]{2,1,0:T(8,128)(2,1)S(1)}, bf16[4,688,128]{2,1,0:T(8,128)(2,1)S(1)}, u32[]{:S(2)}, u32[]{:S(2)}) collective-permute-start(bf16[4,688,128]{2,1,0:T(8,128)(2,1)S(1)} %get-tuple-element.60), channel_id=1, source_target_pairs={{0,2},{2,0},{1,3},{3,1},{4,6},{6,4},{5,7},{7,5},{8,10},{10,8},{9,1... | collective-permute-start | bytes 2113544 | tf_op jit(solution)/shard_map/ppermute | solution.py:298
  59.8 18.6 %collective-permute-start.16 = (bf16[64,1664]{1,0:T(8,128)(2,1)S(1)}, bf16[64,1664]{1,0:T(8,128)(2,1)S(1)}, u32[]{:S(2)}, u32[]{:S(2)}) collective-permute-start(bf16[64,1664]{1,0:T(8,128)(2,1)S(1)} %get-tuple-element.65), channel_id=1, source_target_pairs={{0,8},{4,12},{8,0},{12,4},{1,9},{5,13},{9,1},{13,5},{2,10},{6,14},... | collective-permute-start | bytes 638984 | tf_op jit(solution)/shard_map/ppermute | solution.py:292
  60.2 29.0 %collective-permute-start.17 = (bf16[64,1664]{1,0:T(8,128)(2,1)S(1)}, bf16[64,1664]{1,0:T(8,128)(2,1)S(1)}, u32[]{:S(2)}, u32[]{:S(2)}) collective-permute-start(bf16[64,1664]{1,0:T(8,128)(2,1)S(1)} %get-tuple-element.66), channel_id=1, source_target_pairs={{0,12},{4,8},{8,4},{12,0},{1,13},{5,9},{9,5},{13,1},{2,14},{6,10},... | collective-permute-start | bytes 638984 | tf_op jit(solution)/shard_map/ppermute | solution.py:292
  61.9 27.4 %collective-permute-start.18 = (bf16[64,1664]{1,0:T(8,128)(2,1)S(1)}, bf16[64,1664]{1,0:T(8,128)(2,1)S(1)}, u32[]{:S(2)}, u32[]{:S(2)}) collective-permute-start(bf16[64,1664]{1,0:T(8,128)(2,1)S(1)} %get-tuple-element.67), channel_id=1, source_target_pairs={{0,4},{4,0},{8,12},{12,8},{1,5},{5,1},{9,13},{13,9},{2,6},{6,2},{1... | collective-permute-start | bytes 638984 | tf_op jit(solution)/shard_map/ppermute | solution.py:292
  76.3 14.6 %collective-permute-start.21 = (bf16[688,128]{1,0:T(8,128)(2,1)S(1)}, bf16[688,128]{1,0:T(8,128)(2,1)S(1)}, u32[]{:S(2)}, u32[]{:S(2)}) collective-permute-start(bf16[688,128]{1,0:T(8,128)(2,1)S(1)} %get-tuple-element.73), channel_id=1, source_target_pairs={{0,8},{4,12},{8,0},{12,4},{1,9},{5,13},{9,1},{13,5},{2,10},{6,14},... | collective-permute-start | bytes 528392 | tf_op jit(solution)/shard_map/ppermute | solution.py:292
  76.7 19.2 %collective-permute-start.22 = (bf16[688,128]{1,0:T(8,128)(2,1)S(1)}, bf16[688,128]{1,0:T(8,128)(2,1)S(1)}, u32[]{:S(2)}, u32[]{:S(2)}) collective-permute-start(bf16[688,128]{1,0:T(8,128)(2,1)S(1)} %get-tuple-element.74), channel_id=1, source_target_pairs={{0,12},{4,8},{8,4},{12,0},{1,13},{5,9},{9,5},{13,1},{2,14},{6,10},... | collective-permute-start | bytes 528392 | tf_op jit(solution)/shard_map/ppermute | solution.py:292
  78.4 17.5 %collective-permute-start.23 = (bf16[688,128]{1,0:T(8,128)(2,1)S(1)}, bf16[688,128]{1,0:T(8,128)(2,1)S(1)}, u32[]{:S(2)}, u32[]{:S(2)}) collective-permute-start(bf16[688,128]{1,0:T(8,128)(2,1)S(1)} %get-tuple-element.75), channel_id=1, source_target_pairs={{0,4},{4,0},{8,12},{12,8},{1,5},{5,1},{9,13},{13,9},{2,6},{6,2},{1... | collective-permute-start | bytes 528392 | tf_op jit(solution)/shard_map/ppermute | solution.py:292
  89.7 6.2 %collective-permute-start.19 = (bf16[32,1664]{1,0:T(8,128)(2,1)S(1)}, bf16[32,1664]{1,0:T(8,128)(2,1)S(1)}, u32[]{:S(2)}, u32[]{:S(2)}) collective-permute-start(bf16[32,1664]{1,0:T(8,128)(2,1)S(1)} %get-tuple-element.68.refs_0_), channel_id=1, source_target_pairs={{0,1},{1,0},{2,3},{3,2},{4,5},{5,4},{6,7},{7,6},{8,9},{9,8},{10,11... | collective-permute-start | bytes 319496 | tf_op jit(solution)/shard_map/ppermute | solution.py:298
  89.8 6.1 %collective-permute-start.20 = (bf16[32,1664]{1,0:T(8,128)(2,1)S(1)}, bf16[32,1664]{1,0:T(8,128)(2,1)S(1)}, u32[]{:S(2)}, u32[]{:S(2)}) collective-permute-start(bf16[32,1664]{1,0:T(8,128)(2,1)S(1)} %get-tuple-element.69.refs_1_), channel_id=1, source_target_pairs={{0,1},{1,0},{2,3},{3,2},{4,5},{5,4},{6,7},{7,6},{8,9},{9,8},{10,11... | collective-permute-start | bytes 319496 | tf_op jit(solution)/shard_map/ppermute | solution.py:298

commit v8 on v7

--- a/solution.py
+++ b/solution.py
@@ -89,7 +89,7 @@
         for j, tile in enumerate(packed(mats)):
             staged[head, j * share : j * share + tile.shape[0], :] = tile
     first = pl.multiple_of(group * (staged.shape[1] - count), 16)
-    for out, k in zip(outs, ORDER):
+    for k, out in enumerate(outs):
         out[...] = staged[me ^ k, pl.ds(first, count), :]
 
 
@@ -123,7 +123,7 @@
 
 def merge_kernel(*refs):
     share = refs[0].shape[0]
-    for k, ref in zip(ORDER, refs[:-1]):
+    for k, ref in enumerate(refs[:-1]):
         refs[-1][k * share : (k + 1) * share] = ref[...]
 
 
@@ -172,21 +172,20 @@
     scale = HD ** (-0.5)
     key_rows = made[:, SLOT : 2 * SLOT]
     value_rows = made[:, 2 * SLOT : 3 * SLOT]
+    grad_out_all = made[:, 3 * SLOT :]
+    scores = nt(made[:, :SLOT], key_rows) * scale
+    weight = jnp.exp(scores - jnp.max(scores, axis=1, keepdims=True))
+    probs_all = (weight / jnp.sum(weight, axis=1, keepdims=True)).astype(BF)
+    attended = nn(probs_all, value_rows).astype(BF)
+    delta = jnp.sum(grad_out_all.astype(F32) * attended.astype(F32), axis=1, keepdims=True)
+    dprobs = nt(grad_out_all, value_rows)
+    dscores_all = (probs_all.astype(F32) * (dprobs - delta) * scale).astype(BF)
+    grads[:, :SLOT] = nn(dscores_all, key_rows).astype(BF)
+    grads[:, 3 * SLOT :] = attended
     for b in range(n):
         span = slice(b * rows, (b + 1) * rows)
-        query = made[span, :SLOT]
-        grad_out = made[span, 3 * SLOT :]
-        scores = nt(query, key_rows) * scale
-        weight = jnp.exp(scores - jnp.max(scores, axis=1, keepdims=True))
-        probs = (weight / jnp.sum(weight, axis=1, keepdims=True)).astype(BF)
-        attended = nn(probs, value_rows).astype(BF)
-        delta = jnp.sum(grad_out.astype(F32) * attended.astype(F32), axis=1, keepdims=True)
-        dprobs = nt(grad_out, value_rows)
-        dscores = (probs.astype(F32) * (dprobs - delta) * scale).astype(BF)
-        grads[span, :SLOT] = nn(dscores, key_rows).astype(BF)
-        grads[span, 3 * SLOT :] = attended
-        key_term = tn(dscores, query).astype(BF).astype(F32)
-        value_term = tn(probs, grad_out).astype(BF).astype(F32)
+        key_term = tn(dscores_all[span], made[span, :SLOT]).astype(BF).astype(F32)
+        value_term = tn(probs_all[span], made[span, 3 * SLOT :]).astype(BF).astype(F32)
         if b == 0:
             term_k[...] = key_term
             term_v[...] = value_term
@@ -195,9 +194,9 @@
             term_v[...] += value_term
     grads[:, SLOT : 2 * SLOT] = term_k[...].astype(BF)
     grads[:, 2 * SLOT : 3 * SLOT] = term_v[...].astype(BF)
+    whole = nt(grads[:, : 3 * SLOT], w_ref[:, : 3 * SLOT]).astype(BF)
     for b in range(n):
-        span = slice(b * rows, (b + 1) * rows)
-        part = nt(grads[span, : 3 * SLOT], w_ref[:, : 3 * SLOT]).astype(BF)
+        part = whole[b * rows : (b + 1) * rows]
         keep_ref[b] = part[:half]
         give_ref[b] = part[half:]
 
@@ -306,10 +305,11 @@
         [pltpu.VMEM((n, full, SLOT), BF)],
         plain=1,
     )
-    arrived = exchange(chunks)
+    arrived = [across(chunks[k], k) for k in range(1, n)]
     send, rest = call(
         norm_kernel, [((rows, width), BF)] * 2, (x, up), [pltpu.VMEM((rows, width), BF)], plain=2
     )
+    send, arrived[0] = lax.optimization_barrier((send, arrived[0]))
     merged = call(merge_kernel, ((n * count, SLOT), BF), (chunks[0], *arrived))
     beside = swap(merged, "dp")
     above = swap(merged, "grp")

time: 98.1 us -> 94 us (0.958)
  starting transfers between devices: 31.1 us -> 29 us
  Pallas kernels: 12.9 us -> 10.8 us
    ppermute x11, waiting for transfers between devices: 20.6 us -> 23.9 us  [swap(): return lax.ppermute(value, axis, [(0, 1), (1, 0)])]
    ppermute x11, waiting for transfers between devices: 29.2 us -> 26 us  [across(): return lax.ppermute(value, 'seq', [(i, i ^ k) for i in range(n)])]
    pallas_call x11, Pallas kernels: 12.9 us -> 10.8 us  [call(): pl.pallas_call(kernel, out_shape=[out_space(*s) for s in shapes], in_spec...]
    ppermute x1, starting transfers between devices: 4.87 us -> 3.66 us  [local_heads(): middle = lax.ppermute(later, 'seq', [(1, 2), (2, 1)])]
where the time goes in v8:
time: 94 us; the launch traced here: 93.7 us
  waiting for transfers between devices  49.9 us (53%)
  starting transfers between devices  29 us (31%)
  Pallas kernels  10.8 us (11%)
  local copies, waits for them, and re-layouts  3.18 us (3%)
    ppermute x11, waiting for transfers between devices, across(): return lax.ppermute(value, 'seq', [(i, i ^ k) for i in range(n)])  26 us
    ppermute x11, waiting for transfers between devices, swap(): return lax.ppermute(value, axis, [(0, 1), (1, 0)])  23.9 us
    ppermute x11, starting transfers between devices, across(): return lax.ppermute(value, 'seq', [(i, i ^ k) for i in range(n)])  16 us
    pallas_call x11, Pallas kernels, call(): pl.pallas_call(kernel, out_shape=[out_space(*s) for s in shapes], in_spec...  10.8 us
    ppermute x11, starting transfers between devices, swap(): return lax.ppermute(value, axis, [(0, 1), (1, 0)])  8.05 us
    ppermute x1, starting transfers between devices, local_heads(): middle = lax.ppermute(later, 'seq', [(1, 2), (2, 1)])  3.66 us
    unnamed x10, local copies, waits for them, and re-layouts  3.18 us
  transfers between devices with their start and end apart: 24, of which 11 were waited for; matrix products, arithmetic and copies ran while one was open for 0% of the time, Pallas kernels for 6%

profile of v8, /device:TPU:8, one launch (start us, length us, event | category | flops | bytes accessed | tf_op | source)
XLA Modules:
  0.0 93.7 jit_solution(7211551383004647554)
XLA Ops:
  0.6 1.1 %copy-done.4 = bf16[4,208,416]{2,1,0:T(8,128)(2,1)S(1)} copy-done((bf16[4,208,416]{2,1,0:T(8,128)(2,1)S(1)}, bf16[4,208,416]{2,1,0:T(8,128)(2,1)}, u32[]{:S(2)}) %copy-start.4) | copy-done | bytes 692248
  1.8 0.6 shard_map.51
  2.4 0.1 collective-permute-start
  2.4 3.0 %collective-permute-start.3 = (bf16[352,128]{1,0:T(8,128)(2,1)S(1)}, bf16[352,128]{1,0:T(8,128)(2,1)S(1)}, u32[]{:S(2)}, u32[]{:S(2)}) collective-permute-start(bf16[352,128]{1,0:T(8,128)(2,1)S(1)} %get-tuple-element.48), channel_id=1, source_target_pairs={{0,8},{4,12},{8,0},{12,4},{1,9},{5,13},{9,1},{13,5},{2,10},{6,14},... | collective-permute-start | bytes 270344 | tf_op jit(solution)/shard_map/ppermute | solution.py:291
  5.5 0.5 collective-permute-start.4
  5.9 1.0 %copy-done = bf16[1,128,1664]{2,1,0:T(8,128)(2,1)S(1)} copy-done((bf16[1,128,1664]{2,1,0:T(8,128)(2,1)S(1)}, bf16[1,128,1664]{2,1,0:T(8,128)(2,1)}, u32[]{:S(2)}) %copy-start) | copy-done | bytes 426008
  6.9 1.0 %copy-done.2 = bf16[1,128,1664]{2,1,0:T(8,128)(2,1)S(1)} copy-done((bf16[1,128,1664]{2,1,0:T(8,128)(2,1)S(1)}, bf16[1,128,1664]{2,1,0:T(8,128)(2,1)}, u32[]{:S(2)}) %copy-start.2) | copy-done | bytes 426008
  7.9 0.3 shard_map.50
  8.3 3.6 %collective-permute-start.2 = (bf16[128,1664]{1,0:T(8,128)(2,1)S(1)}, bf16[128,1664]{1,0:T(8,128)(2,1)S(1)}, u32[]{:S(2)}, u32[]{:S(2)}) collective-permute-start(bf16[128,1664]{1,0:T(8,128)(2,1)S(1)} %get-tuple-element.54.refs_0_), channel_id=1, source_target_pairs={{0,8},{4,12},{8,0},{12,4},{1,9},{5,13},{9,1},{13,5},{2,10},{6,14},... | collective-permute-start | bytes 1277960 | tf_op jit(solution)/shard_map/ppermute | solution.py:291
  11.8 9.0 %collective-permute-done.3.refs_2_ = bf16[352,128]{1,0:T(8,128)(2,1)S(1)} collective-permute-done((bf16[352,128]{1,0:T(8,128)(2,1)S(1)}, bf16[352,128]{1,0:T(8,128)(2,1)S(1)}, u32[]{:S(2)}, u32[]{:S(2)}) %collective-permute-start.3) | collective-permute-done | bytes 90144 | tf_op jit(solution)/shard_map/ppermute | solution.py:291
  20.8 3.1 %collective-permute-done.4.refs_3_ = bf16[352,128]{1,0:T(8,128)(2,1)S(1)} collective-permute-done((bf16[352,128]{1,0:T(8,128)(2,1)S(1)}, bf16[352,128]{1,0:T(8,128)(2,1)S(1)}, u32[]{:S(2)}, u32[]{:S(2)}) %collective-permute-start.4) | collective-permute-done | bytes 90144 | tf_op jit(solution)/shard_map/ppermute | solution.py:291
  24.0 1.6 %collective-permute-start.6 = (bf16[1408,128]{1,0:T(8,128)(2,1)S(1)}, bf16[1408,128]{1,0:T(8,128)(2,1)S(1)}, u32[]{:S(2)}, u32[]{:S(2)}) collective-permute-start(bf16[1408,128]{1,0:T(8,128)(2,1)S(1)} %shard_map.52.refs_0_), channel_id=1, source_target_pairs={{0,16},{16,0},{1,17},{17,1},{2,18},{18,2},{3,19},{19,3},{4,20},{20... | collective-permute-start | bytes 1081352 | tf_op jit(solution)/shard_map/ppermute | solution.py:297
  25.6 1.5 %collective-permute-start.5 = (bf16[1408,128]{1,0:T(8,128)(2,1)S(1)}, bf16[1408,128]{1,0:T(8,128)(2,1)S(1)}, u32[]{:S(2)}, u32[]{:S(2)}) collective-permute-start(bf16[1408,128]{1,0:T(8,128)(2,1)S(1)} %shard_map.52.refs_0_), channel_id=1, source_target_pairs={{0,2},{2,0},{1,3},{3,1},{4,6},{6,4},{5,7},{7,5},{8,10},{10,8},{9,1... | collective-permute-start | bytes 1081352 | tf_op jit(solution)/shard_map/ppermute | solution.py:297
  27.0 4.5 %collective-permute-done.6.refs_2_ = bf16[1408,128]{1,0:T(8,128)(2,1)S(1)} collective-permute-done((bf16[1408,128]{1,0:T(8,128)(2,1)S(1)}, bf16[1408,128]{1,0:T(8,128)(2,1)S(1)}, u32[]{:S(2)}, u32[]{:S(2)}) %collective-permute-start.6) | collective-permute-done | bytes 360480 | tf_op jit(solution)/shard_map/ppermute | solution.py:297
  31.6 1.4 %collective-permute-done.5.refs_1_ = bf16[1408,128]{1,0:T(8,128)(2,1)S(1)} collective-permute-done((bf16[1408,128]{1,0:T(8,128)(2,1)S(1)}, bf16[1408,128]{1,0:T(8,128)(2,1)S(1)}, u32[]{:S(2)}, u32[]{:S(2)}) %collective-permute-start.5) | collective-permute-done | bytes 360480 | tf_op jit(solution)/shard_map/ppermute | solution.py:297
  33.0 3.7 %collective-permute-start.10 = (bf16[128,1664]{1,0:T(8,128)(2,1)S(1)}, bf16[128,1664]{1,0:T(8,128)(2,1)S(1)}, u32[]{:S(2)}, u32[]{:S(2)}) collective-permute-start(bf16[128,1664]{1,0:T(8,128)(2,1)S(1)} %get-tuple-element.54.refs_0_), channel_id=1, source_target_pairs={{4,8},{8,4},{5,9},{9,5},{6,10},{10,6},{7,11},{11,7},{20,24},{24,20... | collective-permute-start | bytes 1277960 | tf_op jit(solution)/shard_map/ppermute | solution.py:328
  36.7 1.3 %collective-permute-start.11 = (bf16[128,1664]{1,0:T(8,128)(2,1)S(1)}, bf16[128,1664]{1,0:T(8,128)(2,1)S(1)}, u32[]{:S(2)}, u32[]{:S(2)}) collective-permute-start(bf16[128,1664]{1,0:T(8,128)(2,1)S(1)} %collective-permute-done.2.refs_4_), channel_id=1, source_target_pairs={{8,12},{4,0},{9,13},{5,1},{10,14},{6,2},{11,15},{7,3},{24,28},{20,... | collective-permute-start | bytes 1277960 | tf_op jit(solution)/shard_map/ppermute | solution.py:329
  38.0 1.6 %collective-permute-start.9 = (bf16[1408,128]{1,0:T(8,128)(2,1)S(1)}, bf16[1408,128]{1,0:T(8,128)(2,1)S(1)}, u32[]{:S(2)}, u32[]{:S(2)}) collective-permute-start(bf16[1408,128]{1,0:T(8,128)(2,1)S(1)} %collective-permute-done.6.refs_2_), channel_id=1, source_target_pairs={{0,2},{2,0},{1,3},{3,1},{4,6},{6,4},{5,7},{7,5},{8,10},{10,8},{9,1... | collective-permute-start | bytes 1081352 | tf_op jit(solution)/shard_map/ppermute | solution.py:297
  39.5 0.5 collective-permute-start.7
  40.1 5.4 %collective-permute-done.9.refs_3_ = bf16[1408,128]{1,0:T(8,128)(2,1)S(1)} collective-permute-done((bf16[1408,128]{1,0:T(8,128)(2,1)S(1)}, bf16[1408,128]{1,0:T(8,128)(2,1)S(1)}, u32[]{:S(2)}, u32[]{:S(2)}) %collective-permute-start.9) | collective-permute-done | bytes 360480 | tf_op jit(solution)/shard_map/ppermute | solution.py:297
  45.5 0.9 shard_map.53.refs_6_.refs_5_
  46.4 0.1 collective-permute-start.12
  46.5 0.5 collective-permute-start.13
  47.0 1.2 %shard_map.54 = (bf16[384,1664]{1,0:T(8,128)(2,1)S(1)}, bf16[384,1664]{1,0:T(8,128)(2,1)S(1)}, bf16[384,512]{1,0:T(8,128)(2,1)S(1)}) custom-call(bf16[128,1664]{1,0:T(8,128)(2,1)S(1)} %get-tuple-element.54.refs_0_, bf16[128,1664]{1,0:T(8,128)(2,1)S(1)} %get-tuple-element.45.refs_1_, bf16[128,1664]{1,0:T(8,128)(2,1)S(1)} %collective-permute-done.1.refs_2_, ...), custom_call_target="tpu_custom_call" | custom-call | tf_op jit(solution)/shard_map/pallas_call | solution.py:270
  48.2 0.1 collective-permute-done.12.refs_1_
  48.3 0.6 collective-permute-done.13.refs_3_
  48.9 2.8 %shard_map.55 = (bf16[4,64,1664]{2,1,0:T(8,128)(2,1)S(1)}, bf16[4,64,1664]{2,1,0:T(8,128)(2,1)S(1)}, bf16[512,512]{1,0:T(8,128)(2,1)S(1)}, bf16[128,1664]{1,0:T(8,128)(2,1)S(1)}, bf16[128,1664]{1,0:T(8,128)(2,1)S(1)}) custom-call(bf16[128,1664]{1,0:T(8,128)(2,1)S(1)} %collective-permute-done.10.refs_0_, ...), custom_call_target="tpu_custom_call" | custom-call | tf_op jit(solution)/shard_map/pallas_call | solution.py:270
  51.7 0.2 collective-permute-start.15
  51.9 2.2 %shard_map.56 = (bf16[4,688,128]{2,1,0:T(8,128)(2,1)S(1)}, bf16[4,688,128]{2,1,0:T(8,128)(2,1)S(1)}) custom-call(bf16[384,1664]{1,0:T(8,128)(2,1)S(1)} %get-tuple-element.56.x_ref, bf16[128,1664]{1,0:T(8,128)(2,1)S(1)} %get-tuple-element.60.x_last, bf16[384,1664]{1,0:T(8,128)(2,1)S(1)} %get-tuple-element.61.up_ref, ...), custom_call_target="tpu_custom_call" | custom-call | tf_op jit(solution)/shard_map/pallas_call | solution.py:270
  54.1 0.0 copy-start.1
  54.2 0.0 copy-start.3
  54.2 1.6 %collective-permute-start.14 = (bf16[4,688,128]{2,1,0:T(8,128)(2,1)S(1)}, bf16[4,688,128]{2,1,0:T(8,128)(2,1)S(1)}, u32[]{:S(2)}, u32[]{:S(2)}) collective-permute-start(bf16[4,688,128]{2,1,0:T(8,128)(2,1)S(1)} %get-tuple-element.64), channel_id=1, source_target_pairs={{0,2},{2,0},{1,3},{3,1},{4,6},{6,4},{5,7},{7,5},{8,10},{10,8},{9,1... | collective-permute-start | bytes 2113544 | tf_op jit(solution)/shard_map/ppermute | solution.py:297
  55.7 0.2 shard_map.57
  55.9 1.3 %collective-permute-start.16 = (bf16[64,1664]{1,0:T(8,128)(2,1)S(1)}, bf16[64,1664]{1,0:T(8,128)(2,1)S(1)}, u32[]{:S(2)}, u32[]{:S(2)}) collective-permute-start(bf16[64,1664]{1,0:T(8,128)(2,1)S(1)} %get-tuple-element.69), channel_id=1, source_target_pairs={{0,8},{4,12},{8,0},{12,4},{1,9},{5,13},{9,1},{13,5},{2,10},{6,14},... | collective-permute-start | bytes 638984 | tf_op jit(solution)/shard_map/ppermute | solution.py:291
  57.3 0.5 collective-permute-start.17
  57.8 2.6 %collective-permute-start.18 = (bf16[64,1664]{1,0:T(8,128)(2,1)S(1)}, bf16[64,1664]{1,0:T(8,128)(2,1)S(1)}, u32[]{:S(2)}, u32[]{:S(2)}) collective-permute-start(bf16[64,1664]{1,0:T(8,128)(2,1)S(1)} %get-tuple-element.71), channel_id=1, source_target_pairs={{0,4},{4,0},{8,12},{12,8},{1,5},{5,1},{9,13},{13,9},{2,6},{6,2},{1... | collective-permute-start | bytes 638984 | tf_op jit(solution)/shard_map/ppermute | solution.py:291
  60.4 11.9 %collective-permute-done.14.theirs_ref = bf16[4,688,128]{2,1,0:T(8,128)(2,1)S(1)} collective-permute-done((bf16[4,688,128]{2,1,0:T(8,128)(2,1)S(1)}, bf16[4,688,128]{2,1,0:T(8,128)(2,1)S(1)}, u32[]{:S(2)}, u32[]{:S(2)}) %collective-permute-start.14) | collective-permute-done | bytes 704544 | tf_op jit(solution)/shard_map/ppermute | solution.py:297
  72.3 0.2 shard_map.59
  72.5 1.3 %collective-permute-start.21 = (bf16[688,128]{1,0:T(8,128)(2,1)S(1)}, bf16[688,128]{1,0:T(8,128)(2,1)S(1)}, u32[]{:S(2)}, u32[]{:S(2)}) collective-permute-start(bf16[688,128]{1,0:T(8,128)(2,1)S(1)} %get-tuple-element.77), channel_id=1, source_target_pairs={{0,8},{4,12},{8,0},{12,4},{1,9},{5,13},{9,1},{13,5},{2,10},{6,14},... | collective-permute-start | bytes 528392 | tf_op jit(solution)/shard_map/ppermute | solution.py:291
  73.8 0.5 collective-permute-start.22
  74.3 2.6 %collective-permute-start.23 = (bf16[688,128]{1,0:T(8,128)(2,1)S(1)}, bf16[688,128]{1,0:T(8,128)(2,1)S(1)}, u32[]{:S(2)}, u32[]{:S(2)}) collective-permute-start(bf16[688,128]{1,0:T(8,128)(2,1)S(1)} %get-tuple-element.79), channel_id=1, source_target_pairs={{0,4},{4,0},{8,12},{12,8},{1,5},{5,1},{9,13},{13,9},{2,6},{6,2},{1... | collective-permute-start | bytes 528392 | tf_op jit(solution)/shard_map/ppermute | solution.py:291
  76.9 8.3 %collective-permute-done.17.refs_2_ = bf16[64,1664]{1,0:T(8,128)(2,1)S(1)} collective-permute-done((bf16[64,1664]{1,0:T(8,128)(2,1)S(1)}, bf16[64,1664]{1,0:T(8,128)(2,1)S(1)}, u32[]{:S(2)}, u32[]{:S(2)}) %collective-permute-start.17) | collective-permute-done | bytes 213024 | tf_op jit(solution)/shard_map/ppermute | solution.py:291
  85.2 0.5 shard_map.58
  85.6 0.1 collective-permute-start.19
  85.7 0.5 collective-permute-start.20
  86.2 1.7 %collective-permute-done.21.refs_5_ = bf16[688,128]{1,0:T(8,128)(2,1)S(1)} collective-permute-done((bf16[688,128]{1,0:T(8,128)(2,1)S(1)}, bf16[688,128]{1,0:T(8,128)(2,1)S(1)}, u32[]{:S(2)}, u32[]{:S(2)}) %collective-permute-start.21) | collective-permute-done | bytes 176160 | tf_op jit(solution)/shard_map/ppermute | solution.py:291
  87.9 3.9 %collective-permute-done.22.refs_6_ = bf16[688,128]{1,0:T(8,128)(2,1)S(1)} collective-permute-done((bf16[688,128]{1,0:T(8,128)(2,1)S(1)}, bf16[688,128]{1,0:T(8,128)(2,1)S(1)}, u32[]{:S(2)}, u32[]{:S(2)}) %collective-permute-start.22) | collective-permute-done | bytes 176160 | tf_op jit(solution)/shard_map/ppermute | solution.py:291
  91.9 1.9 %shard_map.60 = (bf16[128,1664]{1,0:T(8,128)(2,1)}, f32[4,208,416]{2,1,0:T(8,128)}) custom-call(bf16[32,1664]{1,0:T(8,128)(2,1)S(1)} %get-tuple-element.72.refs_0_, bf16[32,1664]{1,0:T(8,128)(2,1)S(1)} %get-tuple-element.73.refs_1_, bf16[32,1664]{1,0:T(8,128)(2,1)S(1)} %collective-permute-done.19.refs_2_, ...), custom_call_target="tpu_custom_call" | custom-call | tf_op jit(solution)/shard_map/pallas_call | solution.py:270
  (21 shorter events, 0.1 us)
Async XLA Ops:
  0.6 1.2 %copy-start.4 = (bf16[4,208,416]{2,1,0:T(8,128)(2,1)S(1)}, bf16[4,208,416]{2,1,0:T(8,128)(2,1)}, u32[]{:S(2)}) copy-start(bf16[4,208,416]{2,1,0:T(8,128)(2,1)} %w_ref.1) | copy-start | bytes 2076676
  2.4 5.9 %collective-permute-start = (bf16[352,128]{1,0:T(8,128)(2,1)S(1)}, bf16[352,128]{1,0:T(8,128)(2,1)S(1)}, u32[]{:S(2)}, u32[]{:S(2)}) collective-permute-start(bf16[352,128]{1,0:T(8,128)(2,1)S(1)} %get-tuple-element.43), channel_id=1, source_target_pairs={{0,4},{4,0},{8,12},{12,8},{1,5},{5,1},{9,13},{13,9},{2,6},{6,2},{1... | collective-permute-start | bytes 270344 | tf_op jit(solution)/shard_map/ppermute | solution.py:291
  2.4 18.4 %collective-permute-start.3 = (bf16[352,128]{1,0:T(8,128)(2,1)S(1)}, bf16[352,128]{1,0:T(8,128)(2,1)S(1)}, u32[]{:S(2)}, u32[]{:S(2)}) collective-permute-start(bf16[352,128]{1,0:T(8,128)(2,1)S(1)} %get-tuple-element.48), channel_id=1, source_target_pairs={{0,8},{4,12},{8,0},{12,4},{1,9},{5,13},{9,1},{13,5},{2,10},{6,14},... | collective-permute-start | bytes 270344 | tf_op jit(solution)/shard_map/ppermute | solution.py:291
  5.5 18.5 %collective-permute-start.4 = (bf16[352,128]{1,0:T(8,128)(2,1)S(1)}, bf16[352,128]{1,0:T(8,128)(2,1)S(1)}, u32[]{:S(2)}, u32[]{:S(2)}) collective-permute-start(bf16[352,128]{1,0:T(8,128)(2,1)S(1)} %get-tuple-element.49), channel_id=1, source_target_pairs={{0,12},{4,8},{8,4},{12,0},{1,13},{5,9},{9,5},{13,1},{2,14},{6,10},... | collective-permute-start | bytes 270344 | tf_op jit(solution)/shard_map/ppermute | solution.py:291
  5.9 1.0 %copy-start = (bf16[1,128,1664]{2,1,0:T(8,128)(2,1)S(1)}, bf16[1,128,1664]{2,1,0:T(8,128)(2,1)}, u32[]{:S(2)}) copy-start(bf16[1,128,1664]{2,1,0:T(8,128)(2,1)} %param.3) | copy-start | bytes 1277956
  6.9 1.0 %copy-start.2 = (bf16[1,128,1664]{2,1,0:T(8,128)(2,1)S(1)}, bf16[1,128,1664]{2,1,0:T(8,128)(2,1)}, u32[]{:S(2)}) copy-start(bf16[1,128,1664]{2,1,0:T(8,128)(2,1)} %param.4) | copy-start | bytes 1277956
  8.3 24.7 %collective-permute-start.2 = (bf16[128,1664]{1,0:T(8,128)(2,1)S(1)}, bf16[128,1664]{1,0:T(8,128)(2,1)S(1)}, u32[]{:S(2)}, u32[]{:S(2)}) collective-permute-start(bf16[128,1664]{1,0:T(8,128)(2,1)S(1)} %get-tuple-element.54.refs_0_), channel_id=1, source_target_pairs={{0,8},{4,12},{8,0},{12,4},{1,9},{5,13},{9,1},{13,5},{2,10},{6,14},... | collective-permute-start | bytes 1277960 | tf_op jit(solution)/shard_map/ppermute | solution.py:291
  11.8 21.2 %collective-permute-start.1 = (bf16[128,1664]{1,0:T(8,128)(2,1)S(1)}, bf16[128,1664]{1,0:T(8,128)(2,1)S(1)}, u32[]{:S(2)}, u32[]{:S(2)}) collective-permute-start(bf16[128,1664]{1,0:T(8,128)(2,1)S(1)} %get-tuple-element.54.refs_0_), channel_id=1, source_target_pairs={{0,4},{4,0},{8,12},{12,8},{1,5},{5,1},{9,13},{13,9},{2,6},{6,2},{1... | collective-permute-start | bytes 1277960 | tf_op jit(solution)/shard_map/ppermute | solution.py:291
  24.0 7.6 %collective-permute-start.6 = (bf16[1408,128]{1,0:T(8,128)(2,1)S(1)}, bf16[1408,128]{1,0:T(8,128)(2,1)S(1)}, u32[]{:S(2)}, u32[]{:S(2)}) collective-permute-start(bf16[1408,128]{1,0:T(8,128)(2,1)S(1)} %shard_map.52.refs_0_), channel_id=1, source_target_pairs={{0,16},{16,0},{1,17},{17,1},{2,18},{18,2},{3,19},{19,3},{4,20},{20... | collective-permute-start | bytes 1081352 | tf_op jit(solution)/shard_map/ppermute | solution.py:297
  25.6 7.4 %collective-permute-start.5 = (bf16[1408,128]{1,0:T(8,128)(2,1)S(1)}, bf16[1408,128]{1,0:T(8,128)(2,1)S(1)}, u32[]{:S(2)}, u32[]{:S(2)}) collective-permute-start(bf16[1408,128]{1,0:T(8,128)(2,1)S(1)} %shard_map.52.refs_0_), channel_id=1, source_target_pairs={{0,2},{2,0},{1,3},{3,1},{4,6},{6,4},{5,7},{7,5},{8,10},{10,8},{9,1... | collective-permute-start | bytes 1081352 | tf_op jit(solution)/shard_map/ppermute | solution.py:297
  33.0 13.4 %collective-permute-start.10 = (bf16[128,1664]{1,0:T(8,128)(2,1)S(1)}, bf16[128,1664]{1,0:T(8,128)(2,1)S(1)}, u32[]{:S(2)}, u32[]{:S(2)}) collective-permute-start(bf16[128,1664]{1,0:T(8,128)(2,1)S(1)} %get-tuple-element.54.refs_0_), channel_id=1, source_target_pairs={{4,8},{8,4},{5,9},{9,5},{6,10},{10,6},{7,11},{11,7},{20,24},{24,20... | collective-permute-start | bytes 1277960 | tf_op jit(solution)/shard_map/ppermute | solution.py:328
  36.7 9.8 %collective-permute-start.11 = (bf16[128,1664]{1,0:T(8,128)(2,1)S(1)}, bf16[128,1664]{1,0:T(8,128)(2,1)S(1)}, u32[]{:S(2)}, u32[]{:S(2)}) collective-permute-start(bf16[128,1664]{1,0:T(8,128)(2,1)S(1)} %collective-permute-done.2.refs_4_), channel_id=1, source_target_pairs={{8,12},{4,0},{9,13},{5,1},{10,14},{6,2},{11,15},{7,3},{24,28},{20,... | collective-permute-start | bytes 1277960 | tf_op jit(solution)/shard_map/ppermute | solution.py:329
  38.0 7.5 %collective-permute-start.9 = (bf16[1408,128]{1,0:T(8,128)(2,1)S(1)}, bf16[1408,128]{1,0:T(8,128)(2,1)S(1)}, u32[]{:S(2)}, u32[]{:S(2)}) collective-permute-start(bf16[1408,128]{1,0:T(8,128)(2,1)S(1)} %collective-permute-done.6.refs_2_), channel_id=1, source_target_pairs={{0,2},{2,0},{1,3},{3,1},{4,6},{6,4},{5,7},{7,5},{8,10},{10,8},{9,1... | collective-permute-start | bytes 1081352 | tf_op jit(solution)/shard_map/ppermute | solution.py:297
  39.5 7.5 %collective-permute-start.8 = (bf16[128,1664]{1,0:T(8,128)(2,1)S(1)}, bf16[128,1664]{1,0:T(8,128)(2,1)S(1)}, u32[]{:S(2)}, u32[]{:S(2)}) collective-permute-start(bf16[128,1664]{1,0:T(8,128)(2,1)S(1)} %collective-permute-done.2.refs_4_), channel_id=1, source_target_pairs={{0,1},{1,0},{2,3},{3,2},{4,5},{5,4},{6,7},{7,6},{8,9},{9,8},{10,11... | collective-permute-start | bytes 1277960 | tf_op jit(solution)/shard_map/ppermute | solution.py:297
  39.5 7.5 %collective-permute-start.7 = (bf16[128,1664]{1,0:T(8,128)(2,1)S(1)}, bf16[128,1664]{1,0:T(8,128)(2,1)S(1)}, u32[]{:S(2)}, u32[]{:S(2)}) collective-permute-start(bf16[128,1664]{1,0:T(8,128)(2,1)S(1)} %collective-permute-done.1.refs_2_), channel_id=1, source_target_pairs={{0,1},{1,0},{2,3},{3,2},{4,5},{5,4},{6,7},{7,6},{8,9},{9,8},{10,11... | collective-permute-start | bytes 1277960 | tf_op jit(solution)/shard_map/ppermute | solution.py:297
  46.4 1.8 %collective-permute-start.12 = (bf16[128,1664]{1,0:T(8,128)(2,1)S(1)}, bf16[128,1664]{1,0:T(8,128)(2,1)S(1)}, u32[]{:S(2)}, u32[]{:S(2)}) collective-permute-start(bf16[128,1664]{1,0:T(8,128)(2,1)S(1)} %collective-permute-done.10.refs_0_), channel_id=1, source_target_pairs={{0,1},{1,0},{2,3},{3,2},{4,5},{5,4},{6,7},{7,6},{8,9},{9,8},{10,11... | collective-permute-start | bytes 1277960 | tf_op jit(solution)/shard_map/ppermute | solution.py:297
  46.5 2.4 %collective-permute-start.13 = (bf16[128,1664]{1,0:T(8,128)(2,1)S(1)}, bf16[128,1664]{1,0:T(8,128)(2,1)S(1)}, u32[]{:S(2)}, u32[]{:S(2)}) collective-permute-start(bf16[128,1664]{1,0:T(8,128)(2,1)S(1)} %collective-permute-done.11.refs_2_), channel_id=1, source_target_pairs={{0,1},{1,0},{2,3},{3,2},{4,5},{5,4},{6,7},{7,6},{8,9},{9,8},{10,11... | collective-permute-start | bytes 1277960 | tf_op jit(solution)/shard_map/ppermute | solution.py:297
  51.7 4.0 %collective-permute-start.15 = (bf16[4,64,1664]{2,1,0:T(8,128)(2,1)S(1)}, bf16[4,64,1664]{2,1,0:T(8,128)(2,1)S(1)}, u32[]{:S(2)}, u32[]{:S(2)}) collective-permute-start(bf16[4,64,1664]{2,1,0:T(8,128)(2,1)S(1)} %get-tuple-element.66), channel_id=1, source_target_pairs={{0,1},{1,0},{2,3},{3,2},{4,5},{5,4},{6,7},{7,6},{8,9},{9,8},{10,11... | collective-permute-start | bytes 2555912 | tf_op jit(solution)/shard_map/ppermute | solution.py:297
  54.1 31.0 %copy-start.1 = (bf16[1,128,1664]{2,1,0:T(8,128)(2,1)S(1)}, bf16[1,128,1664]{2,1,0:T(8,128)(2,1)}, u32[]{:S(2)}) copy-start(bf16[1,128,1664]{2,1,0:T(8,128)(2,1)} %param.3) | copy-start | bytes 1277956
  54.2 31.0 %copy-start.3 = (bf16[1,128,1664]{2,1,0:T(8,128)(2,1)S(1)}, bf16[1,128,1664]{2,1,0:T(8,128)(2,1)}, u32[]{:S(2)}) copy-start(bf16[1,128,1664]{2,1,0:T(8,128)(2,1)} %param.4) | copy-start | bytes 1277956
  54.2 18.1 %collective-permute-start.14 = (bf16[4,688,128]{2,1,0:T(8,128)(2,1)S(1)}, bf16[4,688,128]{2,1,0:T(8,128)(2,1)S(1)}, u32[]{:S(2)}, u32[]{:S(2)}) collective-permute-start(bf16[4,688,128]{2,1,0:T(8,128)(2,1)S(1)} %get-tuple-element.64), channel_id=1, source_target_pairs={{0,2},{2,0},{1,3},{3,1},{4,6},{6,4},{5,7},{7,5},{8,10},{10,8},{9,1... | collective-permute-start | bytes 2113544 | tf_op jit(solution)/shard_map/ppermute | solution.py:297
  55.9 18.4 %collective-permute-start.16 = (bf16[64,1664]{1,0:T(8,128)(2,1)S(1)}, bf16[64,1664]{1,0:T(8,128)(2,1)S(1)}, u32[]{:S(2)}, u32[]{:S(2)}) collective-permute-start(bf16[64,1664]{1,0:T(8,128)(2,1)S(1)} %get-tuple-element.69), channel_id=1, source_target_pairs={{0,8},{4,12},{8,0},{12,4},{1,9},{5,13},{9,1},{13,5},{2,10},{6,14},... | collective-permute-start | bytes 638984 | tf_op jit(solution)/shard_map/ppermute | solution.py:291
  57.3 27.9 %collective-permute-start.17 = (bf16[64,1664]{1,0:T(8,128)(2,1)S(1)}, bf16[64,1664]{1,0:T(8,128)(2,1)S(1)}, u32[]{:S(2)}, u32[]{:S(2)}) collective-permute-start(bf16[64,1664]{1,0:T(8,128)(2,1)S(1)} %get-tuple-element.70), channel_id=1, source_target_pairs={{0,12},{4,8},{8,4},{12,0},{1,13},{5,9},{9,5},{13,1},{2,14},{6,10},... | collective-permute-start | bytes 638984 | tf_op jit(solution)/shard_map/ppermute | solution.py:291
  57.8 27.4 %collective-permute-start.18 = (bf16[64,1664]{1,0:T(8,128)(2,1)S(1)}, bf16[64,1664]{1,0:T(8,128)(2,1)S(1)}, u32[]{:S(2)}, u32[]{:S(2)}) collective-permute-start(bf16[64,1664]{1,0:T(8,128)(2,1)S(1)} %get-tuple-element.71), channel_id=1, source_target_pairs={{0,4},{4,0},{8,12},{12,8},{1,5},{5,1},{9,13},{13,9},{2,6},{6,2},{1... | collective-permute-start | bytes 638984 | tf_op jit(solution)/shard_map/ppermute | solution.py:291
  72.5 15.5 %collective-permute-start.21 = (bf16[688,128]{1,0:T(8,128)(2,1)S(1)}, bf16[688,128]{1,0:T(8,128)(2,1)S(1)}, u32[]{:S(2)}, u32[]{:S(2)}) collective-permute-start(bf16[688,128]{1,0:T(8,128)(2,1)S(1)} %get-tuple-element.77), channel_id=1, source_target_pairs={{0,8},{4,12},{8,0},{12,4},{1,9},{5,13},{9,1},{13,5},{2,10},{6,14},... | collective-permute-start | bytes 528392 | tf_op jit(solution)/shard_map/ppermute | solution.py:291
  73.8 18.1 %collective-permute-start.22 = (bf16[688,128]{1,0:T(8,128)(2,1)S(1)}, bf16[688,128]{1,0:T(8,128)(2,1)S(1)}, u32[]{:S(2)}, u32[]{:S(2)}) collective-permute-start(bf16[688,128]{1,0:T(8,128)(2,1)S(1)} %get-tuple-element.78), channel_id=1, source_target_pairs={{0,12},{4,8},{8,4},{12,0},{1,13},{5,9},{9,5},{13,1},{2,14},{6,10},... | collective-permute-start | bytes 528392 | tf_op jit(solution)/shard_map/ppermute | solution.py:291
  74.3 17.5 %collective-permute-start.23 = (bf16[688,128]{1,0:T(8,128)(2,1)S(1)}, bf16[688,128]{1,0:T(8,128)(2,1)S(1)}, u32[]{:S(2)}, u32[]{:S(2)}) collective-permute-start(bf16[688,128]{1,0:T(8,128)(2,1)S(1)} %get-tuple-element.79), channel_id=1, source_target_pairs={{0,4},{4,0},{8,12},{12,8},{1,5},{5,1},{9,13},{13,9},{2,6},{6,2},{1... | collective-permute-start | bytes 528392 | tf_op jit(solution)/shard_map/ppermute | solution.py:291
  85.6 6.2 %collective-permute-start.19 = (bf16[32,1664]{1,0:T(8,128)(2,1)S(1)}, bf16[32,1664]{1,0:T(8,128)(2,1)S(1)}, u32[]{:S(2)}, u32[]{:S(2)}) collective-permute-start(bf16[32,1664]{1,0:T(8,128)(2,1)S(1)} %get-tuple-element.72.refs_0_), channel_id=1, source_target_pairs={{0,1},{1,0},{2,3},{3,2},{4,5},{5,4},{6,7},{7,6},{8,9},{9,8},{10,11... | collective-permute-start | bytes 319496 | tf_op jit(solution)/shard_map/ppermute | solution.py:297
  85.7 6.1 %collective-permute-start.20 = (bf16[32,1664]{1,0:T(8,128)(2,1)S(1)}, bf16[32,1664]{1,0:T(8,128)(2,1)S(1)}, u32[]{:S(2)}, u32[]{:S(2)}) collective-permute-start(bf16[32,1664]{1,0:T(8,128)(2,1)S(1)} %get-tuple-element.73.refs_1_), channel_id=1, source_target_pairs={{0,1},{1,0},{2,3},{3,2},{4,5},{5,4},{6,7},{7,6},{8,9},{9,8},{10,11... | collective-permute-start | bytes 319496 | tf_op jit(solution)/shard_map/ppermute | solution.py:297

commit v9 on v8

--- a/solution.py
+++ b/solution.py
@@ -246,19 +246,32 @@
 
 
 def join_kernel(n, *refs):
-    pairs, parts, (input_ref, out_ref, staged) = refs[:4], refs[4 : 4 + n], refs[4 + n :]
+    pairs, parts = refs[:4], refs[4 : 4 + n]
+    input_ref, out_ref, staged, joined, made, sems = refs[4 + n :]
     me = lax.axis_index("seq")
     core = lax.axis_index("pipe")
+    share = made.shape[1]
     count = pairs[0].shape[0]
     for i, ref in enumerate(pairs):
         side = core if i < 2 else 1 - core
         first = pl.multiple_of((2 * side + i % 2) * count, count)
-        input_ref[pl.ds(first, count), :] = ref[...]
+        joined[pl.ds(first, count), :] = ref[...]
+    copies = [pltpu.make_async_copy(joined, input_ref, sems.at[4])]
+    copies[0].start()
     for part, k in zip(parts, ORDER):
         staged[me ^ k] = part[...]
-    for head in range(n):
-        for mat, block in enumerate(unpacked(staged.at[head], out_ref.shape[1])):
-            out_ref[mat, :, head * HD : (head + 1) * HD] = block.astype(F32)
+    for mat in range(4):
+        for head in range(n):
+            lanes = slice(head * HD, (head + 1) * HD)
+            if mat < 3:
+                block = staged[head, mat * share : (mat + 1) * share, :HD]
+            else:
+                block = unpacked(staged.at[head], share)[3]
+            made[mat, :, lanes] = block.astype(F32)
+        copies.append(pltpu.make_async_copy(made.at[mat], out_ref.at[mat], sems.at[mat]))
+        copies[-1].start()
+    for copy in copies:
+        copy.wait()
 
 
 def call(kernel, out_shape, args, scratch=(), plain=0, out_space=pltpu.VMEM):
@@ -271,7 +284,7 @@
         kernel,
         out_shape=[out_space(*s) for s in shapes],
         in_specs=[VMEM_SPEC] * len(args),
-        out_specs=[VMEM_SPEC] * len(shapes),
+        out_specs=[VMEM_SPEC if out_space is pltpu.VMEM else ANY_SPEC] * len(shapes),
         scratch_shapes=list(scratch),
         compiler_params=PARAMS,
     )(*args)
@@ -370,7 +383,12 @@
         functools.partial(join_kernel, n),
         [((rows, width), BF), ((4, share, n * HD), F32)],
         (*mine, *[swap(m, "pipe") for m in mine], *w_parts),
-        [pltpu.VMEM((n, full, SLOT), BF)],
+        [
+            pltpu.VMEM((n, full, SLOT), BF),
+            pltpu.VMEM((rows, width), BF),
+            pltpu.VMEM((4, share, n * HD), F32),
+            pltpu.SemaphoreType.DMA((5,)),
+        ],
         out_space=jax.ShapeDtypeStruct,
     )
     return (input_gradient[None], weight_grads)

time: 94 us -> 93.8 us (level)
  no operation moved by 1% of the time
where the time goes in v9:
time: 93.8 us; the launch traced here: 93.5 us
  waiting for transfers between devices  49.9 us (53%)
  starting transfers between devices  29 us (31%)
  Pallas kernels  10.5 us (11%)
  local copies, waits for them, and re-layouts  3.18 us (3%)
    ppermute x11, waiting for transfers between devices, across(): return lax.ppermute(value, 'seq', [(i, i ^ k) for i in range(n)])  26 us
    ppermute x11, waiting for transfers between devices, swap(): return lax.ppermute(value, axis, [(0, 1), (1, 0)])  23.9 us
    ppermute x11, starting transfers between devices, across(): return lax.ppermute(value, 'seq', [(i, i ^ k) for i in range(n)])  16 us
    pallas_call x11, Pallas kernels, call(): pl.pallas_call(kernel, out_shape=[out_space(*s) for s in shapes], in_spec...  10.5 us
    ppermute x11, starting transfers between devices, swap(): return lax.ppermute(value, axis, [(0, 1), (1, 0)])  8.05 us
    ppermute x1, starting transfers between devices, local_heads(): middle = lax.ppermute(later, 'seq', [(1, 2), (2, 1)])  3.66 us
    unnamed x10, local copies, waits for them, and re-layouts  3.18 us
  transfers between devices with their start and end apart: 24, of which 11 were waited for; matrix products, arithmetic and copies ran while one was open for 0% of the time, Pallas kernels for 6%

profile of v9, /device:TPU:8, one launch (start us, length us, event | category | flops | bytes accessed | tf_op | source)
XLA Modules:
  0.0 93.5 jit_solution(14910291012452668870)
XLA Ops:
  0.6 1.1 %copy-done.4 = bf16[4,208,416]{2,1,0:T(8,128)(2,1)S(1)} copy-done((bf16[4,208,416]{2,1,0:T(8,128)(2,1)S(1)}, bf16[4,208,416]{2,1,0:T(8,128)(2,1)}, u32[]{:S(2)}) %copy-start.4) | copy-done | bytes 692248
  1.8 0.6 shard_map.51
  2.4 0.1 collective-permute-start
  2.4 3.0 %collective-permute-start.3 = (bf16[352,128]{1,0:T(8,128)(2,1)S(1)}, bf16[352,128]{1,0:T(8,128)(2,1)S(1)}, u32[]{:S(2)}, u32[]{:S(2)}) collective-permute-start(bf16[352,128]{1,0:T(8,128)(2,1)S(1)} %get-tuple-element.48), channel_id=1, source_target_pairs={{0,8},{4,12},{8,0},{12,4},{1,9},{5,13},{9,1},{13,5},{2,10},{6,14},... | collective-permute-start | bytes 270344 | tf_op jit(solution)/shard_map/ppermute | solution.py:304
  5.5 0.5 collective-permute-start.4
  5.9 1.0 %copy-done = bf16[1,128,1664]{2,1,0:T(8,128)(2,1)S(1)} copy-done((bf16[1,128,1664]{2,1,0:T(8,128)(2,1)S(1)}, bf16[1,128,1664]{2,1,0:T(8,128)(2,1)}, u32[]{:S(2)}) %copy-start) | copy-done | bytes 426008
  6.9 1.0 %copy-done.2 = bf16[1,128,1664]{2,1,0:T(8,128)(2,1)S(1)} copy-done((bf16[1,128,1664]{2,1,0:T(8,128)(2,1)S(1)}, bf16[1,128,1664]{2,1,0:T(8,128)(2,1)}, u32[]{:S(2)}) %copy-start.2) | copy-done | bytes 426008
  7.9 0.3 shard_map.50
  8.3 3.6 %collective-permute-start.2 = (bf16[128,1664]{1,0:T(8,128)(2,1)S(1)}, bf16[128,1664]{1,0:T(8,128)(2,1)S(1)}, u32[]{:S(2)}, u32[]{:S(2)}) collective-permute-start(bf16[128,1664]{1,0:T(8,128)(2,1)S(1)} %get-tuple-element.54.refs_0_), channel_id=1, source_target_pairs={{0,8},{4,12},{8,0},{12,4},{1,9},{5,13},{9,1},{13,5},{2,10},{6,14},... | collective-permute-start | bytes 1277960 | tf_op jit(solution)/shard_map/ppermute | solution.py:304
  11.8 9.0 %collective-permute-done.3.refs_2_ = bf16[352,128]{1,0:T(8,128)(2,1)S(1)} collective-permute-done((bf16[352,128]{1,0:T(8,128)(2,1)S(1)}, bf16[352,128]{1,0:T(8,128)(2,1)S(1)}, u32[]{:S(2)}, u32[]{:S(2)}) %collective-permute-start.3) | collective-permute-done | bytes 90144 | tf_op jit(solution)/shard_map/ppermute | solution.py:304
  20.8 3.1 %collective-permute-done.4.refs_3_ = bf16[352,128]{1,0:T(8,128)(2,1)S(1)} collective-permute-done((bf16[352,128]{1,0:T(8,128)(2,1)S(1)}, bf16[352,128]{1,0:T(8,128)(2,1)S(1)}, u32[]{:S(2)}, u32[]{:S(2)}) %collective-permute-start.4) | collective-permute-done | bytes 90144 | tf_op jit(solution)/shard_map/ppermute | solution.py:304
  24.0 1.6 %collective-permute-start.6 = (bf16[1408,128]{1,0:T(8,128)(2,1)S(1)}, bf16[1408,128]{1,0:T(8,128)(2,1)S(1)}, u32[]{:S(2)}, u32[]{:S(2)}) collective-permute-start(bf16[1408,128]{1,0:T(8,128)(2,1)S(1)} %shard_map.52.refs_0_), channel_id=1, source_target_pairs={{0,16},{16,0},{1,17},{17,1},{2,18},{18,2},{3,19},{19,3},{4,20},{20... | collective-permute-start | bytes 1081352 | tf_op jit(solution)/shard_map/ppermute | solution.py:310
  25.6 1.5 %collective-permute-start.5 = (bf16[1408,128]{1,0:T(8,128)(2,1)S(1)}, bf16[1408,128]{1,0:T(8,128)(2,1)S(1)}, u32[]{:S(2)}, u32[]{:S(2)}) collective-permute-start(bf16[1408,128]{1,0:T(8,128)(2,1)S(1)} %shard_map.52.refs_0_), channel_id=1, source_target_pairs={{0,2},{2,0},{1,3},{3,1},{4,6},{6,4},{5,7},{7,5},{8,10},{10,8},{9,1... | collective-permute-start | bytes 1081352 | tf_op jit(solution)/shard_map/ppermute | solution.py:310
  27.0 4.5 %collective-permute-done.6.refs_2_ = bf16[1408,128]{1,0:T(8,128)(2,1)S(1)} collective-permute-done((bf16[1408,128]{1,0:T(8,128)(2,1)S(1)}, bf16[1408,128]{1,0:T(8,128)(2,1)S(1)}, u32[]{:S(2)}, u32[]{:S(2)}) %collective-permute-start.6) | collective-permute-done | bytes 360480 | tf_op jit(solution)/shard_map/ppermute | solution.py:310
  31.6 1.4 %collective-permute-done.5.refs_1_ = bf16[1408,128]{1,0:T(8,128)(2,1)S(1)} collective-permute-done((bf16[1408,128]{1,0:T(8,128)(2,1)S(1)}, bf16[1408,128]{1,0:T(8,128)(2,1)S(1)}, u32[]{:S(2)}, u32[]{:S(2)}) %collective-permute-start.5) | collective-permute-done | bytes 360480 | tf_op jit(solution)/shard_map/ppermute | solution.py:310
  33.0 3.7 %collective-permute-start.10 = (bf16[128,1664]{1,0:T(8,128)(2,1)S(1)}, bf16[128,1664]{1,0:T(8,128)(2,1)S(1)}, u32[]{:S(2)}, u32[]{:S(2)}) collective-permute-start(bf16[128,1664]{1,0:T(8,128)(2,1)S(1)} %get-tuple-element.54.refs_0_), channel_id=1, source_target_pairs={{4,8},{8,4},{5,9},{9,5},{6,10},{10,6},{7,11},{11,7},{20,24},{24,20... | collective-permute-start | bytes 1277960 | tf_op jit(solution)/shard_map/ppermute | solution.py:341
  36.7 1.3 %collective-permute-start.11 = (bf16[128,1664]{1,0:T(8,128)(2,1)S(1)}, bf16[128,1664]{1,0:T(8,128)(2,1)S(1)}, u32[]{:S(2)}, u32[]{:S(2)}) collective-permute-start(bf16[128,1664]{1,0:T(8,128)(2,1)S(1)} %collective-permute-done.2.refs_4_), channel_id=1, source_target_pairs={{8,12},{4,0},{9,13},{5,1},{10,14},{6,2},{11,15},{7,3},{24,28},{20,... | collective-permute-start | bytes 1277960 | tf_op jit(solution)/shard_map/ppermute | solution.py:342
  38.0 1.6 %collective-permute-start.9 = (bf16[1408,128]{1,0:T(8,128)(2,1)S(1)}, bf16[1408,128]{1,0:T(8,128)(2,1)S(1)}, u32[]{:S(2)}, u32[]{:S(2)}) collective-permute-start(bf16[1408,128]{1,0:T(8,128)(2,1)S(1)} %collective-permute-done.6.refs_2_), channel_id=1, source_target_pairs={{0,2},{2,0},{1,3},{3,1},{4,6},{6,4},{5,7},{7,5},{8,10},{10,8},{9,1... | collective-permute-start | bytes 1081352 | tf_op jit(solution)/shard_map/ppermute | solution.py:310
  39.5 0.5 collective-permute-start.7
  40.1 5.4 %collective-permute-done.9.refs_3_ = bf16[1408,128]{1,0:T(8,128)(2,1)S(1)} collective-permute-done((bf16[1408,128]{1,0:T(8,128)(2,1)S(1)}, bf16[1408,128]{1,0:T(8,128)(2,1)S(1)}, u32[]{:S(2)}, u32[]{:S(2)}) %collective-permute-start.9) | collective-permute-done | bytes 360480 | tf_op jit(solution)/shard_map/ppermute | solution.py:310
  45.5 0.9 shard_map.53.refs_6_.refs_5_
  46.4 0.1 collective-permute-start.12
  46.5 0.5 collective-permute-start.13
  47.0 1.2 %shard_map.54 = (bf16[384,1664]{1,0:T(8,128)(2,1)S(1)}, bf16[384,1664]{1,0:T(8,128)(2,1)S(1)}, bf16[384,512]{1,0:T(8,128)(2,1)S(1)}) custom-call(bf16[128,1664]{1,0:T(8,128)(2,1)S(1)} %get-tuple-element.54.refs_0_, bf16[128,1664]{1,0:T(8,128)(2,1)S(1)} %get-tuple-element.45.refs_1_, bf16[128,1664]{1,0:T(8,128)(2,1)S(1)} %collective-permute-done.1.refs_2_, ...), custom_call_target="tpu_custom_call" | custom-call | tf_op jit(solution)/shard_map/pallas_call | solution.py:283
  48.2 0.1 collective-permute-done.12.refs_1_
  48.3 0.6 collective-permute-done.13.refs_3_
  48.9 2.8 %shard_map.55 = (bf16[4,64,1664]{2,1,0:T(8,128)(2,1)S(1)}, bf16[4,64,1664]{2,1,0:T(8,128)(2,1)S(1)}, bf16[512,512]{1,0:T(8,128)(2,1)S(1)}, bf16[128,1664]{1,0:T(8,128)(2,1)S(1)}, bf16[128,1664]{1,0:T(8,128)(2,1)S(1)}) custom-call(bf16[128,1664]{1,0:T(8,128)(2,1)S(1)} %collective-permute-done.10.refs_0_, ...), custom_call_target="tpu_custom_call" | custom-call | tf_op jit(solution)/shard_map/pallas_call | solution.py:283
  51.7 0.2 collective-permute-start.15
  51.9 2.2 %shard_map.56 = (bf16[4,688,128]{2,1,0:T(8,128)(2,1)S(1)}, bf16[4,688,128]{2,1,0:T(8,128)(2,1)S(1)}) custom-call(bf16[384,1664]{1,0:T(8,128)(2,1)S(1)} %get-tuple-element.56.x_ref, bf16[128,1664]{1,0:T(8,128)(2,1)S(1)} %get-tuple-element.60.x_last, bf16[384,1664]{1,0:T(8,128)(2,1)S(1)} %get-tuple-element.61.up_ref, ...), custom_call_target="tpu_custom_call" | custom-call | tf_op jit(solution)/shard_map/pallas_call | solution.py:283
  54.1 0.0 copy-start.1
  54.2 0.0 copy-start.3
  54.2 1.6 %collective-permute-start.14 = (bf16[4,688,128]{2,1,0:T(8,128)(2,1)S(1)}, bf16[4,688,128]{2,1,0:T(8,128)(2,1)S(1)}, u32[]{:S(2)}, u32[]{:S(2)}) collective-permute-start(bf16[4,688,128]{2,1,0:T(8,128)(2,1)S(1)} %get-tuple-element.64), channel_id=1, source_target_pairs={{0,2},{2,0},{1,3},{3,1},{4,6},{6,4},{5,7},{7,5},{8,10},{10,8},{9,1... | collective-permute-start | bytes 2113544 | tf_op jit(solution)/shard_map/ppermute | solution.py:310
  55.7 0.2 shard_map.57
  55.9 1.3 %collective-permute-start.16 = (bf16[64,1664]{1,0:T(8,128)(2,1)S(1)}, bf16[64,1664]{1,0:T(8,128)(2,1)S(1)}, u32[]{:S(2)}, u32[]{:S(2)}) collective-permute-start(bf16[64,1664]{1,0:T(8,128)(2,1)S(1)} %get-tuple-element.69), channel_id=1, source_target_pairs={{0,8},{4,12},{8,0},{12,4},{1,9},{5,13},{9,1},{13,5},{2,10},{6,14},... | collective-permute-start | bytes 638984 | tf_op jit(solution)/shard_map/ppermute | solution.py:304
  57.3 0.5 collective-permute-start.17
  57.8 2.6 %collective-permute-start.18 = (bf16[64,1664]{1,0:T(8,128)(2,1)S(1)}, bf16[64,1664]{1,0:T(8,128)(2,1)S(1)}, u32[]{:S(2)}, u32[]{:S(2)}) collective-permute-start(bf16[64,1664]{1,0:T(8,128)(2,1)S(1)} %get-tuple-element.71), channel_id=1, source_target_pairs={{0,4},{4,0},{8,12},{12,8},{1,5},{5,1},{9,13},{13,9},{2,6},{6,2},{1... | collective-permute-start | bytes 638984 | tf_op jit(solution)/shard_map/ppermute | solution.py:304
  60.4 11.9 %collective-permute-done.14.theirs_ref = bf16[4,688,128]{2,1,0:T(8,128)(2,1)S(1)} collective-permute-done((bf16[4,688,128]{2,1,0:T(8,128)(2,1)S(1)}, bf16[4,688,128]{2,1,0:T(8,128)(2,1)S(1)}, u32[]{:S(2)}, u32[]{:S(2)}) %collective-permute-start.14) | collective-permute-done | bytes 704544 | tf_op jit(solution)/shard_map/ppermute | solution.py:310
  72.3 0.2 shard_map.59
  72.5 1.3 %collective-permute-start.21 = (bf16[688,128]{1,0:T(8,128)(2,1)S(1)}, bf16[688,128]{1,0:T(8,128)(2,1)S(1)}, u32[]{:S(2)}, u32[]{:S(2)}) collective-permute-start(bf16[688,128]{1,0:T(8,128)(2,1)S(1)} %get-tuple-element.77), channel_id=1, source_target_pairs={{0,8},{4,12},{8,0},{12,4},{1,9},{5,13},{9,1},{13,5},{2,10},{6,14},... | collective-permute-start | bytes 528392 | tf_op jit(solution)/shard_map/ppermute | solution.py:304
  73.8 0.5 collective-permute-start.22
  74.3 2.6 %collective-permute-start.23 = (bf16[688,128]{1,0:T(8,128)(2,1)S(1)}, bf16[688,128]{1,0:T(8,128)(2,1)S(1)}, u32[]{:S(2)}, u32[]{:S(2)}) collective-permute-start(bf16[688,128]{1,0:T(8,128)(2,1)S(1)} %get-tuple-element.79), channel_id=1, source_target_pairs={{0,4},{4,0},{8,12},{12,8},{1,5},{5,1},{9,13},{13,9},{2,6},{6,2},{1... | collective-permute-start | bytes 528392 | tf_op jit(solution)/shard_map/ppermute | solution.py:304
  76.9 8.3 %collective-permute-done.17.refs_2_ = bf16[64,1664]{1,0:T(8,128)(2,1)S(1)} collective-permute-done((bf16[64,1664]{1,0:T(8,128)(2,1)S(1)}, bf16[64,1664]{1,0:T(8,128)(2,1)S(1)}, u32[]{:S(2)}, u32[]{:S(2)}) %collective-permute-start.17) | collective-permute-done | bytes 213024 | tf_op jit(solution)/shard_map/ppermute | solution.py:304
  85.2 0.5 shard_map.58
  85.6 0.1 collective-permute-start.19
  85.7 0.5 collective-permute-start.20
  86.2 1.7 %collective-permute-done.21.refs_5_ = bf16[688,128]{1,0:T(8,128)(2,1)S(1)} collective-permute-done((bf16[688,128]{1,0:T(8,128)(2,1)S(1)}, bf16[688,128]{1,0:T(8,128)(2,1)S(1)}, u32[]{:S(2)}, u32[]{:S(2)}) %collective-permute-start.21) | collective-permute-done | bytes 176160 | tf_op jit(solution)/shard_map/ppermute | solution.py:304
  87.9 3.9 %collective-permute-done.22.refs_6_ = bf16[688,128]{1,0:T(8,128)(2,1)S(1)} collective-permute-done((bf16[688,128]{1,0:T(8,128)(2,1)S(1)}, bf16[688,128]{1,0:T(8,128)(2,1)S(1)}, u32[]{:S(2)}, u32[]{:S(2)}) %collective-permute-start.22) | collective-permute-done | bytes 176160 | tf_op jit(solution)/shard_map/ppermute | solution.py:304
  91.9 1.6 %shard_map.60 = (bf16[128,1664]{1,0:T(8,128)(2,1)}, f32[4,208,416]{2,1,0:T(8,128)}) custom-call(bf16[32,1664]{1,0:T(8,128)(2,1)S(1)} %get-tuple-element.72.refs_0_, bf16[32,1664]{1,0:T(8,128)(2,1)S(1)} %get-tuple-element.73.refs_1_, bf16[32,1664]{1,0:T(8,128)(2,1)S(1)} %collective-permute-done.19.refs_2_, ...), custom_call_target="tpu_custom_call" | custom-call | tf_op jit(solution)/shard_map/pallas_call | solution.py:283
  (21 shorter events, 0.1 us)
Async XLA Ops:
  0.6 1.2 %copy-start.4 = (bf16[4,208,416]{2,1,0:T(8,128)(2,1)S(1)}, bf16[4,208,416]{2,1,0:T(8,128)(2,1)}, u32[]{:S(2)}) copy-start(bf16[4,208,416]{2,1,0:T(8,128)(2,1)} %w_ref.1) | copy-start | bytes 2076676
  2.4 5.9 %collective-permute-start = (bf16[352,128]{1,0:T(8,128)(2,1)S(1)}, bf16[352,128]{1,0:T(8,128)(2,1)S(1)}, u32[]{:S(2)}, u32[]{:S(2)}) collective-permute-start(bf16[352,128]{1,0:T(8,128)(2,1)S(1)} %get-tuple-element.43), channel_id=1, source_target_pairs={{0,4},{4,0},{8,12},{12,8},{1,5},{5,1},{9,13},{13,9},{2,6},{6,2},{1... | collective-permute-start | bytes 270344 | tf_op jit(solution)/shard_map/ppermute | solution.py:304
  2.4 18.4 %collective-permute-start.3 = (bf16[352,128]{1,0:T(8,128)(2,1)S(1)}, bf16[352,128]{1,0:T(8,128)(2,1)S(1)}, u32[]{:S(2)}, u32[]{:S(2)}) collective-permute-start(bf16[352,128]{1,0:T(8,128)(2,1)S(1)} %get-tuple-element.48), channel_id=1, source_target_pairs={{0,8},{4,12},{8,0},{12,4},{1,9},{5,13},{9,1},{13,5},{2,10},{6,14},... | collective-permute-start | bytes 270344 | tf_op jit(solution)/shard_map/ppermute | solution.py:304
  5.5 18.5 %collective-permute-start.4 = (bf16[352,128]{1,0:T(8,128)(2,1)S(1)}, bf16[352,128]{1,0:T(8,128)(2,1)S(1)}, u32[]{:S(2)}, u32[]{:S(2)}) collective-permute-start(bf16[352,128]{1,0:T(8,128)(2,1)S(1)} %get-tuple-element.49), channel_id=1, source_target_pairs={{0,12},{4,8},{8,4},{12,0},{1,13},{5,9},{9,5},{13,1},{2,14},{6,10},... | collective-permute-start | bytes 270344 | tf_op jit(solution)/shard_map/ppermute | solution.py:304
  5.9 1.0 %copy-start = (bf16[1,128,1664]{2,1,0:T(8,128)(2,1)S(1)}, bf16[1,128,1664]{2,1,0:T(8,128)(2,1)}, u32[]{:S(2)}) copy-start(bf16[1,128,1664]{2,1,0:T(8,128)(2,1)} %param.3) | copy-start | bytes 1277956
  6.9 1.0 %copy-start.2 = (bf16[1,128,1664]{2,1,0:T(8,128)(2,1)S(1)}, bf16[1,128,1664]{2,1,0:T(8,128)(2,1)}, u32[]{:S(2)}) copy-start(bf16[1,128,1664]{2,1,0:T(8,128)(2,1)} %param.4) | copy-start | bytes 1277956
  8.3 24.7 %collective-permute-start.2 = (bf16[128,1664]{1,0:T(8,128)(2,1)S(1)}, bf16[128,1664]{1,0:T(8,128)(2,1)S(1)}, u32[]{:S(2)}, u32[]{:S(2)}) collective-permute-start(bf16[128,1664]{1,0:T(8,128)(2,1)S(1)} %get-tuple-element.54.refs_0_), channel_id=1, source_target_pairs={{0,8},{4,12},{8,0},{12,4},{1,9},{5,13},{9,1},{13,5},{2,10},{6,14},... | collective-permute-start | bytes 1277960 | tf_op jit(solution)/shard_map/ppermute | solution.py:304
  11.8 21.2 %collective-permute-start.1 = (bf16[128,1664]{1,0:T(8,128)(2,1)S(1)}, bf16[128,1664]{1,0:T(8,128)(2,1)S(1)}, u32[]{:S(2)}, u32[]{:S(2)}) collective-permute-start(bf16[128,1664]{1,0:T(8,128)(2,1)S(1)} %get-tuple-element.54.refs_0_), channel_id=1, source_target_pairs={{0,4},{4,0},{8,12},{12,8},{1,5},{5,1},{9,13},{13,9},{2,6},{6,2},{1... | collective-permute-start | bytes 1277960 | tf_op jit(solution)/shard_map/ppermute | solution.py:304
  24.0 7.6 %collective-permute-start.6 = (bf16[1408,128]{1,0:T(8,128)(2,1)S(1)}, bf16[1408,128]{1,0:T(8,128)(2,1)S(1)}, u32[]{:S(2)}, u32[]{:S(2)}) collective-permute-start(bf16[1408,128]{1,0:T(8,128)(2,1)S(1)} %shard_map.52.refs_0_), channel_id=1, source_target_pairs={{0,16},{16,0},{1,17},{17,1},{2,18},{18,2},{3,19},{19,3},{4,20},{20... | collective-permute-start | bytes 1081352 | tf_op jit(solution)/shard_map/ppermute | solution.py:310
  25.6 7.4 %collective-permute-start.5 = (bf16[1408,128]{1,0:T(8,128)(2,1)S(1)}, bf16[1408,128]{1,0:T(8,128)(2,1)S(1)}, u32[]{:S(2)}, u32[]{:S(2)}) collective-permute-start(bf16[1408,128]{1,0:T(8,128)(2,1)S(1)} %shard_map.52.refs_0_), channel_id=1, source_target_pairs={{0,2},{2,0},{1,3},{3,1},{4,6},{6,4},{5,7},{7,5},{8,10},{10,8},{9,1... | collective-permute-start | bytes 1081352 | tf_op jit(solution)/shard_map/ppermute | solution.py:310
  33.0 13.4 %collective-permute-start.10 = (bf16[128,1664]{1,0:T(8,128)(2,1)S(1)}, bf16[128,1664]{1,0:T(8,128)(2,1)S(1)}, u32[]{:S(2)}, u32[]{:S(2)}) collective-permute-start(bf16[128,1664]{1,0:T(8,128)(2,1)S(1)} %get-tuple-element.54.refs_0_), channel_id=1, source_target_pairs={{4,8},{8,4},{5,9},{9,5},{6,10},{10,6},{7,11},{11,7},{20,24},{24,20... | collective-permute-start | bytes 1277960 | tf_op jit(solution)/shard_map/ppermute | solution.py:341
  36.7 9.8 %collective-permute-start.11 = (bf16[128,1664]{1,0:T(8,128)(2,1)S(1)}, bf16[128,1664]{1,0:T(8,128)(2,1)S(1)}, u32[]{:S(2)}, u32[]{:S(2)}) collective-permute-start(bf16[128,1664]{1,0:T(8,128)(2,1)S(1)} %collective-permute-done.2.refs_4_), channel_id=1, source_target_pairs={{8,12},{4,0},{9,13},{5,1},{10,14},{6,2},{11,15},{7,3},{24,28},{20,... | collective-permute-start | bytes 1277960 | tf_op jit(solution)/shard_map/ppermute | solution.py:342
  38.0 7.5 %collective-permute-start.9 = (bf16[1408,128]{1,0:T(8,128)(2,1)S(1)}, bf16[1408,128]{1,0:T(8,128)(2,1)S(1)}, u32[]{:S(2)}, u32[]{:S(2)}) collective-permute-start(bf16[1408,128]{1,0:T(8,128)(2,1)S(1)} %collective-permute-done.6.refs_2_), channel_id=1, source_target_pairs={{0,2},{2,0},{1,3},{3,1},{4,6},{6,4},{5,7},{7,5},{8,10},{10,8},{9,1... | collective-permute-start | bytes 1081352 | tf_op jit(solution)/shard_map/ppermute | solution.py:310
  39.5 7.5 %collective-permute-start.8 = (bf16[128,1664]{1,0:T(8,128)(2,1)S(1)}, bf16[128,1664]{1,0:T(8,128)(2,1)S(1)}, u32[]{:S(2)}, u32[]{:S(2)}) collective-permute-start(bf16[128,1664]{1,0:T(8,128)(2,1)S(1)} %collective-permute-done.2.refs_4_), channel_id=1, source_target_pairs={{0,1},{1,0},{2,3},{3,2},{4,5},{5,4},{6,7},{7,6},{8,9},{9,8},{10,11... | collective-permute-start | bytes 1277960 | tf_op jit(solution)/shard_map/ppermute | solution.py:310
  39.5 7.5 %collective-permute-start.7 = (bf16[128,1664]{1,0:T(8,128)(2,1)S(1)}, bf16[128,1664]{1,0:T(8,128)(2,1)S(1)}, u32[]{:S(2)}, u32[]{:S(2)}) collective-permute-start(bf16[128,1664]{1,0:T(8,128)(2,1)S(1)} %collective-permute-done.1.refs_2_), channel_id=1, source_target_pairs={{0,1},{1,0},{2,3},{3,2},{4,5},{5,4},{6,7},{7,6},{8,9},{9,8},{10,11... | collective-permute-start | bytes 1277960 | tf_op jit(solution)/shard_map/ppermute | solution.py:310
  46.4 1.8 %collective-permute-start.12 = (bf16[128,1664]{1,0:T(8,128)(2,1)S(1)}, bf16[128,1664]{1,0:T(8,128)(2,1)S(1)}, u32[]{:S(2)}, u32[]{:S(2)}) collective-permute-start(bf16[128,1664]{1,0:T(8,128)(2,1)S(1)} %collective-permute-done.10.refs_0_), channel_id=1, source_target_pairs={{0,1},{1,0},{2,3},{3,2},{4,5},{5,4},{6,7},{7,6},{8,9},{9,8},{10,11... | collective-permute-start | bytes 1277960 | tf_op jit(solution)/shard_map/ppermute | solution.py:310
  46.5 2.4 %collective-permute-start.13 = (bf16[128,1664]{1,0:T(8,128)(2,1)S(1)}, bf16[128,1664]{1,0:T(8,128)(2,1)S(1)}, u32[]{:S(2)}, u32[]{:S(2)}) collective-permute-start(bf16[128,1664]{1,0:T(8,128)(2,1)S(1)} %collective-permute-done.11.refs_2_), channel_id=1, source_target_pairs={{0,1},{1,0},{2,3},{3,2},{4,5},{5,4},{6,7},{7,6},{8,9},{9,8},{10,11... | collective-permute-start | bytes 1277960 | tf_op jit(solution)/shard_map/ppermute | solution.py:310
  51.7 4.0 %collective-permute-start.15 = (bf16[4,64,1664]{2,1,0:T(8,128)(2,1)S(1)}, bf16[4,64,1664]{2,1,0:T(8,128)(2,1)S(1)}, u32[]{:S(2)}, u32[]{:S(2)}) collective-permute-start(bf16[4,64,1664]{2,1,0:T(8,128)(2,1)S(1)} %get-tuple-element.66), channel_id=1, source_target_pairs={{0,1},{1,0},{2,3},{3,2},{4,5},{5,4},{6,7},{7,6},{8,9},{9,8},{10,11... | collective-permute-start | bytes 2555912 | tf_op jit(solution)/shard_map/ppermute | solution.py:310
  54.1 31.0 %copy-start.1 = (bf16[1,128,1664]{2,1,0:T(8,128)(2,1)S(1)}, bf16[1,128,1664]{2,1,0:T(8,128)(2,1)}, u32[]{:S(2)}) copy-start(bf16[1,128,1664]{2,1,0:T(8,128)(2,1)} %param.3) | copy-start | bytes 1277956
  54.2 31.0 %copy-start.3 = (bf16[1,128,1664]{2,1,0:T(8,128)(2,1)S(1)}, bf16[1,128,1664]{2,1,0:T(8,128)(2,1)}, u32[]{:S(2)}) copy-start(bf16[1,128,1664]{2,1,0:T(8,128)(2,1)} %param.4) | copy-start | bytes 1277956
  54.2 18.1 %collective-permute-start.14 = (bf16[4,688,128]{2,1,0:T(8,128)(2,1)S(1)}, bf16[4,688,128]{2,1,0:T(8,128)(2,1)S(1)}, u32[]{:S(2)}, u32[]{:S(2)}) collective-permute-start(bf16[4,688,128]{2,1,0:T(8,128)(2,1)S(1)} %get-tuple-element.64), channel_id=1, source_target_pairs={{0,2},{2,0},{1,3},{3,1},{4,6},{6,4},{5,7},{7,5},{8,10},{10,8},{9,1... | collective-permute-start | bytes 2113544 | tf_op jit(solution)/shard_map/ppermute | solution.py:310
  55.9 18.4 %collective-permute-start.16 = (bf16[64,1664]{1,0:T(8,128)(2,1)S(1)}, bf16[64,1664]{1,0:T(8,128)(2,1)S(1)}, u32[]{:S(2)}, u32[]{:S(2)}) collective-permute-start(bf16[64,1664]{1,0:T(8,128)(2,1)S(1)} %get-tuple-element.69), channel_id=1, source_target_pairs={{0,8},{4,12},{8,0},{12,4},{1,9},{5,13},{9,1},{13,5},{2,10},{6,14},... | collective-permute-start | bytes 638984 | tf_op jit(solution)/shard_map/ppermute | solution.py:304
  57.3 27.9 %collective-permute-start.17 = (bf16[64,1664]{1,0:T(8,128)(2,1)S(1)}, bf16[64,1664]{1,0:T(8,128)(2,1)S(1)}, u32[]{:S(2)}, u32[]{:S(2)}) collective-permute-start(bf16[64,1664]{1,0:T(8,128)(2,1)S(1)} %get-tuple-element.70), channel_id=1, source_target_pairs={{0,12},{4,8},{8,4},{12,0},{1,13},{5,9},{9,5},{13,1},{2,14},{6,10},... | collective-permute-start | bytes 638984 | tf_op jit(solution)/shard_map/ppermute | solution.py:304
  57.8 27.4 %collective-permute-start.18 = (bf16[64,1664]{1,0:T(8,128)(2,1)S(1)}, bf16[64,1664]{1,0:T(8,128)(2,1)S(1)}, u32[]{:S(2)}, u32[]{:S(2)}) collective-permute-start(bf16[64,1664]{1,0:T(8,128)(2,1)S(1)} %get-tuple-element.71), channel_id=1, source_target_pairs={{0,4},{4,0},{8,12},{12,8},{1,5},{5,1},{9,13},{13,9},{2,6},{6,2},{1... | collective-permute-start | bytes 638984 | tf_op jit(solution)/shard_map/ppermute | solution.py:304
  72.5 15.5 %collective-permute-start.21 = (bf16[688,128]{1,0:T(8,128)(2,1)S(1)}, bf16[688,128]{1,0:T(8,128)(2,1)S(1)}, u32[]{:S(2)}, u32[]{:S(2)}) collective-permute-start(bf16[688,128]{1,0:T(8,128)(2,1)S(1)} %get-tuple-element.77), channel_id=1, source_target_pairs={{0,8},{4,12},{8,0},{12,4},{1,9},{5,13},{9,1},{13,5},{2,10},{6,14},... | collective-permute-start | bytes 528392 | tf_op jit(solution)/shard_map/ppermute | solution.py:304
  73.8 18.1 %collective-permute-start.22 = (bf16[688,128]{1,0:T(8,128)(2,1)S(1)}, bf16[688,128]{1,0:T(8,128)(2,1)S(1)}, u32[]{:S(2)}, u32[]{:S(2)}) collective-permute-start(bf16[688,128]{1,0:T(8,128)(2,1)S(1)} %get-tuple-element.78), channel_id=1, source_target_pairs={{0,12},{4,8},{8,4},{12,0},{1,13},{5,9},{9,5},{13,1},{2,14},{6,10},... | collective-permute-start | bytes 528392 | tf_op jit(solution)/shard_map/ppermute | solution.py:304
  74.3 17.5 %collective-permute-start.23 = (bf16[688,128]{1,0:T(8,128)(2,1)S(1)}, bf16[688,128]{1,0:T(8,128)(2,1)S(1)}, u32[]{:S(2)}, u32[]{:S(2)}) collective-permute-start(bf16[688,128]{1,0:T(8,128)(2,1)S(1)} %get-tuple-element.79), channel_id=1, source_target_pairs={{0,4},{4,0},{8,12},{12,8},{1,5},{5,1},{9,13},{13,9},{2,6},{6,2},{1... | collective-permute-start | bytes 528392 | tf_op jit(solution)/shard_map/ppermute | solution.py:304
  85.6 6.2 %collective-permute-start.19 = (bf16[32,1664]{1,0:T(8,128)(2,1)S(1)}, bf16[32,1664]{1,0:T(8,128)(2,1)S(1)}, u32[]{:S(2)}, u32[]{:S(2)}) collective-permute-start(bf16[32,1664]{1,0:T(8,128)(2,1)S(1)} %get-tuple-element.72.refs_0_), channel_id=1, source_target_pairs={{0,1},{1,0},{2,3},{3,2},{4,5},{5,4},{6,7},{7,6},{8,9},{9,8},{10,11... | collective-permute-start | bytes 319496 | tf_op jit(solution)/shard_map/ppermute | solution.py:310
  85.7 6.1 %collective-permute-start.20 = (bf16[32,1664]{1,0:T(8,128)(2,1)S(1)}, bf16[32,1664]{1,0:T(8,128)(2,1)S(1)}, u32[]{:S(2)}, u32[]{:S(2)}) collective-permute-start(bf16[32,1664]{1,0:T(8,128)(2,1)S(1)} %get-tuple-element.73.refs_1_), channel_id=1, source_target_pairs={{0,1},{1,0},{2,3},{3,2},{4,5},{5,4},{6,7},{7,6},{8,9},{9,8},{10,11... | collective-permute-start | bytes 319496 | tf_op jit(solution)/shard_map/ppermute | solution.py:310

commit v10 on v9

--- a/solution.py
+++ b/solution.py
@@ -151,22 +151,14 @@
 
 
 def head_kernel(n, *refs):
-    middle, passed = refs[:2], refs[2:4]
-    made_ref, w_ref, keep_ref, give_ref, grads, x_ref, up_ref = refs[4:11]
-    made, term_k, term_v = refs[11:]
-    me = lax.axis_index("seq")
+    third = refs[:2]
+    made_ref, w_ref, keep_ref, give_ref, grads, x_ref, up_ref = refs[2:9]
+    made, term_k, term_v = refs[9:]
     rows = x_ref.shape[0]
     half = rows // 2
     ready = (n - 1) * rows
 
-    @pl.when((me == 0) | (me == n - 1))
-    def _():
-        place(0, passed, x_ref, up_ref)
-
-    @pl.when((me != 0) & (me != n - 1))
-    def _():
-        place(0, middle, x_ref, up_ref)
-
+    place(0, third, x_ref, up_ref)
     made[:ready, :] = made_ref[...]
     made[ready:, : 3 * SLOT], made[ready:, 3 * SLOT :] = project(x_ref[...], up_ref[...], w_ref)
     scale = HD ** (-0.5)
@@ -328,9 +320,7 @@
     above = swap(merged, "grp")
     second = across(send, 2)
     first = across(send, 1)
-    later, first, second, beside, above = lax.optimization_barrier(
-        (send, first, second, beside, above)
-    )
+    first, second, beside, above = lax.optimization_barrier((first, second, beside, above))
     corner = swap(above, "dp")
     weights = call(
         functools.partial(weights_kernel, n, share),
@@ -338,9 +328,8 @@
         (merged, beside, above, corner),
         [pltpu.VMEM((2 * n, full, SLOT), BF)],
     )
-    middle = lax.ppermute(later, "seq", [(1, 2), (2, 1)])
-    passed = lax.ppermute(second, "seq", [(2, 3), (1, 0)])
-    weights, middle, passed = lax.optimization_barrier((weights, middle, passed))
+    third = across(second, 1)
+    weights, third = lax.optimization_barrier((weights, third))
     ready = patches - rows
     x_head, up_head, made = call(
         functools.partial(project_kernel, n),
@@ -350,7 +339,7 @@
     keep, give, grads, x_last, up_last = call(
         functools.partial(head_kernel, n),
         [((n, half, width), BF)] * 2 + [((patches, 4 * SLOT), BF)] + [((rows, width), BF)] * 2,
-        (middle, swap(middle, "pipe"), passed, swap(passed, "pipe"), made, weights),
+        (third, swap(third, "pipe"), made, weights),
         [
             pltpu.VMEM((patches, 4 * SLOT), BF),
             pltpu.VMEM((patches, SLOT), F32),

time: 93.8 us -> 90.5 us (0.965)
  starting transfers between devices: 29 us -> 24 us
  waiting for transfers between devices: 49.9 us -> 51.8 us
    ppermute x2 -> x0, starting transfers between devices: 4.98 us -> none  [the longest x1 3.66 us: local_heads(): middle = lax.ppermute(later, 'seq', [(1, 2), (2, 1)])]
    ppermute x11 -> x10, waiting for transfers between devices: 23.9 us -> 25.5 us  [swap(): return lax.ppermute(value, axis, [(0, 1), (1, 0)])]
    ppermute x11 -> x10, starting transfers between devices: 8.05 us -> 7.49 us  [swap(): return lax.ppermute(value, axis, [(0, 1), (1, 0)])]
    ppermute x11 -> x12, starting transfers between devices: 16 us -> 16.5 us  [across(): return lax.ppermute(value, 'seq', [(i, i ^ k) for i in range(n)])]
    ppermute x11 -> x12, waiting for transfers between devices: 26 us -> 26.4 us  [across(): return lax.ppermute(value, 'seq', [(i, i ^ k) for i in range(n)])]
  transfers between devices with their start and end apart: 24 -> 22, of which waited for: 11 -> 10; matrix products, arithmetic and copies ran while one was open for 0% -> 0% of each run, Pallas kernels for 6% -> 6%
where the time goes in v10:
time: 90.5 us; the launch traced here: 90.2 us
  waiting for transfers between devices  51.8 us (57%)
  starting transfers between devices  24 us (27%)
  Pallas kernels  10.5 us (12%)
  local copies, waits for them, and re-layouts  3.18 us (4%)
    ppermute x12, waiting for transfers between devices, across(): return lax.ppermute(value, 'seq', [(i, i ^ k) for i in range(n)])  26.4 us
    ppermute x10, waiting for transfers between devices, swap(): return lax.ppermute(value, axis, [(0, 1), (1, 0)])  25.5 us
    ppermute x12, starting transfers between devices, across(): return lax.ppermute(value, 'seq', [(i, i ^ k) for i in range(n)])  16.5 us
    pallas_call x11, Pallas kernels, call(): pl.pallas_call(kernel, out_shape=[out_space(*s) for s in shapes], in_spec...  10.5 us
    ppermute x10, starting transfers between devices, swap(): return lax.ppermute(value, axis, [(0, 1), (1, 0)])  7.49 us
    unnamed x10, local copies, waits for them, and re-layouts  3.18 us
  transfers between devices with their start and end apart: 22, of which 10 were waited for; matrix products, arithmetic and copies ran while one was open for 0% of the time, Pallas kernels for 6%

profile of v10, /device:TPU:8, one launch (start us, length us, event | category | flops | bytes accessed | tf_op | source)
XLA Modules:
  0.0 90.2 jit_solution(3876588423476111684)
XLA Ops:
  0.6 1.1 %copy-done.4 = bf16[4,208,416]{2,1,0:T(8,128)(2,1)S(1)} copy-done((bf16[4,208,416]{2,1,0:T(8,128)(2,1)S(1)}, bf16[4,208,416]{2,1,0:T(8,128)(2,1)}, u32[]{:S(2)}) %copy-start.4) | copy-done | bytes 692248
  1.8 0.6 shard_map.51
  2.4 0.1 collective-permute-start
  2.4 3.0 %collective-permute-start.3 = (bf16[352,128]{1,0:T(8,128)(2,1)S(1)}, bf16[352,128]{1,0:T(8,128)(2,1)S(1)}, u32[]{:S(2)}, u32[]{:S(2)}) collective-permute-start(bf16[352,128]{1,0:T(8,128)(2,1)S(1)} %get-tuple-element.46), channel_id=1, source_target_pairs={{0,8},{4,12},{8,0},{12,4},{1,9},{5,13},{9,1},{13,5},{2,10},{6,14},... | collective-permute-start | bytes 270344 | tf_op jit(solution)/shard_map/ppermute | solution.py:296
  5.5 0.5 collective-permute-start.4
  5.9 1.0 %copy-done = bf16[1,128,1664]{2,1,0:T(8,128)(2,1)S(1)} copy-done((bf16[1,128,1664]{2,1,0:T(8,128)(2,1)S(1)}, bf16[1,128,1664]{2,1,0:T(8,128)(2,1)}, u32[]{:S(2)}) %copy-start) | copy-done | bytes 426008
  6.9 1.0 %copy-done.2 = bf16[1,128,1664]{2,1,0:T(8,128)(2,1)S(1)} copy-done((bf16[1,128,1664]{2,1,0:T(8,128)(2,1)S(1)}, bf16[1,128,1664]{2,1,0:T(8,128)(2,1)}, u32[]{:S(2)}) %copy-start.2) | copy-done | bytes 426008
  7.9 0.3 shard_map.50
  8.3 0.0 collective-permute-done.refs_1_
  8.3 3.6 %collective-permute-start.2 = (bf16[128,1664]{1,0:T(8,128)(2,1)S(1)}, bf16[128,1664]{1,0:T(8,128)(2,1)S(1)}, u32[]{:S(2)}, u32[]{:S(2)}) collective-permute-start(bf16[128,1664]{1,0:T(8,128)(2,1)S(1)} %get-tuple-element.42.refs_0_), channel_id=1, source_target_pairs={{0,8},{4,12},{8,0},{12,4},{1,9},{5,13},{9,1},{13,5},{2,10},{6,14},... | collective-permute-start | bytes 1277960 | tf_op jit(solution)/shard_map/ppermute | solution.py:296
  11.8 9.0 %collective-permute-done.3.refs_2_ = bf16[352,128]{1,0:T(8,128)(2,1)S(1)} collective-permute-done((bf16[352,128]{1,0:T(8,128)(2,1)S(1)}, bf16[352,128]{1,0:T(8,128)(2,1)S(1)}, u32[]{:S(2)}, u32[]{:S(2)}) %collective-permute-start.3) | collective-permute-done | bytes 90144 | tf_op jit(solution)/shard_map/ppermute | solution.py:296
  20.8 3.1 %collective-permute-done.4.refs_3_ = bf16[352,128]{1,0:T(8,128)(2,1)S(1)} collective-permute-done((bf16[352,128]{1,0:T(8,128)(2,1)S(1)}, bf16[352,128]{1,0:T(8,128)(2,1)S(1)}, u32[]{:S(2)}, u32[]{:S(2)}) %collective-permute-start.4) | collective-permute-done | bytes 90144 | tf_op jit(solution)/shard_map/ppermute | solution.py:296
  24.0 1.6 %collective-permute-start.6 = (bf16[1408,128]{1,0:T(8,128)(2,1)S(1)}, bf16[1408,128]{1,0:T(8,128)(2,1)S(1)}, u32[]{:S(2)}, u32[]{:S(2)}) collective-permute-start(bf16[1408,128]{1,0:T(8,128)(2,1)S(1)} %shard_map.52.refs_0_), channel_id=1, source_target_pairs={{0,16},{16,0},{1,17},{17,1},{2,18},{18,2},{3,19},{19,3},{4,20},{20... | collective-permute-start | bytes 1081352 | tf_op jit(solution)/shard_map/ppermute | solution.py:302
  25.6 1.5 %collective-permute-start.5 = (bf16[1408,128]{1,0:T(8,128)(2,1)S(1)}, bf16[1408,128]{1,0:T(8,128)(2,1)S(1)}, u32[]{:S(2)}, u32[]{:S(2)}) collective-permute-start(bf16[1408,128]{1,0:T(8,128)(2,1)S(1)} %shard_map.52.refs_0_), channel_id=1, source_target_pairs={{0,2},{2,0},{1,3},{3,1},{4,6},{6,4},{5,7},{7,5},{8,10},{10,8},{9,1... | collective-permute-start | bytes 1081352 | tf_op jit(solution)/shard_map/ppermute | solution.py:302
  27.0 4.5 %collective-permute-done.6.refs_2_ = bf16[1408,128]{1,0:T(8,128)(2,1)S(1)} collective-permute-done((bf16[1408,128]{1,0:T(8,128)(2,1)S(1)}, bf16[1408,128]{1,0:T(8,128)(2,1)S(1)}, u32[]{:S(2)}, u32[]{:S(2)}) %collective-permute-start.6) | collective-permute-done | bytes 360480 | tf_op jit(solution)/shard_map/ppermute | solution.py:302
  31.6 1.4 %collective-permute-done.5.refs_1_ = bf16[1408,128]{1,0:T(8,128)(2,1)S(1)} collective-permute-done((bf16[1408,128]{1,0:T(8,128)(2,1)S(1)}, bf16[1408,128]{1,0:T(8,128)(2,1)S(1)}, u32[]{:S(2)}, u32[]{:S(2)}) %collective-permute-start.5) | collective-permute-done | bytes 360480 | tf_op jit(solution)/shard_map/ppermute | solution.py:302
  33.0 0.0 collective-permute-done.2.refs_4_
  33.0 0.0 collective-permute-done.1.refs_2_
  33.0 0.5 collective-permute-start.10
  33.5 1.5 %collective-permute-start.9 = (bf16[1408,128]{1,0:T(8,128)(2,1)S(1)}, bf16[1408,128]{1,0:T(8,128)(2,1)S(1)}, u32[]{:S(2)}, u32[]{:S(2)}) collective-permute-start(bf16[1408,128]{1,0:T(8,128)(2,1)S(1)} %collective-permute-done.6.refs_2_), channel_id=1, source_target_pairs={{0,2},{2,0},{1,3},{3,1},{4,6},{6,4},{5,7},{7,5},{8,10},{10,8},{9,1... | collective-permute-start | bytes 1081352 | tf_op jit(solution)/shard_map/ppermute | solution.py:302
  35.0 0.5 collective-permute-start.7
  35.5 7.1 %collective-permute-done.9.refs_3_ = bf16[1408,128]{1,0:T(8,128)(2,1)S(1)} collective-permute-done((bf16[1408,128]{1,0:T(8,128)(2,1)S(1)}, bf16[1408,128]{1,0:T(8,128)(2,1)S(1)}, u32[]{:S(2)}, u32[]{:S(2)}) %collective-permute-start.9) | collective-permute-done | bytes 360480 | tf_op jit(solution)/shard_map/ppermute | solution.py:302
  42.6 0.9 %shard_map.53.refs_6_.refs_3_ = bf16[1664,512]{1,0:T(8,128)(2,1)S(1)} custom-call(bf16[1408,128]{1,0:T(8,128)(2,1)S(1)} %shard_map.52.refs_0_, bf16[1408,128]{1,0:T(8,128)(2,1)S(1)} %collective-permute-done.5.refs_1_, bf16[1408,128]{1,0:T(8,128)(2,1)S(1)} %collective-permute-done.6.refs_2_, bf16[1408,128]{1,0:T(8,128)(2,1)S(1)} %collective-permute-done.9.refs_3_), custom_call_target="tpu_custom_call" | custom-call | tf_op jit(solution)/shard_map/pallas_call | solution.py:275
  43.5 0.1 collective-permute-start.11
  43.6 1.2 %shard_map.54 = (bf16[384,1664]{1,0:T(8,128)(2,1)S(1)}, bf16[384,1664]{1,0:T(8,128)(2,1)S(1)}, bf16[384,512]{1,0:T(8,128)(2,1)S(1)}) custom-call(bf16[128,1664]{1,0:T(8,128)(2,1)S(1)} %get-tuple-element.42.refs_0_, bf16[128,1664]{1,0:T(8,128)(2,1)S(1)} %get-tuple-element.43.refs_1_, bf16[128,1664]{1,0:T(8,128)(2,1)S(1)} %collective-permute-done.1.refs_2_, ...), custom_call_target="tpu_custom_call" | custom-call | tf_op jit(solution)/shard_map/pallas_call | solution.py:275
  44.8 0.5 collective-permute-done.11.refs_1_
  45.3 2.8 %shard_map.55 = (bf16[4,64,1664]{2,1,0:T(8,128)(2,1)S(1)}, bf16[4,64,1664]{2,1,0:T(8,128)(2,1)S(1)}, bf16[512,512]{1,0:T(8,128)(2,1)S(1)}, bf16[128,1664]{1,0:T(8,128)(2,1)S(1)}, bf16[128,1664]{1,0:T(8,128)(2,1)S(1)}) custom-call(bf16[128,1664]{1,0:T(8,128)(2,1)S(1)} %collective-permute-done.10.refs_0_, ...), custom_call_target="tpu_custom_call" | custom-call | tf_op jit(solution)/shard_map/pallas_call | solution.py:275
  48.1 0.2 collective-permute-start.13
  48.3 2.2 %shard_map.56 = (bf16[4,688,128]{2,1,0:T(8,128)(2,1)S(1)}, bf16[4,688,128]{2,1,0:T(8,128)(2,1)S(1)}) custom-call(bf16[384,1664]{1,0:T(8,128)(2,1)S(1)} %get-tuple-element.53.x_ref, bf16[128,1664]{1,0:T(8,128)(2,1)S(1)} %get-tuple-element.56.x_last, bf16[384,1664]{1,0:T(8,128)(2,1)S(1)} %get-tuple-element.57.up_ref, ...), custom_call_target="tpu_custom_call" | custom-call | tf_op jit(solution)/shard_map/pallas_call | solution.py:275
  50.5 0.0 copy-start.1
  50.5 0.0 copy-start.3
  50.6 1.6 %collective-permute-start.12 = (bf16[4,688,128]{2,1,0:T(8,128)(2,1)S(1)}, bf16[4,688,128]{2,1,0:T(8,128)(2,1)S(1)}, u32[]{:S(2)}, u32[]{:S(2)}) collective-permute-start(bf16[4,688,128]{2,1,0:T(8,128)(2,1)S(1)} %get-tuple-element.60), channel_id=1, source_target_pairs={{0,2},{2,0},{1,3},{3,1},{4,6},{6,4},{5,7},{7,5},{8,10},{10,8},{9,1... | collective-permute-start | bytes 2113544 | tf_op jit(solution)/shard_map/ppermute | solution.py:302
  52.1 0.2 shard_map.57
  52.3 1.7 %collective-permute-start.14 = (bf16[64,1664]{1,0:T(8,128)(2,1)S(1)}, bf16[64,1664]{1,0:T(8,128)(2,1)S(1)}, u32[]{:S(2)}, u32[]{:S(2)}) collective-permute-start(bf16[64,1664]{1,0:T(8,128)(2,1)S(1)} %get-tuple-element.65), channel_id=1, source_target_pairs={{0,8},{4,12},{8,0},{12,4},{1,9},{5,13},{9,1},{13,5},{2,10},{6,14},... | collective-permute-start | bytes 638984 | tf_op jit(solution)/shard_map/ppermute | solution.py:296
  54.0 0.5 collective-permute-start.15
  54.5 2.2 %collective-permute-start.16 = (bf16[64,1664]{1,0:T(8,128)(2,1)S(1)}, bf16[64,1664]{1,0:T(8,128)(2,1)S(1)}, u32[]{:S(2)}, u32[]{:S(2)}) collective-permute-start(bf16[64,1664]{1,0:T(8,128)(2,1)S(1)} %get-tuple-element.67), channel_id=1, source_target_pairs={{0,4},{4,0},{8,12},{12,8},{1,5},{5,1},{9,13},{13,9},{2,6},{6,2},{1... | collective-permute-start | bytes 638984 | tf_op jit(solution)/shard_map/ppermute | solution.py:296
  56.8 11.9 %collective-permute-done.12.theirs_ref = bf16[4,688,128]{2,1,0:T(8,128)(2,1)S(1)} collective-permute-done((bf16[4,688,128]{2,1,0:T(8,128)(2,1)S(1)}, bf16[4,688,128]{2,1,0:T(8,128)(2,1)S(1)}, u32[]{:S(2)}, u32[]{:S(2)}) %collective-permute-start.12) | collective-permute-done | bytes 704544 | tf_op jit(solution)/shard_map/ppermute | solution.py:302
  68.7 0.2 shard_map.59
  68.9 1.7 %collective-permute-start.19 = (bf16[688,128]{1,0:T(8,128)(2,1)S(1)}, bf16[688,128]{1,0:T(8,128)(2,1)S(1)}, u32[]{:S(2)}, u32[]{:S(2)}) collective-permute-start(bf16[688,128]{1,0:T(8,128)(2,1)S(1)} %get-tuple-element.73), channel_id=1, source_target_pairs={{0,8},{4,12},{8,0},{12,4},{1,9},{5,13},{9,1},{13,5},{2,10},{6,14},... | collective-permute-start | bytes 528392 | tf_op jit(solution)/shard_map/ppermute | solution.py:296
  70.5 0.5 collective-permute-start.20
  71.1 2.2 %collective-permute-start.21 = (bf16[688,128]{1,0:T(8,128)(2,1)S(1)}, bf16[688,128]{1,0:T(8,128)(2,1)S(1)}, u32[]{:S(2)}, u32[]{:S(2)}) collective-permute-start(bf16[688,128]{1,0:T(8,128)(2,1)S(1)} %get-tuple-element.75), channel_id=1, source_target_pairs={{0,4},{4,0},{8,12},{12,8},{1,5},{5,1},{9,13},{13,9},{2,6},{6,2},{1... | collective-permute-start | bytes 528392 | tf_op jit(solution)/shard_map/ppermute | solution.py:296
  73.3 8.6 %collective-permute-done.15.refs_2_ = bf16[64,1664]{1,0:T(8,128)(2,1)S(1)} collective-permute-done((bf16[64,1664]{1,0:T(8,128)(2,1)S(1)}, bf16[64,1664]{1,0:T(8,128)(2,1)S(1)}, u32[]{:S(2)}, u32[]{:S(2)}) %collective-permute-start.15) | collective-permute-done | bytes 213024 | tf_op jit(solution)/shard_map/ppermute | solution.py:296
  81.9 0.5 shard_map.58
  82.4 0.1 collective-permute-start.17
  82.5 0.5 collective-permute-start.18
  82.9 1.7 %collective-permute-done.19.refs_5_ = bf16[688,128]{1,0:T(8,128)(2,1)S(1)} collective-permute-done((bf16[688,128]{1,0:T(8,128)(2,1)S(1)}, bf16[688,128]{1,0:T(8,128)(2,1)S(1)}, u32[]{:S(2)}, u32[]{:S(2)}) %collective-permute-start.19) | collective-permute-done | bytes 176160 | tf_op jit(solution)/shard_map/ppermute | solution.py:296
  84.7 3.9 %collective-permute-done.20.refs_6_ = bf16[688,128]{1,0:T(8,128)(2,1)S(1)} collective-permute-done((bf16[688,128]{1,0:T(8,128)(2,1)S(1)}, bf16[688,128]{1,0:T(8,128)(2,1)S(1)}, u32[]{:S(2)}, u32[]{:S(2)}) %collective-permute-start.20) | collective-permute-done | bytes 176160 | tf_op jit(solution)/shard_map/ppermute | solution.py:296
  88.6 1.6 %shard_map.60 = (bf16[128,1664]{1,0:T(8,128)(2,1)}, f32[4,208,416]{2,1,0:T(8,128)}) custom-call(bf16[32,1664]{1,0:T(8,128)(2,1)S(1)} %get-tuple-element.68.refs_0_, bf16[32,1664]{1,0:T(8,128)(2,1)S(1)} %get-tuple-element.69.refs_1_, bf16[32,1664]{1,0:T(8,128)(2,1)S(1)} %collective-permute-done.17.refs_2_, ...), custom_call_target="tpu_custom_call" | custom-call | tf_op jit(solution)/shard_map/pallas_call | solution.py:275
  (17 shorter events, 0.1 us)
Async XLA Ops:
  0.6 1.2 %copy-start.4 = (bf16[4,208,416]{2,1,0:T(8,128)(2,1)S(1)}, bf16[4,208,416]{2,1,0:T(8,128)(2,1)}, u32[]{:S(2)}) copy-start(bf16[4,208,416]{2,1,0:T(8,128)(2,1)} %w_ref.1) | copy-start | bytes 2076676
  2.4 5.9 %collective-permute-start = (bf16[352,128]{1,0:T(8,128)(2,1)S(1)}, bf16[352,128]{1,0:T(8,128)(2,1)S(1)}, u32[]{:S(2)}, u32[]{:S(2)}) collective-permute-start(bf16[352,128]{1,0:T(8,128)(2,1)S(1)} %get-tuple-element.41), channel_id=1, source_target_pairs={{0,4},{4,0},{8,12},{12,8},{1,5},{5,1},{9,13},{13,9},{2,6},{6,2},{1... | collective-permute-start | bytes 270344 | tf_op jit(solution)/shard_map/ppermute | solution.py:296
  2.4 18.4 %collective-permute-start.3 = (bf16[352,128]{1,0:T(8,128)(2,1)S(1)}, bf16[352,128]{1,0:T(8,128)(2,1)S(1)}, u32[]{:S(2)}, u32[]{:S(2)}) collective-permute-start(bf16[352,128]{1,0:T(8,128)(2,1)S(1)} %get-tuple-element.46), channel_id=1, source_target_pairs={{0,8},{4,12},{8,0},{12,4},{1,9},{5,13},{9,1},{13,5},{2,10},{6,14},... | collective-permute-start | bytes 270344 | tf_op jit(solution)/shard_map/ppermute | solution.py:296
  5.5 18.5 %collective-permute-start.4 = (bf16[352,128]{1,0:T(8,128)(2,1)S(1)}, bf16[352,128]{1,0:T(8,128)(2,1)S(1)}, u32[]{:S(2)}, u32[]{:S(2)}) collective-permute-start(bf16[352,128]{1,0:T(8,128)(2,1)S(1)} %get-tuple-element.47), channel_id=1, source_target_pairs={{0,12},{4,8},{8,4},{12,0},{1,13},{5,9},{9,5},{13,1},{2,14},{6,10},... | collective-permute-start | bytes 270344 | tf_op jit(solution)/shard_map/ppermute | solution.py:296
  5.9 1.0 %copy-start = (bf16[1,128,1664]{2,1,0:T(8,128)(2,1)S(1)}, bf16[1,128,1664]{2,1,0:T(8,128)(2,1)}, u32[]{:S(2)}) copy-start(bf16[1,128,1664]{2,1,0:T(8,128)(2,1)} %param.3) | copy-start | bytes 1277956
  6.9 1.0 %copy-start.2 = (bf16[1,128,1664]{2,1,0:T(8,128)(2,1)S(1)}, bf16[1,128,1664]{2,1,0:T(8,128)(2,1)}, u32[]{:S(2)}) copy-start(bf16[1,128,1664]{2,1,0:T(8,128)(2,1)} %param.4) | copy-start | bytes 1277956
  8.3 24.7 %collective-permute-start.2 = (bf16[128,1664]{1,0:T(8,128)(2,1)S(1)}, bf16[128,1664]{1,0:T(8,128)(2,1)S(1)}, u32[]{:S(2)}, u32[]{:S(2)}) collective-permute-start(bf16[128,1664]{1,0:T(8,128)(2,1)S(1)} %get-tuple-element.42.refs_0_), channel_id=1, source_target_pairs={{0,8},{4,12},{8,0},{12,4},{1,9},{5,13},{9,1},{13,5},{2,10},{6,14},... | collective-permute-start | bytes 1277960 | tf_op jit(solution)/shard_map/ppermute | solution.py:296
  11.8 21.2 %collective-permute-start.1 = (bf16[128,1664]{1,0:T(8,128)(2,1)S(1)}, bf16[128,1664]{1,0:T(8,128)(2,1)S(1)}, u32[]{:S(2)}, u32[]{:S(2)}) collective-permute-start(bf16[128,1664]{1,0:T(8,128)(2,1)S(1)} %get-tuple-element.42.refs_0_), channel_id=1, source_target_pairs={{0,4},{4,0},{8,12},{12,8},{1,5},{5,1},{9,13},{13,9},{2,6},{6,2},{1... | collective-permute-start | bytes 1277960 | tf_op jit(solution)/shard_map/ppermute | solution.py:296
  24.0 7.6 %collective-permute-start.6 = (bf16[1408,128]{1,0:T(8,128)(2,1)S(1)}, bf16[1408,128]{1,0:T(8,128)(2,1)S(1)}, u32[]{:S(2)}, u32[]{:S(2)}) collective-permute-start(bf16[1408,128]{1,0:T(8,128)(2,1)S(1)} %shard_map.52.refs_0_), channel_id=1, source_target_pairs={{0,16},{16,0},{1,17},{17,1},{2,18},{18,2},{3,19},{19,3},{4,20},{20... | collective-permute-start | bytes 1081352 | tf_op jit(solution)/shard_map/ppermute | solution.py:302
  25.6 7.4 %collective-permute-start.5 = (bf16[1408,128]{1,0:T(8,128)(2,1)S(1)}, bf16[1408,128]{1,0:T(8,128)(2,1)S(1)}, u32[]{:S(2)}, u32[]{:S(2)}) collective-permute-start(bf16[1408,128]{1,0:T(8,128)(2,1)S(1)} %shard_map.52.refs_0_), channel_id=1, source_target_pairs={{0,2},{2,0},{1,3},{3,1},{4,6},{6,4},{5,7},{7,5},{8,10},{10,8},{9,1... | collective-permute-start | bytes 1081352 | tf_op jit(solution)/shard_map/ppermute | solution.py:302
  33.0 10.5 %collective-permute-start.10 = (bf16[128,1664]{1,0:T(8,128)(2,1)S(1)}, bf16[128,1664]{1,0:T(8,128)(2,1)S(1)}, u32[]{:S(2)}, u32[]{:S(2)}) collective-permute-start(bf16[128,1664]{1,0:T(8,128)(2,1)S(1)} %collective-permute-done.2.refs_4_), channel_id=1, source_target_pairs={{0,4},{4,0},{8,12},{12,8},{1,5},{5,1},{9,13},{13,9},{2,6},{6,2},{1... | collective-permute-start | bytes 1277960 | tf_op jit(solution)/shard_map/ppermute | solution.py:296
  33.5 9.1 %collective-permute-start.9 = (bf16[1408,128]{1,0:T(8,128)(2,1)S(1)}, bf16[1408,128]{1,0:T(8,128)(2,1)S(1)}, u32[]{:S(2)}, u32[]{:S(2)}) collective-permute-start(bf16[1408,128]{1,0:T(8,128)(2,1)S(1)} %collective-permute-done.6.refs_2_), channel_id=1, source_target_pairs={{0,2},{2,0},{1,3},{3,1},{4,6},{6,4},{5,7},{7,5},{8,10},{10,8},{9,1... | collective-permute-start | bytes 1081352 | tf_op jit(solution)/shard_map/ppermute | solution.py:302
  35.0 8.6 %collective-permute-start.8 = (bf16[128,1664]{1,0:T(8,128)(2,1)S(1)}, bf16[128,1664]{1,0:T(8,128)(2,1)S(1)}, u32[]{:S(2)}, u32[]{:S(2)}) collective-permute-start(bf16[128,1664]{1,0:T(8,128)(2,1)S(1)} %collective-permute-done.2.refs_4_), channel_id=1, source_target_pairs={{0,1},{1,0},{2,3},{3,2},{4,5},{5,4},{6,7},{7,6},{8,9},{9,8},{10,11... | collective-permute-start | bytes 1277960 | tf_op jit(solution)/shard_map/ppermute | solution.py:302
  35.0 8.6 %collective-permute-start.7 = (bf16[128,1664]{1,0:T(8,128)(2,1)S(1)}, bf16[128,1664]{1,0:T(8,128)(2,1)S(1)}, u32[]{:S(2)}, u32[]{:S(2)}) collective-permute-start(bf16[128,1664]{1,0:T(8,128)(2,1)S(1)} %collective-permute-done.1.refs_2_), channel_id=1, source_target_pairs={{0,1},{1,0},{2,3},{3,2},{4,5},{5,4},{6,7},{7,6},{8,9},{9,8},{10,11... | collective-permute-start | bytes 1277960 | tf_op jit(solution)/shard_map/ppermute | solution.py:302
  43.5 1.8 %collective-permute-start.11 = (bf16[128,1664]{1,0:T(8,128)(2,1)S(1)}, bf16[128,1664]{1,0:T(8,128)(2,1)S(1)}, u32[]{:S(2)}, u32[]{:S(2)}) collective-permute-start(bf16[128,1664]{1,0:T(8,128)(2,1)S(1)} %collective-permute-done.10.refs_0_), channel_id=1, source_target_pairs={{0,1},{1,0},{2,3},{3,2},{4,5},{5,4},{6,7},{7,6},{8,9},{9,8},{10,11... | collective-permute-start | bytes 1277960 | tf_op jit(solution)/shard_map/ppermute | solution.py:302
  48.1 4.0 %collective-permute-start.13 = (bf16[4,64,1664]{2,1,0:T(8,128)(2,1)S(1)}, bf16[4,64,1664]{2,1,0:T(8,128)(2,1)S(1)}, u32[]{:S(2)}, u32[]{:S(2)}) collective-permute-start(bf16[4,64,1664]{2,1,0:T(8,128)(2,1)S(1)} %get-tuple-element.62), channel_id=1, source_target_pairs={{0,1},{1,0},{2,3},{3,2},{4,5},{5,4},{6,7},{7,6},{8,9},{9,8},{10,11... | collective-permute-start | bytes 2555912 | tf_op jit(solution)/shard_map/ppermute | solution.py:302
  50.5 31.4 %copy-start.1 = (bf16[1,128,1664]{2,1,0:T(8,128)(2,1)S(1)}, bf16[1,128,1664]{2,1,0:T(8,128)(2,1)}, u32[]{:S(2)}) copy-start(bf16[1,128,1664]{2,1,0:T(8,128)(2,1)} %param.3) | copy-start | bytes 1277956
  50.5 31.4 %copy-start.3 = (bf16[1,128,1664]{2,1,0:T(8,128)(2,1)S(1)}, bf16[1,128,1664]{2,1,0:T(8,128)(2,1)}, u32[]{:S(2)}) copy-start(bf16[1,128,1664]{2,1,0:T(8,128)(2,1)} %param.4) | copy-start | bytes 1277956
  50.6 18.1 %collective-permute-start.12 = (bf16[4,688,128]{2,1,0:T(8,128)(2,1)S(1)}, bf16[4,688,128]{2,1,0:T(8,128)(2,1)S(1)}, u32[]{:S(2)}, u32[]{:S(2)}) collective-permute-start(bf16[4,688,128]{2,1,0:T(8,128)(2,1)S(1)} %get-tuple-element.60), channel_id=1, source_target_pairs={{0,2},{2,0},{1,3},{3,1},{4,6},{6,4},{5,7},{7,5},{8,10},{10,8},{9,1... | collective-permute-start | bytes 2113544 | tf_op jit(solution)/shard_map/ppermute | solution.py:302
  52.3 18.7 %collective-permute-start.14 = (bf16[64,1664]{1,0:T(8,128)(2,1)S(1)}, bf16[64,1664]{1,0:T(8,128)(2,1)S(1)}, u32[]{:S(2)}, u32[]{:S(2)}) collective-permute-start(bf16[64,1664]{1,0:T(8,128)(2,1)S(1)} %get-tuple-element.65), channel_id=1, source_target_pairs={{0,8},{4,12},{8,0},{12,4},{1,9},{5,13},{9,1},{13,5},{2,10},{6,14},... | collective-permute-start | bytes 638984 | tf_op jit(solution)/shard_map/ppermute | solution.py:296
  54.0 27.9 %collective-permute-start.15 = (bf16[64,1664]{1,0:T(8,128)(2,1)S(1)}, bf16[64,1664]{1,0:T(8,128)(2,1)S(1)}, u32[]{:S(2)}, u32[]{:S(2)}) collective-permute-start(bf16[64,1664]{1,0:T(8,128)(2,1)S(1)} %get-tuple-element.66), channel_id=1, source_target_pairs={{0,12},{4,8},{8,4},{12,0},{1,13},{5,9},{9,5},{13,1},{2,14},{6,10},... | collective-permute-start | bytes 638984 | tf_op jit(solution)/shard_map/ppermute | solution.py:296
  54.5 27.4 %collective-permute-start.16 = (bf16[64,1664]{1,0:T(8,128)(2,1)S(1)}, bf16[64,1664]{1,0:T(8,128)(2,1)S(1)}, u32[]{:S(2)}, u32[]{:S(2)}) collective-permute-start(bf16[64,1664]{1,0:T(8,128)(2,1)S(1)} %get-tuple-element.67), channel_id=1, source_target_pairs={{0,4},{4,0},{8,12},{12,8},{1,5},{5,1},{9,13},{13,9},{2,6},{6,2},{1... | collective-permute-start | bytes 638984 | tf_op jit(solution)/shard_map/ppermute | solution.py:296
  68.9 15.8 %collective-permute-start.19 = (bf16[688,128]{1,0:T(8,128)(2,1)S(1)}, bf16[688,128]{1,0:T(8,128)(2,1)S(1)}, u32[]{:S(2)}, u32[]{:S(2)}) collective-permute-start(bf16[688,128]{1,0:T(8,128)(2,1)S(1)} %get-tuple-element.73), channel_id=1, source_target_pairs={{0,8},{4,12},{8,0},{12,4},{1,9},{5,13},{9,1},{13,5},{2,10},{6,14},... | collective-permute-start | bytes 528392 | tf_op jit(solution)/shard_map/ppermute | solution.py:296
  70.5 18.1 %collective-permute-start.20 = (bf16[688,128]{1,0:T(8,128)(2,1)S(1)}, bf16[688,128]{1,0:T(8,128)(2,1)S(1)}, u32[]{:S(2)}, u32[]{:S(2)}) collective-permute-start(bf16[688,128]{1,0:T(8,128)(2,1)S(1)} %get-tuple-element.74), channel_id=1, source_target_pairs={{0,12},{4,8},{8,4},{12,0},{1,13},{5,9},{9,5},{13,1},{2,14},{6,10},... | collective-permute-start | bytes 528392 | tf_op jit(solution)/shard_map/ppermute | solution.py:296
  71.1 17.5 %collective-permute-start.21 = (bf16[688,128]{1,0:T(8,128)(2,1)S(1)}, bf16[688,128]{1,0:T(8,128)(2,1)S(1)}, u32[]{:S(2)}, u32[]{:S(2)}) collective-permute-start(bf16[688,128]{1,0:T(8,128)(2,1)S(1)} %get-tuple-element.75), channel_id=1, source_target_pairs={{0,4},{4,0},{8,12},{12,8},{1,5},{5,1},{9,13},{13,9},{2,6},{6,2},{1... | collective-permute-start | bytes 528392 | tf_op jit(solution)/shard_map/ppermute | solution.py:296
  82.4 6.2 %collective-permute-start.17 = (bf16[32,1664]{1,0:T(8,128)(2,1)S(1)}, bf16[32,1664]{1,0:T(8,128)(2,1)S(1)}, u32[]{:S(2)}, u32[]{:S(2)}) collective-permute-start(bf16[32,1664]{1,0:T(8,128)(2,1)S(1)} %get-tuple-element.68.refs_0_), channel_id=1, source_target_pairs={{0,1},{1,0},{2,3},{3,2},{4,5},{5,4},{6,7},{7,6},{8,9},{9,8},{10,11... | collective-permute-start | bytes 319496 | tf_op jit(solution)/shard_map/ppermute | solution.py:302
  82.5 6.2 %collective-permute-start.18 = (bf16[32,1664]{1,0:T(8,128)(2,1)S(1)}, bf16[32,1664]{1,0:T(8,128)(2,1)S(1)}, u32[]{:S(2)}, u32[]{:S(2)}) collective-permute-start(bf16[32,1664]{1,0:T(8,128)(2,1)S(1)} %get-tuple-element.69.refs_1_), channel_id=1, source_target_pairs={{0,1},{1,0},{2,3},{3,2},{4,5},{5,4},{6,7},{7,6},{8,9},{9,8},{10,11... | collective-permute-start | bytes 319496 | tf_op jit(solution)/shard_map/ppermute | solution.py:302

commit v11 on v10

--- a/solution.py
+++ b/solution.py
@@ -40,6 +40,8 @@
 
 
 SPARE = SLOT - HD
+W_ORDER = (0, 2, 3, 1)
+X_ORDER = (0, 2, 3, 1)
 ORDER = (0, 2, 3, 1)
 LEFT = HD - 3 * SPARE
 FOLD = SLOT // LEFT
@@ -89,7 +91,7 @@
         for j, tile in enumerate(packed(mats)):
             staged[head, j * share : j * share + tile.shape[0], :] = tile
     first = pl.multiple_of(group * (staged.shape[1] - count), 16)
-    for k, out in enumerate(outs):
+    for k, out in zip(W_ORDER, outs):
         out[...] = staged[me ^ k, pl.ds(first, count), :]
 
 
@@ -123,7 +125,7 @@
 
 def merge_kernel(*refs):
     share = refs[0].shape[0]
-    for k, ref in enumerate(refs[:-1]):
+    for k, ref in zip(W_ORDER, refs[:-1]):
         refs[-1][k * share : (k + 1) * share] = ref[...]
 
 
@@ -167,7 +169,7 @@
     grad_out_all = made[:, 3 * SLOT :]
     scores = nt(made[:, :SLOT], key_rows) * scale
     weight = jnp.exp(scores - jnp.max(scores, axis=1, keepdims=True))
-    probs_all = (weight / jnp.sum(weight, axis=1, keepdims=True)).astype(BF)
+    probs_all = (weight * (1.0 / jnp.sum(weight, axis=1, keepdims=True))).astype(BF)
     attended = nn(probs_all, value_rows).astype(BF)
     delta = jnp.sum(grad_out_all.astype(F32) * attended.astype(F32), axis=1, keepdims=True)
     dprobs = nt(grad_out_all, value_rows)
@@ -214,8 +216,8 @@
                 target[k, j * share : j * share + tile.shape[0], :] = tile
 
 
-def sum_kernel(mine_ref, theirs_ref, *outs):
-    for out, k in zip(outs, ORDER):
+def sum_kernel(order, mine_ref, theirs_ref, *outs):
+    for out, k in zip(outs, order):
         out[...] = (mine_ref[k].astype(F32) + theirs_ref[k].astype(F32)).astype(BF)
 
 
@@ -295,8 +297,8 @@
     def across(value, k):
         return lax.ppermute(value, "seq", [(i, i ^ k) for i in range(n)])
 
-    def exchange(values):
-        return [across(value, k) for value, k in zip(values[1:], ORDER[1:])]
+    def exchange(values, order):
+        return [across(value, k) for value, k in zip(values[1:], order[1:])]
 
     def swap(value, axis):
         return lax.ppermute(value, axis, [(0, 1), (1, 0)])
@@ -310,18 +312,18 @@
         [pltpu.VMEM((n, full, SLOT), BF)],
         plain=1,
     )
-    arrived = [across(chunks[k], k) for k in range(1, n)]
+    arrived = [across(c, k) for c, k in zip(chunks[1:], W_ORDER[1:])]
     send, rest = call(
         norm_kernel, [((rows, width), BF)] * 2, (x, up), [pltpu.VMEM((rows, width), BF)], plain=2
     )
-    send, arrived[0] = lax.optimization_barrier((send, arrived[0]))
+    send, arrived[2] = lax.optimization_barrier((send, arrived[2]))
     merged = call(merge_kernel, ((n * count, SLOT), BF), (chunks[0], *arrived))
     beside = swap(merged, "dp")
     above = swap(merged, "grp")
+    corner = swap(above, "dp")
     second = across(send, 2)
     first = across(send, 1)
     first, second, beside, above = lax.optimization_barrier((first, second, beside, above))
-    corner = swap(above, "dp")
     weights = call(
         functools.partial(weights_kernel, n, share),
         ((width, 4 * SLOT), BF),
@@ -355,13 +357,13 @@
     )
     taken = swap(give, "pipe")
     w_taken = swap(w_give, "dp")
-    sums = call(sum_kernel, [((half, width), BF)] * n, (keep, taken))
-    parts = exchange(sums)
+    sums = call(functools.partial(sum_kernel, X_ORDER), [((half, width), BF)] * n, (keep, taken))
+    parts = exchange(sums, X_ORDER)
     w_taken, sums[0] = lax.optimization_barrier((w_taken, sums[0]))
     w_sums = call(
-        sum_kernel, [((full, SLOT), BF)] * n, (w_keep, w_taken)
-    )
-    w_parts = [w_sums[0]] + exchange(w_sums)
+        functools.partial(sum_kernel, ORDER), [((full, SLOT), BF)] * n, (w_keep, w_taken)
+    )
+    w_parts = [w_sums[0]] + exchange(w_sums, ORDER)
     mine = call(
         functools.partial(final_kernel, n),
         [((half // 2, width), BF)] * 2,

time: 90.5 us -> 90.5 us (level)
  no operation moved by 1% of the time
where the time goes in v11:
time: 90.5 us; the launch traced here: 90.2 us
  waiting for transfers between devices  51.8 us (57%)
  starting transfers between devices  24 us (27%)
  Pallas kernels  10.5 us (12%)
  local copies, waits for them, and re-layouts  3.18 us (4%)
    ppermute x12, waiting for transfers between devices, across(): return lax.ppermute(value, 'seq', [(i, i ^ k) for i in range(n)])  26.4 us
    ppermute x10, waiting for transfers between devices, swap(): return lax.ppermute(value, axis, [(0, 1), (1, 0)])  25.5 us
    ppermute x12, starting transfers between devices, across(): return lax.ppermute(value, 'seq', [(i, i ^ k) for i in range(n)])  16.5 us
    pallas_call x11, Pallas kernels, call(): pl.pallas_call(kernel, out_shape=[out_space(*s) for s in shapes], in_spec...  10.5 us
    ppermute x10, starting transfers between devices, swap(): return lax.ppermute(value, axis, [(0, 1), (1, 0)])  7.49 us
    unnamed x10, local copies, waits for them, and re-layouts  3.18 us
  transfers between devices with their start and end apart: 22, of which 10 were waited for; matrix products, arithmetic and copies ran while one was open for 0% of the time, Pallas kernels for 6%

profile of v11, /device:TPU:8, one launch (start us, length us, event | category | flops | bytes accessed | tf_op | source)
XLA Modules:
  0.0 90.2 jit_solution(13987495374100853088)
XLA Ops:
  0.6 1.1 %copy-done.4 = bf16[4,208,416]{2,1,0:T(8,128)(2,1)S(1)} copy-done((bf16[4,208,416]{2,1,0:T(8,128)(2,1)S(1)}, bf16[4,208,416]{2,1,0:T(8,128)(2,1)}, u32[]{:S(2)}) %copy-start.4) | copy-done | bytes 692248
  1.8 0.6 shard_map.51
  2.4 0.1 collective-permute-start
  2.4 3.0 %collective-permute-start.3 = (bf16[352,128]{1,0:T(8,128)(2,1)S(1)}, bf16[352,128]{1,0:T(8,128)(2,1)S(1)}, u32[]{:S(2)}, u32[]{:S(2)}) collective-permute-start(bf16[352,128]{1,0:T(8,128)(2,1)S(1)} %get-tuple-element.45), channel_id=1, source_target_pairs={{0,8},{4,12},{8,0},{12,4},{1,9},{5,13},{9,1},{13,5},{2,10},{6,14},... | collective-permute-start | bytes 270344 | tf_op jit(solution)/shard_map/ppermute | solution.py:298
  5.5 0.5 collective-permute-start.4
  5.9 1.0 %copy-done = bf16[1,128,1664]{2,1,0:T(8,128)(2,1)S(1)} copy-done((bf16[1,128,1664]{2,1,0:T(8,128)(2,1)S(1)}, bf16[1,128,1664]{2,1,0:T(8,128)(2,1)}, u32[]{:S(2)}) %copy-start) | copy-done | bytes 426008
  6.9 1.0 %copy-done.2 = bf16[1,128,1664]{2,1,0:T(8,128)(2,1)S(1)} copy-done((bf16[1,128,1664]{2,1,0:T(8,128)(2,1)S(1)}, bf16[1,128,1664]{2,1,0:T(8,128)(2,1)}, u32[]{:S(2)}) %copy-start.2) | copy-done | bytes 426008
  7.9 0.3 shard_map.50
  8.3 0.0 collective-permute-done.refs_3_
  8.3 3.6 %collective-permute-start.2 = (bf16[128,1664]{1,0:T(8,128)(2,1)S(1)}, bf16[128,1664]{1,0:T(8,128)(2,1)S(1)}, u32[]{:S(2)}, u32[]{:S(2)}) collective-permute-start(bf16[128,1664]{1,0:T(8,128)(2,1)S(1)} %get-tuple-element.42.refs_0_), channel_id=1, source_target_pairs={{0,8},{4,12},{8,0},{12,4},{1,9},{5,13},{9,1},{13,5},{2,10},{6,14},... | collective-permute-start | bytes 1277960 | tf_op jit(solution)/shard_map/ppermute | solution.py:298
  11.8 9.0 %collective-permute-done.3.refs_1_ = bf16[352,128]{1,0:T(8,128)(2,1)S(1)} collective-permute-done((bf16[352,128]{1,0:T(8,128)(2,1)S(1)}, bf16[352,128]{1,0:T(8,128)(2,1)S(1)}, u32[]{:S(2)}, u32[]{:S(2)}) %collective-permute-start.3) | collective-permute-done | bytes 90144 | tf_op jit(solution)/shard_map/ppermute | solution.py:298
  20.8 3.1 %collective-permute-done.4.refs_2_ = bf16[352,128]{1,0:T(8,128)(2,1)S(1)} collective-permute-done((bf16[352,128]{1,0:T(8,128)(2,1)S(1)}, bf16[352,128]{1,0:T(8,128)(2,1)S(1)}, u32[]{:S(2)}, u32[]{:S(2)}) %collective-permute-start.4) | collective-permute-done | bytes 90144 | tf_op jit(solution)/shard_map/ppermute | solution.py:298
  24.0 1.6 %collective-permute-start.6 = (bf16[1408,128]{1,0:T(8,128)(2,1)S(1)}, bf16[1408,128]{1,0:T(8,128)(2,1)S(1)}, u32[]{:S(2)}, u32[]{:S(2)}) collective-permute-start(bf16[1408,128]{1,0:T(8,128)(2,1)S(1)} %shard_map.52.refs_0_), channel_id=1, source_target_pairs={{0,16},{16,0},{1,17},{17,1},{2,18},{18,2},{3,19},{19,3},{4,20},{20... | collective-permute-start | bytes 1081352 | tf_op jit(solution)/shard_map/ppermute | solution.py:304
  25.6 1.5 %collective-permute-start.5 = (bf16[1408,128]{1,0:T(8,128)(2,1)S(1)}, bf16[1408,128]{1,0:T(8,128)(2,1)S(1)}, u32[]{:S(2)}, u32[]{:S(2)}) collective-permute-start(bf16[1408,128]{1,0:T(8,128)(2,1)S(1)} %shard_map.52.refs_0_), channel_id=1, source_target_pairs={{0,2},{2,0},{1,3},{3,1},{4,6},{6,4},{5,7},{7,5},{8,10},{10,8},{9,1... | collective-permute-start | bytes 1081352 | tf_op jit(solution)/shard_map/ppermute | solution.py:304
  27.0 4.5 %collective-permute-done.6.refs_2_ = bf16[1408,128]{1,0:T(8,128)(2,1)S(1)} collective-permute-done((bf16[1408,128]{1,0:T(8,128)(2,1)S(1)}, bf16[1408,128]{1,0:T(8,128)(2,1)S(1)}, u32[]{:S(2)}, u32[]{:S(2)}) %collective-permute-start.6) | collective-permute-done | bytes 360480 | tf_op jit(solution)/shard_map/ppermute | solution.py:304
  31.6 1.4 %collective-permute-done.5.refs_1_ = bf16[1408,128]{1,0:T(8,128)(2,1)S(1)} collective-permute-done((bf16[1408,128]{1,0:T(8,128)(2,1)S(1)}, bf16[1408,128]{1,0:T(8,128)(2,1)S(1)}, u32[]{:S(2)}, u32[]{:S(2)}) %collective-permute-start.5) | collective-permute-done | bytes 360480 | tf_op jit(solution)/shard_map/ppermute | solution.py:304
  33.0 0.0 collective-permute-done.2.refs_4_
  33.0 0.0 collective-permute-done.1.refs_2_
  33.0 0.5 collective-permute-start.10
  33.5 1.5 %collective-permute-start.9 = (bf16[1408,128]{1,0:T(8,128)(2,1)S(1)}, bf16[1408,128]{1,0:T(8,128)(2,1)S(1)}, u32[]{:S(2)}, u32[]{:S(2)}) collective-permute-start(bf16[1408,128]{1,0:T(8,128)(2,1)S(1)} %collective-permute-done.6.refs_2_), channel_id=1, source_target_pairs={{0,2},{2,0},{1,3},{3,1},{4,6},{6,4},{5,7},{7,5},{8,10},{10,8},{9,1... | collective-permute-start | bytes 1081352 | tf_op jit(solution)/shard_map/ppermute | solution.py:304
  35.0 0.5 collective-permute-start.7
  35.5 7.1 %collective-permute-done.9.refs_3_ = bf16[1408,128]{1,0:T(8,128)(2,1)S(1)} collective-permute-done((bf16[1408,128]{1,0:T(8,128)(2,1)S(1)}, bf16[1408,128]{1,0:T(8,128)(2,1)S(1)}, u32[]{:S(2)}, u32[]{:S(2)}) %collective-permute-start.9) | collective-permute-done | bytes 360480 | tf_op jit(solution)/shard_map/ppermute | solution.py:304
  42.6 0.9 %shard_map.53.refs_6_.refs_3_ = bf16[1664,512]{1,0:T(8,128)(2,1)S(1)} custom-call(bf16[1408,128]{1,0:T(8,128)(2,1)S(1)} %shard_map.52.refs_0_, bf16[1408,128]{1,0:T(8,128)(2,1)S(1)} %collective-permute-done.5.refs_1_, bf16[1408,128]{1,0:T(8,128)(2,1)S(1)} %collective-permute-done.6.refs_2_, bf16[1408,128]{1,0:T(8,128)(2,1)S(1)} %collective-permute-done.9.refs_3_), custom_call_target="tpu_custom_call" | custom-call | tf_op jit(solution)/shard_map/pallas_call | solution.py:277
  43.5 0.1 collective-permute-start.11
  43.6 1.2 %shard_map.54 = (bf16[384,1664]{1,0:T(8,128)(2,1)S(1)}, bf16[384,1664]{1,0:T(8,128)(2,1)S(1)}, bf16[384,512]{1,0:T(8,128)(2,1)S(1)}) custom-call(bf16[128,1664]{1,0:T(8,128)(2,1)S(1)} %get-tuple-element.42.refs_0_, bf16[128,1664]{1,0:T(8,128)(2,1)S(1)} %get-tuple-element.43.refs_1_, bf16[128,1664]{1,0:T(8,128)(2,1)S(1)} %collective-permute-done.1.refs_2_, ...), custom_call_target="tpu_custom_call" | custom-call | tf_op jit(solution)/shard_map/pallas_call | solution.py:277
  44.8 0.5 collective-permute-done.11.refs_1_
  45.3 2.8 %shard_map.55 = (bf16[4,64,1664]{2,1,0:T(8,128)(2,1)S(1)}, bf16[4,64,1664]{2,1,0:T(8,128)(2,1)S(1)}, bf16[512,512]{1,0:T(8,128)(2,1)S(1)}, bf16[128,1664]{1,0:T(8,128)(2,1)S(1)}, bf16[128,1664]{1,0:T(8,128)(2,1)S(1)}) custom-call(bf16[128,1664]{1,0:T(8,128)(2,1)S(1)} %collective-permute-done.10.refs_0_, ...), custom_call_target="tpu_custom_call" | custom-call | tf_op jit(solution)/shard_map/pallas_call | solution.py:277
  48.1 0.2 collective-permute-start.13
  48.3 2.2 %shard_map.56 = (bf16[4,688,128]{2,1,0:T(8,128)(2,1)S(1)}, bf16[4,688,128]{2,1,0:T(8,128)(2,1)S(1)}) custom-call(bf16[384,1664]{1,0:T(8,128)(2,1)S(1)} %get-tuple-element.53.x_ref, bf16[128,1664]{1,0:T(8,128)(2,1)S(1)} %get-tuple-element.56.x_last, bf16[384,1664]{1,0:T(8,128)(2,1)S(1)} %get-tuple-element.57.up_ref, ...), custom_call_target="tpu_custom_call" | custom-call | tf_op jit(solution)/shard_map/pallas_call | solution.py:277
  50.5 0.0 copy-start.1
  50.5 0.0 copy-start.3
  50.6 1.6 %collective-permute-start.12 = (bf16[4,688,128]{2,1,0:T(8,128)(2,1)S(1)}, bf16[4,688,128]{2,1,0:T(8,128)(2,1)S(1)}, u32[]{:S(2)}, u32[]{:S(2)}) collective-permute-start(bf16[4,688,128]{2,1,0:T(8,128)(2,1)S(1)} %get-tuple-element.60), channel_id=1, source_target_pairs={{0,2},{2,0},{1,3},{3,1},{4,6},{6,4},{5,7},{7,5},{8,10},{10,8},{9,1... | collective-permute-start | bytes 2113544 | tf_op jit(solution)/shard_map/ppermute | solution.py:304
  52.1 0.2 shard_map.57
  52.3 1.7 %collective-permute-start.14 = (bf16[64,1664]{1,0:T(8,128)(2,1)S(1)}, bf16[64,1664]{1,0:T(8,128)(2,1)S(1)}, u32[]{:S(2)}, u32[]{:S(2)}) collective-permute-start(bf16[64,1664]{1,0:T(8,128)(2,1)S(1)} %get-tuple-element.65), channel_id=1, source_target_pairs={{0,8},{4,12},{8,0},{12,4},{1,9},{5,13},{9,1},{13,5},{2,10},{6,14},... | collective-permute-start | bytes 638984 | tf_op jit(solution)/shard_map/ppermute | solution.py:298
  54.0 0.5 collective-permute-start.15
  54.5 2.2 %collective-permute-start.16 = (bf16[64,1664]{1,0:T(8,128)(2,1)S(1)}, bf16[64,1664]{1,0:T(8,128)(2,1)S(1)}, u32[]{:S(2)}, u32[]{:S(2)}) collective-permute-start(bf16[64,1664]{1,0:T(8,128)(2,1)S(1)} %get-tuple-element.67), channel_id=1, source_target_pairs={{0,4},{4,0},{8,12},{12,8},{1,5},{5,1},{9,13},{13,9},{2,6},{6,2},{1... | collective-permute-start | bytes 638984 | tf_op jit(solution)/shard_map/ppermute | solution.py:298
  56.8 11.9 %collective-permute-done.12.theirs_ref = bf16[4,688,128]{2,1,0:T(8,128)(2,1)S(1)} collective-permute-done((bf16[4,688,128]{2,1,0:T(8,128)(2,1)S(1)}, bf16[4,688,128]{2,1,0:T(8,128)(2,1)S(1)}, u32[]{:S(2)}, u32[]{:S(2)}) %collective-permute-start.12) | collective-permute-done | bytes 704544 | tf_op jit(solution)/shard_map/ppermute | solution.py:304
  68.7 0.2 shard_map.59
  68.9 1.7 %collective-permute-start.19 = (bf16[688,128]{1,0:T(8,128)(2,1)S(1)}, bf16[688,128]{1,0:T(8,128)(2,1)S(1)}, u32[]{:S(2)}, u32[]{:S(2)}) collective-permute-start(bf16[688,128]{1,0:T(8,128)(2,1)S(1)} %get-tuple-element.73), channel_id=1, source_target_pairs={{0,8},{4,12},{8,0},{12,4},{1,9},{5,13},{9,1},{13,5},{2,10},{6,14},... | collective-permute-start | bytes 528392 | tf_op jit(solution)/shard_map/ppermute | solution.py:298
  70.5 0.5 collective-permute-start.20
  71.1 2.2 %collective-permute-start.21 = (bf16[688,128]{1,0:T(8,128)(2,1)S(1)}, bf16[688,128]{1,0:T(8,128)(2,1)S(1)}, u32[]{:S(2)}, u32[]{:S(2)}) collective-permute-start(bf16[688,128]{1,0:T(8,128)(2,1)S(1)} %get-tuple-element.75), channel_id=1, source_target_pairs={{0,4},{4,0},{8,12},{12,8},{1,5},{5,1},{9,13},{13,9},{2,6},{6,2},{1... | collective-permute-start | bytes 528392 | tf_op jit(solution)/shard_map/ppermute | solution.py:298
  73.3 8.6 %collective-permute-done.15.refs_2_ = bf16[64,1664]{1,0:T(8,128)(2,1)S(1)} collective-permute-done((bf16[64,1664]{1,0:T(8,128)(2,1)S(1)}, bf16[64,1664]{1,0:T(8,128)(2,1)S(1)}, u32[]{:S(2)}, u32[]{:S(2)}) %collective-permute-start.15) | collective-permute-done | bytes 213024 | tf_op jit(solution)/shard_map/ppermute | solution.py:298
  81.9 0.5 shard_map.58
  82.4 0.1 collective-permute-start.17
  82.5 0.5 collective-permute-start.18
  82.9 1.7 %collective-permute-done.19.refs_5_ = bf16[688,128]{1,0:T(8,128)(2,1)S(1)} collective-permute-done((bf16[688,128]{1,0:T(8,128)(2,1)S(1)}, bf16[688,128]{1,0:T(8,128)(2,1)S(1)}, u32[]{:S(2)}, u32[]{:S(2)}) %collective-permute-start.19) | collective-permute-done | bytes 176160 | tf_op jit(solution)/shard_map/ppermute | solution.py:298
  84.7 3.9 %collective-permute-done.20.refs_6_ = bf16[688,128]{1,0:T(8,128)(2,1)S(1)} collective-permute-done((bf16[688,128]{1,0:T(8,128)(2,1)S(1)}, bf16[688,128]{1,0:T(8,128)(2,1)S(1)}, u32[]{:S(2)}, u32[]{:S(2)}) %collective-permute-start.20) | collective-permute-done | bytes 176160 | tf_op jit(solution)/shard_map/ppermute | solution.py:298
  88.6 1.6 %shard_map.60 = (bf16[128,1664]{1,0:T(8,128)(2,1)}, f32[4,208,416]{2,1,0:T(8,128)}) custom-call(bf16[32,1664]{1,0:T(8,128)(2,1)S(1)} %get-tuple-element.68.refs_0_, bf16[32,1664]{1,0:T(8,128)(2,1)S(1)} %get-tuple-element.69.refs_1_, bf16[32,1664]{1,0:T(8,128)(2,1)S(1)} %collective-permute-done.17.refs_2_, ...), custom_call_target="tpu_custom_call" | custom-call | tf_op jit(solution)/shard_map/pallas_call | solution.py:277
  (17 shorter events, 0.1 us)
Async XLA Ops:
  0.6 1.2 %copy-start.4 = (bf16[4,208,416]{2,1,0:T(8,128)(2,1)S(1)}, bf16[4,208,416]{2,1,0:T(8,128)(2,1)}, u32[]{:S(2)}) copy-start(bf16[4,208,416]{2,1,0:T(8,128)(2,1)} %w_ref.1) | copy-start | bytes 2076676
  2.4 5.9 %collective-permute-start = (bf16[352,128]{1,0:T(8,128)(2,1)S(1)}, bf16[352,128]{1,0:T(8,128)(2,1)S(1)}, u32[]{:S(2)}, u32[]{:S(2)}) collective-permute-start(bf16[352,128]{1,0:T(8,128)(2,1)S(1)} %get-tuple-element.41), channel_id=1, source_target_pairs={{0,4},{4,0},{8,12},{12,8},{1,5},{5,1},{9,13},{13,9},{2,6},{6,2},{1... | collective-permute-start | bytes 270344 | tf_op jit(solution)/shard_map/ppermute | solution.py:298
  2.4 18.4 %collective-permute-start.3 = (bf16[352,128]{1,0:T(8,128)(2,1)S(1)}, bf16[352,128]{1,0:T(8,128)(2,1)S(1)}, u32[]{:S(2)}, u32[]{:S(2)}) collective-permute-start(bf16[352,128]{1,0:T(8,128)(2,1)S(1)} %get-tuple-element.45), channel_id=1, source_target_pairs={{0,8},{4,12},{8,0},{12,4},{1,9},{5,13},{9,1},{13,5},{2,10},{6,14},... | collective-permute-start | bytes 270344 | tf_op jit(solution)/shard_map/ppermute | solution.py:298
  5.5 18.5 %collective-permute-start.4 = (bf16[352,128]{1,0:T(8,128)(2,1)S(1)}, bf16[352,128]{1,0:T(8,128)(2,1)S(1)}, u32[]{:S(2)}, u32[]{:S(2)}) collective-permute-start(bf16[352,128]{1,0:T(8,128)(2,1)S(1)} %get-tuple-element.46), channel_id=1, source_target_pairs={{0,12},{4,8},{8,4},{12,0},{1,13},{5,9},{9,5},{13,1},{2,14},{6,10},... | collective-permute-start | bytes 270344 | tf_op jit(solution)/shard_map/ppermute | solution.py:298
  5.9 1.0 %copy-start = (bf16[1,128,1664]{2,1,0:T(8,128)(2,1)S(1)}, bf16[1,128,1664]{2,1,0:T(8,128)(2,1)}, u32[]{:S(2)}) copy-start(bf16[1,128,1664]{2,1,0:T(8,128)(2,1)} %param.3) | copy-start | bytes 1277956
  6.9 1.0 %copy-start.2 = (bf16[1,128,1664]{2,1,0:T(8,128)(2,1)S(1)}, bf16[1,128,1664]{2,1,0:T(8,128)(2,1)}, u32[]{:S(2)}) copy-start(bf16[1,128,1664]{2,1,0:T(8,128)(2,1)} %param.4) | copy-start | bytes 1277956
  8.3 24.7 %collective-permute-start.2 = (bf16[128,1664]{1,0:T(8,128)(2,1)S(1)}, bf16[128,1664]{1,0:T(8,128)(2,1)S(1)}, u32[]{:S(2)}, u32[]{:S(2)}) collective-permute-start(bf16[128,1664]{1,0:T(8,128)(2,1)S(1)} %get-tuple-element.42.refs_0_), channel_id=1, source_target_pairs={{0,8},{4,12},{8,0},{12,4},{1,9},{5,13},{9,1},{13,5},{2,10},{6,14},... | collective-permute-start | bytes 1277960 | tf_op jit(solution)/shard_map/ppermute | solution.py:298
  11.8 21.2 %collective-permute-start.1 = (bf16[128,1664]{1,0:T(8,128)(2,1)S(1)}, bf16[128,1664]{1,0:T(8,128)(2,1)S(1)}, u32[]{:S(2)}, u32[]{:S(2)}) collective-permute-start(bf16[128,1664]{1,0:T(8,128)(2,1)S(1)} %get-tuple-element.42.refs_0_), channel_id=1, source_target_pairs={{0,4},{4,0},{8,12},{12,8},{1,5},{5,1},{9,13},{13,9},{2,6},{6,2},{1... | collective-permute-start | bytes 1277960 | tf_op jit(solution)/shard_map/ppermute | solution.py:298
  24.0 7.6 %collective-permute-start.6 = (bf16[1408,128]{1,0:T(8,128)(2,1)S(1)}, bf16[1408,128]{1,0:T(8,128)(2,1)S(1)}, u32[]{:S(2)}, u32[]{:S(2)}) collective-permute-start(bf16[1408,128]{1,0:T(8,128)(2,1)S(1)} %shard_map.52.refs_0_), channel_id=1, source_target_pairs={{0,16},{16,0},{1,17},{17,1},{2,18},{18,2},{3,19},{19,3},{4,20},{20... | collective-permute-start | bytes 1081352 | tf_op jit(solution)/shard_map/ppermute | solution.py:304
  25.6 7.4 %collective-permute-start.5 = (bf16[1408,128]{1,0:T(8,128)(2,1)S(1)}, bf16[1408,128]{1,0:T(8,128)(2,1)S(1)}, u32[]{:S(2)}, u32[]{:S(2)}) collective-permute-start(bf16[1408,128]{1,0:T(8,128)(2,1)S(1)} %shard_map.52.refs_0_), channel_id=1, source_target_pairs={{0,2},{2,0},{1,3},{3,1},{4,6},{6,4},{5,7},{7,5},{8,10},{10,8},{9,1... | collective-permute-start | bytes 1081352 | tf_op jit(solution)/shard_map/ppermute | solution.py:304
  33.0 10.5 %collective-permute-start.10 = (bf16[128,1664]{1,0:T(8,128)(2,1)S(1)}, bf16[128,1664]{1,0:T(8,128)(2,1)S(1)}, u32[]{:S(2)}, u32[]{:S(2)}) collective-permute-start(bf16[128,1664]{1,0:T(8,128)(2,1)S(1)} %collective-permute-done.2.refs_4_), channel_id=1, source_target_pairs={{0,4},{4,0},{8,12},{12,8},{1,5},{5,1},{9,13},{13,9},{2,6},{6,2},{1... | collective-permute-start | bytes 1277960 | tf_op jit(solution)/shard_map/ppermute | solution.py:298
  33.5 9.1 %collective-permute-start.9 = (bf16[1408,128]{1,0:T(8,128)(2,1)S(1)}, bf16[1408,128]{1,0:T(8,128)(2,1)S(1)}, u32[]{:S(2)}, u32[]{:S(2)}) collective-permute-start(bf16[1408,128]{1,0:T(8,128)(2,1)S(1)} %collective-permute-done.6.refs_2_), channel_id=1, source_target_pairs={{0,2},{2,0},{1,3},{3,1},{4,6},{6,4},{5,7},{7,5},{8,10},{10,8},{9,1... | collective-permute-start | bytes 1081352 | tf_op jit(solution)/shard_map/ppermute | solution.py:304
  35.0 8.6 %collective-permute-start.8 = (bf16[128,1664]{1,0:T(8,128)(2,1)S(1)}, bf16[128,1664]{1,0:T(8,128)(2,1)S(1)}, u32[]{:S(2)}, u32[]{:S(2)}) collective-permute-start(bf16[128,1664]{1,0:T(8,128)(2,1)S(1)} %collective-permute-done.2.refs_4_), channel_id=1, source_target_pairs={{0,1},{1,0},{2,3},{3,2},{4,5},{5,4},{6,7},{7,6},{8,9},{9,8},{10,11... | collective-permute-start | bytes 1277960 | tf_op jit(solution)/shard_map/ppermute | solution.py:304
  35.0 8.6 %collective-permute-start.7 = (bf16[128,1664]{1,0:T(8,128)(2,1)S(1)}, bf16[128,1664]{1,0:T(8,128)(2,1)S(1)}, u32[]{:S(2)}, u32[]{:S(2)}) collective-permute-start(bf16[128,1664]{1,0:T(8,128)(2,1)S(1)} %collective-permute-done.1.refs_2_), channel_id=1, source_target_pairs={{0,1},{1,0},{2,3},{3,2},{4,5},{5,4},{6,7},{7,6},{8,9},{9,8},{10,11... | collective-permute-start | bytes 1277960 | tf_op jit(solution)/shard_map/ppermute | solution.py:304
  43.5 1.8 %collective-permute-start.11 = (bf16[128,1664]{1,0:T(8,128)(2,1)S(1)}, bf16[128,1664]{1,0:T(8,128)(2,1)S(1)}, u32[]{:S(2)}, u32[]{:S(2)}) collective-permute-start(bf16[128,1664]{1,0:T(8,128)(2,1)S(1)} %collective-permute-done.10.refs_0_), channel_id=1, source_target_pairs={{0,1},{1,0},{2,3},{3,2},{4,5},{5,4},{6,7},{7,6},{8,9},{9,8},{10,11... | collective-permute-start | bytes 1277960 | tf_op jit(solution)/shard_map/ppermute | solution.py:304
  48.1 4.0 %collective-permute-start.13 = (bf16[4,64,1664]{2,1,0:T(8,128)(2,1)S(1)}, bf16[4,64,1664]{2,1,0:T(8,128)(2,1)S(1)}, u32[]{:S(2)}, u32[]{:S(2)}) collective-permute-start(bf16[4,64,1664]{2,1,0:T(8,128)(2,1)S(1)} %get-tuple-element.62), channel_id=1, source_target_pairs={{0,1},{1,0},{2,3},{3,2},{4,5},{5,4},{6,7},{7,6},{8,9},{9,8},{10,11... | collective-permute-start | bytes 2555912 | tf_op jit(solution)/shard_map/ppermute | solution.py:304
  50.5 31.4 %copy-start.1 = (bf16[1,128,1664]{2,1,0:T(8,128)(2,1)S(1)}, bf16[1,128,1664]{2,1,0:T(8,128)(2,1)}, u32[]{:S(2)}) copy-start(bf16[1,128,1664]{2,1,0:T(8,128)(2,1)} %param.3) | copy-start | bytes 1277956
  50.5 31.4 %copy-start.3 = (bf16[1,128,1664]{2,1,0:T(8,128)(2,1)S(1)}, bf16[1,128,1664]{2,1,0:T(8,128)(2,1)}, u32[]{:S(2)}) copy-start(bf16[1,128,1664]{2,1,0:T(8,128)(2,1)} %param.4) | copy-start | bytes 1277956
  50.6 18.1 %collective-permute-start.12 = (bf16[4,688,128]{2,1,0:T(8,128)(2,1)S(1)}, bf16[4,688,128]{2,1,0:T(8,128)(2,1)S(1)}, u32[]{:S(2)}, u32[]{:S(2)}) collective-permute-start(bf16[4,688,128]{2,1,0:T(8,128)(2,1)S(1)} %get-tuple-element.60), channel_id=1, source_target_pairs={{0,2},{2,0},{1,3},{3,1},{4,6},{6,4},{5,7},{7,5},{8,10},{10,8},{9,1... | collective-permute-start | bytes 2113544 | tf_op jit(solution)/shard_map/ppermute | solution.py:304
  52.3 18.7 %collective-permute-start.14 = (bf16[64,1664]{1,0:T(8,128)(2,1)S(1)}, bf16[64,1664]{1,0:T(8,128)(2,1)S(1)}, u32[]{:S(2)}, u32[]{:S(2)}) collective-permute-start(bf16[64,1664]{1,0:T(8,128)(2,1)S(1)} %get-tuple-element.65), channel_id=1, source_target_pairs={{0,8},{4,12},{8,0},{12,4},{1,9},{5,13},{9,1},{13,5},{2,10},{6,14},... | collective-permute-start | bytes 638984 | tf_op jit(solution)/shard_map/ppermute | solution.py:298
  54.0 27.9 %collective-permute-start.15 = (bf16[64,1664]{1,0:T(8,128)(2,1)S(1)}, bf16[64,1664]{1,0:T(8,128)(2,1)S(1)}, u32[]{:S(2)}, u32[]{:S(2)}) collective-permute-start(bf16[64,1664]{1,0:T(8,128)(2,1)S(1)} %get-tuple-element.66), channel_id=1, source_target_pairs={{0,12},{4,8},{8,4},{12,0},{1,13},{5,9},{9,5},{13,1},{2,14},{6,10},... | collective-permute-start | bytes 638984 | tf_op jit(solution)/shard_map/ppermute | solution.py:298
  54.5 27.4 %collective-permute-start.16 = (bf16[64,1664]{1,0:T(8,128)(2,1)S(1)}, bf16[64,1664]{1,0:T(8,128)(2,1)S(1)}, u32[]{:S(2)}, u32[]{:S(2)}) collective-permute-start(bf16[64,1664]{1,0:T(8,128)(2,1)S(1)} %get-tuple-element.67), channel_id=1, source_target_pairs={{0,4},{4,0},{8,12},{12,8},{1,5},{5,1},{9,13},{13,9},{2,6},{6,2},{1... | collective-permute-start | bytes 638984 | tf_op jit(solution)/shard_map/ppermute | solution.py:298
  68.9 15.8 %collective-permute-start.19 = (bf16[688,128]{1,0:T(8,128)(2,1)S(1)}, bf16[688,128]{1,0:T(8,128)(2,1)S(1)}, u32[]{:S(2)}, u32[]{:S(2)}) collective-permute-start(bf16[688,128]{1,0:T(8,128)(2,1)S(1)} %get-tuple-element.73), channel_id=1, source_target_pairs={{0,8},{4,12},{8,0},{12,4},{1,9},{5,13},{9,1},{13,5},{2,10},{6,14},... | collective-permute-start | bytes 528392 | tf_op jit(solution)/shard_map/ppermute | solution.py:298
  70.5 18.1 %collective-permute-start.20 = (bf16[688,128]{1,0:T(8,128)(2,1)S(1)}, bf16[688,128]{1,0:T(8,128)(2,1)S(1)}, u32[]{:S(2)}, u32[]{:S(2)}) collective-permute-start(bf16[688,128]{1,0:T(8,128)(2,1)S(1)} %get-tuple-element.74), channel_id=1, source_target_pairs={{0,12},{4,8},{8,4},{12,0},{1,13},{5,9},{9,5},{13,1},{2,14},{6,10},... | collective-permute-start | bytes 528392 | tf_op jit(solution)/shard_map/ppermute | solution.py:298
  71.1 17.5 %collective-permute-start.21 = (bf16[688,128]{1,0:T(8,128)(2,1)S(1)}, bf16[688,128]{1,0:T(8,128)(2,1)S(1)}, u32[]{:S(2)}, u32[]{:S(2)}) collective-permute-start(bf16[688,128]{1,0:T(8,128)(2,1)S(1)} %get-tuple-element.75), channel_id=1, source_target_pairs={{0,4},{4,0},{8,12},{12,8},{1,5},{5,1},{9,13},{13,9},{2,6},{6,2},{1... | collective-permute-start | bytes 528392 | tf_op jit(solution)/shard_map/ppermute | solution.py:298
  82.4 6.2 %collective-permute-start.17 = (bf16[32,1664]{1,0:T(8,128)(2,1)S(1)}, bf16[32,1664]{1,0:T(8,128)(2,1)S(1)}, u32[]{:S(2)}, u32[]{:S(2)}) collective-permute-start(bf16[32,1664]{1,0:T(8,128)(2,1)S(1)} %get-tuple-element.68.refs_0_), channel_id=1, source_target_pairs={{0,1},{1,0},{2,3},{3,2},{4,5},{5,4},{6,7},{7,6},{8,9},{9,8},{10,11... | collective-permute-start | bytes 319496 | tf_op jit(solution)/shard_map/ppermute | solution.py:304
  82.5 6.2 %collective-permute-start.18 = (bf16[32,1664]{1,0:T(8,128)(2,1)S(1)}, bf16[32,1664]{1,0:T(8,128)(2,1)S(1)}, u32[]{:S(2)}, u32[]{:S(2)}) collective-permute-start(bf16[32,1664]{1,0:T(8,128)(2,1)S(1)} %get-tuple-element.69.refs_1_), channel_id=1, source_target_pairs={{0,1},{1,0},{2,3},{3,2},{4,5},{5,4},{6,7},{7,6},{8,9},{9,8},{10,11... | collective-permute-start | bytes 319496 | tf_op jit(solution)/shard_map/ppermute | solution.py:304
